TPU v7x, 512 devices: a whole 4x8x8 slice. The times are simulated.
512 devices in a mesh: prompt: 16 (over x, y_lo), feat: 32 (over y_hi, z, core).
Axes of the slice: x: 4, y: 8 (y_hi: 2, y_lo: 4; y = y_hi * 4 + y_lo), z: 8, core: 2. Of those that a mesh axis runs over, the one named last changes fastest.
Arguments:
- decoder: bfloat16 [8192, 5376], P('feat'), may hold values from -0.078125 to 0.078125
- encoder: bfloat16 [24576, 5376], P(('feat', 'prompt')), may hold values from -6 to 6
- row_ids: int32 [16, 512], P('prompt', 'feat'), may hold values from 0 to 255
- counts: int32 [16, 32], P('prompt'), may hold values from 1 to 16, 307 in all within a row
- activity: float32 [16, 512], P('prompt'), may hold values from 0.25 to 4
Outputs:
- edges: bfloat16 [16, 512, 24576], P('prompt', None, 'feat')
Inputs may be any that keep to these rules, and one draw needn't show every extreme that they name: counts of one prompt sum to 307; some owner of each prompt holds exactly 16.
All inputs are finite; a program needn't handle non-finite values.
Results may differ from a plain program's by a relative error of at most 0.001.
Values may be sent and summed in bfloat16 or wider, within the bound.
No kernel may reach another device: no remote copies, remote signals or barrier semaphores. Data moves between devices by JAX's collectives and lax.ppermute only.
A program may use at most 64 MiB of HBM per device.

v0:
```python
import jax
import jax.numpy as jnp
from jax import lax
from jax.sharding import PartitionSpec as P


def per_device(decoder, encoder, row_ids, counts, activity):
    slot_count = row_ids.shape[1]
    owner_index = lax.axis_index("feat")
    picked_rows = jnp.take(decoder, row_ids[0], axis=0)
    live_count = lax.dynamic_index_in_dim(counts[0], owner_index, 0, keepdims=False)
    live_slots = jnp.arange(slot_count, dtype=jnp.int32) < live_count
    source_rows = jnp.where(live_slots[:, None], picked_rows, jnp.zeros((), picked_rows.dtype))
    weights = activity[0]
    whole_rows = lax.all_gather(source_rows, "feat", axis=0, tiled=True)
    products = lax.dot_general(
        whole_rows,
        lax.all_gather(encoder, "prompt", axis=0, tiled=True),
        (((1,), (1,)), ((), ())),
        preferred_element_type=jnp.float32,
    )
    edges = (weights[:, None] * products).astype(jnp.bfloat16)
    return edges[None]


def solution(mesh):
    in_specs = (
        P("feat", None),
        P(("feat", "prompt"), None),
        P("prompt", "feat"),
        P("prompt", None),
        P("prompt", None),
    )
    out_specs = P("prompt", None, "feat")
    return jax.shard_map(
        per_device, mesh=mesh, in_specs=in_specs, out_specs=out_specs, check_vma=False
    )
```

profile of v0, /device:TPU:1, one launch (start us, length us, event | category | flops | bytes accessed | tf_op | source)
XLA Modules:
  0.0 330.1 jit_solution(3956088950940566915)
XLA Ops:
  6.5 0.0 copy-start
  6.5 0.0 all-gather.3.cloned.1.call-start
  6.5 0.8 fusion.1
  7.3 1.3 constant_dynamic-slice_fusion
  8.6 1.3 compare_and_fusion
  9.9 0.0 copy-done
  9.9 0.7 gather_fusion
  10.6 0.8 select_select_fusion
  11.4 0.0 all-gather.3.cloned.1.call-update
  11.4 0.0 all-gather.5.cloned.1.call-start
  11.4 0.7 all-gather.5.cloned.1.call-update
  12.1 120.5 %all-gather.3.cloned.1.call-done = bf16[512,5376]{1,0:T(8,128)(2,1)} async-done(((bf16[16,5376]{1,0:T(8,128)(2,1)}), bf16[512,5376]{1,0:T(8,128)(2,1)}) %all-gather.3.cloned.1.call-update) | async-done | bytes 5505040 | tf_op jit(solution)/shard_map/all_gather | solution.py:15
  132.7 180.4 %all-gather.5.cloned.1.call-done = bf16[768,5376]{1,0:T(8,128)(2,1)} async-done(((bf16[48,5376]{1,0:T(8,128)(2,1)}), bf16[768,5376]{1,0:T(8,128)(2,1)}) %all-gather.5.cloned.1.call-update) | async-done | bytes 8257552 | tf_op jit(solution)/shard_map/all_gather | solution.py:18
  313.0 10.2 %fusion = bf16[1,512,768]{2,1,0:T(8,128)(2,1)} fusion(bf16[512,5376]{1,0:T(8,128)(2,1)} %all-gather.3.cloned.1.call-done, bf16[768,5376]{1,0:T(8,128)(2,1)} %all-gather.5.cloned.1.call-done, f32[512]{0:T(512)} %bitcast.12), kind=kOutput, calls=%fused_computation.2 | convolution fusion | flops 4228644864 | bytes 14551040 | tf_op jit(solution)/shard_map/dot_general | solution.py:16
  (1 shorter events, 0.0 us)
Async XLA Ops:
  6.5 3.4 %copy-start = (bf16[256,5376]{1,0:T(8,128)(2,1)S(1)}, bf16[256,5376]{1,0:T(8,128)(2,1)}, u32[]{:S(2)}) copy-start(bf16[256,5376]{1,0:T(8,128)(2,1)} %param.5) | copy-start | bytes 8257540
  6.5 126.1 %all-gather.3.cloned.1.call-start = ((), (), s32[]{:S(2)}) async-start(), calls=%async_computation | async-start | bytes 5677056 | tf_op jit(solution)/shard_map/all_gather | solution.py:15
  11.4 301.6 %all-gather.5.cloned.1.call-start = ((), (), s32[]{:S(2)}) async-start(), calls=%async_computation.1 | async-start | bytes 8773632 | tf_op jit(solution)/shard_map/all_gather | solution.py:18
Sparse Core Ops, SparseCore 0:
  11.5 121.0 all-gather.2
  134.7 178.2 all-gather.4
where the time goes:
time: 330 us
  waiting for transfers between devices  302 us (92%)
  between operations  13.4 us (4%)
  matrix products  10.2 us (3%)
    all_gather x1, waiting for transfers between devices, per_device(): lax.all_gather(encoder, 'prompt', axis=0, tiled=True)  180 us
    all_gather x1, waiting for transfers between devices, per_device(): whole_rows = lax.all_gather(source_rows, 'feat', axis=0, tiled=True)  121 us
    dot_general x1, matrix products, per_device(): lax.dot_general(whole_rows, lax.all_gather(encoder, 'prompt', axis=0, til...  10.2 us
  transfers between devices with their start and end apart: 2, of which 2 were waited for; matrix products, arithmetic and copies ran while one was open for 0% of the time, Pallas kernels for 0%

commit v1 on v0

v1 whole, which is shorter than its diff:
```python
import jax
import jax.numpy as jnp
from jax import lax
from jax.experimental import pallas as pl
from jax.experimental.pallas import tpu as pltpu
from jax.sharding import PartitionSpec as P


AXES = ("prompt", "feat")


def routes(move):
    pairs = []
    for x in range(4):
        for y in range(8):
            for z in range(8):
                for core in range(2):
                    pairs.append((flat(x, y, z, core), flat(*move(x, y, z, core))))
    return pairs


def flat(x, y, z, core):
    prompt = (x % 4) * 4 + y % 4
    feat = ((y // 4) % 2 * 8 + z % 8) * 2 + core
    return prompt * 32 + feat


RING_X = routes(lambda x, y, z, c: (x + (1 - 2 * c), y, z, c))
RING_Y = routes(lambda x, y, z, c: (x, y // 4 * 4 + (y + (1 - 2 * c)) % 4, z, c))
RING_Z = routes(lambda x, y, z, c: (x, y, z + (1 - 2 * c), c))
OTHER_Y = routes(lambda x, y, z, c: (x, (y + 4) % 8, z, c))
CORE = routes(lambda x, y, z, c: (x, y, z, 1 - c))


def send(value, pairs):
    return lax.ppermute(value, AXES, pairs)


def product_kernel(row_at, act_ref, order_ref, *refs):
    n_rows = act_ref.shape[0]
    operands, (out_ref, rows, cols, acc, sem) = refs[:-5], refs[-5:]
    copies, at, into = [], 0, rows
    for i, operand in enumerate(operands):
        if at == n_rows and into is rows:
            at, into = 0, cols
        size = operand.shape[0]
        copies.append(pltpu.make_async_copy(operand, into.at[pl.ds(at, size)], sem.at[i]))
        at += size
    for copy in copies:
        copy.start()
    for copy in copies:
        copy.wait()
    depth = rows.shape[1]
    step = 768
    acc[...] = jnp.zeros_like(acc)

    @pl.loop(0, depth // step)
    def _(k):
        part = pl.ds(pl.multiple_of(k * step, step), step)
        acc[...] += lax.dot_general(
            rows[:, part], cols[:, part], (((1,), (1,)), ((), ())), preferred_element_type=jnp.float32
        )

    edges = (acc[...] * act_ref[...]).astype(jnp.bfloat16)
    placed = jnp.dot(edges, order_ref[...], preferred_element_type=jnp.float32).astype(jnp.bfloat16)
    for g in range(n_rows // 16):
        out_ref[pl.ds(pl.multiple_of(row_at[g], 16), 16), :] = placed[g * 16 : (g + 1) * 16]


def product(row_at, act, order, sources, targets):
    n_rows, n_cols, depth = act.shape[0], order.shape[0], sources[0].shape[1]
    whole = pl.BlockSpec(memory_space=pltpu.VMEM)
    return pl.pallas_call(
        product_kernel,
        out_shape=jax.ShapeDtypeStruct((n_rows, n_cols), jnp.bfloat16),
        in_specs=[pl.BlockSpec(memory_space=pltpu.SMEM), whole, whole]
        + [pl.BlockSpec(memory_space=pl.ANY)] * (len(sources) + len(targets)),
        out_specs=whole,
        scratch_shapes=[
            pltpu.VMEM((n_rows, depth), jnp.bfloat16),
            pltpu.VMEM((n_cols, depth), jnp.bfloat16),
            pltpu.VMEM((n_rows, n_cols), jnp.float32),
            pltpu.SemaphoreType.DMA((len(sources) + len(targets),)),
        ],
        compiler_params=pltpu.CompilerParams(vmem_limit_bytes=40 << 20),
        name="product",
    )(row_at, act, order, *sources, *targets)


def edges_of(decoder, encoder, row_ids, counts, activity):
    slot_count = row_ids.shape[1]
    prompt, owner = lax.axis_index("prompt"), lax.axis_index("feat")
    core, chip = owner % 2, owner // 2
    half, z = chip // 8, chip % 8
    x, y = prompt // 4, prompt % 4
    sign = 1 - 2 * core

    picked_rows = jnp.take(decoder, row_ids[0], axis=0)
    live_count = lax.dynamic_index_in_dim(counts[0], owner, 0, keepdims=False)
    live_slots = jnp.arange(slot_count, dtype=jnp.int32) < live_count
    source_rows = jnp.where(live_slots[:, None], picked_rows, jnp.zeros((), picked_rows.dtype))

    y0 = encoder
    y1 = send(y0, RING_Y)
    y2 = send(y1, RING_Y)
    y3 = send(y2, RING_Y)
    targets = []
    for block in (y0, y1, y2, y3):
        targets.append(block)
        for step in "123":
            block = send(block, RING_X)
            targets.append(block)

    both = jnp.concatenate([source_rows, send(source_rows, OTHER_Y)], axis=0)
    chunk = jnp.concatenate([both, send(both, CORE)], axis=0)
    sources, swaps = [chunk], []
    for step in "1234":
        chunk = send(chunk, RING_Z)
        sources.append(chunk)
        if step != "4":
            swaps.append(send(chunk, CORE))
    sources += swaps

    hop = jnp.array([0, -1, -2, -3, -4, 1, 2, 3], jnp.int32)[:, None, None]
    lead = jnp.array([0, 0, 0, 0, 0, 1, 1, 1], jnp.int32)[:, None, None]
    side = jnp.arange(2, dtype=jnp.int32)[None, :, None]
    flip = jnp.arange(2, dtype=jnp.int32)[None, None, :]
    z_from = (z + sign * hop) % 8
    feat_from = ((half ^ flip) * 8 + z_from) * 2 + (core ^ lead ^ side)
    group_from = feat_from.reshape(-1).astype(jnp.int32)
    ring = jnp.arange(4, dtype=jnp.int32)
    x_from = (x - sign * ring) % 4
    y_from = (y - sign * ring) % 4
    origin = (x_from[None, :] * 4 + y_from[:, None]).reshape(-1)
    width = encoder.shape[0]
    col_at = (origin[:, None] * width + jnp.arange(width, dtype=jnp.int32)[None, :]).reshape(-1)
    order = (col_at[:, None] == jnp.arange(col_at.shape[0], dtype=jnp.int32)[None, :]).astype(jnp.bfloat16)
    act = activity[0].reshape(-1, slot_count)[group_from].reshape(-1, 1)

    return product(group_from * slot_count, act, order, sources, targets)[None]


def solution(mesh):
    in_specs = (
        P("feat", None),
        P(("feat", "prompt"), None),
        P("prompt", "feat"),
        P("prompt", None),
        P("prompt", None),
    )
    out_specs = P("prompt", None, "feat")
    return jax.shard_map(edges_of, mesh=mesh, in_specs=in_specs, out_specs=out_specs, check_vma=False)
```

time: 330 us -> 146 us (0.44)
  waiting for transfers between devices: 302 us -> 19.1 us
  starting transfers between devices: 0.04 us -> 101 us
  Pallas kernels: 0 us -> 14 us
  between operations: 13.4 us -> 0.51 us
  matrix products: 10.2 us -> 0 us
  local copies, waits for them, and re-layouts: 1.92 us -> 6.05 us
    all_gather x2 -> x0, waiting for transfers between devices: 301 us -> none  [the longest x1 180 us: per_device(): lax.all_gather(encoder, 'prompt', axis=0, tiled=True)]
    ppermute x0 -> x24, starting transfers between devices: none -> 101 us  [send(): return lax.ppermute(value, AXES, pairs)]
    ppermute x0 -> x24, waiting for transfers between devices: none -> 19.1 us  [send(): return lax.ppermute(value, AXES, pairs)]
    pallas_call x0 -> x1, Pallas kernels: none -> 14 us  [product(): pl.pallas_call(product_kernel, out_shape=jax.ShapeDtypeStruct((n_rows, n_...]
    dot_general x1 -> x0, matrix products: 10.2 us -> none  [per_device(): lax.dot_general(whole_rows, lax.all_gather(encoder, 'prompt', axis=0, til...]
  transfers between devices with their start and end apart: 2 -> 24, of which waited for: 2 -> 5; matrix products, arithmetic and copies ran while one was open for 0% -> 3% of each run, Pallas kernels for 0% -> 0%
where the time goes in v1:
time: 146 us; the launch traced here: 145 us
  starting transfers between devices  101 us (69%)
  waiting for transfers between devices  19.1 us (13%)
  Pallas kernels  14 us (10%)
  local copies, waits for them, and re-layouts  6.05 us (4%)
  other arithmetic  4.48 us (3%)
    ppermute x24, starting transfers between devices, send(): return lax.ppermute(value, AXES, pairs)  101 us
    ppermute x24, waiting for transfers between devices, send(): return lax.ppermute(value, AXES, pairs)  19.1 us
    pallas_call x1, Pallas kernels, product(): pl.pallas_call(product_kernel, out_shape=jax.ShapeDtypeStruct((n_rows, n_...  14 us
  transfers between devices with their start and end apart: 24, of which 5 were waited for; matrix products, arithmetic and copies ran while one was open for 3% of the time, Pallas kernels for 0%

profile of v1, /device:TPU:1, one launch (start us, length us, event | category | flops | bytes accessed | tf_op | source)
XLA Modules:
  0.0 145.4 jit_solution(5670815485731693058)
XLA Ops:
  0.0 0.8 fusion.6
  0.8 1.3 constant_dynamic-slice_fusion
  2.1 1.3 compare_and_fusion
  3.4 0.7 gather_fusion.1
  4.1 0.1 select_select_fusion
  4.2 8.3 %collective-permute-start = (bf16[16,5376]{1,0:T(8,128)(2,1)S(1)}, bf16[16,5376]{1,0:T(8,128)(2,1)S(1)}, u32[]{:S(2)}, u32[]{:S(2)}) collective-permute-start(bf16[16,5376]{1,0:T(8,128)(2,1)S(1)} %select_select_fusion), channel_id=1, source_target_pairs={{0,16},{1,17},{2,18},{3,19},{4,20},{5,21},{6,22},{7,23},{8,24},{9,... | collective-permute-start | bytes 516104 | tf_op jit(solution)/shard_map/ppermute | solution.py:36
  12.5 6.8 %collective-permute-done = bf16[16,5376]{1,0:T(8,128)(2,1)S(1)} collective-permute-done((bf16[16,5376]{1,0:T(8,128)(2,1)S(1)}, bf16[16,5376]{1,0:T(8,128)(2,1)S(1)}, u32[]{:S(2)}, u32[]{:S(2)}) %collective-permute-start) | collective-permute-done | bytes 172064 | tf_op jit(solution)/shard_map/ppermute | solution.py:36
  19.3 6.9 %collective-permute-start.1 = (bf16[32,5376]{1,0:T(8,128)(2,1)S(1)}, bf16[32,5376]{1,0:T(8,128)(2,1)S(1)}, u32[]{:S(2)}, u32[]{:S(2)}) collective-permute-start(bf16[32,5376]{1,0:T(8,128)(2,1)S(1)} %pad_maximum_fusion.1), channel_id=1, source_target_pairs={{0,1},{1,0},{2,3},{3,2},{4,5},{5,4},{6,7},{7,6},{8,9},{9,8},{10,11... | collective-permute-start | bytes 1032200 | tf_op jit(solution)/shard_map/ppermute | solution.py:36
  26.2 1.9 %collective-permute-start.9 = (bf16[48,5376]{1,0:T(8,128)(2,1)}, bf16[48,5376]{1,0:T(8,128)(2,1)}, u32[]{:S(2)}, u32[]{:S(2)}) collective-permute-start(bf16[48,5376]{1,0:T(8,128)(2,1)} %refs_8_.1), channel_id=1, source_target_pairs={{0,128},{1,385},{2,130},{3,387},{4,132},{5,389},{6,134},{7,391},{8... | collective-permute-start | bytes 1548296 | tf_op jit(solution)/shard_map/ppermute | solution.py:36
  28.1 3.6 %collective-permute-start.12 = (bf16[48,5376]{1,0:T(8,128)(2,1)}, bf16[48,5376]{1,0:T(8,128)(2,1)}, u32[]{:S(2)}, u32[]{:S(2)}) collective-permute-start(bf16[48,5376]{1,0:T(8,128)(2,1)} %refs_8_.1), channel_id=1, source_target_pairs={{0,32},{1,97},{2,34},{3,99},{4,36},{5,101},{6,38},{7,103},{8,40},{... | collective-permute-start | bytes 1548296 | tf_op jit(solution)/shard_map/ppermute | solution.py:36
  31.8 10.7 %collective-permute-start.2 = (bf16[64,5376]{1,0:T(8,128)(2,1)S(1)}, bf16[64,5376]{1,0:T(8,128)(2,1)}, u32[]{:S(2)}, u32[]{:S(2)}) collective-permute-start(bf16[64,5376]{1,0:T(8,128)(2,1)S(1)} %pad_maximum_fusion.refs_0_), channel_id=1, source_target_pairs={{0,2},{1,15},{2,4},{3,1},{4,6},{5,3},{6,8},{7,5},{8,10},{9,7},{10,... | collective-permute-start | bytes 2064392 | tf_op jit(solution)/shard_map/ppermute | solution.py:36
  42.5 5.4 %collective-permute-start.16 = (bf16[48,5376]{1,0:T(8,128)(2,1)}, bf16[48,5376]{1,0:T(8,128)(2,1)}, u32[]{:S(2)}, u32[]{:S(2)}) collective-permute-start(bf16[48,5376]{1,0:T(8,128)(2,1)} %collective-permute-done.12.refs_12_), channel_id=1, source_target_pairs={{0,32},{1,97},{2,34},{3,99},{4,36},{5,101},{6,38},{7,103},{8,40},{... | collective-permute-start | bytes 1548296 | tf_op jit(solution)/shard_map/ppermute | solution.py:36
  47.8 2.9 %collective-permute-start.10 = (bf16[48,5376]{1,0:T(8,128)(2,1)}, bf16[48,5376]{1,0:T(8,128)(2,1)}, u32[]{:S(2)}, u32[]{:S(2)}) collective-permute-start(bf16[48,5376]{1,0:T(8,128)(2,1)} %collective-permute-done.9.refs_9_), channel_id=1, source_target_pairs={{0,128},{1,385},{2,130},{3,387},{4,132},{5,389},{6,134},{7,391},{8... | collective-permute-start | bytes 1548296 | tf_op jit(solution)/shard_map/ppermute | solution.py:36
  50.7 2.8 %collective-permute-start.13 = (bf16[48,5376]{1,0:T(8,128)(2,1)}, bf16[48,5376]{1,0:T(8,128)(2,1)}, u32[]{:S(2)}, u32[]{:S(2)}) collective-permute-start(bf16[48,5376]{1,0:T(8,128)(2,1)} %collective-permute-done.12.refs_12_), channel_id=1, source_target_pairs={{0,128},{1,385},{2,130},{3,387},{4,132},{5,389},{6,134},{7,391},{8... | collective-permute-start | bytes 1548296 | tf_op jit(solution)/shard_map/ppermute | solution.py:36
  53.5 5.9 %collective-permute-done.16.refs_16_ = bf16[48,5376]{1,0:T(8,128)(2,1)} collective-permute-done((bf16[48,5376]{1,0:T(8,128)(2,1)}, bf16[48,5376]{1,0:T(8,128)(2,1)}, u32[]{:S(2)}, u32[]{:S(2)}) %collective-permute-start.16) | collective-permute-done | bytes 516128 | tf_op jit(solution)/shard_map/ppermute | solution.py:36
  59.4 5.6 %collective-permute-start.20 = (bf16[48,5376]{1,0:T(8,128)(2,1)}, bf16[48,5376]{1,0:T(8,128)(2,1)}, u32[]{:S(2)}, u32[]{:S(2)}) collective-permute-start(bf16[48,5376]{1,0:T(8,128)(2,1)} %collective-permute-done.16.refs_16_), channel_id=1, source_target_pairs={{0,32},{1,97},{2,34},{3,99},{4,36},{5,101},{6,38},{7,103},{8,40},{... | collective-permute-start | bytes 1548296 | tf_op jit(solution)/shard_map/ppermute | solution.py:36
  65.0 9.5 %collective-permute-start.3 = (bf16[64,5376]{1,0:T(8,128)(2,1)}, bf16[64,5376]{1,0:T(8,128)(2,1)}, u32[]{:S(2)}, u32[]{:S(2)}) collective-permute-start(bf16[64,5376]{1,0:T(8,128)(2,1)} %collective-permute-done.2.refs_1_), channel_id=1, source_target_pairs={{0,2},{1,15},{2,4},{3,1},{4,6},{5,3},{6,8},{7,5},{8,10},{9,7},{10,... | collective-permute-start | bytes 2064392 | tf_op jit(solution)/shard_map/ppermute | solution.py:36
  74.6 3.6 %collective-permute-start.11 = (bf16[48,5376]{1,0:T(8,128)(2,1)}, bf16[48,5376]{1,0:T(8,128)(2,1)S(1)}, u32[]{:S(2)}, u32[]{:S(2)}) collective-permute-start(bf16[48,5376]{1,0:T(8,128)(2,1)} %collective-permute-done.10.refs_10_), channel_id=1, source_target_pairs={{0,128},{1,385},{2,130},{3,387},{4,132},{5,389},{6,134},{7,391},{8... | collective-permute-start | bytes 1548296 | tf_op jit(solution)/shard_map/ppermute | solution.py:36
  78.2 2.9 %collective-permute-start.17 = (bf16[48,5376]{1,0:T(8,128)(2,1)}, bf16[48,5376]{1,0:T(8,128)(2,1)}, u32[]{:S(2)}, u32[]{:S(2)}) collective-permute-start(bf16[48,5376]{1,0:T(8,128)(2,1)} %collective-permute-done.16.refs_16_), channel_id=1, source_target_pairs={{0,128},{1,385},{2,130},{3,387},{4,132},{5,389},{6,134},{7,391},{8... | collective-permute-start | bytes 1548296 | tf_op jit(solution)/shard_map/ppermute | solution.py:36
  81.1 2.3 %collective-permute-start.14 = (bf16[48,5376]{1,0:T(8,128)(2,1)}, bf16[48,5376]{1,0:T(8,128)(2,1)}, u32[]{:S(2)}, u32[]{:S(2)}) collective-permute-start(bf16[48,5376]{1,0:T(8,128)(2,1)} %collective-permute-done.13.refs_13_), channel_id=1, source_target_pairs={{0,128},{1,385},{2,130},{3,387},{4,132},{5,389},{6,134},{7,391},{8... | collective-permute-start | bytes 1548296 | tf_op jit(solution)/shard_map/ppermute | solution.py:36
  83.5 2.3 %collective-permute-start.21 = (bf16[48,5376]{1,0:T(8,128)(2,1)}, bf16[48,5376]{1,0:T(8,128)(2,1)}, u32[]{:S(2)}, u32[]{:S(2)}) collective-permute-start(bf16[48,5376]{1,0:T(8,128)(2,1)} %collective-permute-done.20.refs_20_), channel_id=1, source_target_pairs={{0,128},{1,385},{2,130},{3,387},{4,132},{5,389},{6,134},{7,391},{8... | collective-permute-start | bytes 1548296 | tf_op jit(solution)/shard_map/ppermute | solution.py:36
  85.9 0.8 copy-done.2
  86.7 1.9 %collective-permute-start.6 = (bf16[64,5376]{1,0:T(8,128)(2,1)}, bf16[64,5376]{1,0:T(8,128)(2,1)}, u32[]{:S(2)}, u32[]{:S(2)}) collective-permute-start(bf16[64,5376]{1,0:T(8,128)(2,1)} %collective-permute-done.2.refs_1_), channel_id=1, source_target_pairs={{0,1},{1,0},{2,3},{3,2},{4,5},{5,4},{6,7},{7,6},{8,9},{9,8},{10,11... | collective-permute-start | bytes 2064392 | tf_op jit(solution)/shard_map/ppermute | solution.py:36
  88.6 4.9 %collective-permute-start.4 = (bf16[64,5376]{1,0:T(8,128)(2,1)}, bf16[64,5376]{1,0:T(8,128)(2,1)}, u32[]{:S(2)}, u32[]{:S(2)}) collective-permute-start(bf16[64,5376]{1,0:T(8,128)(2,1)} %collective-permute-done.3.refs_2_), channel_id=1, source_target_pairs={{0,2},{1,15},{2,4},{3,1},{4,6},{5,3},{6,8},{7,5},{8,10},{9,7},{10,... | collective-permute-start | bytes 2064392 | tf_op jit(solution)/shard_map/ppermute | solution.py:36
  93.5 3.5 %collective-permute-start.18 = (bf16[48,5376]{1,0:T(8,128)(2,1)}, bf16[48,5376]{1,0:T(8,128)(2,1)}, u32[]{:S(2)}, u32[]{:S(2)}) collective-permute-start(bf16[48,5376]{1,0:T(8,128)(2,1)} %collective-permute-done.17.refs_17_), channel_id=1, source_target_pairs={{0,128},{1,385},{2,130},{3,387},{4,132},{5,389},{6,134},{7,391},{8... | collective-permute-start | bytes 1548296 | tf_op jit(solution)/shard_map/ppermute | solution.py:36
  97.1 3.8 %collective-permute-start.15 = (bf16[48,5376]{1,0:T(8,128)(2,1)}, bf16[48,5376]{1,0:T(8,128)(2,1)}, u32[]{:S(2)}, u32[]{:S(2)}) collective-permute-start(bf16[48,5376]{1,0:T(8,128)(2,1)} %collective-permute-done.14.refs_14_), channel_id=1, source_target_pairs={{0,128},{1,385},{2,130},{3,387},{4,132},{5,389},{6,134},{7,391},{8... | collective-permute-start | bytes 1548296 | tf_op jit(solution)/shard_map/ppermute | solution.py:36
  100.9 0.7 collective-permute-done.21.refs_21_
  101.6 4.8 %collective-permute-start.22 = (bf16[48,5376]{1,0:T(8,128)(2,1)}, bf16[48,5376]{1,0:T(8,128)(2,1)}, u32[]{:S(2)}, u32[]{:S(2)}) collective-permute-start(bf16[48,5376]{1,0:T(8,128)(2,1)} %collective-permute-done.21.refs_21_), channel_id=1, source_target_pairs={{0,128},{1,385},{2,130},{3,387},{4,132},{5,389},{6,134},{7,391},{8... | collective-permute-start | bytes 1548296 | tf_op jit(solution)/shard_map/ppermute | solution.py:36
  106.5 0.1 mul.81
  106.6 0.1 broadcast_add_fusion
  106.7 1.9 %collective-permute-start.7 = (bf16[64,5376]{1,0:T(8,128)(2,1)}, bf16[64,5376]{1,0:T(8,128)(2,1)}, u32[]{:S(2)}, u32[]{:S(2)}) collective-permute-start(bf16[64,5376]{1,0:T(8,128)(2,1)} %collective-permute-done.3.refs_2_), channel_id=1, source_target_pairs={{0,1},{1,0},{2,3},{3,2},{4,5},{5,4},{6,7},{7,6},{8,9},{9,8},{10,11... | collective-permute-start | bytes 2064392 | tf_op jit(solution)/shard_map/ppermute | solution.py:36
  108.6 2.4 %collective-permute-start.8 = (bf16[64,5376]{1,0:T(8,128)(2,1)}, bf16[64,5376]{1,0:T(8,128)(2,1)}, u32[]{:S(2)}, u32[]{:S(2)}) collective-permute-start(bf16[64,5376]{1,0:T(8,128)(2,1)} %collective-permute-done.4.refs_3_), channel_id=1, source_target_pairs={{0,1},{1,0},{2,3},{3,2},{4,5},{5,4},{6,7},{7,6},{8,9},{9,8},{10,11... | collective-permute-start | bytes 2064392 | tf_op jit(solution)/shard_map/ppermute | solution.py:36
  111.0 1.9 %collective-permute-start.5 = (bf16[64,5376]{1,0:T(8,128)(2,1)}, bf16[64,5376]{1,0:T(8,128)(2,1)}, u32[]{:S(2)}, u32[]{:S(2)}) collective-permute-start(bf16[64,5376]{1,0:T(8,128)(2,1)} %collective-permute-done.4.refs_3_), channel_id=1, source_target_pairs={{0,2},{1,15},{2,4},{3,1},{4,6},{5,3},{6,8},{7,5},{8,10},{9,7},{10,... | collective-permute-start | bytes 2064392 | tf_op jit(solution)/shard_map/ppermute | solution.py:36
  113.0 0.1 add.182
  113.1 0.1 add.170
  113.2 0.1 mul.76.row_at
  113.3 0.5 broadcast.237
  113.8 0.6 reduce.3
  114.4 0.1 reshape_squeeze.3
  114.5 2.7 %collective-permute-start.19 = (bf16[48,5376]{1,0:T(8,128)(2,1)}, bf16[48,5376]{1,0:T(8,128)(2,1)}, u32[]{:S(2)}, u32[]{:S(2)}) collective-permute-start(bf16[48,5376]{1,0:T(8,128)(2,1)} %collective-permute-done.18.refs_18_), channel_id=1, source_target_pairs={{0,128},{1,385},{2,130},{3,387},{4,132},{5,389},{6,134},{7,391},{8... | collective-permute-start | bytes 1548296 | tf_op jit(solution)/shard_map/ppermute | solution.py:36
  117.2 1.0 collective-permute-done.22.refs_22_
  118.2 4.8 %collective-permute-start.23 = (bf16[48,5376]{1,0:T(8,128)(2,1)}, bf16[48,5376]{1,0:T(8,128)(2,1)}, u32[]{:S(2)}, u32[]{:S(2)}) collective-permute-start(bf16[48,5376]{1,0:T(8,128)(2,1)} %collective-permute-done.22.refs_22_), channel_id=1, source_target_pairs={{0,128},{1,385},{2,130},{3,387},{4,132},{5,389},{6,134},{7,391},{8... | collective-permute-start | bytes 1548296 | tf_op jit(solution)/shard_map/ppermute | solution.py:36
  123.1 0.6 gather_fusion
  123.6 0.9 reshape.230.act_ref
  124.5 1.3 fusion.order_ref
  125.8 4.7 %collective-permute-done.23.refs_23_ = bf16[48,5376]{1,0:T(8,128)(2,1)} collective-permute-done((bf16[48,5376]{1,0:T(8,128)(2,1)}, bf16[48,5376]{1,0:T(8,128)(2,1)}, u32[]{:S(2)}, u32[]{:S(2)}) %collective-permute-start.23) | collective-permute-done | bytes 516128 | tf_op jit(solution)/shard_map/ppermute | solution.py:36
  130.5 0.9 copy-done.1
  131.4 14.0 %product.1 = bf16[512,768]{1,0:T(8,128)(2,1)} custom-call(s32[32]{0:T(128)S(1)} %mul.76.row_at, f32[512,1]{1,0:T(8,128)S(1)} %copy-done.1, bf16[768,768]{1,0:T(8,128)(2,1)} %fusion.order_ref, bf16[64,5376]{1,0:T(8,128)(2,1)S(1)} %pad_maximum_fusion.refs_0_, bf16[64,5376]{1,0:T(8,128)(2,1)} %collective-permute-done.2.refs_1_, ...), custom_call_target="tpu_custom_call" | custom-call | tf_op jit(solution)/shard_map/product/pallas_call | solution.py:73
  (43 shorter events, 0.4 us)
Async XLA Ops:
  0.0 3.4 %copy-start = (bf16[256,5376]{1,0:T(8,128)(2,1)S(1)}, bf16[256,5376]{1,0:T(8,128)(2,1)}, u32[]{:S(2)}) copy-start(bf16[256,5376]{1,0:T(8,128)(2,1)} %param.7) | copy-start | bytes 8257540
  4.1 74.1 %copy-start.6 = (s32[8]{0:T(128)S(1)}, s32[8]{0:T(128)}, u32[]{:S(2)}) copy-start(s32[8]{0:T(128)} %constant.128.clone) | copy-start | bytes 100
  4.1 81.7 %copy-start.5 = (s32[8]{0:T(128)S(1)}, s32[8]{0:T(128)}, u32[]{:S(2)}) copy-start(s32[8]{0:T(128)} %constant.127.clone) | copy-start | bytes 100
  4.1 109.7 %copy-start.4 = (f32[1,512]{1,0:T(1,128)S(1)}, f32[1,512]{1,0:T(1,128)}, u32[]{:S(2)}) copy-start(f32[1,512]{1,0:T(1,128)} %param.11) | copy-start | bytes 6148
  4.2 15.1 %collective-permute-start = (bf16[16,5376]{1,0:T(8,128)(2,1)S(1)}, bf16[16,5376]{1,0:T(8,128)(2,1)S(1)}, u32[]{:S(2)}, u32[]{:S(2)}) collective-permute-start(bf16[16,5376]{1,0:T(8,128)(2,1)S(1)} %select_select_fusion), channel_id=1, source_target_pairs={{0,16},{1,17},{2,18},{3,19},{4,20},{5,21},{6,22},{7,23},{8,24},{9,... | collective-permute-start | bytes 516104 | tf_op jit(solution)/shard_map/ppermute | solution.py:36
  19.3 12.4 %collective-permute-start.1 = (bf16[32,5376]{1,0:T(8,128)(2,1)S(1)}, bf16[32,5376]{1,0:T(8,128)(2,1)S(1)}, u32[]{:S(2)}, u32[]{:S(2)}) collective-permute-start(bf16[32,5376]{1,0:T(8,128)(2,1)S(1)} %pad_maximum_fusion.1), channel_id=1, source_target_pairs={{0,1},{1,0},{2,3},{3,2},{4,5},{5,4},{6,7},{7,6},{8,9},{9,8},{10,11... | collective-permute-start | bytes 1032200 | tf_op jit(solution)/shard_map/ppermute | solution.py:36
  26.2 21.6 %collective-permute-start.9 = (bf16[48,5376]{1,0:T(8,128)(2,1)}, bf16[48,5376]{1,0:T(8,128)(2,1)}, u32[]{:S(2)}, u32[]{:S(2)}) collective-permute-start(bf16[48,5376]{1,0:T(8,128)(2,1)} %refs_8_.1), channel_id=1, source_target_pairs={{0,128},{1,385},{2,130},{3,387},{4,132},{5,389},{6,134},{7,391},{8... | collective-permute-start | bytes 1548296 | tf_op jit(solution)/shard_map/ppermute | solution.py:36
  28.1 14.3 %collective-permute-start.12 = (bf16[48,5376]{1,0:T(8,128)(2,1)}, bf16[48,5376]{1,0:T(8,128)(2,1)}, u32[]{:S(2)}, u32[]{:S(2)}) collective-permute-start(bf16[48,5376]{1,0:T(8,128)(2,1)} %refs_8_.1), channel_id=1, source_target_pairs={{0,32},{1,97},{2,34},{3,99},{4,36},{5,101},{6,38},{7,103},{8,40},{... | collective-permute-start | bytes 1548296 | tf_op jit(solution)/shard_map/ppermute | solution.py:36
  31.8 33.3 %collective-permute-start.2 = (bf16[64,5376]{1,0:T(8,128)(2,1)S(1)}, bf16[64,5376]{1,0:T(8,128)(2,1)}, u32[]{:S(2)}, u32[]{:S(2)}) collective-permute-start(bf16[64,5376]{1,0:T(8,128)(2,1)S(1)} %pad_maximum_fusion.refs_0_), channel_id=1, source_target_pairs={{0,2},{1,15},{2,4},{3,1},{4,6},{5,3},{6,8},{7,5},{8,10},{9,7},{10,... | collective-permute-start | bytes 2064392 | tf_op jit(solution)/shard_map/ppermute | solution.py:36
  42.5 17.0 %collective-permute-start.16 = (bf16[48,5376]{1,0:T(8,128)(2,1)}, bf16[48,5376]{1,0:T(8,128)(2,1)}, u32[]{:S(2)}, u32[]{:S(2)}) collective-permute-start(bf16[48,5376]{1,0:T(8,128)(2,1)} %collective-permute-done.12.refs_12_), channel_id=1, source_target_pairs={{0,32},{1,97},{2,34},{3,99},{4,36},{5,101},{6,38},{7,103},{8,40},{... | collective-permute-start | bytes 1548296 | tf_op jit(solution)/shard_map/ppermute | solution.py:36
  47.8 26.7 %collective-permute-start.10 = (bf16[48,5376]{1,0:T(8,128)(2,1)}, bf16[48,5376]{1,0:T(8,128)(2,1)}, u32[]{:S(2)}, u32[]{:S(2)}) collective-permute-start(bf16[48,5376]{1,0:T(8,128)(2,1)} %collective-permute-done.9.refs_9_), channel_id=1, source_target_pairs={{0,128},{1,385},{2,130},{3,387},{4,132},{5,389},{6,134},{7,391},{8... | collective-permute-start | bytes 1548296 | tf_op jit(solution)/shard_map/ppermute | solution.py:36
  50.7 30.4 %collective-permute-start.13 = (bf16[48,5376]{1,0:T(8,128)(2,1)}, bf16[48,5376]{1,0:T(8,128)(2,1)}, u32[]{:S(2)}, u32[]{:S(2)}) collective-permute-start(bf16[48,5376]{1,0:T(8,128)(2,1)} %collective-permute-done.12.refs_12_), channel_id=1, source_target_pairs={{0,128},{1,385},{2,130},{3,387},{4,132},{5,389},{6,134},{7,391},{8... | collective-permute-start | bytes 1548296 | tf_op jit(solution)/shard_map/ppermute | solution.py:36
  59.4 24.1 %collective-permute-start.20 = (bf16[48,5376]{1,0:T(8,128)(2,1)}, bf16[48,5376]{1,0:T(8,128)(2,1)}, u32[]{:S(2)}, u32[]{:S(2)}) collective-permute-start(bf16[48,5376]{1,0:T(8,128)(2,1)} %collective-permute-done.16.refs_16_), channel_id=1, source_target_pairs={{0,32},{1,97},{2,34},{3,99},{4,36},{5,101},{6,38},{7,103},{8,40},{... | collective-permute-start | bytes 1548296 | tf_op jit(solution)/shard_map/ppermute | solution.py:36
  65.0 23.5 %collective-permute-start.3 = (bf16[64,5376]{1,0:T(8,128)(2,1)}, bf16[64,5376]{1,0:T(8,128)(2,1)}, u32[]{:S(2)}, u32[]{:S(2)}) collective-permute-start(bf16[64,5376]{1,0:T(8,128)(2,1)} %collective-permute-done.2.refs_1_), channel_id=1, source_target_pairs={{0,2},{1,15},{2,4},{3,1},{4,6},{5,3},{6,8},{7,5},{8,10},{9,7},{10,... | collective-permute-start | bytes 2064392 | tf_op jit(solution)/shard_map/ppermute | solution.py:36
  74.6 11.3 %collective-permute-start.11 = (bf16[48,5376]{1,0:T(8,128)(2,1)}, bf16[48,5376]{1,0:T(8,128)(2,1)S(1)}, u32[]{:S(2)}, u32[]{:S(2)}) collective-permute-start(bf16[48,5376]{1,0:T(8,128)(2,1)} %collective-permute-done.10.refs_10_), channel_id=1, source_target_pairs={{0,128},{1,385},{2,130},{3,387},{4,132},{5,389},{6,134},{7,391},{8... | collective-permute-start | bytes 1548296 | tf_op jit(solution)/shard_map/ppermute | solution.py:36
  78.2 15.3 %collective-permute-start.17 = (bf16[48,5376]{1,0:T(8,128)(2,1)}, bf16[48,5376]{1,0:T(8,128)(2,1)}, u32[]{:S(2)}, u32[]{:S(2)}) collective-permute-start(bf16[48,5376]{1,0:T(8,128)(2,1)} %collective-permute-done.16.refs_16_), channel_id=1, source_target_pairs={{0,128},{1,385},{2,130},{3,387},{4,132},{5,389},{6,134},{7,391},{8... | collective-permute-start | bytes 1548296 | tf_op jit(solution)/shard_map/ppermute | solution.py:36
  81.1 16.0 %collective-permute-start.14 = (bf16[48,5376]{1,0:T(8,128)(2,1)}, bf16[48,5376]{1,0:T(8,128)(2,1)}, u32[]{:S(2)}, u32[]{:S(2)}) collective-permute-start(bf16[48,5376]{1,0:T(8,128)(2,1)} %collective-permute-done.13.refs_13_), channel_id=1, source_target_pairs={{0,128},{1,385},{2,130},{3,387},{4,132},{5,389},{6,134},{7,391},{8... | collective-permute-start | bytes 1548296 | tf_op jit(solution)/shard_map/ppermute | solution.py:36
  83.5 18.1 %collective-permute-start.21 = (bf16[48,5376]{1,0:T(8,128)(2,1)}, bf16[48,5376]{1,0:T(8,128)(2,1)}, u32[]{:S(2)}, u32[]{:S(2)}) collective-permute-start(bf16[48,5376]{1,0:T(8,128)(2,1)} %collective-permute-done.20.refs_20_), channel_id=1, source_target_pairs={{0,128},{1,385},{2,130},{3,387},{4,132},{5,389},{6,134},{7,391},{8... | collective-permute-start | bytes 1548296 | tf_op jit(solution)/shard_map/ppermute | solution.py:36
  85.9 0.8 copy-start.2
  86.7 20.0 %collective-permute-start.6 = (bf16[64,5376]{1,0:T(8,128)(2,1)}, bf16[64,5376]{1,0:T(8,128)(2,1)}, u32[]{:S(2)}, u32[]{:S(2)}) collective-permute-start(bf16[64,5376]{1,0:T(8,128)(2,1)} %collective-permute-done.2.refs_1_), channel_id=1, source_target_pairs={{0,1},{1,0},{2,3},{3,2},{4,5},{5,4},{6,7},{7,6},{8,9},{9,8},{10,11... | collective-permute-start | bytes 2064392 | tf_op jit(solution)/shard_map/ppermute | solution.py:36
  88.6 20.0 %collective-permute-start.4 = (bf16[64,5376]{1,0:T(8,128)(2,1)}, bf16[64,5376]{1,0:T(8,128)(2,1)}, u32[]{:S(2)}, u32[]{:S(2)}) collective-permute-start(bf16[64,5376]{1,0:T(8,128)(2,1)} %collective-permute-done.3.refs_2_), channel_id=1, source_target_pairs={{0,2},{1,15},{2,4},{3,1},{4,6},{5,3},{6,8},{7,5},{8,10},{9,7},{10,... | collective-permute-start | bytes 2064392 | tf_op jit(solution)/shard_map/ppermute | solution.py:36
  93.5 17.5 %collective-permute-start.18 = (bf16[48,5376]{1,0:T(8,128)(2,1)}, bf16[48,5376]{1,0:T(8,128)(2,1)}, u32[]{:S(2)}, u32[]{:S(2)}) collective-permute-start(bf16[48,5376]{1,0:T(8,128)(2,1)} %collective-permute-done.17.refs_17_), channel_id=1, source_target_pairs={{0,128},{1,385},{2,130},{3,387},{4,132},{5,389},{6,134},{7,391},{8... | collective-permute-start | bytes 1548296 | tf_op jit(solution)/shard_map/ppermute | solution.py:36
  97.1 17.4 %collective-permute-start.15 = (bf16[48,5376]{1,0:T(8,128)(2,1)}, bf16[48,5376]{1,0:T(8,128)(2,1)}, u32[]{:S(2)}, u32[]{:S(2)}) collective-permute-start(bf16[48,5376]{1,0:T(8,128)(2,1)} %collective-permute-done.14.refs_14_), channel_id=1, source_target_pairs={{0,128},{1,385},{2,130},{3,387},{4,132},{5,389},{6,134},{7,391},{8... | collective-permute-start | bytes 1548296 | tf_op jit(solution)/shard_map/ppermute | solution.py:36
  101.6 16.6 %collective-permute-start.22 = (bf16[48,5376]{1,0:T(8,128)(2,1)}, bf16[48,5376]{1,0:T(8,128)(2,1)}, u32[]{:S(2)}, u32[]{:S(2)}) collective-permute-start(bf16[48,5376]{1,0:T(8,128)(2,1)} %collective-permute-done.21.refs_21_), channel_id=1, source_target_pairs={{0,128},{1,385},{2,130},{3,387},{4,132},{5,389},{6,134},{7,391},{8... | collective-permute-start | bytes 1548296 | tf_op jit(solution)/shard_map/ppermute | solution.py:36
  106.7 19.1 %collective-permute-start.7 = (bf16[64,5376]{1,0:T(8,128)(2,1)}, bf16[64,5376]{1,0:T(8,128)(2,1)}, u32[]{:S(2)}, u32[]{:S(2)}) collective-permute-start(bf16[64,5376]{1,0:T(8,128)(2,1)} %collective-permute-done.3.refs_2_), channel_id=1, source_target_pairs={{0,1},{1,0},{2,3},{3,2},{4,5},{5,4},{6,7},{7,6},{8,9},{9,8},{10,11... | collective-permute-start | bytes 2064392 | tf_op jit(solution)/shard_map/ppermute | solution.py:36
  108.6 21.9 %collective-permute-start.8 = (bf16[64,5376]{1,0:T(8,128)(2,1)}, bf16[64,5376]{1,0:T(8,128)(2,1)}, u32[]{:S(2)}, u32[]{:S(2)}) collective-permute-start(bf16[64,5376]{1,0:T(8,128)(2,1)} %collective-permute-done.4.refs_3_), channel_id=1, source_target_pairs={{0,1},{1,0},{2,3},{3,2},{4,5},{5,4},{6,7},{7,6},{8,9},{9,8},{10,11... | collective-permute-start | bytes 2064392 | tf_op jit(solution)/shard_map/ppermute | solution.py:36
  111.0 19.4 %collective-permute-start.5 = (bf16[64,5376]{1,0:T(8,128)(2,1)}, bf16[64,5376]{1,0:T(8,128)(2,1)}, u32[]{:S(2)}, u32[]{:S(2)}) collective-permute-start(bf16[64,5376]{1,0:T(8,128)(2,1)} %collective-permute-done.4.refs_3_), channel_id=1, source_target_pairs={{0,2},{1,15},{2,4},{3,1},{4,6},{5,3},{6,8},{7,5},{8,10},{9,7},{10,... | collective-permute-start | bytes 2064392 | tf_op jit(solution)/shard_map/ppermute | solution.py:36
  114.5 11.3 %collective-permute-start.19 = (bf16[48,5376]{1,0:T(8,128)(2,1)}, bf16[48,5376]{1,0:T(8,128)(2,1)}, u32[]{:S(2)}, u32[]{:S(2)}) collective-permute-start(bf16[48,5376]{1,0:T(8,128)(2,1)} %collective-permute-done.18.refs_18_), channel_id=1, source_target_pairs={{0,128},{1,385},{2,130},{3,387},{4,132},{5,389},{6,134},{7,391},{8... | collective-permute-start | bytes 1548296 | tf_op jit(solution)/shard_map/ppermute | solution.py:36
  118.2 12.3 %collective-permute-start.23 = (bf16[48,5376]{1,0:T(8,128)(2,1)}, bf16[48,5376]{1,0:T(8,128)(2,1)}, u32[]{:S(2)}, u32[]{:S(2)}) collective-permute-start(bf16[48,5376]{1,0:T(8,128)(2,1)} %collective-permute-done.22.refs_22_), channel_id=1, source_target_pairs={{0,128},{1,385},{2,130},{3,387},{4,132},{5,389},{6,134},{7,391},{8... | collective-permute-start | bytes 1548296 | tf_op jit(solution)/shard_map/ppermute | solution.py:36
  124.5 6.0 %copy-start.3 = (bf16[48,5376]{1,0:T(8,128)(2,1)S(1)}, bf16[48,5376]{1,0:T(8,128)(2,1)}, u32[]{:S(2)}) copy-start(bf16[48,5376]{1,0:T(8,128)(2,1)} %copy-done.2) | copy-start | bytes 1548292
  130.5 1.0 copy-start.1

commit v2 on v1

v2 whole, which is shorter than its diff:
```python
import functools

import jax
import jax.numpy as jnp
from jax import lax
from jax.experimental import pallas as pl
from jax.experimental.pallas import tpu as pltpu
from jax.sharding import PartitionSpec as P


AXES = ("prompt", "feat")


def routes(move):
    pairs = []
    for x in range(4):
        for y in range(8):
            for z in range(8):
                for core in range(2):
                    pairs.append((flat(x, y, z, core), flat(*move(x, y, z, core))))
    return pairs


def flat(x, y, z, core):
    prompt = (x % 4) * 4 + y % 4
    feat = ((y // 4) % 2 * 8 + z % 8) * 2 + core
    return prompt * 32 + feat


UP_X = routes(lambda x, y, z, c: (x + 1, y, z, c))
DOWN_X = routes(lambda x, y, z, c: (x - 1, y, z, c))
RING_X = routes(lambda x, y, z, c: (x + (1 - 2 * c), y, z, c))
RING_Y = routes(lambda x, y, z, c: (x, y // 4 * 4 + (y + (1 - 2 * c)) % 4, z, c))
OTHER_Y = routes(lambda x, y, z, c: (x, (y + 4) % 8, z, c))
UP_Z = routes(lambda x, y, z, c: (x, y, z + 1, c))
DOWN_Z = routes(lambda x, y, z, c: (x, y, z - 1, c))
FAR_Z = routes(lambda x, y, z, c: (x, y, z + 4, c))
CORE = routes(lambda x, y, z, c: (x, y, z, 1 - c))


def send(value, pairs):
    return lax.ppermute(value, AXES, pairs)


def stack(*pieces):
    return jnp.concatenate(pieces, axis=0)


def turn(core, up, down):
    return jnp.where(core == 0, up, down)


def gather_rows(operands, into, sem, first):
    copies, at = [], 0
    for i, operand in enumerate(operands):
        size = operand.shape[0]
        copies.append(pltpu.make_async_copy(operand, into.at[pl.ds(at, size)], sem.at[first + i]))
        at += size
    for copy in copies:
        copy.start()
    return copies


def product_kernel(n_sources, n_targets, last, act_ref, order_ref, *refs):
    sources, targets = refs[:n_sources], refs[n_sources : n_sources + n_targets]
    refs = refs[n_sources + n_targets :]
    if last:
        row_at, before_ref = refs[:2]
        refs = refs[2:]
    out_ref, rows, cols, acc, sem = refs
    copies = gather_rows(sources, rows, sem, 0) + gather_rows(targets, cols, sem, n_sources)
    for copy in copies:
        copy.wait()
    depth = rows.shape[1]
    step = 768
    acc[...] = jnp.zeros_like(acc)

    @pl.loop(0, depth // step)
    def _(k):
        part = pl.ds(pl.multiple_of(k * step, step), step)
        acc[...] += lax.dot_general(
            rows[:, part], cols[:, part], (((1,), (1,)), ((), ())), preferred_element_type=jnp.float32
        )

    edges = (acc[...] * act_ref[...]).astype(jnp.bfloat16)
    placed = jnp.dot(edges, order_ref[...], preferred_element_type=jnp.float32)
    if not last:
        out_ref[...] = placed.astype(jnp.bfloat16)
        return
    placed = (placed + before_ref[...].astype(jnp.float32)).astype(jnp.bfloat16)
    for g in range(out_ref.shape[0] // 16):
        out_ref[pl.ds(pl.multiple_of(row_at[g], 16), 16), :] = placed[g * 16 : (g + 1) * 16]


def product(act, order, sources, targets, row_at=None, before=None):
    n_rows, (n_cols, n_out), depth = act.shape[0], order.shape, sources[0].shape[1]
    whole, smem, anywhere = (pl.BlockSpec(memory_space=m) for m in (pltpu.VMEM, pltpu.SMEM, pl.ANY))
    last = before is not None
    return pl.pallas_call(
        functools.partial(product_kernel, len(sources), len(targets), last),
        out_shape=jax.ShapeDtypeStruct((n_rows, n_out), jnp.bfloat16),
        in_specs=[whole, whole] + [anywhere] * (len(sources) + len(targets)) + ([smem, whole] if last else []),
        out_specs=whole,
        scratch_shapes=[
            pltpu.VMEM((n_rows, depth), jnp.bfloat16),
            pltpu.VMEM((n_cols, depth), jnp.bfloat16),
            pltpu.VMEM((n_rows, n_cols), jnp.float32),
            pltpu.SemaphoreType.DMA((len(sources) + len(targets),)),
        ],
        compiler_params=pltpu.CompilerParams(vmem_limit_bytes=32 << 20),
        name="last_product" if last else "first_product",
    )(act, order, *sources, *targets, *((row_at, before) if last else ()))


def edges_of(decoder, encoder, row_ids, counts, activity):
    slot_count = row_ids.shape[1]
    prompt, owner = lax.axis_index("prompt"), lax.axis_index("feat")
    core, chip = owner % 2, owner // 2
    half, z = chip // 8, chip % 8
    x, y = prompt // 4, prompt % 4
    sign = 1 - 2 * core

    picked_rows = jnp.take(decoder, row_ids[0], axis=0)
    live_count = lax.dynamic_index_in_dim(counts[0], owner, 0, keepdims=False)
    live_slots = jnp.arange(slot_count, dtype=jnp.int32) < live_count
    source_rows = jnp.where(live_slots[:, None], picked_rows, jnp.zeros((), picked_rows.dtype))

    y0 = encoder
    y1 = send(y0, RING_Y)
    y2 = send(y1, RING_Y)
    y3 = send(y2, RING_Y)
    a1, a2 = send(y0, UP_X), send(y0, DOWN_X)
    b1, b2 = send(y1, UP_X), send(y1, DOWN_X)
    c1, c2 = send(y2, UP_X), send(y2, DOWN_X)
    d1, d2 = send(y3, UP_X), send(y3, DOWN_X)
    a3 = send(turn(core, a1, a2), RING_X)
    f1 = send(a3, RING_Y)
    f2 = send(f1, RING_Y)
    d3 = send(turn(core, d1, d2), RING_X)

    own = lax.optimization_barrier(stack(source_rows, send(source_rows, OTHER_Y)))
    u1, w1 = send(own, UP_Z), send(own, DOWN_Z)
    u2, w2 = send(u1, UP_Z), send(w1, DOWN_Z)
    u3, w3 = send(u2, UP_Z), send(w2, DOWN_Z)
    zf = send(own, FAR_Z)
    near = stack(own, u1, w1, u2, w2)
    away = stack(u3, w3, zf)
    sources = [near, away, send(near, CORE), send(away, CORE)]

    hop = jnp.array([0, -1, 1, -2, 2, -3, 3, 4], jnp.int32)[None, :, None]
    side = jnp.arange(2, dtype=jnp.int32)[:, None, None]
    flip = jnp.arange(2, dtype=jnp.int32)[None, None, :]
    feat_from = ((half ^ flip) * 8 + (z + hop) % 8) * 2 + (core ^ side)
    group_from = feat_from.reshape(-1).astype(jnp.int32)
    x_from = (x + jnp.array([0, -1, 1, 2], jnp.int32)) % 4
    y_from = (y - sign * jnp.arange(4, dtype=jnp.int32)) % 4
    origin = x_from[None, :] * 4 + y_from[:, None]
    width = encoder.shape[0]
    first_of = origin.reshape(-1)[:12]
    last_of = origin.reshape(-1)[12:]
    act = activity[0].reshape(-1, slot_count)[group_from].reshape(-1, 1)

    def order(blocks):
        col_at = (blocks[:, None] * width + jnp.arange(width, dtype=jnp.int32)[None, :]).reshape(-1)
        place = jnp.arange(origin.size * width, dtype=jnp.int32)
        return (col_at[:, None] == place[None, :]).astype(jnp.bfloat16)

    part = product(act, order(first_of), sources, [y0, a1, a2, a3, y1, b1, b2, f1, y2, c1, c2, f2])
    edges = product(act, order(last_of), sources, [y3, d1, d2, d3], group_from * slot_count, part)
    return edges[None]


def solution(mesh):
    in_specs = (
        P("feat", None),
        P(("feat", "prompt"), None),
        P("prompt", "feat"),
        P("prompt", None),
        P("prompt", None),
    )
    out_specs = P("prompt", None, "feat")
    return jax.shard_map(edges_of, mesh=mesh, in_specs=in_specs, out_specs=out_specs, check_vma=False)
```

time: 146 us -> 197 us (1.35); the launches traced: 145 us -> 194 us
  waiting for transfers between devices: 19.1 us -> 58.4 us
  local copies, waits for them, and re-layouts: 6.05 us -> 21.2 us
  starting transfers between devices: 101 us -> 86.2 us
  other arithmetic: 4.48 us -> 9.25 us
  Pallas kernels: 14 us -> 18 us
    ppermute x24 -> x25, waiting for transfers between devices: 19.1 us -> 58.4 us  [send(): return lax.ppermute(value, AXES, pairs)]
    ppermute x24 -> x25, starting transfers between devices: 101 us -> 86.2 us  [send(): return lax.ppermute(value, AXES, pairs)]
    unnamed x15 -> x43, local copies, waits for them, and re-layouts: 2.26 us -> 14.6 us
    pallas_call x1 -> x2, Pallas kernels: 14 us -> 18 us  [product(): pl.pallas_call(functools.partial(product_kernel, len(sources), len(target...]
    select_n x2 -> x4, other arithmetic: 0.03 us -> 2.72 us  [the longest x2 2.04 us: turn(): return jnp.where(core == 0, up, down)]
  transfers between devices with their start and end apart: 24 -> 25, of which waited for: 5 -> 10; matrix products, arithmetic and copies ran while one was open for 3% -> 11% of each run, Pallas kernels for 0% -> 5%
where the time goes in v2:
time: 197 us; the launch traced here: 194 us
  starting transfers between devices  86.2 us (44%)
  waiting for transfers between devices  58.4 us (30%)
  local copies, waits for them, and re-layouts  21.2 us (11%)
  Pallas kernels  18 us (9%)
  other arithmetic  9.25 us (5%)
    ppermute x25, starting transfers between devices, send(): return lax.ppermute(value, AXES, pairs)  86.2 us
    ppermute x25, waiting for transfers between devices, send(): return lax.ppermute(value, AXES, pairs)  58.4 us
    pallas_call x2, Pallas kernels, product(): pl.pallas_call(functools.partial(product_kernel, len(sources), len(target...  18 us
    unnamed x43, local copies, waits for them, and re-layouts  14.6 us
  transfers between devices with their start and end apart: 25, of which 10 were waited for; matrix products, arithmetic and copies ran while one was open for 11% of the time, Pallas kernels for 5%

profile of v2, /device:TPU:1, one launch (start us, length us, event | category | flops | bytes accessed | tf_op | source)
XLA Modules:
  0.0 193.6 jit_solution(1124177605634527439)
XLA Ops:
  0.0 4.2 %collective-permute-start.16 = (bf16[48,5376]{1,0:T(8,128)(2,1)}, bf16[48,5376]{1,0:T(8,128)(2,1)S(1)}, u32[]{:S(2)}, u32[]{:S(2)}) collective-permute-start(bf16[48,5376]{1,0:T(8,128)(2,1)} %refs_4_.1), channel_id=1, source_target_pairs={{0,128},{1,129},{2,130},{3,131},{4,132},{5,133},{6,134},{7,135},{8... | collective-permute-start | bytes 1548296 | tf_op jit(solution)/shard_map/ppermute | solution.py:42
  4.2 3.2 %collective-permute-start.17 = (bf16[48,5376]{1,0:T(8,128)(2,1)}, bf16[48,5376]{1,0:T(8,128)(2,1)}, u32[]{:S(2)}, u32[]{:S(2)}) collective-permute-start(bf16[48,5376]{1,0:T(8,128)(2,1)} %refs_4_.1), channel_id=1, source_target_pairs={{0,384},{1,385},{2,386},{3,387},{4,388},{5,389},{6,390},{7,391},{8... | collective-permute-start | bytes 1548296 | tf_op jit(solution)/shard_map/ppermute | solution.py:42
  7.4 5.4 %collective-permute-start.10 = (bf16[48,5376]{1,0:T(8,128)(2,1)}, bf16[48,5376]{1,0:T(8,128)(2,1)}, u32[]{:S(2)}, u32[]{:S(2)}) collective-permute-start(bf16[48,5376]{1,0:T(8,128)(2,1)} %refs_4_.1), channel_id=1, source_target_pairs={{0,32},{1,97},{2,34},{3,99},{4,36},{5,101},{6,38},{7,103},{8,40},{... | collective-permute-start | bytes 1548296 | tf_op jit(solution)/shard_map/ppermute | solution.py:42
  14.5 1.2 constant_dynamic-slice_fusion
  15.7 1.3 compare_and_fusion
  17.1 1.3 gather_fusion.1
  18.4 1.0 select_select_fusion
  19.4 4.8 %collective-permute-start = (bf16[16,5376]{1,0:T(8,128)(2,1)S(1)}, bf16[16,5376]{1,0:T(8,128)(2,1)}, u32[]{:S(2)}, u32[]{:S(2)}) collective-permute-start(bf16[16,5376]{1,0:T(8,128)(2,1)S(1)} %select_select_fusion), channel_id=1, source_target_pairs={{0,16},{1,17},{2,18},{3,19},{4,20},{5,21},{6,22},{7,23},{8,24},{9,... | collective-permute-start | bytes 516104 | tf_op jit(solution)/shard_map/ppermute | solution.py:42
  24.5 6.0 %collective-permute-done = bf16[16,5376]{1,0:T(8,128)(2,1)} collective-permute-done((bf16[16,5376]{1,0:T(8,128)(2,1)S(1)}, bf16[16,5376]{1,0:T(8,128)(2,1)}, u32[]{:S(2)}, u32[]{:S(2)}) %collective-permute-start) | collective-permute-done | bytes 172064 | tf_op jit(solution)/shard_map/ppermute | solution.py:42
  31.4 6.2 %collective-permute-start.1 = (bf16[32,5376]{1,0:T(8,128)(2,1)S(1)}, bf16[32,5376]{1,0:T(8,128)(2,1)S(1)}, u32[]{:S(2)}, u32[]{:S(2)}) collective-permute-start(bf16[32,5376]{1,0:T(8,128)(2,1)S(1)} %pad_maximum_fusion), channel_id=1, source_target_pairs={{0,2},{1,3},{2,4},{3,5},{4,6},{5,7},{6,8},{7,9},{8,10},{9,11},{10,... | collective-permute-start | bytes 1032200 | tf_op jit(solution)/shard_map/ppermute | solution.py:42
  37.6 8.6 %collective-permute-start.2 = (bf16[32,5376]{1,0:T(8,128)(2,1)S(1)}, bf16[32,5376]{1,0:T(8,128)(2,1)S(1)}, u32[]{:S(2)}, u32[]{:S(2)}) collective-permute-start(bf16[32,5376]{1,0:T(8,128)(2,1)S(1)} %pad_maximum_fusion), channel_id=1, source_target_pairs={{0,14},{1,15},{2,0},{3,1},{4,2},{5,3},{6,4},{7,5},{8,6},{9,7},{10,... | collective-permute-start | bytes 1032200 | tf_op jit(solution)/shard_map/ppermute | solution.py:42
  46.9 4.5 %collective-permute-start.7 = (bf16[32,5376]{1,0:T(8,128)(2,1)S(1)}, bf16[32,5376]{1,0:T(8,128)(2,1)S(1)}, u32[]{:S(2)}, u32[]{:S(2)}) collective-permute-start(bf16[32,5376]{1,0:T(8,128)(2,1)S(1)} %pad_maximum_fusion), channel_id=1, source_target_pairs={{0,8},{1,9},{2,10},{3,11},{4,12},{5,13},{6,14},{7,15},{8,0},{9,1},... | collective-permute-start | bytes 1032200 | tf_op jit(solution)/shard_map/ppermute | solution.py:42
  51.5 1.1 broadcast_select_fusion
  52.6 3.2 %collective-permute-start.18 = (bf16[48,5376]{1,0:T(8,128)(2,1)S(1)}, bf16[48,5376]{1,0:T(8,128)(2,1)S(1)}, u32[]{:S(2)}, u32[]{:S(2)}) collective-permute-start(bf16[48,5376]{1,0:T(8,128)(2,1)S(1)} %broadcast_select_fusion), channel_id=1, source_target_pairs={{0,128},{1,385},{2,130},{3,387},{4,132},{5,389},{6,134},{7,391},{8... | collective-permute-start | bytes 1548296 | tf_op jit(solution)/shard_map/ppermute | solution.py:42
  55.8 1.9 collective-permute-start.11
  57.7 2.1 %collective-permute-start.19 = (bf16[48,5376]{1,0:T(8,128)(2,1)}, bf16[48,5376]{1,0:T(8,128)(2,1)S(1)}, u32[]{:S(2)}, u32[]{:S(2)}) collective-permute-start(bf16[48,5376]{1,0:T(8,128)(2,1)} %collective-permute-done.10.refs_8_), channel_id=1, source_target_pairs={{0,128},{1,129},{2,130},{3,131},{4,132},{5,133},{6,134},{7,135},{8... | collective-permute-start | bytes 1548296 | tf_op jit(solution)/shard_map/ppermute | solution.py:42
  60.6 2.7 %collective-permute-done.2 = bf16[32,5376]{1,0:T(8,128)(2,1)S(1)} collective-permute-done((bf16[32,5376]{1,0:T(8,128)(2,1)S(1)}, bf16[32,5376]{1,0:T(8,128)(2,1)S(1)}, u32[]{:S(2)}, u32[]{:S(2)}) %collective-permute-start.2) | collective-permute-done | bytes 344096 | tf_op jit(solution)/shard_map/ppermute | solution.py:42
  63.3 1.9 collective-permute-start.3
  65.9 8.5 %collective-permute-done.3 = bf16[32,5376]{1,0:T(8,128)(2,1)S(1)} collective-permute-done((bf16[32,5376]{1,0:T(8,128)(2,1)S(1)}, bf16[32,5376]{1,0:T(8,128)(2,1)S(1)}, u32[]{:S(2)}, u32[]{:S(2)}) %collective-permute-start.3) | collective-permute-done | bytes 344096 | tf_op jit(solution)/shard_map/ppermute | solution.py:42
  74.5 2.8 %collective-permute-start.4 = (bf16[32,5376]{1,0:T(8,128)(2,1)S(1)}, bf16[32,5376]{1,0:T(8,128)(2,1)S(1)}, u32[]{:S(2)}, u32[]{:S(2)}) collective-permute-start(bf16[32,5376]{1,0:T(8,128)(2,1)S(1)} %collective-permute-done.2), channel_id=1, source_target_pairs={{0,14},{1,15},{2,0},{3,1},{4,2},{5,3},{6,4},{7,5},{8,6},{9,7},{10,... | collective-permute-start | bytes 1032200 | tf_op jit(solution)/shard_map/ppermute | solution.py:42
  78.0 4.4 %collective-permute-done.4 = bf16[32,5376]{1,0:T(8,128)(2,1)S(1)} collective-permute-done((bf16[32,5376]{1,0:T(8,128)(2,1)S(1)}, bf16[32,5376]{1,0:T(8,128)(2,1)S(1)}, u32[]{:S(2)}, u32[]{:S(2)}) %collective-permute-start.4) | collective-permute-done | bytes 344096 | tf_op jit(solution)/shard_map/ppermute | solution.py:42
  82.4 3.4 %collective-permute-start.5 = (bf16[32,5376]{1,0:T(8,128)(2,1)S(1)}, bf16[32,5376]{1,0:T(8,128)(2,1)S(1)}, u32[]{:S(2)}, u32[]{:S(2)}) collective-permute-start(bf16[32,5376]{1,0:T(8,128)(2,1)S(1)} %collective-permute-done.3), channel_id=1, source_target_pairs={{0,2},{1,3},{2,4},{3,5},{4,6},{5,7},{6,8},{7,9},{8,10},{9,11},{10,... | collective-permute-start | bytes 1032200 | tf_op jit(solution)/shard_map/ppermute | solution.py:42
  86.6 5.0 %collective-permute-done.5 = bf16[32,5376]{1,0:T(8,128)(2,1)S(1)} collective-permute-done((bf16[32,5376]{1,0:T(8,128)(2,1)S(1)}, bf16[32,5376]{1,0:T(8,128)(2,1)S(1)}, u32[]{:S(2)}, u32[]{:S(2)}) %collective-permute-start.5) | collective-permute-done | bytes 344096 | tf_op jit(solution)/shard_map/ppermute | solution.py:42
  91.6 2.8 %collective-permute-start.6 = (bf16[32,5376]{1,0:T(8,128)(2,1)S(1)}, bf16[32,5376]{1,0:T(8,128)(2,1)S(1)}, u32[]{:S(2)}, u32[]{:S(2)}) collective-permute-start(bf16[32,5376]{1,0:T(8,128)(2,1)S(1)} %collective-permute-done.4), channel_id=1, source_target_pairs={{0,14},{1,15},{2,0},{3,1},{4,2},{5,3},{6,4},{7,5},{8,6},{9,7},{10,... | collective-permute-start | bytes 1032200 | tf_op jit(solution)/shard_map/ppermute | solution.py:42
  95.2 2.9 %collective-permute-start.20 = (bf16[48,5376]{1,0:T(8,128)(2,1)}, bf16[48,5376]{1,0:T(8,128)(2,1)S(1)}, u32[]{:S(2)}, u32[]{:S(2)}) collective-permute-start(bf16[48,5376]{1,0:T(8,128)(2,1)} %collective-permute-done.10.refs_8_), channel_id=1, source_target_pairs={{0,384},{1,385},{2,386},{3,387},{4,388},{5,389},{6,390},{7,391},{8... | collective-permute-start | bytes 1548296 | tf_op jit(solution)/shard_map/ppermute | solution.py:42
  98.1 1.5 collective-permute-done.6
  99.6 4.0 %collective-permute-start.12 = (bf16[48,5376]{1,0:T(8,128)(2,1)}, bf16[48,5376]{1,0:T(8,128)(2,1)S(1)}, u32[]{:S(2)}, u32[]{:S(2)}) collective-permute-start(bf16[48,5376]{1,0:T(8,128)(2,1)} %collective-permute-done.11.refs_12_), channel_id=1, source_target_pairs={{0,32},{1,97},{2,34},{3,99},{4,36},{5,101},{6,38},{7,103},{8,40},{... | collective-permute-start | bytes 1548296 | tf_op jit(solution)/shard_map/ppermute | solution.py:42
  104.4 19.6 %collective-permute-done.12.refs_4_ = bf16[48,5376]{1,0:T(8,128)(2,1)S(1)} collective-permute-done((bf16[48,5376]{1,0:T(8,128)(2,1)}, bf16[48,5376]{1,0:T(8,128)(2,1)S(1)}, u32[]{:S(2)}, u32[]{:S(2)}) %collective-permute-start.12) | collective-permute-done | bytes 516128 | tf_op jit(solution)/shard_map/ppermute | solution.py:42
  124.1 1.9 collective-permute-start.13
  126.0 4.6 %collective-permute-start.14 = (bf16[48,5376]{1,0:T(8,128)(2,1)S(1)}, bf16[48,5376]{1,0:T(8,128)(2,1)S(1)}, u32[]{:S(2)}, u32[]{:S(2)}) collective-permute-start(bf16[48,5376]{1,0:T(8,128)(2,1)S(1)} %collective-permute-done.12.refs_4_), channel_id=1, source_target_pairs={{0,384},{1,385},{2,386},{3,387},{4,388},{5,389},{6,390},{7,391},{8... | collective-permute-start | bytes 1548296 | tf_op jit(solution)/shard_map/ppermute | solution.py:42
  131.3 1.9 collective-permute-start.8
  134.1 1.9 collective-permute-start.22
  136.0 4.1 %collective-permute-done.13.refs_5_ = bf16[48,5376]{1,0:T(8,128)(2,1)S(1)} collective-permute-done((bf16[48,5376]{1,0:T(8,128)(2,1)S(1)}, bf16[48,5376]{1,0:T(8,128)(2,1)S(1)}, u32[]{:S(2)}, u32[]{:S(2)}) %collective-permute-start.13) | collective-permute-done | bytes 516128 | tf_op jit(solution)/shard_map/ppermute | solution.py:42
  140.1 1.9 collective-permute-start.21
  142.0 5.0 %collective-permute-start.9 = (bf16[96,5376]{1,0:T(8,128)(2,1)}, bf16[96,5376]{1,0:T(8,128)(2,1)}, u32[]{:S(2)}, u32[]{:S(2)}) collective-permute-start(bf16[96,5376]{1,0:T(8,128)(2,1)} %constant_dynamic-update-slice_fusion.5.refs_1_), channel_id=1, source_target_pairs={{0,1},{1,0},{2,3},{3,2},{4,5},{5,4},{6,7},{7,6},{8,9},{9,8},{10,11... | collective-permute-start | bytes 3096584 | tf_op jit(solution)/shard_map/ppermute | solution.py:42
  149.6 2.2 %collective-permute-start.23 = (bf16[48,5376]{1,0:T(8,128)(2,1)}, bf16[48,5376]{1,0:T(8,128)(2,1)}, u32[]{:S(2)}, u32[]{:S(2)}) collective-permute-start(bf16[48,5376]{1,0:T(8,128)(2,1)} %collective-permute-done.11.refs_12_), channel_id=1, source_target_pairs={{0,384},{1,385},{2,386},{3,387},{4,388},{5,389},{6,390},{7,391},{8... | collective-permute-start | bytes 1548296 | tf_op jit(solution)/shard_map/ppermute | solution.py:42
  151.8 3.0 %collective-permute-done.21.refs_11_ = bf16[48,5376]{1,0:T(8,128)(2,1)} collective-permute-done((bf16[48,5376]{1,0:T(8,128)(2,1)S(1)}, bf16[48,5376]{1,0:T(8,128)(2,1)}, u32[]{:S(2)}, u32[]{:S(2)}) %collective-permute-start.21) | collective-permute-done | bytes 516128 | tf_op jit(solution)/shard_map/ppermute | solution.py:42
  154.9 2.0 %collective-permute-start.24 = (bf16[48,5376]{1,0:T(8,128)(2,1)}, bf16[48,5376]{1,0:T(8,128)(2,1)}, u32[]{:S(2)}, u32[]{:S(2)}) collective-permute-start(bf16[48,5376]{1,0:T(8,128)(2,1)} %collective-permute-done.21.refs_11_), channel_id=1, source_target_pairs={{0,32},{1,97},{2,34},{3,99},{4,36},{5,101},{6,38},{7,103},{8,40},{... | collective-permute-start | bytes 1548296 | tf_op jit(solution)/shard_map/ppermute | solution.py:42
  157.8 2.9 %collective-permute-start.15 = (bf16[48,5376]{1,0:T(8,128)(2,1)}, bf16[48,5376]{1,0:T(8,128)(2,1)}, u32[]{:S(2)}, u32[]{:S(2)}) collective-permute-start(bf16[48,5376]{1,0:T(8,128)(2,1)} %broadcast_select_fusion.1), channel_id=1, source_target_pairs={{0,128},{1,385},{2,130},{3,387},{4,132},{5,389},{6,134},{7,391},{8... | collective-permute-start | bytes 1548296 | tf_op jit(solution)/shard_map/ppermute | solution.py:42
  165.8 3.5 %collective-permute-done.24.refs_15_ = bf16[48,5376]{1,0:T(8,128)(2,1)} collective-permute-done((bf16[48,5376]{1,0:T(8,128)(2,1)}, bf16[48,5376]{1,0:T(8,128)(2,1)}, u32[]{:S(2)}, u32[]{:S(2)}) %collective-permute-start.24) | collective-permute-done | bytes 516128 | tf_op jit(solution)/shard_map/ppermute | solution.py:42
  169.3 1.0 copy-done.4
  170.3 1.0 copy-done.7
  171.4 1.0 copy-done.9
  172.4 1.0 copy-done.11
  173.5 1.0 copy-done.13
  174.5 1.0 copy-done.15
  175.5 10.4 %first_product.1.refs_9_ = bf16[512,768]{1,0:T(8,128)(2,1)S(1)} custom-call(f32[512,1]{1,0:T(8,128)S(1)} %reshape.215.act_ref, bf16[576,768]{1,0:T(8,128)(2,1)S(1)} %fusion.order_ref, bf16[160,5376]{1,0:T(8,128)(2,1)} %constant_dynamic-update-slice_fusion.refs_0_, bf16[96,5376]{1,0:T(8,128)(2,1)} %constant_dynamic-update-slice_fusion.5.refs_1_, ...), custom_call_target="tpu_custom_call" | custom-call | tf_op jit(solution)/shard_map/first_product/pallas_call | solution.py:99
  186.0 7.5 %last_product.1 = bf16[512,768]{1,0:T(8,128)(2,1)} custom-call(f32[512,1]{1,0:T(8,128)S(1)} %reshape.215.act_ref, bf16[192,768]{1,0:T(8,128)(2,1)S(1)} %fusion.1.order_ref, bf16[160,5376]{1,0:T(8,128)(2,1)} %constant_dynamic-update-slice_fusion.refs_0_, bf16[96,5376]{1,0:T(8,128)(2,1)} %constant_dynamic-update-slice_fusion.5.refs_1_, ...), custom_call_target="tpu_custom_call" | custom-call | tf_op jit(solution)/shard_map/last_product/pallas_call | solution.py:99
  (81 shorter events, 18.3 us)
Async XLA Ops:
  0.0 17.0 %copy-start = (bf16[256,5376]{1,0:T(8,128)(2,1)S(1)}, bf16[256,5376]{1,0:T(8,128)(2,1)}, u32[]{:S(2)}) copy-start(bf16[256,5376]{1,0:T(8,128)(2,1)} %param.7) | copy-start | bytes 8257540
  0.0 24.2 %copy-start.17 = (s32[4]{0:T(128)S(1)}, s32[4]{0:T(128)}, u32[]{:S(2)}) copy-start(s32[4]{0:T(128)} %constant.130.clone) | copy-start | bytes 52
  0.0 46.9 %collective-permute-start.16 = (bf16[48,5376]{1,0:T(8,128)(2,1)}, bf16[48,5376]{1,0:T(8,128)(2,1)S(1)}, u32[]{:S(2)}, u32[]{:S(2)}) collective-permute-start(bf16[48,5376]{1,0:T(8,128)(2,1)} %refs_4_.1), channel_id=1, source_target_pairs={{0,128},{1,129},{2,130},{3,131},{4,132},{5,133},{6,134},{7,135},{8... | collective-permute-start | bytes 1548296 | tf_op jit(solution)/shard_map/ppermute | solution.py:42
  4.2 47.3 %collective-permute-start.17 = (bf16[48,5376]{1,0:T(8,128)(2,1)}, bf16[48,5376]{1,0:T(8,128)(2,1)}, u32[]{:S(2)}, u32[]{:S(2)}) collective-permute-start(bf16[48,5376]{1,0:T(8,128)(2,1)} %refs_4_.1), channel_id=1, source_target_pairs={{0,384},{1,385},{2,386},{3,387},{4,388},{5,389},{6,390},{7,391},{8... | collective-permute-start | bytes 1548296 | tf_op jit(solution)/shard_map/ppermute | solution.py:42
  7.4 48.4 %collective-permute-start.10 = (bf16[48,5376]{1,0:T(8,128)(2,1)}, bf16[48,5376]{1,0:T(8,128)(2,1)}, u32[]{:S(2)}, u32[]{:S(2)}) collective-permute-start(bf16[48,5376]{1,0:T(8,128)(2,1)} %refs_4_.1), channel_id=1, source_target_pairs={{0,32},{1,97},{2,34},{3,99},{4,36},{5,101},{6,38},{7,103},{8,40},{... | collective-permute-start | bytes 1548296 | tf_op jit(solution)/shard_map/ppermute | solution.py:42
  19.4 11.0 %collective-permute-start = (bf16[16,5376]{1,0:T(8,128)(2,1)S(1)}, bf16[16,5376]{1,0:T(8,128)(2,1)}, u32[]{:S(2)}, u32[]{:S(2)}) collective-permute-start(bf16[16,5376]{1,0:T(8,128)(2,1)S(1)} %select_select_fusion), channel_id=1, source_target_pairs={{0,16},{1,17},{2,18},{3,19},{4,20},{5,21},{6,22},{7,23},{8,24},{9,... | collective-permute-start | bytes 516104 | tf_op jit(solution)/shard_map/ppermute | solution.py:42
  31.4 26.3 %collective-permute-start.1 = (bf16[32,5376]{1,0:T(8,128)(2,1)S(1)}, bf16[32,5376]{1,0:T(8,128)(2,1)S(1)}, u32[]{:S(2)}, u32[]{:S(2)}) collective-permute-start(bf16[32,5376]{1,0:T(8,128)(2,1)S(1)} %pad_maximum_fusion), channel_id=1, source_target_pairs={{0,2},{1,3},{2,4},{3,5},{4,6},{5,7},{6,8},{7,9},{8,10},{9,11},{10,... | collective-permute-start | bytes 1032200 | tf_op jit(solution)/shard_map/ppermute | solution.py:42
  37.6 25.7 %collective-permute-start.2 = (bf16[32,5376]{1,0:T(8,128)(2,1)S(1)}, bf16[32,5376]{1,0:T(8,128)(2,1)S(1)}, u32[]{:S(2)}, u32[]{:S(2)}) collective-permute-start(bf16[32,5376]{1,0:T(8,128)(2,1)S(1)} %pad_maximum_fusion), channel_id=1, source_target_pairs={{0,14},{1,15},{2,0},{3,1},{4,2},{5,3},{6,4},{7,5},{8,6},{9,7},{10,... | collective-permute-start | bytes 1032200 | tf_op jit(solution)/shard_map/ppermute | solution.py:42
  46.9 31.1 %copy-start.3 = (bf16[48,5376]{1,0:T(8,128)(2,1)}, bf16[48,5376]{1,0:T(8,128)(2,1)S(1)}, u32[]{:S(2)}) copy-start(bf16[48,5376]{1,0:T(8,128)(2,1)S(1)} %collective-permute-done.16.refs_5_) | copy-start | bytes 1548292
  46.9 79.0 %collective-permute-start.7 = (bf16[32,5376]{1,0:T(8,128)(2,1)S(1)}, bf16[32,5376]{1,0:T(8,128)(2,1)S(1)}, u32[]{:S(2)}, u32[]{:S(2)}) collective-permute-start(bf16[32,5376]{1,0:T(8,128)(2,1)S(1)} %pad_maximum_fusion), channel_id=1, source_target_pairs={{0,8},{1,9},{2,10},{3,11},{4,12},{5,13},{6,14},{7,15},{8,0},{9,1},... | collective-permute-start | bytes 1032200 | tf_op jit(solution)/shard_map/ppermute | solution.py:42
  52.6 78.7 %collective-permute-start.18 = (bf16[48,5376]{1,0:T(8,128)(2,1)S(1)}, bf16[48,5376]{1,0:T(8,128)(2,1)S(1)}, u32[]{:S(2)}, u32[]{:S(2)}) collective-permute-start(bf16[48,5376]{1,0:T(8,128)(2,1)S(1)} %broadcast_select_fusion), channel_id=1, source_target_pairs={{0,128},{1,385},{2,130},{3,387},{4,132},{5,389},{6,134},{7,391},{8... | collective-permute-start | bytes 1548296 | tf_op jit(solution)/shard_map/ppermute | solution.py:42
  55.8 39.4 %collective-permute-start.11 = (bf16[48,5376]{1,0:T(8,128)(2,1)}, bf16[48,5376]{1,0:T(8,128)(2,1)}, u32[]{:S(2)}, u32[]{:S(2)}) collective-permute-start(bf16[48,5376]{1,0:T(8,128)(2,1)} %collective-permute-done.10.refs_8_), channel_id=1, source_target_pairs={{0,32},{1,97},{2,34},{3,99},{4,36},{5,101},{6,38},{7,103},{8,40},{... | collective-permute-start | bytes 1548296 | tf_op jit(solution)/shard_map/ppermute | solution.py:42
  57.7 75.5 %collective-permute-start.19 = (bf16[48,5376]{1,0:T(8,128)(2,1)}, bf16[48,5376]{1,0:T(8,128)(2,1)S(1)}, u32[]{:S(2)}, u32[]{:S(2)}) collective-permute-start(bf16[48,5376]{1,0:T(8,128)(2,1)} %collective-permute-done.10.refs_8_), channel_id=1, source_target_pairs={{0,128},{1,129},{2,130},{3,131},{4,132},{5,133},{6,134},{7,135},{8... | collective-permute-start | bytes 1548296 | tf_op jit(solution)/shard_map/ppermute | solution.py:42
  63.3 11.2 %collective-permute-start.3 = (bf16[32,5376]{1,0:T(8,128)(2,1)S(1)}, bf16[32,5376]{1,0:T(8,128)(2,1)S(1)}, u32[]{:S(2)}, u32[]{:S(2)}) collective-permute-start(bf16[32,5376]{1,0:T(8,128)(2,1)S(1)} %collective-permute-done.1), channel_id=1, source_target_pairs={{0,2},{1,3},{2,4},{3,5},{4,6},{5,7},{6,8},{7,9},{8,10},{9,11},{10,... | collective-permute-start | bytes 1032200 | tf_op jit(solution)/shard_map/ppermute | solution.py:42
  74.5 8.0 %collective-permute-start.4 = (bf16[32,5376]{1,0:T(8,128)(2,1)S(1)}, bf16[32,5376]{1,0:T(8,128)(2,1)S(1)}, u32[]{:S(2)}, u32[]{:S(2)}) collective-permute-start(bf16[32,5376]{1,0:T(8,128)(2,1)S(1)} %collective-permute-done.2), channel_id=1, source_target_pairs={{0,14},{1,15},{2,0},{3,1},{4,2},{5,3},{6,4},{7,5},{8,6},{9,7},{10,... | collective-permute-start | bytes 1032200 | tf_op jit(solution)/shard_map/ppermute | solution.py:42
  82.4 9.2 %collective-permute-start.5 = (bf16[32,5376]{1,0:T(8,128)(2,1)S(1)}, bf16[32,5376]{1,0:T(8,128)(2,1)S(1)}, u32[]{:S(2)}, u32[]{:S(2)}) collective-permute-start(bf16[32,5376]{1,0:T(8,128)(2,1)S(1)} %collective-permute-done.3), channel_id=1, source_target_pairs={{0,2},{1,3},{2,4},{3,5},{4,6},{5,7},{6,8},{7,9},{8,10},{9,11},{10,... | collective-permute-start | bytes 1032200 | tf_op jit(solution)/shard_map/ppermute | solution.py:42
  86.6 75.9 %copy-start.16 = (f32[1,512]{1,0:T(1,128)S(1)}, f32[1,512]{1,0:T(1,128)}, u32[]{:S(2)}) copy-start(f32[1,512]{1,0:T(1,128)} %param.11) | copy-start | bytes 6148
  91.6 8.0 %collective-permute-start.6 = (bf16[32,5376]{1,0:T(8,128)(2,1)S(1)}, bf16[32,5376]{1,0:T(8,128)(2,1)S(1)}, u32[]{:S(2)}, u32[]{:S(2)}) collective-permute-start(bf16[32,5376]{1,0:T(8,128)(2,1)S(1)} %collective-permute-done.4), channel_id=1, source_target_pairs={{0,14},{1,15},{2,0},{3,1},{4,2},{5,3},{6,4},{7,5},{8,6},{9,7},{10,... | collective-permute-start | bytes 1032200 | tf_op jit(solution)/shard_map/ppermute | solution.py:42
  95.2 53.6 %collective-permute-start.20 = (bf16[48,5376]{1,0:T(8,128)(2,1)}, bf16[48,5376]{1,0:T(8,128)(2,1)S(1)}, u32[]{:S(2)}, u32[]{:S(2)}) collective-permute-start(bf16[48,5376]{1,0:T(8,128)(2,1)} %collective-permute-done.10.refs_8_), channel_id=1, source_target_pairs={{0,384},{1,385},{2,386},{3,387},{4,388},{5,389},{6,390},{7,391},{8... | collective-permute-start | bytes 1548296 | tf_op jit(solution)/shard_map/ppermute | solution.py:42
  99.6 24.4 %collective-permute-start.12 = (bf16[48,5376]{1,0:T(8,128)(2,1)}, bf16[48,5376]{1,0:T(8,128)(2,1)S(1)}, u32[]{:S(2)}, u32[]{:S(2)}) collective-permute-start(bf16[48,5376]{1,0:T(8,128)(2,1)} %collective-permute-done.11.refs_12_), channel_id=1, source_target_pairs={{0,32},{1,97},{2,34},{3,99},{4,36},{5,101},{6,38},{7,103},{8,40},{... | collective-permute-start | bytes 1548296 | tf_op jit(solution)/shard_map/ppermute | solution.py:42
  124.1 18.0 %copy-start.5 = (bf16[48,5376]{1,0:T(8,128)(2,1)}, bf16[48,5376]{1,0:T(8,128)(2,1)S(1)}, u32[]{:S(2)}) copy-start(bf16[48,5376]{1,0:T(8,128)(2,1)S(1)} %collective-permute-done.12.refs_4_) | copy-start | bytes 1548292
  124.1 16.0 %collective-permute-start.13 = (bf16[48,5376]{1,0:T(8,128)(2,1)S(1)}, bf16[48,5376]{1,0:T(8,128)(2,1)S(1)}, u32[]{:S(2)}, u32[]{:S(2)}) collective-permute-start(bf16[48,5376]{1,0:T(8,128)(2,1)S(1)} %collective-permute-done.12.refs_4_), channel_id=1, source_target_pairs={{0,128},{1,129},{2,130},{3,131},{4,132},{5,133},{6,134},{7,135},{8... | collective-permute-start | bytes 1548296 | tf_op jit(solution)/shard_map/ppermute | solution.py:42
  126.0 16.0 %collective-permute-start.14 = (bf16[48,5376]{1,0:T(8,128)(2,1)S(1)}, bf16[48,5376]{1,0:T(8,128)(2,1)S(1)}, u32[]{:S(2)}, u32[]{:S(2)}) collective-permute-start(bf16[48,5376]{1,0:T(8,128)(2,1)S(1)} %collective-permute-done.12.refs_4_), channel_id=1, source_target_pairs={{0,384},{1,385},{2,386},{3,387},{4,388},{5,389},{6,390},{7,391},{8... | collective-permute-start | bytes 1548296 | tf_op jit(solution)/shard_map/ppermute | solution.py:42
  131.3 16.6 %copy-start.8 = (bf16[48,5376]{1,0:T(8,128)(2,1)}, bf16[48,5376]{1,0:T(8,128)(2,1)S(1)}, u32[]{:S(2)}) copy-start(bf16[48,5376]{1,0:T(8,128)(2,1)S(1)} %collective-permute-done.18.refs_7_) | copy-start | bytes 1548292
  131.3 38.0 %collective-permute-start.8 = (bf16[160,5376]{1,0:T(8,128)(2,1)}, bf16[160,5376]{1,0:T(8,128)(2,1)}, u32[]{:S(2)}, u32[]{:S(2)}) collective-permute-start(bf16[160,5376]{1,0:T(8,128)(2,1)} %constant_dynamic-update-slice_fusion.refs_0_), channel_id=1, source_target_pairs={{0,1},{1,0},{2,3},{3,2},{4,5},{5,4},{6,7},{7,6},{8,9},{9,8},{10,11... | collective-permute-start | bytes 5160968 | tf_op jit(solution)/shard_map/ppermute | solution.py:42
  133.3 0.8 copy-start.10
  134.1 22.9 %collective-permute-start.22 = (bf16[48,5376]{1,0:T(8,128)(2,1)}, bf16[48,5376]{1,0:T(8,128)(2,1)S(1)}, u32[]{:S(2)}, u32[]{:S(2)}) collective-permute-start(bf16[48,5376]{1,0:T(8,128)(2,1)} %collective-permute-done.11.refs_12_), channel_id=1, source_target_pairs={{0,128},{1,129},{2,130},{3,131},{4,132},{5,133},{6,134},{7,135},{8... | collective-permute-start | bytes 1548296 | tf_op jit(solution)/shard_map/ppermute | solution.py:42
  140.1 14.8 %collective-permute-start.21 = (bf16[48,5376]{1,0:T(8,128)(2,1)S(1)}, bf16[48,5376]{1,0:T(8,128)(2,1)}, u32[]{:S(2)}, u32[]{:S(2)}) collective-permute-start(bf16[48,5376]{1,0:T(8,128)(2,1)S(1)} %collective-permute-done.18.refs_7_), channel_id=1, source_target_pairs={{0,32},{1,97},{2,34},{3,99},{4,36},{5,101},{6,38},{7,103},{8,40},{... | collective-permute-start | bytes 1548296 | tf_op jit(solution)/shard_map/ppermute | solution.py:42
  142.0 27.3 %collective-permute-start.9 = (bf16[96,5376]{1,0:T(8,128)(2,1)}, bf16[96,5376]{1,0:T(8,128)(2,1)}, u32[]{:S(2)}, u32[]{:S(2)}) collective-permute-start(bf16[96,5376]{1,0:T(8,128)(2,1)} %constant_dynamic-update-slice_fusion.5.refs_1_), channel_id=1, source_target_pairs={{0,1},{1,0},{2,3},{3,2},{4,5},{5,4},{6,7},{7,6},{8,9},{9,8},{10,11... | collective-permute-start | bytes 3096584 | tf_op jit(solution)/shard_map/ppermute | solution.py:42
  147.9 0.8 copy-start.1
  148.8 0.8 copy-start.12
  149.6 16.2 %collective-permute-start.23 = (bf16[48,5376]{1,0:T(8,128)(2,1)}, bf16[48,5376]{1,0:T(8,128)(2,1)}, u32[]{:S(2)}, u32[]{:S(2)}) collective-permute-start(bf16[48,5376]{1,0:T(8,128)(2,1)} %collective-permute-done.11.refs_12_), channel_id=1, source_target_pairs={{0,384},{1,385},{2,386},{3,387},{4,388},{5,389},{6,390},{7,391},{8... | collective-permute-start | bytes 1548296 | tf_op jit(solution)/shard_map/ppermute | solution.py:42
  154.9 14.4 %collective-permute-start.24 = (bf16[48,5376]{1,0:T(8,128)(2,1)}, bf16[48,5376]{1,0:T(8,128)(2,1)}, u32[]{:S(2)}, u32[]{:S(2)}) collective-permute-start(bf16[48,5376]{1,0:T(8,128)(2,1)} %collective-permute-done.21.refs_11_), channel_id=1, source_target_pairs={{0,32},{1,97},{2,34},{3,99},{4,36},{5,101},{6,38},{7,103},{8,40},{... | collective-permute-start | bytes 1548296 | tf_op jit(solution)/shard_map/ppermute | solution.py:42
  156.9 0.9 copy-start.14
  157.8 28.2 %collective-permute-start.15 = (bf16[48,5376]{1,0:T(8,128)(2,1)}, bf16[48,5376]{1,0:T(8,128)(2,1)}, u32[]{:S(2)}, u32[]{:S(2)}) collective-permute-start(bf16[48,5376]{1,0:T(8,128)(2,1)} %broadcast_select_fusion.1), channel_id=1, source_target_pairs={{0,128},{1,385},{2,130},{3,387},{4,132},{5,389},{6,134},{7,391},{8... | collective-permute-start | bytes 1548296 | tf_op jit(solution)/shard_map/ppermute | solution.py:42
  164.9 21.1 %copy-start.6 = (bf16[48,5376]{1,0:T(8,128)(2,1)S(1)}, bf16[48,5376]{1,0:T(8,128)(2,1)}, u32[]{:S(2)}) copy-start(bf16[48,5376]{1,0:T(8,128)(2,1)} %copy-done.5) | copy-start | bytes 1548292
  165.8 20.2 %copy-start.2 = (bf16[48,5376]{1,0:T(8,128)(2,1)S(1)}, bf16[48,5376]{1,0:T(8,128)(2,1)}, u32[]{:S(2)}) copy-start(bf16[48,5376]{1,0:T(8,128)(2,1)} %copy-done.1) | copy-start | bytes 1548292
  169.3 1.0 copy-start.4
  170.3 1.0 copy-start.7
  171.4 1.0 copy-start.9
  172.4 1.0 copy-start.11
  173.4 1.0 copy-start.13
  174.5 1.0 copy-start.15

commit v3 on v2

--- a/solution.py
+++ b/solution.py
@@ -31,19 +31,12 @@
 DOWN_X = routes(lambda x, y, z, c: (x - 1, y, z, c))
 RING_X = routes(lambda x, y, z, c: (x + (1 - 2 * c), y, z, c))
 RING_Y = routes(lambda x, y, z, c: (x, y // 4 * 4 + (y + (1 - 2 * c)) % 4, z, c))
-OTHER_Y = routes(lambda x, y, z, c: (x, (y + 4) % 8, z, c))
-UP_Z = routes(lambda x, y, z, c: (x, y, z + 1, c))
-DOWN_Z = routes(lambda x, y, z, c: (x, y, z - 1, c))
-FAR_Z = routes(lambda x, y, z, c: (x, y, z + 4, c))
 CORE = routes(lambda x, y, z, c: (x, y, z, 1 - c))
+SAME_CORE = [list(range(core, 32, 2)) for core in range(2)]
 
 
 def send(value, pairs):
     return lax.ppermute(value, AXES, pairs)
-
-
-def stack(*pieces):
-    return jnp.concatenate(pieces, axis=0)
 
 
 def turn(core, up, down):
@@ -65,8 +58,8 @@
     sources, targets = refs[:n_sources], refs[n_sources : n_sources + n_targets]
     refs = refs[n_sources + n_targets :]
     if last:
-        row_at, before_ref = refs[:2]
-        refs = refs[2:]
+        row_at, *before_refs = refs[:3]
+        refs = refs[3:]
     out_ref, rows, cols, acc, sem = refs
     copies = gather_rows(sources, rows, sem, 0) + gather_rows(targets, cols, sem, n_sources)
     for copy in copies:
@@ -87,19 +80,20 @@
     if not last:
         out_ref[...] = placed.astype(jnp.bfloat16)
         return
-    placed = (placed + before_ref[...].astype(jnp.float32)).astype(jnp.bfloat16)
+    before = jnp.concatenate([before_ref[...] for before_ref in before_refs], axis=0)
+    placed = (placed + before.astype(jnp.float32)).astype(jnp.bfloat16)
     for g in range(out_ref.shape[0] // 16):
         out_ref[pl.ds(pl.multiple_of(row_at[g], 16), 16), :] = placed[g * 16 : (g + 1) * 16]
 
 
-def product(act, order, sources, targets, row_at=None, before=None):
+def product(act, order, sources, targets, row_at=None, before=()):
     n_rows, (n_cols, n_out), depth = act.shape[0], order.shape, sources[0].shape[1]
     whole, smem, anywhere = (pl.BlockSpec(memory_space=m) for m in (pltpu.VMEM, pltpu.SMEM, pl.ANY))
-    last = before is not None
+    last = len(before) > 0
     return pl.pallas_call(
         functools.partial(product_kernel, len(sources), len(targets), last),
         out_shape=jax.ShapeDtypeStruct((n_rows, n_out), jnp.bfloat16),
-        in_specs=[whole, whole] + [anywhere] * (len(sources) + len(targets)) + ([smem, whole] if last else []),
+        in_specs=[whole, whole] + [anywhere] * (len(sources) + len(targets)) + ([smem] + [whole] * len(before) if last else []),
         out_specs=whole,
         scratch_shapes=[
             pltpu.VMEM((n_rows, depth), jnp.bfloat16),
@@ -108,22 +102,23 @@
             pltpu.SemaphoreType.DMA((len(sources) + len(targets),)),
         ],
         compiler_params=pltpu.CompilerParams(vmem_limit_bytes=32 << 20),
-        name="last_product" if last else "first_product",
-    )(act, order, *sources, *targets, *((row_at, before) if last else ()))
+    )(act, order, *sources, *targets, *((row_at, *before) if last else ()))
 
 
 def edges_of(decoder, encoder, row_ids, counts, activity):
     slot_count = row_ids.shape[1]
     prompt, owner = lax.axis_index("prompt"), lax.axis_index("feat")
-    core, chip = owner % 2, owner // 2
-    half, z = chip // 8, chip % 8
+    core = owner % 2
     x, y = prompt // 4, prompt % 4
     sign = 1 - 2 * core
 
-    picked_rows = jnp.take(decoder, row_ids[0], axis=0)
-    live_count = lax.dynamic_index_in_dim(counts[0], owner, 0, keepdims=False)
+    picked_rows = decoder.at[row_ids[0]].get(mode="promise_in_bounds")
+    owners = jnp.arange(counts.shape[1], dtype=jnp.int32)
+    live_count = jnp.sum(jnp.where(owners == owner, counts[0], 0))
     live_slots = jnp.arange(slot_count, dtype=jnp.int32) < live_count
     source_rows = jnp.where(live_slots[:, None], picked_rows, jnp.zeros((), picked_rows.dtype))
+    mine = lax.all_gather(source_rows, "feat", axis=0, tiled=True, axis_index_groups=SAME_CORE)
+    theirs = send(mine, CORE)
 
     y0 = encoder
     y1 = send(y0, RING_Y)
@@ -138,19 +133,8 @@
     f2 = send(f1, RING_Y)
     d3 = send(turn(core, d1, d2), RING_X)
 
-    own = lax.optimization_barrier(stack(source_rows, send(source_rows, OTHER_Y)))
-    u1, w1 = send(own, UP_Z), send(own, DOWN_Z)
-    u2, w2 = send(u1, UP_Z), send(w1, DOWN_Z)
-    u3, w3 = send(u2, UP_Z), send(w2, DOWN_Z)
-    zf = send(own, FAR_Z)
-    near = stack(own, u1, w1, u2, w2)
-    away = stack(u3, w3, zf)
-    sources = [near, away, send(near, CORE), send(away, CORE)]
-
-    hop = jnp.array([0, -1, 1, -2, 2, -3, 3, 4], jnp.int32)[None, :, None]
-    side = jnp.arange(2, dtype=jnp.int32)[:, None, None]
-    flip = jnp.arange(2, dtype=jnp.int32)[None, None, :]
-    feat_from = ((half ^ flip) * 8 + (z + hop) % 8) * 2 + (core ^ side)
+    side = jnp.arange(2, dtype=jnp.int32)[:, None]
+    feat_from = jnp.arange(16, dtype=jnp.int32)[None, :] * 2 + (core ^ side)
     group_from = feat_from.reshape(-1).astype(jnp.int32)
     x_from = (x + jnp.array([0, -1, 1, 2], jnp.int32)) % 4
     y_from = (y - sign * jnp.arange(4, dtype=jnp.int32)) % 4
@@ -165,8 +149,14 @@
         place = jnp.arange(origin.size * width, dtype=jnp.int32)
         return (col_at[:, None] == place[None, :]).astype(jnp.bfloat16)
 
-    part = product(act, order(first_of), sources, [y0, a1, a2, a3, y1, b1, b2, f1, y2, c1, c2, f2])
-    edges = product(act, order(last_of), sources, [y3, d1, d2, d3], group_from * slot_count, part)
+    early = [y0, a1, a2, a3, y1, b1, b2, f1, y2, c1, c2, f2]
+    half_rows = act.shape[0] // 2
+    part_mine = product(act[:half_rows], order(first_of), [mine], early)
+    part_theirs = product(act[half_rows:], order(first_of), [theirs], early)
+    edges = product(
+        act, order(last_of), [mine, theirs], [y3, d1, d2, d3],
+        group_from * slot_count, (part_mine, part_theirs),
+    )
     return edges[None]
 
 

time: 197 us -> 225 us (1.14)
  waiting for transfers between devices: 58.4 us -> 91 us
  starting transfers between devices: 86.2 us -> 67.9 us
  between operations: 0.54 us -> 13.8 us
  local copies, waits for them, and re-layouts: 21.2 us -> 14.6 us
  Pallas kernels: 18 us -> 22.6 us
  other arithmetic: 9.25 us -> 11.7 us
    all_gather x0 -> x1, waiting for transfers between devices: none -> 69.4 us  [edges_of(): lax.all_gather(source_rows, 'feat', axis=0, tiled=True, axis_index_groups...]
    ppermute x25 -> x16, waiting for transfers between devices: 58.4 us -> 21.6 us  [send(): return lax.ppermute(value, AXES, pairs)]
    ppermute x25 -> x16, starting transfers between devices: 86.2 us -> 67.9 us  [send(): return lax.ppermute(value, AXES, pairs)]
    unnamed x43 -> x27, local copies, waits for them, and re-layouts: 14.6 us -> 8.01 us
    pallas_call x2 -> x3, Pallas kernels: 18 us -> 22.6 us  [product(): pl.pallas_call(functools.partial(product_kernel, len(sources), len(target...]
    slice x0 -> x3, local copies, waits for them, and re-layouts: none -> 2.79 us  [the longest x2 2.05 us: edges_of(): part_theirs = product(act[half_rows:], order(first_of), [theirs], early)]
  transfers between devices with their start and end apart: 25 -> 17, of which waited for: 10 -> 5; matrix products, arithmetic and copies ran while one was open for 11% -> 7% of each run, Pallas kernels for 5% -> 7%
where the time goes in v3:
time: 225 us; the launch traced here: 222 us
  waiting for transfers between devices  91 us (40%)
  starting transfers between devices  67.9 us (30%)
  Pallas kernels  22.6 us (10%)
  local copies, waits for them, and re-layouts  14.6 us (6%)
  between operations  13.8 us (6%)
  other arithmetic  11.7 us (5%)
    all_gather x1, waiting for transfers between devices, edges_of(): lax.all_gather(source_rows, 'feat', axis=0, tiled=True, axis_index_groups...  69.4 us
    ppermute x16, starting transfers between devices, send(): return lax.ppermute(value, AXES, pairs)  67.9 us
    pallas_call x3, Pallas kernels, product(): pl.pallas_call(functools.partial(product_kernel, len(sources), len(target...  22.6 us
    ppermute x16, waiting for transfers between devices, send(): return lax.ppermute(value, AXES, pairs)  21.6 us
    unnamed x27, local copies, waits for them, and re-layouts  8.01 us
  transfers between devices with their start and end apart: 17, of which 5 were waited for; matrix products, arithmetic and copies ran while one was open for 7% of the time, Pallas kernels for 7%

profile of v3, /device:TPU:1, one launch (start us, length us, event | category | flops | bytes accessed | tf_op | source)
XLA Modules:
  0.0 221.6 jit_solution(93902070064399960)
XLA Ops:
  6.5 1.4 fusion.4
  8.0 0.6 iota_compare_fusion.2
  8.6 0.7 fusion.7
  9.3 0.7 gather_fusion.1
  10.0 0.8 broadcast_select_fusion.2
  10.8 3.9 %collective-permute-start.7 = (bf16[48,5376]{1,0:T(8,128)(2,1)}, bf16[48,5376]{1,0:T(8,128)(2,1)S(1)}, u32[]{:S(2)}, u32[]{:S(2)}) collective-permute-start(bf16[48,5376]{1,0:T(8,128)(2,1)} %refs_1_.3), channel_id=1, source_target_pairs={{0,128},{1,129},{2,130},{3,131},{4,132},{5,133},{6,134},{7,135},{8... | collective-permute-start | bytes 1548296 | tf_op jit(solution)/shard_map/ppermute | solution.py:39
  14.7 3.2 %collective-permute-start.8 = (bf16[48,5376]{1,0:T(8,128)(2,1)}, bf16[48,5376]{1,0:T(8,128)(2,1)}, u32[]{:S(2)}, u32[]{:S(2)}) collective-permute-start(bf16[48,5376]{1,0:T(8,128)(2,1)} %refs_1_.3), channel_id=1, source_target_pairs={{0,384},{1,385},{2,386},{3,387},{4,388},{5,389},{6,390},{7,391},{8... | collective-permute-start | bytes 1548296 | tf_op jit(solution)/shard_map/ppermute | solution.py:39
  17.9 5.4 %collective-permute-start.1 = (bf16[48,5376]{1,0:T(8,128)(2,1)}, bf16[48,5376]{1,0:T(8,128)(2,1)}, u32[]{:S(2)}, u32[]{:S(2)}) collective-permute-start(bf16[48,5376]{1,0:T(8,128)(2,1)} %refs_1_.3), channel_id=1, source_target_pairs={{0,32},{1,97},{2,34},{3,99},{4,36},{5,101},{6,38},{7,103},{8,40},{... | collective-permute-start | bytes 1548296 | tf_op jit(solution)/shard_map/ppermute | solution.py:39
  23.4 0.7 and_select_fusion
  24.1 7.7 %collective-permute-done.1.refs_5_ = bf16[48,5376]{1,0:T(8,128)(2,1)} collective-permute-done((bf16[48,5376]{1,0:T(8,128)(2,1)}, bf16[48,5376]{1,0:T(8,128)(2,1)}, u32[]{:S(2)}, u32[]{:S(2)}) %collective-permute-start.1) | collective-permute-done | bytes 516128 | tf_op jit(solution)/shard_map/ppermute | solution.py:39
  31.8 5.6 %collective-permute-start.2 = (bf16[48,5376]{1,0:T(8,128)(2,1)}, bf16[48,5376]{1,0:T(8,128)(2,1)}, u32[]{:S(2)}, u32[]{:S(2)}) collective-permute-start(bf16[48,5376]{1,0:T(8,128)(2,1)} %collective-permute-done.1.refs_5_), channel_id=1, source_target_pairs={{0,32},{1,97},{2,34},{3,99},{4,36},{5,101},{6,38},{7,103},{8,40},{... | collective-permute-start | bytes 1548296 | tf_op jit(solution)/shard_map/ppermute | solution.py:39
  37.4 0.6 broadcast_multiply_fusion
  38.8 1.4 reduce.3
  40.3 6.3 %collective-permute-done.2.refs_9_ = bf16[48,5376]{1,0:T(8,128)(2,1)} collective-permute-done((bf16[48,5376]{1,0:T(8,128)(2,1)}, bf16[48,5376]{1,0:T(8,128)(2,1)}, u32[]{:S(2)}, u32[]{:S(2)}) %collective-permute-start.2) | collective-permute-done | bytes 516128 | tf_op jit(solution)/shard_map/ppermute | solution.py:39
  46.6 3.7 %collective-permute-start.3 = (bf16[48,5376]{1,0:T(8,128)(2,1)}, bf16[48,5376]{1,0:T(8,128)(2,1)}, u32[]{:S(2)}, u32[]{:S(2)}) collective-permute-start(bf16[48,5376]{1,0:T(8,128)(2,1)} %collective-permute-done.2.refs_9_), channel_id=1, source_target_pairs={{0,32},{1,97},{2,34},{3,99},{4,36},{5,101},{6,38},{7,103},{8,40},{... | collective-permute-start | bytes 1548296 | tf_op jit(solution)/shard_map/ppermute | solution.py:39
  50.3 69.4 %all-gather.2.cloned.1.call-done.refs_0_ = bf16[256,5376]{1,0:T(8,128)(2,1)} async-done(((bf16[16,5376]{1,0:T(8,128)(2,1)}), bf16[256,5376]{1,0:T(8,128)(2,1)}) %all-gather.2.cloned.1.call-update) | async-done | bytes 2752528 | tf_op jit(solution)/shard_map/all_gather | solution.py:120
  119.7 13.5 %collective-permute-start = (bf16[256,5376]{1,0:T(8,128)(2,1)}, bf16[256,5376]{1,0:T(8,128)(2,1)}, u32[]{:S(2)}, u32[]{:S(2)}) collective-permute-start(bf16[256,5376]{1,0:T(8,128)(2,1)} %all-gather.2.cloned.1.call-done.refs_0_), channel_id=1, source_target_pairs={{0,1},{1,0},{2,3},{3,2},{4,5},{5,4},{6,7},{7,6},{8,9},{9,8},{10,11... | collective-permute-start | bytes 8257544 | tf_op jit(solution)/shard_map/ppermute | solution.py:39
  133.2 1.9 broadcast_select_fusion
  135.1 5.2 %collective-permute-start.9 = (bf16[48,5376]{1,0:T(8,128)(2,1)}, bf16[48,5376]{1,0:T(8,128)(2,1)}, u32[]{:S(2)}, u32[]{:S(2)}) collective-permute-start(bf16[48,5376]{1,0:T(8,128)(2,1)} %broadcast_select_fusion), channel_id=1, source_target_pairs={{0,128},{1,385},{2,130},{3,387},{4,132},{5,389},{6,134},{7,391},{8... | collective-permute-start | bytes 1548296 | tf_op jit(solution)/shard_map/ppermute | solution.py:39
  140.2 1.9 collective-permute-start.4
  142.2 4.6 %collective-permute-start.5 = (bf16[48,5376]{1,0:T(8,128)(2,1)}, bf16[48,5376]{1,0:T(8,128)(2,1)}, u32[]{:S(2)}, u32[]{:S(2)}) collective-permute-start(bf16[48,5376]{1,0:T(8,128)(2,1)} %collective-permute-done.3.refs_2_), channel_id=1, source_target_pairs={{0,384},{1,385},{2,386},{3,387},{4,388},{5,389},{6,390},{7,391},{8... | collective-permute-start | bytes 1548296 | tf_op jit(solution)/shard_map/ppermute | solution.py:39
  147.3 0.7 iota_add_fusion
  148.6 1.9 collective-permute-start.10
  150.5 4.6 %collective-permute-start.11 = (bf16[48,5376]{1,0:T(8,128)(2,1)}, bf16[48,5376]{1,0:T(8,128)(2,1)S(1)}, u32[]{:S(2)}, u32[]{:S(2)}) collective-permute-start(bf16[48,5376]{1,0:T(8,128)(2,1)} %collective-permute-done.1.refs_5_), channel_id=1, source_target_pairs={{0,384},{1,385},{2,386},{3,387},{4,388},{5,389},{6,390},{7,391},{8... | collective-permute-start | bytes 1548296 | tf_op jit(solution)/shard_map/ppermute | solution.py:39
  155.1 2.3 %collective-permute-done.4.refs_3_ = bf16[48,5376]{1,0:T(8,128)(2,1)} collective-permute-done((bf16[48,5376]{1,0:T(8,128)(2,1)}, bf16[48,5376]{1,0:T(8,128)(2,1)}, u32[]{:S(2)}, u32[]{:S(2)}) %collective-permute-start.4) | collective-permute-done | bytes 516128 | tf_op jit(solution)/shard_map/ppermute | solution.py:39
  157.4 1.9 collective-permute-start.13
  159.4 1.9 collective-permute-start.12
  161.3 1.9 broadcast_select_fusion.1
  163.2 5.2 %collective-permute-done.10.refs_6_ = bf16[48,5376]{1,0:T(8,128)(2,1)S(1)} collective-permute-done((bf16[48,5376]{1,0:T(8,128)(2,1)}, bf16[48,5376]{1,0:T(8,128)(2,1)S(1)}, u32[]{:S(2)}, u32[]{:S(2)}) %collective-permute-start.10) | collective-permute-done | bytes 516128 | tf_op jit(solution)/shard_map/ppermute | solution.py:39
  168.4 0.8 copy-done.5
  169.2 1.9 collective-permute-start.14
  171.1 3.1 %collective-permute-start.15 = (bf16[48,5376]{1,0:T(8,128)(2,1)}, bf16[48,5376]{1,0:T(8,128)(2,1)}, u32[]{:S(2)}, u32[]{:S(2)}) collective-permute-start(bf16[48,5376]{1,0:T(8,128)(2,1)} %collective-permute-done.12.refs_8_), channel_id=1, source_target_pairs={{0,32},{1,97},{2,34},{3,99},{4,36},{5,101},{6,38},{7,103},{8,40},{... | collective-permute-start | bytes 1548296 | tf_op jit(solution)/shard_map/ppermute | solution.py:39
  174.2 0.8 copy-done.8
  175.0 5.6 %collective-permute-start.6 = (bf16[48,5376]{1,0:T(8,128)(2,1)}, bf16[48,5376]{1,0:T(8,128)(2,1)}, u32[]{:S(2)}, u32[]{:S(2)}) collective-permute-start(bf16[48,5376]{1,0:T(8,128)(2,1)} %broadcast_select_fusion.1), channel_id=1, source_target_pairs={{0,128},{1,385},{2,130},{3,387},{4,132},{5,389},{6,134},{7,391},{8... | collective-permute-start | bytes 1548296 | tf_op jit(solution)/shard_map/ppermute | solution.py:39
  180.6 0.6 iota_add_fusion.1
  181.5 0.8 add.159
  182.2 1.5 slice.27.act_ref
  183.7 0.7 slice.26.act_ref
  184.4 0.7 add.154
  185.2 0.7 mul.65.refs_6_
  186.3 1.8 copy-done.1
  188.0 1.0 copy-done.3
  189.1 1.0 copy-done.6
  190.1 1.0 copy-done.9
  191.2 0.9 copy-done.12
  192.1 7.7 %shard_map.64.refs_7_ = bf16[256,768]{1,0:T(8,128)(2,1)S(1)} custom-call(f32[256,1]{1,0:T(8,128)S(1)} %copy-done.12, bf16[576,768]{1,0:T(8,128)(2,1)S(1)} %fusion.order_ref, bf16[256,5376]{1,0:T(8,128)(2,1)S(1)} %copy-done.1, bf16[48,5376]{1,0:T(8,128)(2,1)S(1)} %copy-done.3, bf16[48,5376]{1,0:T(8,128)(2,1)S(1)} %collective-permute-done.7.refs_2_, ...), custom_call_target="tpu_custom_call" | custom-call | tf_op jit(solution)/shard_map/pallas_call | solution.py:93
  199.9 7.5 %shard_map.65.refs_8_ = bf16[256,768]{1,0:T(8,128)(2,1)S(1)} custom-call(f32[256,1]{1,0:T(8,128)S(1)} %copy-done.11, bf16[576,768]{1,0:T(8,128)(2,1)S(1)} %fusion.order_ref, bf16[256,5376]{1,0:T(8,128)(2,1)} %collective-permute-done.refs_0_.refs_1_, bf16[48,5376]{1,0:T(8,128)(2,1)S(1)} %copy-done.4, bf16[48,5376]{1,0:T(8,128)(2,1)S(1)} %collective-permute-done.7.refs_2_, ...), custom_call_target="tpu_custom_call" | custom-call | tf_op jit(solution)/shard_map/pallas_call | solution.py:93
  207.4 7.3 %shard_map.66 = bf16[512,768]{1,0:T(8,128)(2,1)} custom-call(f32[512,1]{1,0:T(8,128)S(1)} %reshape.167.act_ref, bf16[192,768]{1,0:T(8,128)(2,1)S(1)} %fusion.1.order_ref, bf16[256,5376]{1,0:T(8,128)(2,1)S(1)} %copy-done.2, bf16[256,5376]{1,0:T(8,128)(2,1)} %collective-permute-done.refs_0_.refs_1_, bf16[48,5376]{1,0:T(8,128)(2,1)} %collective-permute-done.3.refs_2_, ...), custom_call_target="tpu_custom_call" | custom-call | tf_op jit(solution)/shard_map/pallas_call | solution.py:93
  (50 shorter events, 2.7 us)
Async XLA Ops:
  6.5 2.8 %copy-start = (bf16[256,5376]{1,0:T(8,128)(2,1)S(1)}, bf16[256,5376]{1,0:T(8,128)(2,1)}, u32[]{:S(2)}) copy-start(bf16[256,5376]{1,0:T(8,128)(2,1)} %param.6) | copy-start | bytes 8257540
  6.5 113.1 %all-gather.2.cloned.1.call-start = ((), (), s32[]{:S(2)}) async-start(), calls=%async_computation | async-start | bytes 2924544 | tf_op jit(solution)/shard_map/all_gather | solution.py:120
  10.8 122.4 %collective-permute-start.7 = (bf16[48,5376]{1,0:T(8,128)(2,1)}, bf16[48,5376]{1,0:T(8,128)(2,1)S(1)}, u32[]{:S(2)}, u32[]{:S(2)}) collective-permute-start(bf16[48,5376]{1,0:T(8,128)(2,1)} %refs_1_.3), channel_id=1, source_target_pairs={{0,128},{1,129},{2,130},{3,131},{4,132},{5,133},{6,134},{7,135},{8... | collective-permute-start | bytes 1548296 | tf_op jit(solution)/shard_map/ppermute | solution.py:39
  14.7 118.5 %collective-permute-start.8 = (bf16[48,5376]{1,0:T(8,128)(2,1)}, bf16[48,5376]{1,0:T(8,128)(2,1)}, u32[]{:S(2)}, u32[]{:S(2)}) collective-permute-start(bf16[48,5376]{1,0:T(8,128)(2,1)} %refs_1_.3), channel_id=1, source_target_pairs={{0,384},{1,385},{2,386},{3,387},{4,388},{5,389},{6,390},{7,391},{8... | collective-permute-start | bytes 1548296 | tf_op jit(solution)/shard_map/ppermute | solution.py:39
  17.9 13.9 %collective-permute-start.1 = (bf16[48,5376]{1,0:T(8,128)(2,1)}, bf16[48,5376]{1,0:T(8,128)(2,1)}, u32[]{:S(2)}, u32[]{:S(2)}) collective-permute-start(bf16[48,5376]{1,0:T(8,128)(2,1)} %refs_1_.3), channel_id=1, source_target_pairs={{0,32},{1,97},{2,34},{3,99},{4,36},{5,101},{6,38},{7,103},{8,40},{... | collective-permute-start | bytes 1548296 | tf_op jit(solution)/shard_map/ppermute | solution.py:39
  31.8 14.8 %collective-permute-start.2 = (bf16[48,5376]{1,0:T(8,128)(2,1)}, bf16[48,5376]{1,0:T(8,128)(2,1)}, u32[]{:S(2)}, u32[]{:S(2)}) collective-permute-start(bf16[48,5376]{1,0:T(8,128)(2,1)} %collective-permute-done.1.refs_5_), channel_id=1, source_target_pairs={{0,32},{1,97},{2,34},{3,99},{4,36},{5,101},{6,38},{7,103},{8,40},{... | collective-permute-start | bytes 1548296 | tf_op jit(solution)/shard_map/ppermute | solution.py:39
  46.6 93.6 %collective-permute-start.3 = (bf16[48,5376]{1,0:T(8,128)(2,1)}, bf16[48,5376]{1,0:T(8,128)(2,1)}, u32[]{:S(2)}, u32[]{:S(2)}) collective-permute-start(bf16[48,5376]{1,0:T(8,128)(2,1)} %collective-permute-done.2.refs_9_), channel_id=1, source_target_pairs={{0,32},{1,97},{2,34},{3,99},{4,36},{5,101},{6,38},{7,103},{8,40},{... | collective-permute-start | bytes 1548296 | tf_op jit(solution)/shard_map/ppermute | solution.py:39
  119.7 80.1 %collective-permute-start = (bf16[256,5376]{1,0:T(8,128)(2,1)}, bf16[256,5376]{1,0:T(8,128)(2,1)}, u32[]{:S(2)}, u32[]{:S(2)}) collective-permute-start(bf16[256,5376]{1,0:T(8,128)(2,1)} %all-gather.2.cloned.1.call-done.refs_0_), channel_id=1, source_target_pairs={{0,1},{1,0},{2,3},{3,2},{4,5},{5,4},{6,7},{7,6},{8,9},{9,8},{10,11... | collective-permute-start | bytes 8257544 | tf_op jit(solution)/shard_map/ppermute | solution.py:39
  135.1 15.4 %collective-permute-start.9 = (bf16[48,5376]{1,0:T(8,128)(2,1)}, bf16[48,5376]{1,0:T(8,128)(2,1)}, u32[]{:S(2)}, u32[]{:S(2)}) collective-permute-start(bf16[48,5376]{1,0:T(8,128)(2,1)} %broadcast_select_fusion), channel_id=1, source_target_pairs={{0,128},{1,385},{2,130},{3,387},{4,132},{5,389},{6,134},{7,391},{8... | collective-permute-start | bytes 1548296 | tf_op jit(solution)/shard_map/ppermute | solution.py:39
  140.2 17.2 %collective-permute-start.4 = (bf16[48,5376]{1,0:T(8,128)(2,1)}, bf16[48,5376]{1,0:T(8,128)(2,1)}, u32[]{:S(2)}, u32[]{:S(2)}) collective-permute-start(bf16[48,5376]{1,0:T(8,128)(2,1)} %collective-permute-done.3.refs_2_), channel_id=1, source_target_pairs={{0,128},{1,129},{2,130},{3,131},{4,132},{5,133},{6,134},{7,135},{8... | collective-permute-start | bytes 1548296 | tf_op jit(solution)/shard_map/ppermute | solution.py:39
  142.2 17.2 %collective-permute-start.5 = (bf16[48,5376]{1,0:T(8,128)(2,1)}, bf16[48,5376]{1,0:T(8,128)(2,1)}, u32[]{:S(2)}, u32[]{:S(2)}) collective-permute-start(bf16[48,5376]{1,0:T(8,128)(2,1)} %collective-permute-done.3.refs_2_), channel_id=1, source_target_pairs={{0,384},{1,385},{2,386},{3,387},{4,388},{5,389},{6,390},{7,391},{8... | collective-permute-start | bytes 1548296 | tf_op jit(solution)/shard_map/ppermute | solution.py:39
  148.6 19.8 %collective-permute-start.10 = (bf16[48,5376]{1,0:T(8,128)(2,1)}, bf16[48,5376]{1,0:T(8,128)(2,1)S(1)}, u32[]{:S(2)}, u32[]{:S(2)}) collective-permute-start(bf16[48,5376]{1,0:T(8,128)(2,1)} %collective-permute-done.1.refs_5_), channel_id=1, source_target_pairs={{0,128},{1,129},{2,130},{3,131},{4,132},{5,133},{6,134},{7,135},{8... | collective-permute-start | bytes 1548296 | tf_op jit(solution)/shard_map/ppermute | solution.py:39
  150.5 23.7 %collective-permute-start.11 = (bf16[48,5376]{1,0:T(8,128)(2,1)}, bf16[48,5376]{1,0:T(8,128)(2,1)S(1)}, u32[]{:S(2)}, u32[]{:S(2)}) collective-permute-start(bf16[48,5376]{1,0:T(8,128)(2,1)} %collective-permute-done.1.refs_5_), channel_id=1, source_target_pairs={{0,384},{1,385},{2,386},{3,387},{4,388},{5,389},{6,390},{7,391},{8... | collective-permute-start | bytes 1548296 | tf_op jit(solution)/shard_map/ppermute | solution.py:39
  157.4 28.8 %collective-permute-start.13 = (bf16[48,5376]{1,0:T(8,128)(2,1)}, bf16[48,5376]{1,0:T(8,128)(2,1)}, u32[]{:S(2)}, u32[]{:S(2)}) collective-permute-start(bf16[48,5376]{1,0:T(8,128)(2,1)} %collective-permute-done.2.refs_9_), channel_id=1, source_target_pairs={{0,128},{1,129},{2,130},{3,131},{4,132},{5,133},{6,134},{7,135},{8... | collective-permute-start | bytes 1548296 | tf_op jit(solution)/shard_map/ppermute | solution.py:39
  159.4 11.7 %collective-permute-start.12 = (bf16[48,5376]{1,0:T(8,128)(2,1)}, bf16[48,5376]{1,0:T(8,128)(2,1)}, u32[]{:S(2)}, u32[]{:S(2)}) collective-permute-start(bf16[48,5376]{1,0:T(8,128)(2,1)} %collective-permute-done.9.refs_4_), channel_id=1, source_target_pairs={{0,32},{1,97},{2,34},{3,99},{4,36},{5,101},{6,38},{7,103},{8,40},{... | collective-permute-start | bytes 1548296 | tf_op jit(solution)/shard_map/ppermute | solution.py:39
  168.4 0.8 copy-start.5
  169.2 17.1 %collective-permute-start.14 = (bf16[48,5376]{1,0:T(8,128)(2,1)}, bf16[48,5376]{1,0:T(8,128)(2,1)}, u32[]{:S(2)}, u32[]{:S(2)}) collective-permute-start(bf16[48,5376]{1,0:T(8,128)(2,1)} %collective-permute-done.2.refs_9_), channel_id=1, source_target_pairs={{0,384},{1,385},{2,386},{3,387},{4,388},{5,389},{6,390},{7,391},{8... | collective-permute-start | bytes 1548296 | tf_op jit(solution)/shard_map/ppermute | solution.py:39
  171.1 15.1 %collective-permute-start.15 = (bf16[48,5376]{1,0:T(8,128)(2,1)}, bf16[48,5376]{1,0:T(8,128)(2,1)}, u32[]{:S(2)}, u32[]{:S(2)}) collective-permute-start(bf16[48,5376]{1,0:T(8,128)(2,1)} %collective-permute-done.12.refs_8_), channel_id=1, source_target_pairs={{0,32},{1,97},{2,34},{3,99},{4,36},{5,101},{6,38},{7,103},{8,40},{... | collective-permute-start | bytes 1548296 | tf_op jit(solution)/shard_map/ppermute | solution.py:39
  174.2 0.8 copy-start.8
  175.0 32.4 %collective-permute-start.6 = (bf16[48,5376]{1,0:T(8,128)(2,1)}, bf16[48,5376]{1,0:T(8,128)(2,1)}, u32[]{:S(2)}, u32[]{:S(2)}) collective-permute-start(bf16[48,5376]{1,0:T(8,128)(2,1)} %broadcast_select_fusion.1), channel_id=1, source_target_pairs={{0,128},{1,385},{2,130},{3,387},{4,132},{5,389},{6,134},{7,391},{8... | collective-permute-start | bytes 1548296 | tf_op jit(solution)/shard_map/ppermute | solution.py:39
  185.9 14.0 %copy-start.7 = (bf16[48,5376]{1,0:T(8,128)(2,1)S(1)}, bf16[48,5376]{1,0:T(8,128)(2,1)}, u32[]{:S(2)}) copy-start(bf16[48,5376]{1,0:T(8,128)(2,1)} %copy-done.5) | copy-start | bytes 1548292
  186.0 13.8 %copy-start.4 = (bf16[48,5376]{1,0:T(8,128)(2,1)S(1)}, bf16[48,5376]{1,0:T(8,128)(2,1)}, u32[]{:S(2)}) copy-start(bf16[48,5376]{1,0:T(8,128)(2,1)} %refs_1_.3) | copy-start | bytes 1548292
  186.0 13.8 %copy-start.11 = (f32[256,1]{1,0:T(8,128)S(1)}, f32[256,1]{1,0:T(8,128)}, u32[]{:S(2)}) copy-start(f32[256,1]{1,0:T(8,128)} %slice.27.act_ref) | copy-start | bytes 3076
  186.3 1.8 copy-start.1
  188.0 1.0 copy-start.3
  189.1 1.0 copy-start.6
  190.1 1.0 copy-start.9
  191.2 0.9 copy-start.12
  192.1 7.8 %copy-start.10 = (bf16[48,5376]{1,0:T(8,128)(2,1)S(1)}, bf16[48,5376]{1,0:T(8,128)(2,1)}, u32[]{:S(2)}) copy-start(bf16[48,5376]{1,0:T(8,128)(2,1)} %copy-done.8) | copy-start | bytes 1548292
  199.8 7.6 %copy-start.2 = (bf16[256,5376]{1,0:T(8,128)(2,1)S(1)}, bf16[256,5376]{1,0:T(8,128)(2,1)}, u32[]{:S(2)}) copy-start(bf16[256,5376]{1,0:T(8,128)(2,1)} %all-gather.2.cloned.1.call-done.refs_0_) | copy-start | bytes 8257540
Sparse Core Ops, SparseCore 0:
  10.9 108.7 all-gather.1

commit v4 on v2

v4 whole, which is shorter than its diff:
```python
import functools

import jax
import jax.numpy as jnp
from jax import lax
from jax.experimental import pallas as pl
from jax.experimental.pallas import tpu as pltpu
from jax.sharding import PartitionSpec as P


AXES = ("prompt", "feat")


def routes(move):
    pairs = []
    for x in range(4):
        for y in range(8):
            for z in range(8):
                for core in range(2):
                    pairs.append((flat(x, y, z, core), flat(*move(x, y, z, core))))
    return pairs


def flat(x, y, z, core):
    prompt = (x % 4) * 4 + y % 4
    feat = ((y // 4) % 2 * 8 + z % 8) * 2 + core
    return prompt * 32 + feat


UP_X = routes(lambda x, y, z, c: (x + 1, y, z, c))
DOWN_X = routes(lambda x, y, z, c: (x - 1, y, z, c))
FAR_X = routes(lambda x, y, z, c: (x + 2, y, z, c))
RING_Y = routes(lambda x, y, z, c: (x, y // 4 * 4 + (y + (1 - 2 * c)) % 4, z, c))
OTHER_Y = routes(lambda x, y, z, c: (x, (y + 4) % 8, z, c))
UP_Z = routes(lambda x, y, z, c: (x, y, z + 1, c))
DOWN_Z = routes(lambda x, y, z, c: (x, y, z - 1, c))
CORE = routes(lambda x, y, z, c: (x, y, z, 1 - c))

HOPS_Z = (0, -1, 1, -2, 2, -3, 3, -4)
HOPS_X = (0, -1, 1, 2)
PARTS = 3


def send(value, pairs):
    return lax.ppermute(value, AXES, pairs)


def stack_kernel(*refs):
    operands, (out_ref, sem) = refs[:-2], refs[-2:]
    copies, at = [], 0
    for i, operand in enumerate(operands):
        size = operand.shape[0]
        copies.append(pltpu.make_async_copy(operand, out_ref.at[pl.ds(at, size)], sem.at[i]))
        at += size
    for copy in copies:
        copy.start()
    for copy in copies:
        copy.wait()


def stack(*pieces):
    n_rows = sum(piece.shape[0] for piece in pieces)
    anywhere = pl.BlockSpec(memory_space=pl.ANY)
    return pl.pallas_call(
        stack_kernel,
        out_shape=jax.ShapeDtypeStruct((n_rows, pieces[0].shape[1]), pieces[0].dtype),
        in_specs=[anywhere] * len(pieces),
        out_specs=anywhere,
        scratch_shapes=[pltpu.SemaphoreType.DMA((len(pieces),))],
    )(*pieces)


def place():
    prompt, owner = lax.axis_index("prompt"), lax.axis_index("feat")
    chip = owner // 2
    return prompt // 4, prompt % 4, chip // 8, chip % 8, owner % 2


def product_kernel(n_sources, n_targets, first_block, last, *refs):
    act_ref, refs = refs[0], refs[1:]
    if last:
        (rows, before_ref), refs = refs[:2], refs[2:]
        sources = ()
    else:
        sources, refs = refs[:n_sources], refs[n_sources:]
    targets, refs = refs[:n_targets], refs[n_targets:]
    if last:
        out_ref, cols, acc, order, act, sem = refs
    else:
        out_ref, rows, cols, acc, order, act, sem = refs
    depth = rows.shape[1]
    width = depth // PARTS

    def copies(part):
        at_depth = pl.ds(pl.multiple_of(part * width, 128), width)
        found, i = [], 0
        for into, operands in ((rows, sources), (cols, targets)):
            at = 0
            for operand in operands:
                size = operand.shape[0]
                found.append(
                    pltpu.make_async_copy(
                        operand.at[:, at_depth], into.at[pl.ds(at, size), at_depth], sem.at[part, i]
                    )
                )
                at += size
                i += 1
        return found

    for part in range(PARTS):
        for copy in copies(part):
            copy.start()

    x, y, half, z, core = place()
    slots = act_ref.shape[0] // 32
    row_at = []
    for side in range(2):
        for hop in HOPS_Z:
            for flip in range(2):
                feat = ((half ^ flip) * 8 + ((z + hop) & 7)) * 2 + (core ^ side)
                row_at.append(pl.multiple_of(feat * slots, slots))
    for g, at in enumerate(row_at):
        act[g * slots : (g + 1) * slots] = act_ref[pl.ds(at, slots)]
    block = out_ref.shape[1] // 16
    lane = lax.broadcasted_iota(jnp.int32, (block, out_ref.shape[1]), 1)
    line = lax.broadcasted_iota(jnp.int32, (block, out_ref.shape[1]), 0)
    for i in range(cols.shape[0] // block):
        step_y, hop = divmod(first_block + i, len(HOPS_X))
        origin = ((x + HOPS_X[hop]) & 3) * 4 + ((y - (1 - 2 * core) * step_y) & 3)
        order[i * block : (i + 1) * block] = jnp.where(lane == line + origin * block, 1.0, 0.0).astype(jnp.bfloat16)

    acc[...] = jnp.zeros_like(acc)

    @pl.loop(0, PARTS)
    def _(part):
        for copy in copies(part):
            copy.wait()
        at_depth = pl.ds(pl.multiple_of(part * width, 128), width)
        acc[...] += lax.dot_general(
            rows[:, at_depth], cols[:, at_depth], (((1,), (1,)), ((), ())), preferred_element_type=jnp.float32
        )

    edges = (acc[...] * act[...]).astype(jnp.bfloat16)
    placed = jnp.dot(edges, order[...], preferred_element_type=jnp.float32)
    if not last:
        out_ref[...] = placed.astype(jnp.bfloat16)
        return
    placed = (placed + before_ref[...].astype(jnp.float32)).astype(jnp.bfloat16)
    for g, at in enumerate(row_at):
        out_ref[pl.ds(at, slots), :] = placed[g * slots : (g + 1) * slots]


def product(act, first_block, sources, targets, rows=None, before=None):
    depth = targets[0].shape[1]
    n_rows = act.shape[0]
    n_cols, n_out = sum(t.shape[0] for t in targets), targets[0].shape[0] * 16
    whole, anywhere = pl.BlockSpec(memory_space=pltpu.VMEM), pl.BlockSpec(memory_space=pl.ANY)
    last = before is not None
    operands = (act, rows, before, *targets) if last else (act, *sources, *targets)
    edges_shape = jax.ShapeDtypeStruct((n_rows, n_out), jnp.bfloat16)
    rows_shape = jax.ShapeDtypeStruct((n_rows, depth), jnp.bfloat16)
    return pl.pallas_call(
        functools.partial(product_kernel, len(sources), len(targets), first_block, last),
        out_shape=edges_shape if last else (edges_shape, rows_shape),
        in_specs=[whole] * (3 if last else 1) + [anywhere] * (len(sources) + len(targets)),
        out_specs=whole if last else (whole, whole),
        scratch_shapes=[
            pltpu.VMEM((n_cols, depth), jnp.bfloat16),
            pltpu.VMEM((n_rows, n_cols), jnp.float32),
            pltpu.VMEM((n_cols, n_out), jnp.bfloat16),
            pltpu.VMEM((n_rows, 1), jnp.float32),
            pltpu.SemaphoreType.DMA((PARTS, len(sources) + len(targets))),
        ],
        compiler_params=pltpu.CompilerParams(vmem_limit_bytes=24 << 20),
    )(*operands)


def edges_of(decoder, encoder, row_ids, counts, activity):
    slot_count = row_ids.shape[1]
    owner = lax.axis_index("feat")

    picked_rows = decoder.at[row_ids[0]].get(mode="promise_in_bounds")
    owners = jnp.arange(counts.shape[1], dtype=jnp.int32)
    live_count = jnp.sum(jnp.where(owners == owner, counts[0], 0))
    live_slots = jnp.arange(slot_count, dtype=jnp.int32) < live_count
    source_rows = jnp.where(live_slots[:, None], picked_rows, jnp.zeros((), picked_rows.dtype))

    y0 = encoder
    y1 = send(y0, RING_Y)
    y2 = send(y1, RING_Y)
    y3 = send(y2, RING_Y)
    a1, a2, a3 = send(y0, UP_X), send(y0, DOWN_X), send(y0, FAR_X)
    b1, b2 = send(y1, UP_X), send(y1, DOWN_X)
    c1, c2 = send(y2, UP_X), send(y2, DOWN_X)
    d1, d2, d3 = send(y3, UP_X), send(y3, DOWN_X), send(y3, FAR_X)
    f1 = send(a3, RING_Y)
    f2 = send(f1, RING_Y)

    other = send(source_rows, OTHER_Y)
    own = jnp.concatenate([source_rows, other], axis=0)
    u1, w1 = send(own, UP_Z), send(own, DOWN_Z)
    u2, w2 = send(u1, UP_Z), send(w1, DOWN_Z)
    u3, w3 = send(u2, UP_Z), send(w2, DOWN_Z)
    u4 = send(u3, UP_Z)
    near = stack(own, u1, w1, u2, w2)
    away = stack(u3, w3, u4)
    sources = [near, away, send(near, CORE), send(away, CORE)]

    act = activity.reshape(-1, 1)
    part, rows = product(act, 0, sources, [y0, a1, a2, a3, y1, b1, b2, f1, y2, c1, c2, f2])
    edges = product(act, 12, [], [y3, d1, d2, d3], rows, part)
    return edges[None]


def solution(mesh):
    in_specs = (
        P("feat", None),
        P(("feat", "prompt"), None),
        P("prompt", "feat"),
        P("prompt", None),
        P("prompt", None),
    )
    out_specs = P("prompt", None, "feat")
    return jax.shard_map(edges_of, mesh=mesh, in_specs=in_specs, out_specs=out_specs, check_vma=False)
```

time: 197 us -> 225 us (1.14)
  Pallas kernels: 18 us -> 98.1 us
  waiting for transfers between devices: 58.4 us -> 19.1 us
  local copies, waits for them, and re-layouts: 21.2 us -> 7.2 us
  starting transfers between devices: 86.2 us -> 95.2 us
  other arithmetic: 9.25 us -> 2.89 us
    pallas_call x0 -> x2, Pallas kernels: none -> 85.7 us  [stack(): pl.pallas_call(stack_kernel, out_shape=jax.ShapeDtypeStruct((n_rows, piec...]
    ppermute x25, waiting for transfers between devices: 58.4 us -> 19.1 us  [send(): return lax.ppermute(value, AXES, pairs)]
    ppermute x25, starting transfers between devices: 86.2 us -> 95.2 us  [send(): return lax.ppermute(value, AXES, pairs)]
    unnamed x43 -> x26, local copies, waits for them, and re-layouts: 14.6 us -> 6.4 us
    pallas_call x2, Pallas kernels: 18 us -> 12.4 us  [product(): pl.pallas_call(functools.partial(product_kernel, len(sources), len(target...]
    select_n x6 -> x1, other arithmetic: 3.39 us -> 0.81 us  [edges_of(): picked_rows = decoder.at[row_ids[0]].get(mode='promise_in_bounds')]
  transfers between devices with their start and end apart: 25 -> 25, of which waited for: 10 -> 4; matrix products, arithmetic and copies ran while one was open for 11% -> 0% of each run, Pallas kernels for 5% -> 42%
where the time goes in v4:
time: 225 us; the launch traced here: 223 us
  Pallas kernels  98.1 us (44%)
  starting transfers between devices  95.2 us (42%)
  waiting for transfers between devices  19.1 us (8%)
  local copies, waits for them, and re-layouts  7.2 us (3%)
  other arithmetic  2.89 us (1%)
    ppermute x25, starting transfers between devices, send(): return lax.ppermute(value, AXES, pairs)  95.2 us
    pallas_call x2, Pallas kernels, stack(): pl.pallas_call(stack_kernel, out_shape=jax.ShapeDtypeStruct((n_rows, piec...  85.7 us
    ppermute x25, waiting for transfers between devices, send(): return lax.ppermute(value, AXES, pairs)  19.1 us
    pallas_call x2, Pallas kernels, product(): pl.pallas_call(functools.partial(product_kernel, len(sources), len(target...  12.4 us
    unnamed x26, local copies, waits for them, and re-layouts  6.4 us
  transfers between devices with their start and end apart: 25, of which 4 were waited for; matrix products, arithmetic and copies ran while one was open for 0% of the time, Pallas kernels for 42%

profile of v4, /device:TPU:1, one launch (start us, length us, event | category | flops | bytes accessed | tf_op | source)
XLA Modules:
  0.0 223.0 jit_solution(16978363677231664061)
XLA Ops:
  0.0 0.8 fusion.1
  0.8 1.3 fusion
  2.1 0.6 iota_compare_fusion
  2.8 0.7 gather_fusion
  3.5 0.1 broadcast_select_fusion
  3.6 8.3 %collective-permute-start = (bf16[16,5376]{1,0:T(8,128)(2,1)S(1)}, bf16[16,5376]{1,0:T(8,128)(2,1)S(1)}, u32[]{:S(2)}, u32[]{:S(2)}) collective-permute-start(bf16[16,5376]{1,0:T(8,128)(2,1)S(1)} %broadcast_select_fusion), channel_id=1, source_target_pairs={{0,16},{1,17},{2,18},{3,19},{4,20},{5,21},{6,22},{7,23},{8,24},{9,... | collective-permute-start | bytes 516104 | tf_op jit(solution)/shard_map/ppermute | solution.py:45
  11.8 6.8 %collective-permute-done = bf16[16,5376]{1,0:T(8,128)(2,1)S(1)} collective-permute-done((bf16[16,5376]{1,0:T(8,128)(2,1)S(1)}, bf16[16,5376]{1,0:T(8,128)(2,1)S(1)}, u32[]{:S(2)}, u32[]{:S(2)}) %collective-permute-start) | collective-permute-done | bytes 172064 | tf_op jit(solution)/shard_map/ppermute | solution.py:45
  18.6 0.0 copy-start.8
  18.6 0.0 copy-start.12
  18.7 0.0 copy-start.3
  18.7 2.1 collective-permute-start.1
  20.7 5.2 %collective-permute-start.13 = (bf16[48,5376]{1,0:T(8,128)(2,1)}, bf16[48,5376]{1,0:T(8,128)(2,1)}, u32[]{:S(2)}, u32[]{:S(2)}) collective-permute-start(bf16[48,5376]{1,0:T(8,128)(2,1)} %refs_5_.1), channel_id=1, source_target_pairs={{0,32},{1,97},{2,34},{3,99},{4,36},{5,101},{6,38},{7,103},{8,40},{... | collective-permute-start | bytes 1548296 | tf_op jit(solution)/shard_map/ppermute | solution.py:45
  26.0 4.7 %collective-permute-start.12 = (bf16[48,5376]{1,0:T(8,128)(2,1)}, bf16[48,5376]{1,0:T(8,128)(2,1)}, u32[]{:S(2)}, u32[]{:S(2)}) collective-permute-start(bf16[48,5376]{1,0:T(8,128)(2,1)} %refs_5_.1), channel_id=1, source_target_pairs={{0,256},{1,257},{2,258},{3,259},{4,260},{5,261},{6,262},{7,263},{8... | collective-permute-start | bytes 1548296 | tf_op jit(solution)/shard_map/ppermute | solution.py:45
  30.7 8.6 %collective-permute-start.2 = (bf16[32,5376]{1,0:T(8,128)(2,1)S(1)}, bf16[32,5376]{1,0:T(8,128)(2,1)S(1)}, u32[]{:S(2)}, u32[]{:S(2)}) collective-permute-start(bf16[32,5376]{1,0:T(8,128)(2,1)S(1)} %pad_maximum_fusion.refs_0_), channel_id=1, source_target_pairs={{0,14},{1,15},{2,0},{3,1},{4,2},{5,3},{6,4},{7,5},{8,6},{9,7},{10,... | collective-permute-start | bytes 1032200 | tf_op jit(solution)/shard_map/ppermute | solution.py:45
  39.3 1.9 collective-permute-start.3
  41.2 2.2 collective-permute-start.10
  43.4 1.5 collective-permute-done.2.refs_2_
  45.0 5.4 %collective-permute-start.4 = (bf16[32,5376]{1,0:T(8,128)(2,1)S(1)}, bf16[32,5376]{1,0:T(8,128)(2,1)}, u32[]{:S(2)}, u32[]{:S(2)}) collective-permute-start(bf16[32,5376]{1,0:T(8,128)(2,1)S(1)} %collective-permute-done.2.refs_2_), channel_id=1, source_target_pairs={{0,14},{1,15},{2,0},{3,1},{4,2},{5,3},{6,4},{7,5},{8,6},{9,7},{10,... | collective-permute-start | bytes 1032200 | tf_op jit(solution)/shard_map/ppermute | solution.py:45
  50.4 1.9 collective-permute-start.5
  52.4 2.8 %collective-permute-start.11 = (bf16[48,5376]{1,0:T(8,128)(2,1)}, bf16[48,5376]{1,0:T(8,128)(2,1)}, u32[]{:S(2)}, u32[]{:S(2)}) collective-permute-start(bf16[48,5376]{1,0:T(8,128)(2,1)} %refs_5_.1), channel_id=1, source_target_pairs={{0,384},{1,385},{2,386},{3,387},{4,388},{5,389},{6,390},{7,391},{8... | collective-permute-start | bytes 1548296 | tf_op jit(solution)/shard_map/ppermute | solution.py:45
  55.2 7.0 %collective-permute-start.17 = (bf16[48,5376]{1,0:T(8,128)(2,1)}, bf16[48,5376]{1,0:T(8,128)(2,1)}, u32[]{:S(2)}, u32[]{:S(2)}) collective-permute-start(bf16[48,5376]{1,0:T(8,128)(2,1)} %collective-permute-done.13.refs_9_), channel_id=1, source_target_pairs={{0,32},{1,97},{2,34},{3,99},{4,36},{5,101},{6,38},{7,103},{8,40},{... | collective-permute-start | bytes 1548296 | tf_op jit(solution)/shard_map/ppermute | solution.py:45
  62.2 4.6 %collective-permute-start.6 = (bf16[32,5376]{1,0:T(8,128)(2,1)}, bf16[32,5376]{1,0:T(8,128)(2,1)}, u32[]{:S(2)}, u32[]{:S(2)}) collective-permute-start(bf16[32,5376]{1,0:T(8,128)(2,1)} %collective-permute-done.4.refs_4_), channel_id=1, source_target_pairs={{0,14},{1,15},{2,0},{3,1},{4,2},{5,3},{6,4},{7,5},{8,6},{9,7},{10,... | collective-permute-start | bytes 1032200 | tf_op jit(solution)/shard_map/ppermute | solution.py:45
  66.8 1.9 collective-permute-start.7
  68.7 53.3 %shard_map.55.refs_1_ = bf16[160,5376]{1,0:T(8,128)(2,1)} custom-call(bf16[32,5376]{1,0:T(8,128)(2,1)} %copy-done.8, bf16[32,5376]{1,0:T(8,128)(2,1)} %copy-done.9, bf16[32,5376]{1,0:T(8,128)(2,1)} %copy-done.10, bf16[32,5376]{1,0:T(8,128)(2,1)} %copy-done.11, bf16[32,5376]{1,0:T(8,128)(2,1)} %collective-permute-done.4.refs_4_), custom_call_target="tpu_custom_call" | custom-call | tf_op jit(solution)/shard_map/pallas_call | solution.py:64
  122.0 2.1 collective-permute-start.8
  124.1 2.3 %collective-permute-start.14 = (bf16[48,5376]{1,0:T(8,128)(2,1)}, bf16[48,5376]{1,0:T(8,128)(2,1)}, u32[]{:S(2)}, u32[]{:S(2)}) collective-permute-start(bf16[48,5376]{1,0:T(8,128)(2,1)} %collective-permute-done.13.refs_9_), channel_id=1, source_target_pairs={{0,128},{1,129},{2,130},{3,131},{4,132},{5,133},{6,134},{7,135},{8... | collective-permute-start | bytes 1548296 | tf_op jit(solution)/shard_map/ppermute | solution.py:45
  126.5 4.2 %collective-permute-start.15 = (bf16[48,5376]{1,0:T(8,128)(2,1)}, bf16[48,5376]{1,0:T(8,128)(2,1)}, u32[]{:S(2)}, u32[]{:S(2)}) collective-permute-start(bf16[48,5376]{1,0:T(8,128)(2,1)} %collective-permute-done.13.refs_9_), channel_id=1, source_target_pairs={{0,384},{1,385},{2,386},{3,387},{4,388},{5,389},{6,390},{7,391},{8... | collective-permute-start | bytes 1548296 | tf_op jit(solution)/shard_map/ppermute | solution.py:45
  130.7 4.4 %collective-permute-start.16 = (bf16[48,5376]{1,0:T(8,128)(2,1)}, bf16[48,5376]{1,0:T(8,128)(2,1)}, u32[]{:S(2)}, u32[]{:S(2)}) collective-permute-start(bf16[48,5376]{1,0:T(8,128)(2,1)} %collective-permute-done.12.refs_8_), channel_id=1, source_target_pairs={{0,32},{1,97},{2,34},{3,99},{4,36},{5,101},{6,38},{7,103},{8,40},{... | collective-permute-start | bytes 1548296 | tf_op jit(solution)/shard_map/ppermute | solution.py:45
  135.1 1.9 collective-permute-start.18
  137.0 32.4 %shard_map.56.refs_2_ = bf16[96,5376]{1,0:T(8,128)(2,1)} custom-call(bf16[32,5376]{1,0:T(8,128)(2,1)} %collective-permute-done.5.refs_0_, bf16[32,5376]{1,0:T(8,128)(2,1)} %collective-permute-done.6.refs_1_, bf16[32,5376]{1,0:T(8,128)(2,1)} %collective-permute-done.7.refs_2_), custom_call_target="tpu_custom_call" | custom-call | tf_op jit(solution)/shard_map/pallas_call | solution.py:64
  169.4 3.2 %collective-permute-start.21 = (bf16[48,5376]{1,0:T(8,128)(2,1)}, bf16[48,5376]{1,0:T(8,128)(2,1)}, u32[]{:S(2)}, u32[]{:S(2)}) collective-permute-start(bf16[48,5376]{1,0:T(8,128)(2,1)} %collective-permute-done.17.refs_13_), channel_id=1, source_target_pairs={{0,32},{1,97},{2,34},{3,99},{4,36},{5,101},{6,38},{7,103},{8,40},{... | collective-permute-start | bytes 1548296 | tf_op jit(solution)/shard_map/ppermute | solution.py:45
  172.6 2.1 collective-permute-start.9
  174.8 4.9 %collective-permute-start.19 = (bf16[48,5376]{1,0:T(8,128)(2,1)}, bf16[48,5376]{1,0:T(8,128)(2,1)S(1)}, u32[]{:S(2)}, u32[]{:S(2)}) collective-permute-start(bf16[48,5376]{1,0:T(8,128)(2,1)} %collective-permute-done.17.refs_13_), channel_id=1, source_target_pairs={{0,384},{1,385},{2,386},{3,387},{4,388},{5,389},{6,390},{7,391},{8... | collective-permute-start | bytes 1548296 | tf_op jit(solution)/shard_map/ppermute | solution.py:45
  179.6 4.5 %collective-permute-start.20 = (bf16[48,5376]{1,0:T(8,128)(2,1)}, bf16[48,5376]{1,0:T(8,128)(2,1)S(1)}, u32[]{:S(2)}, u32[]{:S(2)}) collective-permute-start(bf16[48,5376]{1,0:T(8,128)(2,1)} %collective-permute-done.16.refs_12_), channel_id=1, source_target_pairs={{0,32},{1,97},{2,34},{3,99},{4,36},{5,101},{6,38},{7,103},{8,40},{... | collective-permute-start | bytes 1548296 | tf_op jit(solution)/shard_map/ppermute | solution.py:45
  184.1 1.9 collective-permute-start.22
  186.1 4.9 %collective-permute-done.19.refs_15_ = bf16[48,5376]{1,0:T(8,128)(2,1)S(1)} collective-permute-done((bf16[48,5376]{1,0:T(8,128)(2,1)}, bf16[48,5376]{1,0:T(8,128)(2,1)S(1)}, u32[]{:S(2)}, u32[]{:S(2)}) %collective-permute-start.19) | collective-permute-done | bytes 516128 | tf_op jit(solution)/shard_map/ppermute | solution.py:45
  191.0 0.8 copy-done.4
  191.8 5.2 %collective-permute-start.23 = (bf16[48,5376]{1,0:T(8,128)(2,1)}, bf16[48,5376]{1,0:T(8,128)(2,1)}, u32[]{:S(2)}, u32[]{:S(2)}) collective-permute-start(bf16[48,5376]{1,0:T(8,128)(2,1)} %collective-permute-done.21.refs_3_), channel_id=1, source_target_pairs={{0,384},{1,385},{2,386},{3,387},{4,388},{5,389},{6,390},{7,391},{8... | collective-permute-start | bytes 1548296 | tf_op jit(solution)/shard_map/ppermute | solution.py:45
  197.0 0.8 copy-done.6
  197.8 1.9 collective-permute-start.24
  199.8 0.1 copy.7.refs_0_
  200.0 1.5 copy-done.1
  201.4 1.2 copy-done.2
  202.6 1.0 copy-done.5
  203.7 1.0 copy-done.7
  204.7 7.9 %shard_map.57 = (bf16[512,768]{1,0:T(8,128)(2,1)S(1)}, bf16[512,5376]{1,0:T(8,128)(2,1)S(1)}) custom-call(f32[512,1]{1,0:T(8,128)S(1)} %copy.7.refs_0_, bf16[160,5376]{1,0:T(8,128)(2,1)S(1)} %copy-done.1, bf16[96,5376]{1,0:T(8,128)(2,1)S(1)} %copy-done.2, bf16[160,5376]{1,0:T(8,128)(2,1)} %collective-permute-done.8.refs_3_, ...), custom_call_target="tpu_custom_call" | custom-call | tf_op jit(solution)/shard_map/pallas_call | solution.py:162
  212.6 5.8 %collective-permute-done.23.refs_5_ = bf16[48,5376]{1,0:T(8,128)(2,1)} collective-permute-done((bf16[48,5376]{1,0:T(8,128)(2,1)}, bf16[48,5376]{1,0:T(8,128)(2,1)}, u32[]{:S(2)}, u32[]{:S(2)}) %collective-permute-start.23) | collective-permute-done | bytes 516128 | tf_op jit(solution)/shard_map/ppermute | solution.py:45
  218.4 4.5 %shard_map.58 = bf16[512,768]{1,0:T(8,128)(2,1)} custom-call(f32[512,1]{1,0:T(8,128)S(1)} %copy.7.refs_0_, bf16[512,5376]{1,0:T(8,128)(2,1)S(1)} %get-tuple-element.7.refs_1_, bf16[512,768]{1,0:T(8,128)(2,1)S(1)} %get-tuple-element.8.refs_2_, bf16[48,5376]{1,0:T(8,128)(2,1)} %collective-permute-done.21.refs_3_, ...), custom_call_target="tpu_custom_call" | custom-call | tf_op jit(solution)/shard_map/pallas_call | solution.py:162
  (40 shorter events, 0.1 us)
Async XLA Ops:
  0.0 2.8 %copy-start = (bf16[256,5376]{1,0:T(8,128)(2,1)S(1)}, bf16[256,5376]{1,0:T(8,128)(2,1)}, u32[]{:S(2)}) copy-start(bf16[256,5376]{1,0:T(8,128)(2,1)} %param.5) | copy-start | bytes 8257540
  3.6 15.1 %collective-permute-start = (bf16[16,5376]{1,0:T(8,128)(2,1)S(1)}, bf16[16,5376]{1,0:T(8,128)(2,1)S(1)}, u32[]{:S(2)}, u32[]{:S(2)}) collective-permute-start(bf16[16,5376]{1,0:T(8,128)(2,1)S(1)} %broadcast_select_fusion), channel_id=1, source_target_pairs={{0,16},{1,17},{2,18},{3,19},{4,20},{5,21},{6,22},{7,23},{8,24},{9,... | collective-permute-start | bytes 516104 | tf_op jit(solution)/shard_map/ppermute | solution.py:45
  18.6 12.0 %copy-start.8 = (bf16[32,5376]{1,0:T(8,128)(2,1)}, bf16[32,5376]{1,0:T(8,128)(2,1)S(1)}, u32[]{:S(2)}) copy-start(bf16[32,5376]{1,0:T(8,128)(2,1)S(1)} %pad_maximum_fusion.refs_0_) | copy-start | bytes 1032196
  18.6 181.1 %copy-start.12 = (f32[1,512]{1,0:T(1,128)S(1)}, f32[1,512]{1,0:T(1,128)}, u32[]{:S(2)}) copy-start(f32[1,512]{1,0:T(1,128)} %param.9) | copy-start | bytes 6148
  18.7 181.3 %copy-start.3 = (bf16[48,5376]{1,0:T(8,128)(2,1)S(1)}, bf16[48,5376]{1,0:T(8,128)(2,1)}, u32[]{:S(2)}) copy-start(bf16[48,5376]{1,0:T(8,128)(2,1)} %refs_5_.1) | copy-start | bytes 1548292
  18.7 20.6 %collective-permute-start.1 = (bf16[32,5376]{1,0:T(8,128)(2,1)S(1)}, bf16[32,5376]{1,0:T(8,128)(2,1)S(1)}, u32[]{:S(2)}, u32[]{:S(2)}) collective-permute-start(bf16[32,5376]{1,0:T(8,128)(2,1)S(1)} %pad_maximum_fusion.refs_0_), channel_id=1, source_target_pairs={{0,2},{1,3},{2,4},{3,5},{4,6},{5,7},{6,8},{7,9},{8,10},{9,11},{10,... | collective-permute-start | bytes 1032200 | tf_op jit(solution)/shard_map/ppermute | solution.py:45
  20.7 31.6 %collective-permute-start.13 = (bf16[48,5376]{1,0:T(8,128)(2,1)}, bf16[48,5376]{1,0:T(8,128)(2,1)}, u32[]{:S(2)}, u32[]{:S(2)}) collective-permute-start(bf16[48,5376]{1,0:T(8,128)(2,1)} %refs_5_.1), channel_id=1, source_target_pairs={{0,32},{1,97},{2,34},{3,99},{4,36},{5,101},{6,38},{7,103},{8,40},{... | collective-permute-start | bytes 1548296 | tf_op jit(solution)/shard_map/ppermute | solution.py:45
  26.0 29.2 %collective-permute-start.12 = (bf16[48,5376]{1,0:T(8,128)(2,1)}, bf16[48,5376]{1,0:T(8,128)(2,1)}, u32[]{:S(2)}, u32[]{:S(2)}) collective-permute-start(bf16[48,5376]{1,0:T(8,128)(2,1)} %refs_5_.1), channel_id=1, source_target_pairs={{0,256},{1,257},{2,258},{3,259},{4,260},{5,261},{6,262},{7,263},{8... | collective-permute-start | bytes 1548296 | tf_op jit(solution)/shard_map/ppermute | solution.py:45
  30.7 14.3 %collective-permute-start.2 = (bf16[32,5376]{1,0:T(8,128)(2,1)S(1)}, bf16[32,5376]{1,0:T(8,128)(2,1)S(1)}, u32[]{:S(2)}, u32[]{:S(2)}) collective-permute-start(bf16[32,5376]{1,0:T(8,128)(2,1)S(1)} %pad_maximum_fusion.refs_0_), channel_id=1, source_target_pairs={{0,14},{1,15},{2,0},{3,1},{4,2},{5,3},{6,4},{7,5},{8,6},{9,7},{10,... | collective-permute-start | bytes 1032200 | tf_op jit(solution)/shard_map/ppermute | solution.py:45
  39.3 5.7 %copy-start.9 = (bf16[32,5376]{1,0:T(8,128)(2,1)}, bf16[32,5376]{1,0:T(8,128)(2,1)S(1)}, u32[]{:S(2)}) copy-start(bf16[32,5376]{1,0:T(8,128)(2,1)S(1)} %collective-permute-done.1.refs_1_) | copy-start | bytes 1032196
  39.3 11.1 %collective-permute-start.3 = (bf16[32,5376]{1,0:T(8,128)(2,1)S(1)}, bf16[32,5376]{1,0:T(8,128)(2,1)S(1)}, u32[]{:S(2)}, u32[]{:S(2)}) collective-permute-start(bf16[32,5376]{1,0:T(8,128)(2,1)S(1)} %collective-permute-done.1.refs_1_), channel_id=1, source_target_pairs={{0,2},{1,3},{2,4},{3,5},{4,6},{5,7},{6,8},{7,9},{8,10},{9,11},{10,... | collective-permute-start | bytes 1032200 | tf_op jit(solution)/shard_map/ppermute | solution.py:45
  41.2 80.8 %collective-permute-start.10 = (bf16[48,5376]{1,0:T(8,128)(2,1)}, bf16[48,5376]{1,0:T(8,128)(2,1)}, u32[]{:S(2)}, u32[]{:S(2)}) collective-permute-start(bf16[48,5376]{1,0:T(8,128)(2,1)} %refs_5_.1), channel_id=1, source_target_pairs={{0,128},{1,129},{2,130},{3,131},{4,132},{5,133},{6,134},{7,135},{8... | collective-permute-start | bytes 1548296 | tf_op jit(solution)/shard_map/ppermute | solution.py:45
  45.0 5.4 %copy-start.10 = (bf16[32,5376]{1,0:T(8,128)(2,1)}, bf16[32,5376]{1,0:T(8,128)(2,1)S(1)}, u32[]{:S(2)}) copy-start(bf16[32,5376]{1,0:T(8,128)(2,1)S(1)} %collective-permute-done.2.refs_2_) | copy-start | bytes 1032196
  45.0 17.2 %collective-permute-start.4 = (bf16[32,5376]{1,0:T(8,128)(2,1)S(1)}, bf16[32,5376]{1,0:T(8,128)(2,1)}, u32[]{:S(2)}, u32[]{:S(2)}) collective-permute-start(bf16[32,5376]{1,0:T(8,128)(2,1)S(1)} %collective-permute-done.2.refs_2_), channel_id=1, source_target_pairs={{0,14},{1,15},{2,0},{3,1},{4,2},{5,3},{6,4},{7,5},{8,6},{9,7},{10,... | collective-permute-start | bytes 1032200 | tf_op jit(solution)/shard_map/ppermute | solution.py:45
  50.4 11.8 %copy-start.11 = (bf16[32,5376]{1,0:T(8,128)(2,1)}, bf16[32,5376]{1,0:T(8,128)(2,1)S(1)}, u32[]{:S(2)}) copy-start(bf16[32,5376]{1,0:T(8,128)(2,1)S(1)} %collective-permute-done.3.refs_3_) | copy-start | bytes 1032196
  50.4 16.4 %collective-permute-start.5 = (bf16[32,5376]{1,0:T(8,128)(2,1)S(1)}, bf16[32,5376]{1,0:T(8,128)(2,1)}, u32[]{:S(2)}, u32[]{:S(2)}) collective-permute-start(bf16[32,5376]{1,0:T(8,128)(2,1)S(1)} %collective-permute-done.3.refs_3_), channel_id=1, source_target_pairs={{0,2},{1,3},{2,4},{3,5},{4,6},{5,7},{6,8},{7,9},{8,10},{9,11},{10,... | collective-permute-start | bytes 1032200 | tf_op jit(solution)/shard_map/ppermute | solution.py:45
  52.4 71.8 %collective-permute-start.11 = (bf16[48,5376]{1,0:T(8,128)(2,1)}, bf16[48,5376]{1,0:T(8,128)(2,1)}, u32[]{:S(2)}, u32[]{:S(2)}) collective-permute-start(bf16[48,5376]{1,0:T(8,128)(2,1)} %refs_5_.1), channel_id=1, source_target_pairs={{0,384},{1,385},{2,386},{3,387},{4,388},{5,389},{6,390},{7,391},{8... | collective-permute-start | bytes 1548296 | tf_op jit(solution)/shard_map/ppermute | solution.py:45
  55.2 71.3 %collective-permute-start.17 = (bf16[48,5376]{1,0:T(8,128)(2,1)}, bf16[48,5376]{1,0:T(8,128)(2,1)}, u32[]{:S(2)}, u32[]{:S(2)}) collective-permute-start(bf16[48,5376]{1,0:T(8,128)(2,1)} %collective-permute-done.13.refs_9_), channel_id=1, source_target_pairs={{0,32},{1,97},{2,34},{3,99},{4,36},{5,101},{6,38},{7,103},{8,40},{... | collective-permute-start | bytes 1548296 | tf_op jit(solution)/shard_map/ppermute | solution.py:45
  62.2 68.5 %collective-permute-start.6 = (bf16[32,5376]{1,0:T(8,128)(2,1)}, bf16[32,5376]{1,0:T(8,128)(2,1)}, u32[]{:S(2)}, u32[]{:S(2)}) collective-permute-start(bf16[32,5376]{1,0:T(8,128)(2,1)} %collective-permute-done.4.refs_4_), channel_id=1, source_target_pairs={{0,14},{1,15},{2,0},{3,1},{4,2},{5,3},{6,4},{7,5},{8,6},{9,7},{10,... | collective-permute-start | bytes 1032200 | tf_op jit(solution)/shard_map/ppermute | solution.py:45
  66.8 68.3 %collective-permute-start.7 = (bf16[32,5376]{1,0:T(8,128)(2,1)}, bf16[32,5376]{1,0:T(8,128)(2,1)}, u32[]{:S(2)}, u32[]{:S(2)}) collective-permute-start(bf16[32,5376]{1,0:T(8,128)(2,1)} %collective-permute-done.5.refs_0_), channel_id=1, source_target_pairs={{0,2},{1,3},{2,4},{3,5},{4,6},{5,7},{6,8},{7,9},{8,10},{9,11},{10,... | collective-permute-start | bytes 1032200 | tf_op jit(solution)/shard_map/ppermute | solution.py:45
  122.0 77.9 %collective-permute-start.8 = (bf16[160,5376]{1,0:T(8,128)(2,1)}, bf16[160,5376]{1,0:T(8,128)(2,1)}, u32[]{:S(2)}, u32[]{:S(2)}) collective-permute-start(bf16[160,5376]{1,0:T(8,128)(2,1)} %shard_map.55.refs_1_), channel_id=1, source_target_pairs={{0,1},{1,0},{2,3},{3,2},{4,5},{5,4},{6,7},{7,6},{8,9},{9,8},{10,11... | collective-permute-start | bytes 5160968 | tf_op jit(solution)/shard_map/ppermute | solution.py:45
  124.1 45.3 %collective-permute-start.14 = (bf16[48,5376]{1,0:T(8,128)(2,1)}, bf16[48,5376]{1,0:T(8,128)(2,1)}, u32[]{:S(2)}, u32[]{:S(2)}) collective-permute-start(bf16[48,5376]{1,0:T(8,128)(2,1)} %collective-permute-done.13.refs_9_), channel_id=1, source_target_pairs={{0,128},{1,129},{2,130},{3,131},{4,132},{5,133},{6,134},{7,135},{8... | collective-permute-start | bytes 1548296 | tf_op jit(solution)/shard_map/ppermute | solution.py:45
  126.5 46.1 %collective-permute-start.15 = (bf16[48,5376]{1,0:T(8,128)(2,1)}, bf16[48,5376]{1,0:T(8,128)(2,1)}, u32[]{:S(2)}, u32[]{:S(2)}) collective-permute-start(bf16[48,5376]{1,0:T(8,128)(2,1)} %collective-permute-done.13.refs_9_), channel_id=1, source_target_pairs={{0,384},{1,385},{2,386},{3,387},{4,388},{5,389},{6,390},{7,391},{8... | collective-permute-start | bytes 1548296 | tf_op jit(solution)/shard_map/ppermute | solution.py:45
  130.7 44.1 %collective-permute-start.16 = (bf16[48,5376]{1,0:T(8,128)(2,1)}, bf16[48,5376]{1,0:T(8,128)(2,1)}, u32[]{:S(2)}, u32[]{:S(2)}) collective-permute-start(bf16[48,5376]{1,0:T(8,128)(2,1)} %collective-permute-done.12.refs_8_), channel_id=1, source_target_pairs={{0,32},{1,97},{2,34},{3,99},{4,36},{5,101},{6,38},{7,103},{8,40},{... | collective-permute-start | bytes 1548296 | tf_op jit(solution)/shard_map/ppermute | solution.py:45
  135.1 44.6 %collective-permute-start.18 = (bf16[48,5376]{1,0:T(8,128)(2,1)}, bf16[48,5376]{1,0:T(8,128)(2,1)}, u32[]{:S(2)}, u32[]{:S(2)}) collective-permute-start(bf16[48,5376]{1,0:T(8,128)(2,1)} %collective-permute-done.17.refs_13_), channel_id=1, source_target_pairs={{0,128},{1,129},{2,130},{3,131},{4,132},{5,133},{6,134},{7,135},{8... | collective-permute-start | bytes 1548296 | tf_op jit(solution)/shard_map/ppermute | solution.py:45
  169.4 14.7 %collective-permute-start.21 = (bf16[48,5376]{1,0:T(8,128)(2,1)}, bf16[48,5376]{1,0:T(8,128)(2,1)}, u32[]{:S(2)}, u32[]{:S(2)}) collective-permute-start(bf16[48,5376]{1,0:T(8,128)(2,1)} %collective-permute-done.17.refs_13_), channel_id=1, source_target_pairs={{0,32},{1,97},{2,34},{3,99},{4,36},{5,101},{6,38},{7,103},{8,40},{... | collective-permute-start | bytes 1548296 | tf_op jit(solution)/shard_map/ppermute | solution.py:45
  172.6 27.3 %collective-permute-start.9 = (bf16[96,5376]{1,0:T(8,128)(2,1)}, bf16[96,5376]{1,0:T(8,128)(2,1)}, u32[]{:S(2)}, u32[]{:S(2)}) collective-permute-start(bf16[96,5376]{1,0:T(8,128)(2,1)} %shard_map.56.refs_2_), channel_id=1, source_target_pairs={{0,1},{1,0},{2,3},{3,2},{4,5},{5,4},{6,7},{7,6},{8,9},{9,8},{10,11... | collective-permute-start | bytes 3096584 | tf_op jit(solution)/shard_map/ppermute | solution.py:45
  174.8 16.2 %collective-permute-start.19 = (bf16[48,5376]{1,0:T(8,128)(2,1)}, bf16[48,5376]{1,0:T(8,128)(2,1)S(1)}, u32[]{:S(2)}, u32[]{:S(2)}) collective-permute-start(bf16[48,5376]{1,0:T(8,128)(2,1)} %collective-permute-done.17.refs_13_), channel_id=1, source_target_pairs={{0,384},{1,385},{2,386},{3,387},{4,388},{5,389},{6,390},{7,391},{8... | collective-permute-start | bytes 1548296 | tf_op jit(solution)/shard_map/ppermute | solution.py:45
  179.6 17.4 %collective-permute-start.20 = (bf16[48,5376]{1,0:T(8,128)(2,1)}, bf16[48,5376]{1,0:T(8,128)(2,1)S(1)}, u32[]{:S(2)}, u32[]{:S(2)}) collective-permute-start(bf16[48,5376]{1,0:T(8,128)(2,1)} %collective-permute-done.16.refs_12_), channel_id=1, source_target_pairs={{0,32},{1,97},{2,34},{3,99},{4,36},{5,101},{6,38},{7,103},{8,40},{... | collective-permute-start | bytes 1548296 | tf_op jit(solution)/shard_map/ppermute | solution.py:45
  184.1 28.5 %collective-permute-start.22 = (bf16[48,5376]{1,0:T(8,128)(2,1)}, bf16[48,5376]{1,0:T(8,128)(2,1)}, u32[]{:S(2)}, u32[]{:S(2)}) collective-permute-start(bf16[48,5376]{1,0:T(8,128)(2,1)} %collective-permute-done.21.refs_3_), channel_id=1, source_target_pairs={{0,128},{1,129},{2,130},{3,131},{4,132},{5,133},{6,134},{7,135},{8... | collective-permute-start | bytes 1548296 | tf_op jit(solution)/shard_map/ppermute | solution.py:45
  191.0 0.8 copy-start.4
  191.8 26.7 %collective-permute-start.23 = (bf16[48,5376]{1,0:T(8,128)(2,1)}, bf16[48,5376]{1,0:T(8,128)(2,1)}, u32[]{:S(2)}, u32[]{:S(2)}) collective-permute-start(bf16[48,5376]{1,0:T(8,128)(2,1)} %collective-permute-done.21.refs_3_), channel_id=1, source_target_pairs={{0,384},{1,385},{2,386},{3,387},{4,388},{5,389},{6,390},{7,391},{8... | collective-permute-start | bytes 1548296 | tf_op jit(solution)/shard_map/ppermute | solution.py:45
  197.0 0.8 copy-start.6
  197.8 20.6 %collective-permute-start.24 = (bf16[48,5376]{1,0:T(8,128)(2,1)}, bf16[48,5376]{1,0:T(8,128)(2,1)}, u32[]{:S(2)}, u32[]{:S(2)}) collective-permute-start(bf16[48,5376]{1,0:T(8,128)(2,1)} %collective-permute-done.21.refs_3_), channel_id=1, source_target_pairs={{0,256},{1,257},{2,258},{3,259},{4,260},{5,261},{6,262},{7,263},{8... | collective-permute-start | bytes 1548296 | tf_op jit(solution)/shard_map/ppermute | solution.py:45
  200.0 1.5 copy-start.1
  201.4 1.2 copy-start.2
  202.6 1.0 copy-start.5
  203.7 1.0 copy-start.7

commit v5 on v4

--- a/solution.py
+++ b/solution.py
@@ -60,12 +60,11 @@
 
 def stack(*pieces):
     n_rows = sum(piece.shape[0] for piece in pieces)
-    anywhere = pl.BlockSpec(memory_space=pl.ANY)
     return pl.pallas_call(
         stack_kernel,
         out_shape=jax.ShapeDtypeStruct((n_rows, pieces[0].shape[1]), pieces[0].dtype),
-        in_specs=[anywhere] * len(pieces),
-        out_specs=anywhere,
+        in_specs=[pl.BlockSpec(memory_space=pl.ANY)] * len(pieces),
+        out_specs=pl.BlockSpec(memory_space=pltpu.VMEM),
         scratch_shapes=[pltpu.SemaphoreType.DMA((len(pieces),))],
     )(*pieces)
 

time: 225 us -> 147 us (0.65)
  the two profiles are of different devices: /device:TPU:1 before, /device:TPU:62 now
where the time goes in v5:
time: 147 us; the launch traced here: 146 us
  starting transfers between devices  88.5 us (60%)
  waiting for transfers between devices  29.5 us (20%)
  Pallas kernels  17.3 us (12%)
  local copies, waits for them, and re-layouts  7.21 us (5%)
  other arithmetic  2.89 us (2%)
    ppermute x25, starting transfers between devices, send(): return lax.ppermute(value, AXES, pairs)  88.5 us
    ppermute x25, waiting for transfers between devices, send(): return lax.ppermute(value, AXES, pairs)  29.5 us
    pallas_call x2, Pallas kernels, product(): pl.pallas_call(functools.partial(product_kernel, len(sources), len(target...  12.4 us
    unnamed x26, local copies, waits for them, and re-layouts  6.41 us
    pallas_call x2, Pallas kernels, stack(): pl.pallas_call(stack_kernel, out_shape=jax.ShapeDtypeStruct((n_rows, piec...  4.84 us
  transfers between devices with their start and end apart: 25, of which 9 were waited for; matrix products, arithmetic and copies ran while one was open for 0% of the time, Pallas kernels for 9%

profile of v5, /device:TPU:62, one launch (start us, length us, event | category | flops | bytes accessed | tf_op | source)
XLA Modules:
  0.0 145.9 jit_solution(10626481343229828257)
XLA Ops:
  0.0 0.8 fusion.1
  0.8 1.3 fusion
  2.1 0.6 iota_compare_fusion
  2.8 0.7 gather_fusion
  3.6 4.7 %collective-permute-start = (bf16[16,5376]{1,0:T(8,128)(2,1)S(1)}, bf16[16,5376]{1,0:T(8,128)(2,1)S(1)}, u32[]{:S(2)}, u32[]{:S(2)}) collective-permute-start(bf16[16,5376]{1,0:T(8,128)(2,1)S(1)} %broadcast_select_fusion), channel_id=1, source_target_pairs={{0,16},{1,17},{2,18},{3,19},{4,20},{5,21},{6,22},{7,23},{8,24},{9,... | collective-permute-start | bytes 516104 | tf_op jit(solution)/shard_map/ppermute | solution.py:45
  8.3 10.9 %collective-permute-done = bf16[16,5376]{1,0:T(8,128)(2,1)S(1)} collective-permute-done((bf16[16,5376]{1,0:T(8,128)(2,1)S(1)}, bf16[16,5376]{1,0:T(8,128)(2,1)S(1)}, u32[]{:S(2)}, u32[]{:S(2)}) %collective-permute-start) | collective-permute-done | bytes 172064 | tf_op jit(solution)/shard_map/ppermute | solution.py:45
  19.3 4.4 %collective-permute-start.1 = (bf16[32,5376]{1,0:T(8,128)(2,1)S(1)}, bf16[32,5376]{1,0:T(8,128)(2,1)S(1)}, u32[]{:S(2)}, u32[]{:S(2)}) collective-permute-start(bf16[32,5376]{1,0:T(8,128)(2,1)S(1)} %pad_maximum_fusion.refs_0_), channel_id=1, source_target_pairs={{0,2},{1,3},{2,4},{3,5},{4,6},{5,7},{6,8},{7,9},{8,10},{9,11},{10,... | collective-permute-start | bytes 1032200 | tf_op jit(solution)/shard_map/ppermute | solution.py:45
  23.7 4.8 %collective-permute-start.13 = (bf16[48,5376]{1,0:T(8,128)(2,1)}, bf16[48,5376]{1,0:T(8,128)(2,1)}, u32[]{:S(2)}, u32[]{:S(2)}) collective-permute-start(bf16[48,5376]{1,0:T(8,128)(2,1)} %refs_5_.1), channel_id=1, source_target_pairs={{0,32},{1,97},{2,34},{3,99},{4,36},{5,101},{6,38},{7,103},{8,40},{... | collective-permute-start | bytes 1548296 | tf_op jit(solution)/shard_map/ppermute | solution.py:45
  28.5 3.3 %collective-permute-start.12 = (bf16[48,5376]{1,0:T(8,128)(2,1)}, bf16[48,5376]{1,0:T(8,128)(2,1)}, u32[]{:S(2)}, u32[]{:S(2)}) collective-permute-start(bf16[48,5376]{1,0:T(8,128)(2,1)} %refs_5_.1), channel_id=1, source_target_pairs={{0,256},{1,257},{2,258},{3,259},{4,260},{5,261},{6,262},{7,263},{8... | collective-permute-start | bytes 1548296 | tf_op jit(solution)/shard_map/ppermute | solution.py:45
  31.8 8.6 %collective-permute-start.2 = (bf16[32,5376]{1,0:T(8,128)(2,1)S(1)}, bf16[32,5376]{1,0:T(8,128)(2,1)S(1)}, u32[]{:S(2)}, u32[]{:S(2)}) collective-permute-start(bf16[32,5376]{1,0:T(8,128)(2,1)S(1)} %pad_maximum_fusion.refs_0_), channel_id=1, source_target_pairs={{0,14},{1,15},{2,0},{3,1},{4,2},{5,3},{6,4},{7,5},{8,6},{9,7},{10,... | collective-permute-start | bytes 1032200 | tf_op jit(solution)/shard_map/ppermute | solution.py:45
  40.4 1.9 %collective-permute-start.3 = (bf16[32,5376]{1,0:T(8,128)(2,1)S(1)}, bf16[32,5376]{1,0:T(8,128)(2,1)S(1)}, u32[]{:S(2)}, u32[]{:S(2)}) collective-permute-start(bf16[32,5376]{1,0:T(8,128)(2,1)S(1)} %collective-permute-done.1.refs_1_), channel_id=1, source_target_pairs={{0,2},{1,3},{2,4},{3,5},{4,6},{5,7},{6,8},{7,9},{8,10},{9,11},{10,... | collective-permute-start | bytes 1032200 | tf_op jit(solution)/shard_map/ppermute | solution.py:45
  42.3 4.0 %collective-permute-start.10 = (bf16[48,5376]{1,0:T(8,128)(2,1)}, bf16[48,5376]{1,0:T(8,128)(2,1)}, u32[]{:S(2)}, u32[]{:S(2)}) collective-permute-start(bf16[48,5376]{1,0:T(8,128)(2,1)} %refs_5_.1), channel_id=1, source_target_pairs={{0,128},{1,129},{2,130},{3,131},{4,132},{5,133},{6,134},{7,135},{8... | collective-permute-start | bytes 1548296 | tf_op jit(solution)/shard_map/ppermute | solution.py:45
  46.4 5.1 %collective-permute-start.4 = (bf16[32,5376]{1,0:T(8,128)(2,1)S(1)}, bf16[32,5376]{1,0:T(8,128)(2,1)}, u32[]{:S(2)}, u32[]{:S(2)}) collective-permute-start(bf16[32,5376]{1,0:T(8,128)(2,1)S(1)} %collective-permute-done.2.refs_2_), channel_id=1, source_target_pairs={{0,14},{1,15},{2,0},{3,1},{4,2},{5,3},{6,4},{7,5},{8,6},{9,7},{10,... | collective-permute-start | bytes 1032200 | tf_op jit(solution)/shard_map/ppermute | solution.py:45
  51.6 1.9 %collective-permute-start.5 = (bf16[32,5376]{1,0:T(8,128)(2,1)S(1)}, bf16[32,5376]{1,0:T(8,128)(2,1)}, u32[]{:S(2)}, u32[]{:S(2)}) collective-permute-start(bf16[32,5376]{1,0:T(8,128)(2,1)S(1)} %collective-permute-done.3.refs_3_), channel_id=1, source_target_pairs={{0,2},{1,3},{2,4},{3,5},{4,6},{5,7},{6,8},{7,9},{8,10},{9,11},{10,... | collective-permute-start | bytes 1032200 | tf_op jit(solution)/shard_map/ppermute | solution.py:45
  53.5 1.9 %collective-permute-start.11 = (bf16[48,5376]{1,0:T(8,128)(2,1)}, bf16[48,5376]{1,0:T(8,128)(2,1)}, u32[]{:S(2)}, u32[]{:S(2)}) collective-permute-start(bf16[48,5376]{1,0:T(8,128)(2,1)} %refs_5_.1), channel_id=1, source_target_pairs={{0,384},{1,385},{2,386},{3,387},{4,388},{5,389},{6,390},{7,391},{8... | collective-permute-start | bytes 1548296 | tf_op jit(solution)/shard_map/ppermute | solution.py:45
  55.4 4.0 %collective-permute-start.17 = (bf16[48,5376]{1,0:T(8,128)(2,1)}, bf16[48,5376]{1,0:T(8,128)(2,1)}, u32[]{:S(2)}, u32[]{:S(2)}) collective-permute-start(bf16[48,5376]{1,0:T(8,128)(2,1)} %collective-permute-done.13.refs_9_), channel_id=1, source_target_pairs={{0,32},{1,97},{2,34},{3,99},{4,36},{5,101},{6,38},{7,103},{8,40},{... | collective-permute-start | bytes 1548296 | tf_op jit(solution)/shard_map/ppermute | solution.py:45
  59.5 5.1 %collective-permute-start.6 = (bf16[32,5376]{1,0:T(8,128)(2,1)}, bf16[32,5376]{1,0:T(8,128)(2,1)}, u32[]{:S(2)}, u32[]{:S(2)}) collective-permute-start(bf16[32,5376]{1,0:T(8,128)(2,1)} %collective-permute-done.4.refs_4_), channel_id=1, source_target_pairs={{0,14},{1,15},{2,0},{3,1},{4,2},{5,3},{6,4},{7,5},{8,6},{9,7},{10,... | collective-permute-start | bytes 1032200 | tf_op jit(solution)/shard_map/ppermute | solution.py:45
  64.6 1.9 %collective-permute-start.7 = (bf16[32,5376]{1,0:T(8,128)(2,1)}, bf16[32,5376]{1,0:T(8,128)(2,1)}, u32[]{:S(2)}, u32[]{:S(2)}) collective-permute-start(bf16[32,5376]{1,0:T(8,128)(2,1)} %collective-permute-done.5.refs_0_), channel_id=1, source_target_pairs={{0,2},{1,3},{2,4},{3,5},{4,6},{5,7},{6,8},{7,9},{8,10},{9,11},{10,... | collective-permute-start | bytes 1032200 | tf_op jit(solution)/shard_map/ppermute | solution.py:45
  66.5 2.6 %shard_map.55.refs_1_ = bf16[160,5376]{1,0:T(8,128)(2,1)} custom-call(bf16[32,5376]{1,0:T(8,128)(2,1)} %copy-done.8, bf16[32,5376]{1,0:T(8,128)(2,1)} %copy-done.9, bf16[32,5376]{1,0:T(8,128)(2,1)} %copy-done.10, bf16[32,5376]{1,0:T(8,128)(2,1)} %copy-done.11, bf16[32,5376]{1,0:T(8,128)(2,1)} %collective-permute-done.4.refs_4_), custom_call_target="tpu_custom_call" | custom-call | tf_op jit(solution)/shard_map/pallas_call | solution.py:63
  69.2 1.9 %collective-permute-start.8 = (bf16[160,5376]{1,0:T(8,128)(2,1)}, bf16[160,5376]{1,0:T(8,128)(2,1)}, u32[]{:S(2)}, u32[]{:S(2)}) collective-permute-start(bf16[160,5376]{1,0:T(8,128)(2,1)} %shard_map.55.refs_1_), channel_id=1, source_target_pairs={{0,1},{1,0},{2,3},{3,2},{4,5},{5,4},{6,7},{7,6},{8,9},{9,8},{10,11... | collective-permute-start | bytes 5160968 | tf_op jit(solution)/shard_map/ppermute | solution.py:45
  71.1 5.1 %collective-permute-start.14 = (bf16[48,5376]{1,0:T(8,128)(2,1)}, bf16[48,5376]{1,0:T(8,128)(2,1)}, u32[]{:S(2)}, u32[]{:S(2)}) collective-permute-start(bf16[48,5376]{1,0:T(8,128)(2,1)} %collective-permute-done.13.refs_9_), channel_id=1, source_target_pairs={{0,128},{1,129},{2,130},{3,131},{4,132},{5,133},{6,134},{7,135},{8... | collective-permute-start | bytes 1548296 | tf_op jit(solution)/shard_map/ppermute | solution.py:45
  76.3 1.9 %collective-permute-start.15 = (bf16[48,5376]{1,0:T(8,128)(2,1)}, bf16[48,5376]{1,0:T(8,128)(2,1)}, u32[]{:S(2)}, u32[]{:S(2)}) collective-permute-start(bf16[48,5376]{1,0:T(8,128)(2,1)} %collective-permute-done.13.refs_9_), channel_id=1, source_target_pairs={{0,384},{1,385},{2,386},{3,387},{4,388},{5,389},{6,390},{7,391},{8... | collective-permute-start | bytes 1548296 | tf_op jit(solution)/shard_map/ppermute | solution.py:45
  78.2 2.4 %collective-permute-start.16 = (bf16[48,5376]{1,0:T(8,128)(2,1)}, bf16[48,5376]{1,0:T(8,128)(2,1)}, u32[]{:S(2)}, u32[]{:S(2)}) collective-permute-start(bf16[48,5376]{1,0:T(8,128)(2,1)} %collective-permute-done.12.refs_8_), channel_id=1, source_target_pairs={{0,32},{1,97},{2,34},{3,99},{4,36},{5,101},{6,38},{7,103},{8,40},{... | collective-permute-start | bytes 1548296 | tf_op jit(solution)/shard_map/ppermute | solution.py:45
  80.6 5.1 %collective-permute-start.18 = (bf16[48,5376]{1,0:T(8,128)(2,1)}, bf16[48,5376]{1,0:T(8,128)(2,1)}, u32[]{:S(2)}, u32[]{:S(2)}) collective-permute-start(bf16[48,5376]{1,0:T(8,128)(2,1)} %collective-permute-done.17.refs_13_), channel_id=1, source_target_pairs={{0,128},{1,129},{2,130},{3,131},{4,132},{5,133},{6,134},{7,135},{8... | collective-permute-start | bytes 1548296 | tf_op jit(solution)/shard_map/ppermute | solution.py:45
  85.7 2.2 %shard_map.56.refs_2_ = bf16[96,5376]{1,0:T(8,128)(2,1)} custom-call(bf16[32,5376]{1,0:T(8,128)(2,1)} %collective-permute-done.5.refs_0_, bf16[32,5376]{1,0:T(8,128)(2,1)} %collective-permute-done.6.refs_1_, bf16[32,5376]{1,0:T(8,128)(2,1)} %collective-permute-done.7.refs_2_), custom_call_target="tpu_custom_call" | custom-call | tf_op jit(solution)/shard_map/pallas_call | solution.py:63
  88.0 0.8 collective-permute-done.14.refs_10_
  88.7 2.6 %collective-permute-start.21 = (bf16[48,5376]{1,0:T(8,128)(2,1)}, bf16[48,5376]{1,0:T(8,128)(2,1)}, u32[]{:S(2)}, u32[]{:S(2)}) collective-permute-start(bf16[48,5376]{1,0:T(8,128)(2,1)} %collective-permute-done.17.refs_13_), channel_id=1, source_target_pairs={{0,32},{1,97},{2,34},{3,99},{4,36},{5,101},{6,38},{7,103},{8,40},{... | collective-permute-start | bytes 1548296 | tf_op jit(solution)/shard_map/ppermute | solution.py:45
  91.3 2.3 %collective-permute-done.15.refs_11_ = bf16[48,5376]{1,0:T(8,128)(2,1)} collective-permute-done((bf16[48,5376]{1,0:T(8,128)(2,1)}, bf16[48,5376]{1,0:T(8,128)(2,1)}, u32[]{:S(2)}, u32[]{:S(2)}) %collective-permute-start.15) | collective-permute-done | bytes 516128 | tf_op jit(solution)/shard_map/ppermute | solution.py:45
  93.6 1.9 %collective-permute-start.9 = (bf16[96,5376]{1,0:T(8,128)(2,1)}, bf16[96,5376]{1,0:T(8,128)(2,1)}, u32[]{:S(2)}, u32[]{:S(2)}) collective-permute-start(bf16[96,5376]{1,0:T(8,128)(2,1)} %shard_map.56.refs_2_), channel_id=1, source_target_pairs={{0,1},{1,0},{2,3},{3,2},{4,5},{5,4},{6,7},{7,6},{8,9},{9,8},{10,11... | collective-permute-start | bytes 3096584 | tf_op jit(solution)/shard_map/ppermute | solution.py:45
  95.5 0.1 collective-permute-done.16.refs_12_
  95.7 2.3 %collective-permute-start.19 = (bf16[48,5376]{1,0:T(8,128)(2,1)}, bf16[48,5376]{1,0:T(8,128)(2,1)S(1)}, u32[]{:S(2)}, u32[]{:S(2)}) collective-permute-start(bf16[48,5376]{1,0:T(8,128)(2,1)} %collective-permute-done.17.refs_13_), channel_id=1, source_target_pairs={{0,384},{1,385},{2,386},{3,387},{4,388},{5,389},{6,390},{7,391},{8... | collective-permute-start | bytes 1548296 | tf_op jit(solution)/shard_map/ppermute | solution.py:45
  97.9 1.4 collective-permute-done.18.refs_14_
  99.3 2.7 %collective-permute-start.20 = (bf16[48,5376]{1,0:T(8,128)(2,1)}, bf16[48,5376]{1,0:T(8,128)(2,1)S(1)}, u32[]{:S(2)}, u32[]{:S(2)}) collective-permute-start(bf16[48,5376]{1,0:T(8,128)(2,1)} %collective-permute-done.16.refs_12_), channel_id=1, source_target_pairs={{0,32},{1,97},{2,34},{3,99},{4,36},{5,101},{6,38},{7,103},{8,40},{... | collective-permute-start | bytes 1548296 | tf_op jit(solution)/shard_map/ppermute | solution.py:45
  102.0 4.7 %collective-permute-done.21.refs_3_ = bf16[48,5376]{1,0:T(8,128)(2,1)} collective-permute-done((bf16[48,5376]{1,0:T(8,128)(2,1)}, bf16[48,5376]{1,0:T(8,128)(2,1)}, u32[]{:S(2)}, u32[]{:S(2)}) %collective-permute-start.21) | collective-permute-done | bytes 516128 | tf_op jit(solution)/shard_map/ppermute | solution.py:45
  106.7 4.7 %collective-permute-start.22 = (bf16[48,5376]{1,0:T(8,128)(2,1)}, bf16[48,5376]{1,0:T(8,128)(2,1)}, u32[]{:S(2)}, u32[]{:S(2)}) collective-permute-start(bf16[48,5376]{1,0:T(8,128)(2,1)} %collective-permute-done.21.refs_3_), channel_id=1, source_target_pairs={{0,128},{1,129},{2,130},{3,131},{4,132},{5,133},{6,134},{7,135},{8... | collective-permute-start | bytes 1548296 | tf_op jit(solution)/shard_map/ppermute | solution.py:45
  111.4 1.6 %collective-permute-done.19.refs_15_ = bf16[48,5376]{1,0:T(8,128)(2,1)S(1)} collective-permute-done((bf16[48,5376]{1,0:T(8,128)(2,1)}, bf16[48,5376]{1,0:T(8,128)(2,1)S(1)}, u32[]{:S(2)}, u32[]{:S(2)}) %collective-permute-start.19) | collective-permute-done | bytes 516128 | tf_op jit(solution)/shard_map/ppermute | solution.py:45
  113.0 0.8 copy-done.4
  113.8 1.9 %collective-permute-start.23 = (bf16[48,5376]{1,0:T(8,128)(2,1)}, bf16[48,5376]{1,0:T(8,128)(2,1)}, u32[]{:S(2)}, u32[]{:S(2)}) collective-permute-start(bf16[48,5376]{1,0:T(8,128)(2,1)} %collective-permute-done.21.refs_3_), channel_id=1, source_target_pairs={{0,384},{1,385},{2,386},{3,387},{4,388},{5,389},{6,390},{7,391},{8... | collective-permute-start | bytes 1548296 | tf_op jit(solution)/shard_map/ppermute | solution.py:45
  115.7 1.4 collective-permute-done.20.refs_16_
  117.1 0.8 copy-done.6
  117.9 4.2 %collective-permute-start.24 = (bf16[48,5376]{1,0:T(8,128)(2,1)}, bf16[48,5376]{1,0:T(8,128)(2,1)}, u32[]{:S(2)}, u32[]{:S(2)}) collective-permute-start(bf16[48,5376]{1,0:T(8,128)(2,1)} %collective-permute-done.21.refs_3_), channel_id=1, source_target_pairs={{0,256},{1,257},{2,258},{3,259},{4,260},{5,261},{6,262},{7,263},{8... | collective-permute-start | bytes 1548296 | tf_op jit(solution)/shard_map/ppermute | solution.py:45
  122.4 1.5 copy-done.1
  123.8 1.2 copy-done.2
  125.0 1.0 copy-done.5
  126.1 1.0 copy-done.7
  127.1 7.9 %shard_map.57 = (bf16[512,768]{1,0:T(8,128)(2,1)S(1)}, bf16[512,5376]{1,0:T(8,128)(2,1)S(1)}) custom-call(f32[512,1]{1,0:T(8,128)S(1)} %copy.7.refs_0_, bf16[160,5376]{1,0:T(8,128)(2,1)S(1)} %copy-done.1, bf16[96,5376]{1,0:T(8,128)(2,1)S(1)} %copy-done.2, bf16[160,5376]{1,0:T(8,128)(2,1)} %collective-permute-done.8.refs_3_, ...), custom_call_target="tpu_custom_call" | custom-call | tf_op jit(solution)/shard_map/pallas_call | solution.py:161
  135.0 6.4 %collective-permute-done.23.refs_5_ = bf16[48,5376]{1,0:T(8,128)(2,1)} collective-permute-done((bf16[48,5376]{1,0:T(8,128)(2,1)}, bf16[48,5376]{1,0:T(8,128)(2,1)}, u32[]{:S(2)}, u32[]{:S(2)}) %collective-permute-start.23) | collective-permute-done | bytes 516128 | tf_op jit(solution)/shard_map/ppermute | solution.py:45
  141.4 4.5 %shard_map.58 = bf16[512,768]{1,0:T(8,128)(2,1)} custom-call(f32[512,1]{1,0:T(8,128)S(1)} %copy.7.refs_0_, bf16[512,5376]{1,0:T(8,128)(2,1)S(1)} %get-tuple-element.7.refs_1_, bf16[512,768]{1,0:T(8,128)(2,1)S(1)} %get-tuple-element.8.refs_2_, bf16[48,5376]{1,0:T(8,128)(2,1)} %collective-permute-done.21.refs_3_, ...), custom_call_target="tpu_custom_call" | custom-call | tf_op jit(solution)/shard_map/pallas_call | solution.py:161
  (40 shorter events, 0.3 us)
Async XLA Ops:
  0.0 2.8 %copy-start = (bf16[256,5376]{1,0:T(8,128)(2,1)S(1)}, bf16[256,5376]{1,0:T(8,128)(2,1)}, u32[]{:S(2)}) copy-start(bf16[256,5376]{1,0:T(8,128)(2,1)} %param.5) | copy-start | bytes 8257540
  3.6 15.6 %collective-permute-start = (bf16[16,5376]{1,0:T(8,128)(2,1)S(1)}, bf16[16,5376]{1,0:T(8,128)(2,1)S(1)}, u32[]{:S(2)}, u32[]{:S(2)}) collective-permute-start(bf16[16,5376]{1,0:T(8,128)(2,1)S(1)} %broadcast_select_fusion), channel_id=1, source_target_pairs={{0,16},{1,17},{2,18},{3,19},{4,20},{5,21},{6,22},{7,23},{8,24},{9,... | collective-permute-start | bytes 516104 | tf_op jit(solution)/shard_map/ppermute | solution.py:45
  19.2 12.6 %copy-start.8 = (bf16[32,5376]{1,0:T(8,128)(2,1)}, bf16[32,5376]{1,0:T(8,128)(2,1)S(1)}, u32[]{:S(2)}) copy-start(bf16[32,5376]{1,0:T(8,128)(2,1)S(1)} %pad_maximum_fusion.refs_0_) | copy-start | bytes 1032196
  19.2 102.9 %copy-start.12 = (f32[1,512]{1,0:T(1,128)S(1)}, f32[1,512]{1,0:T(1,128)}, u32[]{:S(2)}) copy-start(f32[1,512]{1,0:T(1,128)} %param.9) | copy-start | bytes 6148
  19.3 103.1 %copy-start.3 = (bf16[48,5376]{1,0:T(8,128)(2,1)S(1)}, bf16[48,5376]{1,0:T(8,128)(2,1)}, u32[]{:S(2)}) copy-start(bf16[48,5376]{1,0:T(8,128)(2,1)} %refs_5_.1) | copy-start | bytes 1548292
  19.3 21.1 %collective-permute-start.1 = (bf16[32,5376]{1,0:T(8,128)(2,1)S(1)}, bf16[32,5376]{1,0:T(8,128)(2,1)S(1)}, u32[]{:S(2)}, u32[]{:S(2)}) collective-permute-start(bf16[32,5376]{1,0:T(8,128)(2,1)S(1)} %pad_maximum_fusion.refs_0_), channel_id=1, source_target_pairs={{0,2},{1,3},{2,4},{3,5},{4,6},{5,7},{6,8},{7,9},{8,10},{9,11},{10,... | collective-permute-start | bytes 1032200 | tf_op jit(solution)/shard_map/ppermute | solution.py:45
  23.7 29.8 %collective-permute-start.13 = (bf16[48,5376]{1,0:T(8,128)(2,1)}, bf16[48,5376]{1,0:T(8,128)(2,1)}, u32[]{:S(2)}, u32[]{:S(2)}) collective-permute-start(bf16[48,5376]{1,0:T(8,128)(2,1)} %refs_5_.1), channel_id=1, source_target_pairs={{0,32},{1,97},{2,34},{3,99},{4,36},{5,101},{6,38},{7,103},{8,40},{... | collective-permute-start | bytes 1548296 | tf_op jit(solution)/shard_map/ppermute | solution.py:45
  28.5 27.0 %collective-permute-start.12 = (bf16[48,5376]{1,0:T(8,128)(2,1)}, bf16[48,5376]{1,0:T(8,128)(2,1)}, u32[]{:S(2)}, u32[]{:S(2)}) collective-permute-start(bf16[48,5376]{1,0:T(8,128)(2,1)} %refs_5_.1), channel_id=1, source_target_pairs={{0,256},{1,257},{2,258},{3,259},{4,260},{5,261},{6,262},{7,263},{8... | collective-permute-start | bytes 1548296 | tf_op jit(solution)/shard_map/ppermute | solution.py:45
  31.8 14.6 %collective-permute-start.2 = (bf16[32,5376]{1,0:T(8,128)(2,1)S(1)}, bf16[32,5376]{1,0:T(8,128)(2,1)S(1)}, u32[]{:S(2)}, u32[]{:S(2)}) collective-permute-start(bf16[32,5376]{1,0:T(8,128)(2,1)S(1)} %pad_maximum_fusion.refs_0_), channel_id=1, source_target_pairs={{0,14},{1,15},{2,0},{3,1},{4,2},{5,3},{6,4},{7,5},{8,6},{9,7},{10,... | collective-permute-start | bytes 1032200 | tf_op jit(solution)/shard_map/ppermute | solution.py:45
  40.4 6.0 %copy-start.9 = (bf16[32,5376]{1,0:T(8,128)(2,1)}, bf16[32,5376]{1,0:T(8,128)(2,1)S(1)}, u32[]{:S(2)}) copy-start(bf16[32,5376]{1,0:T(8,128)(2,1)S(1)} %collective-permute-done.1.refs_1_) | copy-start | bytes 1032196
  40.4 11.1 %collective-permute-start.3 = (bf16[32,5376]{1,0:T(8,128)(2,1)S(1)}, bf16[32,5376]{1,0:T(8,128)(2,1)S(1)}, u32[]{:S(2)}, u32[]{:S(2)}) collective-permute-start(bf16[32,5376]{1,0:T(8,128)(2,1)S(1)} %collective-permute-done.1.refs_1_), channel_id=1, source_target_pairs={{0,2},{1,3},{2,4},{3,5},{4,6},{5,7},{6,8},{7,9},{8,10},{9,11},{10,... | collective-permute-start | bytes 1032200 | tf_op jit(solution)/shard_map/ppermute | solution.py:45
  42.3 26.9 %collective-permute-start.10 = (bf16[48,5376]{1,0:T(8,128)(2,1)}, bf16[48,5376]{1,0:T(8,128)(2,1)}, u32[]{:S(2)}, u32[]{:S(2)}) collective-permute-start(bf16[48,5376]{1,0:T(8,128)(2,1)} %refs_5_.1), channel_id=1, source_target_pairs={{0,128},{1,129},{2,130},{3,131},{4,132},{5,133},{6,134},{7,135},{8... | collective-permute-start | bytes 1548296 | tf_op jit(solution)/shard_map/ppermute | solution.py:45
  46.4 5.2 %copy-start.10 = (bf16[32,5376]{1,0:T(8,128)(2,1)}, bf16[32,5376]{1,0:T(8,128)(2,1)S(1)}, u32[]{:S(2)}) copy-start(bf16[32,5376]{1,0:T(8,128)(2,1)S(1)} %collective-permute-done.2.refs_2_) | copy-start | bytes 1032196
  46.4 13.1 %collective-permute-start.4 = (bf16[32,5376]{1,0:T(8,128)(2,1)S(1)}, bf16[32,5376]{1,0:T(8,128)(2,1)}, u32[]{:S(2)}, u32[]{:S(2)}) collective-permute-start(bf16[32,5376]{1,0:T(8,128)(2,1)S(1)} %collective-permute-done.2.refs_2_), channel_id=1, source_target_pairs={{0,14},{1,15},{2,0},{3,1},{4,2},{5,3},{6,4},{7,5},{8,6},{9,7},{10,... | collective-permute-start | bytes 1032200 | tf_op jit(solution)/shard_map/ppermute | solution.py:45
  51.5 7.9 %copy-start.11 = (bf16[32,5376]{1,0:T(8,128)(2,1)}, bf16[32,5376]{1,0:T(8,128)(2,1)S(1)}, u32[]{:S(2)}) copy-start(bf16[32,5376]{1,0:T(8,128)(2,1)S(1)} %collective-permute-done.3.refs_3_) | copy-start | bytes 1032196
  51.6 13.1 %collective-permute-start.5 = (bf16[32,5376]{1,0:T(8,128)(2,1)S(1)}, bf16[32,5376]{1,0:T(8,128)(2,1)}, u32[]{:S(2)}, u32[]{:S(2)}) collective-permute-start(bf16[32,5376]{1,0:T(8,128)(2,1)S(1)} %collective-permute-done.3.refs_3_), channel_id=1, source_target_pairs={{0,2},{1,3},{2,4},{3,5},{4,6},{5,7},{6,8},{7,9},{8,10},{9,11},{10,... | collective-permute-start | bytes 1032200 | tf_op jit(solution)/shard_map/ppermute | solution.py:45
  53.5 17.6 %collective-permute-start.11 = (bf16[48,5376]{1,0:T(8,128)(2,1)}, bf16[48,5376]{1,0:T(8,128)(2,1)}, u32[]{:S(2)}, u32[]{:S(2)}) collective-permute-start(bf16[48,5376]{1,0:T(8,128)(2,1)} %refs_5_.1), channel_id=1, source_target_pairs={{0,384},{1,385},{2,386},{3,387},{4,388},{5,389},{6,390},{7,391},{8... | collective-permute-start | bytes 1548296 | tf_op jit(solution)/shard_map/ppermute | solution.py:45
  55.4 20.8 %collective-permute-start.17 = (bf16[48,5376]{1,0:T(8,128)(2,1)}, bf16[48,5376]{1,0:T(8,128)(2,1)}, u32[]{:S(2)}, u32[]{:S(2)}) collective-permute-start(bf16[48,5376]{1,0:T(8,128)(2,1)} %collective-permute-done.13.refs_9_), channel_id=1, source_target_pairs={{0,32},{1,97},{2,34},{3,99},{4,36},{5,101},{6,38},{7,103},{8,40},{... | collective-permute-start | bytes 1548296 | tf_op jit(solution)/shard_map/ppermute | solution.py:45
  59.5 18.8 %collective-permute-start.6 = (bf16[32,5376]{1,0:T(8,128)(2,1)}, bf16[32,5376]{1,0:T(8,128)(2,1)}, u32[]{:S(2)}, u32[]{:S(2)}) collective-permute-start(bf16[32,5376]{1,0:T(8,128)(2,1)} %collective-permute-done.4.refs_4_), channel_id=1, source_target_pairs={{0,14},{1,15},{2,0},{3,1},{4,2},{5,3},{6,4},{7,5},{8,6},{9,7},{10,... | collective-permute-start | bytes 1032200 | tf_op jit(solution)/shard_map/ppermute | solution.py:45
  64.6 16.0 %collective-permute-start.7 = (bf16[32,5376]{1,0:T(8,128)(2,1)}, bf16[32,5376]{1,0:T(8,128)(2,1)}, u32[]{:S(2)}, u32[]{:S(2)}) collective-permute-start(bf16[32,5376]{1,0:T(8,128)(2,1)} %collective-permute-done.5.refs_0_), channel_id=1, source_target_pairs={{0,2},{1,3},{2,4},{3,5},{4,6},{5,7},{6,8},{7,9},{8,10},{9,11},{10,... | collective-permute-start | bytes 1032200 | tf_op jit(solution)/shard_map/ppermute | solution.py:45
  69.2 53.1 %collective-permute-start.8 = (bf16[160,5376]{1,0:T(8,128)(2,1)}, bf16[160,5376]{1,0:T(8,128)(2,1)}, u32[]{:S(2)}, u32[]{:S(2)}) collective-permute-start(bf16[160,5376]{1,0:T(8,128)(2,1)} %shard_map.55.refs_1_), channel_id=1, source_target_pairs={{0,1},{1,0},{2,3},{3,2},{4,5},{5,4},{6,7},{7,6},{8,9},{9,8},{10,11... | collective-permute-start | bytes 5160968 | tf_op jit(solution)/shard_map/ppermute | solution.py:45
  71.1 17.6 %collective-permute-start.14 = (bf16[48,5376]{1,0:T(8,128)(2,1)}, bf16[48,5376]{1,0:T(8,128)(2,1)}, u32[]{:S(2)}, u32[]{:S(2)}) collective-permute-start(bf16[48,5376]{1,0:T(8,128)(2,1)} %collective-permute-done.13.refs_9_), channel_id=1, source_target_pairs={{0,128},{1,129},{2,130},{3,131},{4,132},{5,133},{6,134},{7,135},{8... | collective-permute-start | bytes 1548296 | tf_op jit(solution)/shard_map/ppermute | solution.py:45
  76.3 17.3 %collective-permute-start.15 = (bf16[48,5376]{1,0:T(8,128)(2,1)}, bf16[48,5376]{1,0:T(8,128)(2,1)}, u32[]{:S(2)}, u32[]{:S(2)}) collective-permute-start(bf16[48,5376]{1,0:T(8,128)(2,1)} %collective-permute-done.13.refs_9_), channel_id=1, source_target_pairs={{0,384},{1,385},{2,386},{3,387},{4,388},{5,389},{6,390},{7,391},{8... | collective-permute-start | bytes 1548296 | tf_op jit(solution)/shard_map/ppermute | solution.py:45
  78.2 17.4 %collective-permute-start.16 = (bf16[48,5376]{1,0:T(8,128)(2,1)}, bf16[48,5376]{1,0:T(8,128)(2,1)}, u32[]{:S(2)}, u32[]{:S(2)}) collective-permute-start(bf16[48,5376]{1,0:T(8,128)(2,1)} %collective-permute-done.12.refs_8_), channel_id=1, source_target_pairs={{0,32},{1,97},{2,34},{3,99},{4,36},{5,101},{6,38},{7,103},{8,40},{... | collective-permute-start | bytes 1548296 | tf_op jit(solution)/shard_map/ppermute | solution.py:45
  80.6 18.7 %collective-permute-start.18 = (bf16[48,5376]{1,0:T(8,128)(2,1)}, bf16[48,5376]{1,0:T(8,128)(2,1)}, u32[]{:S(2)}, u32[]{:S(2)}) collective-permute-start(bf16[48,5376]{1,0:T(8,128)(2,1)} %collective-permute-done.17.refs_13_), channel_id=1, source_target_pairs={{0,128},{1,129},{2,130},{3,131},{4,132},{5,133},{6,134},{7,135},{8... | collective-permute-start | bytes 1548296 | tf_op jit(solution)/shard_map/ppermute | solution.py:45
  88.7 18.0 %collective-permute-start.21 = (bf16[48,5376]{1,0:T(8,128)(2,1)}, bf16[48,5376]{1,0:T(8,128)(2,1)}, u32[]{:S(2)}, u32[]{:S(2)}) collective-permute-start(bf16[48,5376]{1,0:T(8,128)(2,1)} %collective-permute-done.17.refs_13_), channel_id=1, source_target_pairs={{0,32},{1,97},{2,34},{3,99},{4,36},{5,101},{6,38},{7,103},{8,40},{... | collective-permute-start | bytes 1548296 | tf_op jit(solution)/shard_map/ppermute | solution.py:45
  93.6 28.8 %collective-permute-start.9 = (bf16[96,5376]{1,0:T(8,128)(2,1)}, bf16[96,5376]{1,0:T(8,128)(2,1)}, u32[]{:S(2)}, u32[]{:S(2)}) collective-permute-start(bf16[96,5376]{1,0:T(8,128)(2,1)} %shard_map.56.refs_2_), channel_id=1, source_target_pairs={{0,1},{1,0},{2,3},{3,2},{4,5},{5,4},{6,7},{7,6},{8,9},{9,8},{10,11... | collective-permute-start | bytes 3096584 | tf_op jit(solution)/shard_map/ppermute | solution.py:45
  95.7 17.3 %collective-permute-start.19 = (bf16[48,5376]{1,0:T(8,128)(2,1)}, bf16[48,5376]{1,0:T(8,128)(2,1)S(1)}, u32[]{:S(2)}, u32[]{:S(2)}) collective-permute-start(bf16[48,5376]{1,0:T(8,128)(2,1)} %collective-permute-done.17.refs_13_), channel_id=1, source_target_pairs={{0,384},{1,385},{2,386},{3,387},{4,388},{5,389},{6,390},{7,391},{8... | collective-permute-start | bytes 1548296 | tf_op jit(solution)/shard_map/ppermute | solution.py:45
  99.3 17.8 %collective-permute-start.20 = (bf16[48,5376]{1,0:T(8,128)(2,1)}, bf16[48,5376]{1,0:T(8,128)(2,1)S(1)}, u32[]{:S(2)}, u32[]{:S(2)}) collective-permute-start(bf16[48,5376]{1,0:T(8,128)(2,1)} %collective-permute-done.16.refs_12_), channel_id=1, source_target_pairs={{0,32},{1,97},{2,34},{3,99},{4,36},{5,101},{6,38},{7,103},{8,40},{... | collective-permute-start | bytes 1548296 | tf_op jit(solution)/shard_map/ppermute | solution.py:45
  106.7 28.3 %collective-permute-start.22 = (bf16[48,5376]{1,0:T(8,128)(2,1)}, bf16[48,5376]{1,0:T(8,128)(2,1)}, u32[]{:S(2)}, u32[]{:S(2)}) collective-permute-start(bf16[48,5376]{1,0:T(8,128)(2,1)} %collective-permute-done.21.refs_3_), channel_id=1, source_target_pairs={{0,128},{1,129},{2,130},{3,131},{4,132},{5,133},{6,134},{7,135},{8... | collective-permute-start | bytes 1548296 | tf_op jit(solution)/shard_map/ppermute | solution.py:45
  113.0 0.8 copy-start.4
  113.8 27.6 %collective-permute-start.23 = (bf16[48,5376]{1,0:T(8,128)(2,1)}, bf16[48,5376]{1,0:T(8,128)(2,1)}, u32[]{:S(2)}, u32[]{:S(2)}) collective-permute-start(bf16[48,5376]{1,0:T(8,128)(2,1)} %collective-permute-done.21.refs_3_), channel_id=1, source_target_pairs={{0,384},{1,385},{2,386},{3,387},{4,388},{5,389},{6,390},{7,391},{8... | collective-permute-start | bytes 1548296 | tf_op jit(solution)/shard_map/ppermute | solution.py:45
  117.1 0.8 copy-start.6
  117.9 23.5 %collective-permute-start.24 = (bf16[48,5376]{1,0:T(8,128)(2,1)}, bf16[48,5376]{1,0:T(8,128)(2,1)}, u32[]{:S(2)}, u32[]{:S(2)}) collective-permute-start(bf16[48,5376]{1,0:T(8,128)(2,1)} %collective-permute-done.21.refs_3_), channel_id=1, source_target_pairs={{0,256},{1,257},{2,258},{3,259},{4,260},{5,261},{6,262},{7,263},{8... | collective-permute-start | bytes 1548296 | tf_op jit(solution)/shard_map/ppermute | solution.py:45
  122.3 1.5 %copy-start.1 = (bf16[160,5376]{1,0:T(8,128)(2,1)S(1)}, bf16[160,5376]{1,0:T(8,128)(2,1)}, u32[]{:S(2)}) copy-start(bf16[160,5376]{1,0:T(8,128)(2,1)} %shard_map.55.refs_1_) | copy-start | bytes 5160964
  123.8 1.2 copy-start.2
  125.0 1.0 copy-start.5
  126.1 1.0 copy-start.7

commit v6 on v5

--- a/solution.py
+++ b/solution.py
@@ -29,12 +29,12 @@
 
 UP_X = routes(lambda x, y, z, c: (x + 1, y, z, c))
 DOWN_X = routes(lambda x, y, z, c: (x - 1, y, z, c))
-FAR_X = routes(lambda x, y, z, c: (x + 2, y, z, c))
 RING_Y = routes(lambda x, y, z, c: (x, y // 4 * 4 + (y + (1 - 2 * c)) % 4, z, c))
 OTHER_Y = routes(lambda x, y, z, c: (x, (y + 4) % 8, z, c))
 UP_Z = routes(lambda x, y, z, c: (x, y, z + 1, c))
 DOWN_Z = routes(lambda x, y, z, c: (x, y, z - 1, c))
 CORE = routes(lambda x, y, z, c: (x, y, z, 1 - c))
+ROWS_X = [[x * 4 + y for x in range(4)] for y in range(4)]
 
 HOPS_Z = (0, -1, 1, -2, 2, -3, 3, -4)
 HOPS_X = (0, -1, 1, 2)
@@ -43,6 +43,11 @@
 
 def send(value, pairs):
     return lax.ppermute(value, AXES, pairs)
+
+
+def share(value):
+    copies = jnp.broadcast_to(value[None], (4,) + value.shape)
+    return lax.all_to_all(copies, "prompt", 0, 0, axis_index_groups=ROWS_X, tiled=True)
 
 
 def stack_kernel(*refs):
@@ -75,31 +80,21 @@
     return prompt // 4, prompt % 4, chip // 8, chip % 8, owner % 2
 
 
-def product_kernel(n_sources, n_targets, first_block, last, *refs):
-    act_ref, refs = refs[0], refs[1:]
-    if last:
-        (rows, before_ref), refs = refs[:2], refs[2:]
-        sources = ()
-    else:
-        sources, refs = refs[:n_sources], refs[n_sources:]
-    targets, refs = refs[:n_targets], refs[n_targets:]
-    if last:
-        out_ref, cols, acc, order, act, sem = refs
-    else:
-        out_ref, rows, cols, acc, order, act, sem = refs
-    depth = rows.shape[1]
-    width = depth // PARTS
+def product_kernel(n_sources, act_ref, *refs):
+    operands, (out_ref, rows, cols, acc, order, act, sem) = refs[:-7], refs[-7:]
+    sources, targets = operands[:n_sources], operands[n_sources:]
+    width = rows.shape[1] // PARTS
 
     def copies(part):
         at_depth = pl.ds(pl.multiple_of(part * width, 128), width)
         found, i = [], 0
-        for into, operands in ((rows, sources), (cols, targets)):
+        for into, pieces in ((rows, sources), (cols, targets)):
             at = 0
-            for operand in operands:
-                size = operand.shape[0]
+            for piece in pieces:
+                size = piece.shape[0]
                 found.append(
                     pltpu.make_async_copy(
-                        operand.at[:, at_depth], into.at[pl.ds(at, size), at_depth], sem.at[part, i]
+                        piece.at[:, at_depth], into.at[pl.ds(at, size), at_depth], sem.at[part, i]
                     )
                 )
                 at += size
@@ -123,9 +118,10 @@
     block = out_ref.shape[1] // 16
     lane = lax.broadcasted_iota(jnp.int32, (block, out_ref.shape[1]), 1)
     line = lax.broadcasted_iota(jnp.int32, (block, out_ref.shape[1]), 0)
-    for i in range(cols.shape[0] // block):
-        step_y, hop = divmod(first_block + i, len(HOPS_X))
-        origin = ((x + HOPS_X[hop]) & 3) * 4 + ((y - (1 - 2 * core) * step_y) & 3)
+    for i in range(16):
+        step_y, step_x = divmod(i, 4)
+        x_from = step_x if step_y in (0, 3) else (x + HOPS_X[step_x]) & 3
+        origin = x_from * 4 + ((y - (1 - 2 * core) * step_y) & 3)
         order[i * block : (i + 1) * block] = jnp.where(lane == line + origin * block, 1.0, 0.0).astype(jnp.bfloat16)
 
     acc[...] = jnp.zeros_like(acc)
@@ -140,38 +136,31 @@
         )
 
     edges = (acc[...] * act[...]).astype(jnp.bfloat16)
-    placed = jnp.dot(edges, order[...], preferred_element_type=jnp.float32)
-    if not last:
-        out_ref[...] = placed.astype(jnp.bfloat16)
-        return
-    placed = (placed + before_ref[...].astype(jnp.float32)).astype(jnp.bfloat16)
+    placed = jnp.dot(edges, order[...], preferred_element_type=jnp.float32).astype(jnp.bfloat16)
     for g, at in enumerate(row_at):
         out_ref[pl.ds(at, slots), :] = placed[g * slots : (g + 1) * slots]
 
 
-def product(act, first_block, sources, targets, rows=None, before=None):
+def product(act, sources, targets):
     depth = targets[0].shape[1]
-    n_rows = act.shape[0]
-    n_cols, n_out = sum(t.shape[0] for t in targets), targets[0].shape[0] * 16
-    whole, anywhere = pl.BlockSpec(memory_space=pltpu.VMEM), pl.BlockSpec(memory_space=pl.ANY)
-    last = before is not None
-    operands = (act, rows, before, *targets) if last else (act, *sources, *targets)
-    edges_shape = jax.ShapeDtypeStruct((n_rows, n_out), jnp.bfloat16)
-    rows_shape = jax.ShapeDtypeStruct((n_rows, depth), jnp.bfloat16)
+    n_rows, n_cols = act.shape[0], sum(t.shape[0] for t in targets)
+    whole, anywhere = pl.BlockSpec(memory_space=pltpu.VMEM), pl.BlockSpec(memory_space=pltpu.HBM)
     return pl.pallas_call(
-        functools.partial(product_kernel, len(sources), len(targets), first_block, last),
-        out_shape=edges_shape if last else (edges_shape, rows_shape),
-        in_specs=[whole] * (3 if last else 1) + [anywhere] * (len(sources) + len(targets)),
-        out_specs=whole if last else (whole, whole),
+        functools.partial(product_kernel, len(sources)),
+        out_shape=jax.ShapeDtypeStruct((n_rows, n_cols), jnp.bfloat16),
+        in_specs=[whole] + [anywhere] * (len(sources) + len(targets)),
+        out_specs=whole,
         scratch_shapes=[
+            pltpu.VMEM((n_rows, depth), jnp.bfloat16),
             pltpu.VMEM((n_cols, depth), jnp.bfloat16),
             pltpu.VMEM((n_rows, n_cols), jnp.float32),
-            pltpu.VMEM((n_cols, n_out), jnp.bfloat16),
+            pltpu.VMEM((n_cols, n_cols), jnp.bfloat16),
             pltpu.VMEM((n_rows, 1), jnp.float32),
             pltpu.SemaphoreType.DMA((PARTS, len(sources) + len(targets))),
         ],
-        compiler_params=pltpu.CompilerParams(vmem_limit_bytes=24 << 20),
-    )(*operands)
+        compiler_params=pltpu.CompilerParams(vmem_limit_bytes=28 << 20),
+        name="product",
+    )(act, *sources, *targets)
 
 
 def edges_of(decoder, encoder, row_ids, counts, activity):
@@ -188,11 +177,12 @@
     y1 = send(y0, RING_Y)
     y2 = send(y1, RING_Y)
     y3 = send(y2, RING_Y)
-    a1, a2, a3 = send(y0, UP_X), send(y0, DOWN_X), send(y0, FAR_X)
+    width = y0.shape[0]
+    aa, dd = share(y0), share(y3)
     b1, b2 = send(y1, UP_X), send(y1, DOWN_X)
     c1, c2 = send(y2, UP_X), send(y2, DOWN_X)
-    d1, d2, d3 = send(y3, UP_X), send(y3, DOWN_X), send(y3, FAR_X)
-    f1 = send(a3, RING_Y)
+    far = lax.dynamic_index_in_dim(aa, (lax.axis_index("prompt") // 4 + 2) % 4, 0, keepdims=False)
+    f1 = send(far, RING_Y)
     f2 = send(f1, RING_Y)
 
     other = send(source_rows, OTHER_Y)
@@ -205,10 +195,8 @@
     away = stack(u3, w3, u4)
     sources = [near, away, send(near, CORE), send(away, CORE)]
 
-    act = activity.reshape(-1, 1)
-    part, rows = product(act, 0, sources, [y0, a1, a2, a3, y1, b1, b2, f1, y2, c1, c2, f2])
-    edges = product(act, 12, [], [y3, d1, d2, d3], rows, part)
-    return edges[None]
+    targets = [aa.reshape(4 * width, -1), y1, b1, b2, f1, y2, c1, c2, f2, dd.reshape(4 * width, -1)]
+    return product(activity.reshape(-1, 1), sources, targets)[None]
 
 
 def solution(mesh):

time: 147 us -> 147 us (level)
  the two profiles are of different devices: /device:TPU:62 before, /device:TPU:1 now
where the time goes in v6:
time: 147 us; the launch traced here: 145 us
  starting transfers between devices  86.9 us (59%)
  waiting for transfers between devices  30.1 us (20%)
  Pallas kernels  13.9 us (9%)
  local copies, waits for them, and re-layouts  10.3 us (7%)
  other arithmetic  3.79 us (3%)
    ppermute x19, starting transfers between devices, send(): return lax.ppermute(value, AXES, pairs)  78 us
    ppermute x19, waiting for transfers between devices, send(): return lax.ppermute(value, AXES, pairs)  30.1 us
    pallas_call x1, Pallas kernels, product(): pl.pallas_call(functools.partial(product_kernel, len(sources)), out_shape...  9.03 us
    all_to_all x2, starting transfers between devices, share(): lax.all_to_all(copies, 'prompt', 0, 0, axis_index_groups=ROWS_X, tiled=True)  8.88 us
    broadcast_in_dim x2, local copies, waits for them, and re-layouts, share(): copies = jnp.broadcast_to(value[None], (4,) + value.shape)  4.99 us
    pallas_call x2, Pallas kernels, stack(): pl.pallas_call(stack_kernel, out_shape=jax.ShapeDtypeStruct((n_rows, piec...  4.91 us
  transfers between devices with their start and end apart: 21, of which 5 were waited for; matrix products, arithmetic and copies ran while one was open for 5% of the time, Pallas kernels for 3%

profile of v6, /device:TPU:1, one launch (start us, length us, event | category | flops | bytes accessed | tf_op | source)
XLA Modules:
  0.0 145.5 jit_solution(4014058144161000929)
XLA Ops:
  0.0 1.4 fusion
  1.4 0.6 iota_compare_fusion
  2.1 0.7 fusion.1
  2.8 0.7 gather_fusion
  3.4 0.1 broadcast_select_fusion
  3.5 8.3 %collective-permute-start = (bf16[16,5376]{1,0:T(8,128)(2,1)S(1)}, bf16[16,5376]{1,0:T(8,128)(2,1)}, u32[]{:S(2)}, u32[]{:S(2)}) collective-permute-start(bf16[16,5376]{1,0:T(8,128)(2,1)S(1)} %broadcast_select_fusion), channel_id=1, source_target_pairs={{0,16},{1,17},{2,18},{3,19},{4,20},{5,21},{6,22},{7,23},{8,24},{9,... | collective-permute-start | bytes 516104 | tf_op jit(solution)/shard_map/ppermute | solution.py:45
  11.8 2.5 %collective-permute-start.10 = (bf16[48,5376]{1,0:T(8,128)(2,1)}, bf16[48,5376]{1,0:T(8,128)(2,1)S(1)}, u32[]{:S(2)}, u32[]{:S(2)}) collective-permute-start(bf16[48,5376]{1,0:T(8,128)(2,1)} %param.6), channel_id=1, source_target_pairs={{0,32},{1,97},{2,34},{3,99},{4,36},{5,101},{6,38},{7,103},{8,40},{... | collective-permute-start | bytes 1548296 | tf_op jit(solution)/shard_map/ppermute | solution.py:45
  14.3 2.5 %broadcast_in_dim.36 = bf16[4,48,5376]{2,1,0:T(8,128)(2,1)} broadcast(bf16[48,5376]{1,0:T(8,128)(2,1)} %param.6), dimensions={1,2} | broadcast | bytes 2580480 | tf_op jit(solution)/shard_map/broadcast_in_dim | solution.py:49
  16.8 4.4 %all-to-all-start = ((bf16[4,48,5376]{2,1,0:T(8,128)(2,1)}), bf16[4,48,5376]{2,1,0:T(8,128)(2,1)}, u32[]{:S(2)}, u32[]{:S(2)}) async-start(bf16[4,48,5376]{2,1,0:T(8,128)(2,1)} %broadcast_in_dim.36), calls=%async_computation | async-start | bytes 4128768 | tf_op jit(solution)/shard_map/all_to_all | solution.py:50
  21.3 0.0 collective-permute-done
  21.3 0.9 pad_maximum_fusion.refs_0_
  22.2 0.0 copy-start.3
  22.2 4.0 %collective-permute-start.1 = (bf16[32,5376]{1,0:T(8,128)(2,1)S(1)}, bf16[32,5376]{1,0:T(8,128)(2,1)S(1)}, u32[]{:S(2)}, u32[]{:S(2)}) collective-permute-start(bf16[32,5376]{1,0:T(8,128)(2,1)S(1)} %pad_maximum_fusion.refs_0_), channel_id=1, source_target_pairs={{0,2},{1,3},{2,4},{3,5},{4,6},{5,7},{6,8},{7,9},{8,10},{9,11},{10,... | collective-permute-start | bytes 1032200 | tf_op jit(solution)/shard_map/ppermute | solution.py:45
  26.3 5.2 %collective-permute-done.10.refs_5_ = bf16[48,5376]{1,0:T(8,128)(2,1)S(1)} collective-permute-done((bf16[48,5376]{1,0:T(8,128)(2,1)}, bf16[48,5376]{1,0:T(8,128)(2,1)S(1)}, u32[]{:S(2)}, u32[]{:S(2)}) %collective-permute-start.10) | collective-permute-done | bytes 516128 | tf_op jit(solution)/shard_map/ppermute | solution.py:45
  31.4 4.0 %collective-permute-start.14 = (bf16[48,5376]{1,0:T(8,128)(2,1)S(1)}, bf16[48,5376]{1,0:T(8,128)(2,1)}, u32[]{:S(2)}, u32[]{:S(2)}) collective-permute-start(bf16[48,5376]{1,0:T(8,128)(2,1)S(1)} %collective-permute-done.10.refs_5_), channel_id=1, source_target_pairs={{0,32},{1,97},{2,34},{3,99},{4,36},{5,101},{6,38},{7,103},{8,40},{... | collective-permute-start | bytes 1548296 | tf_op jit(solution)/shard_map/ppermute | solution.py:45
  35.5 10.7 %collective-permute-start.2 = (bf16[32,5376]{1,0:T(8,128)(2,1)S(1)}, bf16[32,5376]{1,0:T(8,128)(2,1)}, u32[]{:S(2)}, u32[]{:S(2)}) collective-permute-start(bf16[32,5376]{1,0:T(8,128)(2,1)S(1)} %pad_maximum_fusion.refs_0_), channel_id=1, source_target_pairs={{0,14},{1,15},{2,0},{3,1},{4,2},{5,3},{6,4},{7,5},{8,6},{9,7},{10,... | collective-permute-start | bytes 1032200 | tf_op jit(solution)/shard_map/ppermute | solution.py:45
  46.1 0.0 collective-permute-done.1.refs_1_
  46.1 1.9 %collective-permute-start.3 = (bf16[32,5376]{1,0:T(8,128)(2,1)S(1)}, bf16[32,5376]{1,0:T(8,128)(2,1)}, u32[]{:S(2)}, u32[]{:S(2)}) collective-permute-start(bf16[32,5376]{1,0:T(8,128)(2,1)S(1)} %collective-permute-done.1.refs_1_), channel_id=1, source_target_pairs={{0,2},{1,3},{2,4},{3,5},{4,6},{5,7},{6,8},{7,9},{8,10},{9,11},{10,... | collective-permute-start | bytes 1032200 | tf_op jit(solution)/shard_map/ppermute | solution.py:45
  48.1 0.0 collective-permute-done.14.refs_9_
  48.1 4.3 %collective-permute-start.18 = (bf16[48,5376]{1,0:T(8,128)(2,1)}, bf16[48,5376]{1,0:T(8,128)(2,1)}, u32[]{:S(2)}, u32[]{:S(2)}) collective-permute-start(bf16[48,5376]{1,0:T(8,128)(2,1)} %collective-permute-done.14.refs_9_), channel_id=1, source_target_pairs={{0,32},{1,97},{2,34},{3,99},{4,36},{5,101},{6,38},{7,103},{8,40},{... | collective-permute-start | bytes 1548296 | tf_op jit(solution)/shard_map/ppermute | solution.py:45
  52.4 1.0 collective-permute-done.2.refs_2_
  53.4 9.7 %collective-permute-start.4 = (bf16[32,5376]{1,0:T(8,128)(2,1)}, bf16[32,5376]{1,0:T(8,128)(2,1)}, u32[]{:S(2)}, u32[]{:S(2)}) collective-permute-start(bf16[32,5376]{1,0:T(8,128)(2,1)} %collective-permute-done.2.refs_2_), channel_id=1, source_target_pairs={{0,14},{1,15},{2,0},{3,1},{4,2},{5,3},{6,4},{7,5},{8,6},{9,7},{10,... | collective-permute-start | bytes 1032200 | tf_op jit(solution)/shard_map/ppermute | solution.py:45
  63.1 0.0 collective-permute-done.3.refs_3_
  63.2 1.9 %collective-permute-start.5 = (bf16[32,5376]{1,0:T(8,128)(2,1)}, bf16[32,5376]{1,0:T(8,128)(2,1)}, u32[]{:S(2)}, u32[]{:S(2)}) collective-permute-start(bf16[32,5376]{1,0:T(8,128)(2,1)} %collective-permute-done.3.refs_3_), channel_id=1, source_target_pairs={{0,2},{1,3},{2,4},{3,5},{4,6},{5,7},{6,8},{7,9},{8,10},{9,11},{10,... | collective-permute-start | bytes 1032200 | tf_op jit(solution)/shard_map/ppermute | solution.py:45
  65.1 6.1 %collective-permute-done.4.refs_4_ = bf16[32,5376]{1,0:T(8,128)(2,1)} collective-permute-done((bf16[32,5376]{1,0:T(8,128)(2,1)}, bf16[32,5376]{1,0:T(8,128)(2,1)}, u32[]{:S(2)}, u32[]{:S(2)}) %collective-permute-start.4) | collective-permute-done | bytes 344096 | tf_op jit(solution)/shard_map/ppermute | solution.py:45
  71.2 2.7 %shard_map.55.refs_0_ = bf16[160,5376]{1,0:T(8,128)(2,1)} custom-call(bf16[32,5376]{1,0:T(8,128)(2,1)} %copy-done.3, bf16[32,5376]{1,0:T(8,128)(2,1)} %copy-done.4, bf16[32,5376]{1,0:T(8,128)(2,1)} %collective-permute-done.2.refs_2_, bf16[32,5376]{1,0:T(8,128)(2,1)} %collective-permute-done.3.refs_3_, bf16[32,5376]{1,0:T(8,128)(2,1)} %collective-permute-done.4.refs_4_), custom_call_target="tpu_custom_call" | custom-call | tf_op jit(solution)/shard_map/pallas_call | solution.py:68
  74.0 2.2 %collective-permute-start.8 = (bf16[160,5376]{1,0:T(8,128)(2,1)}, bf16[160,5376]{1,0:T(8,128)(2,1)}, u32[]{:S(2)}, u32[]{:S(2)}) collective-permute-start(bf16[160,5376]{1,0:T(8,128)(2,1)} %shard_map.55.refs_0_), channel_id=1, source_target_pairs={{0,1},{1,0},{2,3},{3,2},{4,5},{5,4},{6,7},{7,6},{8,9},{9,8},{10,11... | collective-permute-start | bytes 5160968 | tf_op jit(solution)/shard_map/ppermute | solution.py:45
  76.2 3.1 %collective-permute-start.11 = (bf16[48,5376]{1,0:T(8,128)(2,1)S(1)}, bf16[48,5376]{1,0:T(8,128)(2,1)}, u32[]{:S(2)}, u32[]{:S(2)}) collective-permute-start(bf16[48,5376]{1,0:T(8,128)(2,1)S(1)} %collective-permute-done.10.refs_5_), channel_id=1, source_target_pairs={{0,128},{1,129},{2,130},{3,131},{4,132},{5,133},{6,134},{7,135},{8... | collective-permute-start | bytes 1548296 | tf_op jit(solution)/shard_map/ppermute | solution.py:45
  79.3 3.4 %collective-permute-start.12 = (bf16[48,5376]{1,0:T(8,128)(2,1)S(1)}, bf16[48,5376]{1,0:T(8,128)(2,1)}, u32[]{:S(2)}, u32[]{:S(2)}) collective-permute-start(bf16[48,5376]{1,0:T(8,128)(2,1)S(1)} %collective-permute-done.10.refs_5_), channel_id=1, source_target_pairs={{0,384},{1,385},{2,386},{3,387},{4,388},{5,389},{6,390},{7,391},{8... | collective-permute-start | bytes 1548296 | tf_op jit(solution)/shard_map/ppermute | solution.py:45
  82.7 5.3 %collective-permute-start.6 = (bf16[32,5376]{1,0:T(8,128)(2,1)}, bf16[32,5376]{1,0:T(8,128)(2,1)}, u32[]{:S(2)}, u32[]{:S(2)}) collective-permute-start(bf16[32,5376]{1,0:T(8,128)(2,1)} %collective-permute-done.4.refs_4_), channel_id=1, source_target_pairs={{0,14},{1,15},{2,0},{3,1},{4,2},{5,3},{6,4},{7,5},{8,6},{9,7},{10,... | collective-permute-start | bytes 1032200 | tf_op jit(solution)/shard_map/ppermute | solution.py:45
  88.0 1.9 %collective-permute-start.7 = (bf16[32,5376]{1,0:T(8,128)(2,1)}, bf16[32,5376]{1,0:T(8,128)(2,1)}, u32[]{:S(2)}, u32[]{:S(2)}) collective-permute-start(bf16[32,5376]{1,0:T(8,128)(2,1)} %collective-permute-done.5.refs_0_), channel_id=1, source_target_pairs={{0,2},{1,3},{2,4},{3,5},{4,6},{5,7},{6,8},{7,9},{8,10},{9,11},{10,... | collective-permute-start | bytes 1032200 | tf_op jit(solution)/shard_map/ppermute | solution.py:45
  90.0 2.5 %broadcast_in_dim.37 = bf16[4,48,5376]{2,1,0:T(8,128)(2,1)} broadcast(bf16[48,5376]{1,0:T(8,128)(2,1)} %collective-permute-done.18), dimensions={1,2} | broadcast | bytes 2580480 | tf_op jit(solution)/shard_map/broadcast_in_dim | solution.py:49
  92.5 4.4 %all-to-all-start.1 = ((bf16[4,48,5376]{2,1,0:T(8,128)(2,1)}), bf16[4,48,5376]{2,1,0:T(8,128)(2,1)}, u32[]{:S(2)}, u32[]{:S(2)}) async-start(bf16[4,48,5376]{2,1,0:T(8,128)(2,1)} %broadcast_in_dim.37), calls=%async_computation.1 | async-start | bytes 4128768 | tf_op jit(solution)/shard_map/all_to_all | solution.py:50
  96.9 0.0 copy-start.5
  96.9 1.9 %dynamic-slice_bitcast_fusion = bf16[48,5376]{1,0:T(8,128)(2,1)} fusion(bf16[4,48,5376]{2,1,0:T(8,128)(2,1)} %all-to-all-done, s32[]{:T(128)S(6)} %select_n.38), kind=kLoop, calls=%fused_computation.1 | loop fusion | bytes 1032196 | tf_op jit(solution)/shard_map/jit(dynamic_index_in_dim)/squeeze | solution.py:184
  98.8 2.1 %collective-permute-start.13 = (bf16[48,5376]{1,0:T(8,128)(2,1)}, bf16[48,5376]{1,0:T(8,128)(2,1)}, u32[]{:S(2)}, u32[]{:S(2)}) collective-permute-start(bf16[48,5376]{1,0:T(8,128)(2,1)} %dynamic-slice_bitcast_fusion), channel_id=1, source_target_pairs={{0,32},{1,97},{2,34},{3,99},{4,36},{5,101},{6,38},{7,103},{8,40},{... | collective-permute-start | bytes 1548296 | tf_op jit(solution)/shard_map/ppermute | solution.py:45
  100.9 0.0 collective-permute-done.7.refs_2_
  100.9 2.2 %shard_map.56.refs_1_ = bf16[96,5376]{1,0:T(8,128)(2,1)} custom-call(bf16[32,5376]{1,0:T(8,128)(2,1)} %collective-permute-done.5.refs_0_, bf16[32,5376]{1,0:T(8,128)(2,1)} %collective-permute-done.6.refs_1_, bf16[32,5376]{1,0:T(8,128)(2,1)} %collective-permute-done.7.refs_2_), custom_call_target="tpu_custom_call" | custom-call | tf_op jit(solution)/shard_map/pallas_call | solution.py:68
  103.1 2.9 %collective-permute-start.9 = (bf16[96,5376]{1,0:T(8,128)(2,1)}, bf16[96,5376]{1,0:T(8,128)(2,1)}, u32[]{:S(2)}, u32[]{:S(2)}) collective-permute-start(bf16[96,5376]{1,0:T(8,128)(2,1)} %shard_map.56.refs_1_), channel_id=1, source_target_pairs={{0,1},{1,0},{2,3},{3,2},{4,5},{5,4},{6,7},{7,6},{8,9},{9,8},{10,11... | collective-permute-start | bytes 3096584 | tf_op jit(solution)/shard_map/ppermute | solution.py:45
  106.0 3.4 %collective-permute-start.15 = (bf16[48,5376]{1,0:T(8,128)(2,1)}, bf16[48,5376]{1,0:T(8,128)(2,1)}, u32[]{:S(2)}, u32[]{:S(2)}) collective-permute-start(bf16[48,5376]{1,0:T(8,128)(2,1)} %collective-permute-done.14.refs_9_), channel_id=1, source_target_pairs={{0,128},{1,129},{2,130},{3,131},{4,132},{5,133},{6,134},{7,135},{8... | collective-permute-start | bytes 1548296 | tf_op jit(solution)/shard_map/ppermute | solution.py:45
  109.4 3.1 %collective-permute-start.16 = (bf16[48,5376]{1,0:T(8,128)(2,1)}, bf16[48,5376]{1,0:T(8,128)(2,1)}, u32[]{:S(2)}, u32[]{:S(2)}) collective-permute-start(bf16[48,5376]{1,0:T(8,128)(2,1)} %collective-permute-done.14.refs_9_), channel_id=1, source_target_pairs={{0,384},{1,385},{2,386},{3,387},{4,388},{5,389},{6,390},{7,391},{8... | collective-permute-start | bytes 1548296 | tf_op jit(solution)/shard_map/ppermute | solution.py:45
  112.6 2.2 %collective-permute-done.13.refs_8_ = bf16[48,5376]{1,0:T(8,128)(2,1)} collective-permute-done((bf16[48,5376]{1,0:T(8,128)(2,1)}, bf16[48,5376]{1,0:T(8,128)(2,1)}, u32[]{:S(2)}, u32[]{:S(2)}) %collective-permute-start.13) | collective-permute-done | bytes 516128 | tf_op jit(solution)/shard_map/ppermute | solution.py:45
  114.8 3.3 %collective-permute-start.17 = (bf16[48,5376]{1,0:T(8,128)(2,1)}, bf16[48,5376]{1,0:T(8,128)(2,1)}, u32[]{:S(2)}, u32[]{:S(2)}) collective-permute-start(bf16[48,5376]{1,0:T(8,128)(2,1)} %collective-permute-done.13.refs_8_), channel_id=1, source_target_pairs={{0,32},{1,97},{2,34},{3,99},{4,36},{5,101},{6,38},{7,103},{8,40},{... | collective-permute-start | bytes 1548296 | tf_op jit(solution)/shard_map/ppermute | solution.py:45
  118.0 0.1 copy.6.act_ref
  118.2 15.5 %collective-permute-done.15.refs_10_ = bf16[48,5376]{1,0:T(8,128)(2,1)} collective-permute-done((bf16[48,5376]{1,0:T(8,128)(2,1)}, bf16[48,5376]{1,0:T(8,128)(2,1)}, u32[]{:S(2)}, u32[]{:S(2)}) %collective-permute-start.15) | collective-permute-done | bytes 516128 | tf_op jit(solution)/shard_map/ppermute | solution.py:45
  133.8 1.5 copy-done.1
  135.2 1.2 copy-done.2
  136.4 9.0 %product.1 = bf16[512,768]{1,0:T(8,128)(2,1)} custom-call(f32[512,1]{1,0:T(8,128)S(1)} %copy.6.act_ref, bf16[160,5376]{1,0:T(8,128)(2,1)S(1)} %copy-done.1, bf16[96,5376]{1,0:T(8,128)(2,1)S(1)} %copy-done.2, bf16[160,5376]{1,0:T(8,128)(2,1)} %collective-permute-done.8.refs_2_, bf16[96,5376]{1,0:T(8,128)(2,1)} %collective-permute-done.9.refs_3_, ...), custom_call_target="tpu_custom_call" | custom-call | tf_op jit(solution)/shard_map/product/pallas_call | solution.py:148
  (20 shorter events, 0.1 us)
Async XLA Ops:
  0.0 2.8 %copy-start = (bf16[256,5376]{1,0:T(8,128)(2,1)S(1)}, bf16[256,5376]{1,0:T(8,128)(2,1)}, u32[]{:S(2)}) copy-start(bf16[256,5376]{1,0:T(8,128)(2,1)} %param.5) | copy-start | bytes 8257540
  3.5 17.8 %collective-permute-start = (bf16[16,5376]{1,0:T(8,128)(2,1)S(1)}, bf16[16,5376]{1,0:T(8,128)(2,1)}, u32[]{:S(2)}, u32[]{:S(2)}) collective-permute-start(bf16[16,5376]{1,0:T(8,128)(2,1)S(1)} %broadcast_select_fusion), channel_id=1, source_target_pairs={{0,16},{1,17},{2,18},{3,19},{4,20},{5,21},{6,22},{7,23},{8,24},{9,... | collective-permute-start | bytes 516104 | tf_op jit(solution)/shard_map/ppermute | solution.py:45
  11.8 19.6 %collective-permute-start.10 = (bf16[48,5376]{1,0:T(8,128)(2,1)}, bf16[48,5376]{1,0:T(8,128)(2,1)S(1)}, u32[]{:S(2)}, u32[]{:S(2)}) collective-permute-start(bf16[48,5376]{1,0:T(8,128)(2,1)} %param.6), channel_id=1, source_target_pairs={{0,32},{1,97},{2,34},{3,99},{4,36},{5,101},{6,38},{7,103},{8,40},{... | collective-permute-start | bytes 1548296 | tf_op jit(solution)/shard_map/ppermute | solution.py:45
  16.8 73.1 %all-to-all-start = ((bf16[4,48,5376]{2,1,0:T(8,128)(2,1)}), bf16[4,48,5376]{2,1,0:T(8,128)(2,1)}, u32[]{:S(2)}, u32[]{:S(2)}) async-start(bf16[4,48,5376]{2,1,0:T(8,128)(2,1)} %broadcast_in_dim.36), calls=%async_computation | async-start | bytes 4128768 | tf_op jit(solution)/shard_map/all_to_all | solution.py:50
  22.2 25.9 %copy-start.3 = (bf16[32,5376]{1,0:T(8,128)(2,1)}, bf16[32,5376]{1,0:T(8,128)(2,1)S(1)}, u32[]{:S(2)}) copy-start(bf16[32,5376]{1,0:T(8,128)(2,1)S(1)} %pad_maximum_fusion.refs_0_) | copy-start | bytes 1032196
  22.2 23.9 %collective-permute-start.1 = (bf16[32,5376]{1,0:T(8,128)(2,1)S(1)}, bf16[32,5376]{1,0:T(8,128)(2,1)S(1)}, u32[]{:S(2)}, u32[]{:S(2)}) collective-permute-start(bf16[32,5376]{1,0:T(8,128)(2,1)S(1)} %pad_maximum_fusion.refs_0_), channel_id=1, source_target_pairs={{0,2},{1,3},{2,4},{3,5},{4,6},{5,7},{6,8},{7,9},{8,10},{9,11},{10,... | collective-permute-start | bytes 1032200 | tf_op jit(solution)/shard_map/ppermute | solution.py:45
  31.4 16.7 %collective-permute-start.14 = (bf16[48,5376]{1,0:T(8,128)(2,1)S(1)}, bf16[48,5376]{1,0:T(8,128)(2,1)}, u32[]{:S(2)}, u32[]{:S(2)}) collective-permute-start(bf16[48,5376]{1,0:T(8,128)(2,1)S(1)} %collective-permute-done.10.refs_5_), channel_id=1, source_target_pairs={{0,32},{1,97},{2,34},{3,99},{4,36},{5,101},{6,38},{7,103},{8,40},{... | collective-permute-start | bytes 1548296 | tf_op jit(solution)/shard_map/ppermute | solution.py:45
  35.5 18.0 %collective-permute-start.2 = (bf16[32,5376]{1,0:T(8,128)(2,1)S(1)}, bf16[32,5376]{1,0:T(8,128)(2,1)}, u32[]{:S(2)}, u32[]{:S(2)}) collective-permute-start(bf16[32,5376]{1,0:T(8,128)(2,1)S(1)} %pad_maximum_fusion.refs_0_), channel_id=1, source_target_pairs={{0,14},{1,15},{2,0},{3,1},{4,2},{5,3},{6,4},{7,5},{8,6},{9,7},{10,... | collective-permute-start | bytes 1032200 | tf_op jit(solution)/shard_map/ppermute | solution.py:45
  46.1 7.3 %copy-start.4 = (bf16[32,5376]{1,0:T(8,128)(2,1)}, bf16[32,5376]{1,0:T(8,128)(2,1)S(1)}, u32[]{:S(2)}) copy-start(bf16[32,5376]{1,0:T(8,128)(2,1)S(1)} %collective-permute-done.1.refs_1_) | copy-start | bytes 1032196
  46.1 17.0 %collective-permute-start.3 = (bf16[32,5376]{1,0:T(8,128)(2,1)S(1)}, bf16[32,5376]{1,0:T(8,128)(2,1)}, u32[]{:S(2)}, u32[]{:S(2)}) collective-permute-start(bf16[32,5376]{1,0:T(8,128)(2,1)S(1)} %collective-permute-done.1.refs_1_), channel_id=1, source_target_pairs={{0,2},{1,3},{2,4},{3,5},{4,6},{5,7},{6,8},{7,9},{8,10},{9,11},{10,... | collective-permute-start | bytes 1032200 | tf_op jit(solution)/shard_map/ppermute | solution.py:45
  48.1 39.9 %collective-permute-start.18 = (bf16[48,5376]{1,0:T(8,128)(2,1)}, bf16[48,5376]{1,0:T(8,128)(2,1)}, u32[]{:S(2)}, u32[]{:S(2)}) collective-permute-start(bf16[48,5376]{1,0:T(8,128)(2,1)} %collective-permute-done.14.refs_9_), channel_id=1, source_target_pairs={{0,32},{1,97},{2,34},{3,99},{4,36},{5,101},{6,38},{7,103},{8,40},{... | collective-permute-start | bytes 1548296 | tf_op jit(solution)/shard_map/ppermute | solution.py:45
  53.4 17.8 %collective-permute-start.4 = (bf16[32,5376]{1,0:T(8,128)(2,1)}, bf16[32,5376]{1,0:T(8,128)(2,1)}, u32[]{:S(2)}, u32[]{:S(2)}) collective-permute-start(bf16[32,5376]{1,0:T(8,128)(2,1)} %collective-permute-done.2.refs_2_), channel_id=1, source_target_pairs={{0,14},{1,15},{2,0},{3,1},{4,2},{5,3},{6,4},{7,5},{8,6},{9,7},{10,... | collective-permute-start | bytes 1032200 | tf_op jit(solution)/shard_map/ppermute | solution.py:45
  63.2 19.5 %collective-permute-start.5 = (bf16[32,5376]{1,0:T(8,128)(2,1)}, bf16[32,5376]{1,0:T(8,128)(2,1)}, u32[]{:S(2)}, u32[]{:S(2)}) collective-permute-start(bf16[32,5376]{1,0:T(8,128)(2,1)} %collective-permute-done.3.refs_3_), channel_id=1, source_target_pairs={{0,2},{1,3},{2,4},{3,5},{4,6},{5,7},{6,8},{7,9},{8,10},{9,11},{10,... | collective-permute-start | bytes 1032200 | tf_op jit(solution)/shard_map/ppermute | solution.py:45
  74.0 59.8 %collective-permute-start.8 = (bf16[160,5376]{1,0:T(8,128)(2,1)}, bf16[160,5376]{1,0:T(8,128)(2,1)}, u32[]{:S(2)}, u32[]{:S(2)}) collective-permute-start(bf16[160,5376]{1,0:T(8,128)(2,1)} %shard_map.55.refs_0_), channel_id=1, source_target_pairs={{0,1},{1,0},{2,3},{3,2},{4,5},{5,4},{6,7},{7,6},{8,9},{9,8},{10,11... | collective-permute-start | bytes 5160968 | tf_op jit(solution)/shard_map/ppermute | solution.py:45
  76.2 29.9 %collective-permute-start.11 = (bf16[48,5376]{1,0:T(8,128)(2,1)S(1)}, bf16[48,5376]{1,0:T(8,128)(2,1)}, u32[]{:S(2)}, u32[]{:S(2)}) collective-permute-start(bf16[48,5376]{1,0:T(8,128)(2,1)S(1)} %collective-permute-done.10.refs_5_), channel_id=1, source_target_pairs={{0,128},{1,129},{2,130},{3,131},{4,132},{5,133},{6,134},{7,135},{8... | collective-permute-start | bytes 1548296 | tf_op jit(solution)/shard_map/ppermute | solution.py:45
  79.3 30.1 %collective-permute-start.12 = (bf16[48,5376]{1,0:T(8,128)(2,1)S(1)}, bf16[48,5376]{1,0:T(8,128)(2,1)}, u32[]{:S(2)}, u32[]{:S(2)}) collective-permute-start(bf16[48,5376]{1,0:T(8,128)(2,1)S(1)} %collective-permute-done.10.refs_5_), channel_id=1, source_target_pairs={{0,384},{1,385},{2,386},{3,387},{4,388},{5,389},{6,390},{7,391},{8... | collective-permute-start | bytes 1548296 | tf_op jit(solution)/shard_map/ppermute | solution.py:45
  82.7 16.1 %collective-permute-start.6 = (bf16[32,5376]{1,0:T(8,128)(2,1)}, bf16[32,5376]{1,0:T(8,128)(2,1)}, u32[]{:S(2)}, u32[]{:S(2)}) collective-permute-start(bf16[32,5376]{1,0:T(8,128)(2,1)} %collective-permute-done.4.refs_4_), channel_id=1, source_target_pairs={{0,14},{1,15},{2,0},{3,1},{4,2},{5,3},{6,4},{7,5},{8,6},{9,7},{10,... | collective-permute-start | bytes 1032200 | tf_op jit(solution)/shard_map/ppermute | solution.py:45
  88.0 12.9 %collective-permute-start.7 = (bf16[32,5376]{1,0:T(8,128)(2,1)}, bf16[32,5376]{1,0:T(8,128)(2,1)}, u32[]{:S(2)}, u32[]{:S(2)}) collective-permute-start(bf16[32,5376]{1,0:T(8,128)(2,1)} %collective-permute-done.5.refs_0_), channel_id=1, source_target_pairs={{0,2},{1,3},{2,4},{3,5},{4,6},{5,7},{6,8},{7,9},{8,10},{9,11},{10,... | collective-permute-start | bytes 1032200 | tf_op jit(solution)/shard_map/ppermute | solution.py:45
  92.5 41.3 %all-to-all-start.1 = ((bf16[4,48,5376]{2,1,0:T(8,128)(2,1)}), bf16[4,48,5376]{2,1,0:T(8,128)(2,1)}, u32[]{:S(2)}, u32[]{:S(2)}) async-start(bf16[4,48,5376]{2,1,0:T(8,128)(2,1)} %broadcast_in_dim.37), calls=%async_computation.1 | async-start | bytes 4128768 | tf_op jit(solution)/shard_map/all_to_all | solution.py:50
  96.9 21.1 %copy-start.5 = (f32[1,512]{1,0:T(1,128)S(1)}, f32[1,512]{1,0:T(1,128)}, u32[]{:S(2)}) copy-start(f32[1,512]{1,0:T(1,128)} %param.9) | copy-start | bytes 6148
  98.8 16.0 %collective-permute-start.13 = (bf16[48,5376]{1,0:T(8,128)(2,1)}, bf16[48,5376]{1,0:T(8,128)(2,1)}, u32[]{:S(2)}, u32[]{:S(2)}) collective-permute-start(bf16[48,5376]{1,0:T(8,128)(2,1)} %dynamic-slice_bitcast_fusion), channel_id=1, source_target_pairs={{0,32},{1,97},{2,34},{3,99},{4,36},{5,101},{6,38},{7,103},{8,40},{... | collective-permute-start | bytes 1548296 | tf_op jit(solution)/shard_map/ppermute | solution.py:45
  103.1 30.6 %collective-permute-start.9 = (bf16[96,5376]{1,0:T(8,128)(2,1)}, bf16[96,5376]{1,0:T(8,128)(2,1)}, u32[]{:S(2)}, u32[]{:S(2)}) collective-permute-start(bf16[96,5376]{1,0:T(8,128)(2,1)} %shard_map.56.refs_1_), channel_id=1, source_target_pairs={{0,1},{1,0},{2,3},{3,2},{4,5},{5,4},{6,7},{7,6},{8,9},{9,8},{10,11... | collective-permute-start | bytes 3096584 | tf_op jit(solution)/shard_map/ppermute | solution.py:45
  106.0 27.7 %collective-permute-start.15 = (bf16[48,5376]{1,0:T(8,128)(2,1)}, bf16[48,5376]{1,0:T(8,128)(2,1)}, u32[]{:S(2)}, u32[]{:S(2)}) collective-permute-start(bf16[48,5376]{1,0:T(8,128)(2,1)} %collective-permute-done.14.refs_9_), channel_id=1, source_target_pairs={{0,128},{1,129},{2,130},{3,131},{4,132},{5,133},{6,134},{7,135},{8... | collective-permute-start | bytes 1548296 | tf_op jit(solution)/shard_map/ppermute | solution.py:45
  109.4 24.3 %collective-permute-start.16 = (bf16[48,5376]{1,0:T(8,128)(2,1)}, bf16[48,5376]{1,0:T(8,128)(2,1)}, u32[]{:S(2)}, u32[]{:S(2)}) collective-permute-start(bf16[48,5376]{1,0:T(8,128)(2,1)} %collective-permute-done.14.refs_9_), channel_id=1, source_target_pairs={{0,384},{1,385},{2,386},{3,387},{4,388},{5,389},{6,390},{7,391},{8... | collective-permute-start | bytes 1548296 | tf_op jit(solution)/shard_map/ppermute | solution.py:45
  114.8 19.0 %collective-permute-start.17 = (bf16[48,5376]{1,0:T(8,128)(2,1)}, bf16[48,5376]{1,0:T(8,128)(2,1)}, u32[]{:S(2)}, u32[]{:S(2)}) collective-permute-start(bf16[48,5376]{1,0:T(8,128)(2,1)} %collective-permute-done.13.refs_8_), channel_id=1, source_target_pairs={{0,32},{1,97},{2,34},{3,99},{4,36},{5,101},{6,38},{7,103},{8,40},{... | collective-permute-start | bytes 1548296 | tf_op jit(solution)/shard_map/ppermute | solution.py:45
  133.8 1.5 %copy-start.1 = (bf16[160,5376]{1,0:T(8,128)(2,1)S(1)}, bf16[160,5376]{1,0:T(8,128)(2,1)}, u32[]{:S(2)}) copy-start(bf16[160,5376]{1,0:T(8,128)(2,1)} %shard_map.55.refs_0_) | copy-start | bytes 5160964
  135.2 1.2 copy-start.2

commit v7 on v6

--- a/solution.py
+++ b/solution.py
@@ -37,40 +37,67 @@
 ROWS_X = [[x * 4 + y for x in range(4)] for y in range(4)]
 
 HOPS_Z = (0, -1, 1, -2, 2, -3, 3, -4)
-HOPS_X = (0, -1, 1, 2)
-PARTS = 3
+ALL_X = tuple((None, x) for x in range(4))
+BLOCKS = (
+    *((0, *at) for at in ALL_X),
+    *((step, hop, None) for hop in (0, -1, 1, 2) for step in (1, 2)),
+    *((3, *at) for at in ALL_X),
+)
+PARTS = 7
 
 
 def send(value, pairs):
     return lax.ppermute(value, AXES, pairs)
 
 
-def share(value):
-    copies = jnp.broadcast_to(value[None], (4,) + value.shape)
-    return lax.all_to_all(copies, "prompt", 0, 0, axis_index_groups=ROWS_X, tiled=True)
-
-
-def stack_kernel(*refs):
-    operands, (out_ref, sem) = refs[:-2], refs[-2:]
-    copies, at = [], 0
-    for i, operand in enumerate(operands):
-        size = operand.shape[0]
-        copies.append(pltpu.make_async_copy(operand, out_ref.at[pl.ds(at, size)], sem.at[i]))
-        at += size
+def spread_kernel(value_ref, out_ref, held, sem):
+    copy = pltpu.make_async_copy(value_ref, held, sem.at[4])
+    copy.start()
+    copy.wait()
+    copies = [pltpu.make_async_copy(held, out_ref.at[i], sem.at[i]) for i in range(4)]
     for copy in copies:
         copy.start()
     for copy in copies:
         copy.wait()
 
 
+def share(value):
+    copies = pl.pallas_call(
+        spread_kernel,
+        out_shape=jax.ShapeDtypeStruct((4,) + value.shape, value.dtype),
+        in_specs=[pl.BlockSpec(memory_space=pl.ANY)],
+        out_specs=pl.BlockSpec(memory_space=pl.ANY),
+        scratch_shapes=[pltpu.VMEM(value.shape, value.dtype), pltpu.SemaphoreType.DMA((5,))],
+        name="spread",
+    )(value)
+    return lax.all_to_all(copies, "prompt", 0, 0, axis_index_groups=ROWS_X, tiled=True)
+
+
+def stack_kernel(*refs):
+    operands, (out_ref, held, sem) = refs[:-3], refs[-3:]
+    inward, outward, at = [], [], 0
+    for i, operand in enumerate(operands):
+        lines = pl.ds(at, operand.shape[0])
+        inward.append(pltpu.make_async_copy(operand, held.at[lines], sem.at[0, i]))
+        outward.append(pltpu.make_async_copy(held.at[lines], out_ref.at[lines], sem.at[1, i]))
+        at += operand.shape[0]
+    for copy in inward:
+        copy.start()
+    for copy, onward in zip(inward, outward):
+        copy.wait()
+        onward.start()
+    for copy in outward:
+        copy.wait()
+
+
 def stack(*pieces):
-    n_rows = sum(piece.shape[0] for piece in pieces)
+    shape = (sum(piece.shape[0] for piece in pieces), pieces[0].shape[1])
     return pl.pallas_call(
         stack_kernel,
-        out_shape=jax.ShapeDtypeStruct((n_rows, pieces[0].shape[1]), pieces[0].dtype),
+        out_shape=jax.ShapeDtypeStruct(shape, pieces[0].dtype),
         in_specs=[pl.BlockSpec(memory_space=pl.ANY)] * len(pieces),
-        out_specs=pl.BlockSpec(memory_space=pltpu.VMEM),
-        scratch_shapes=[pltpu.SemaphoreType.DMA((len(pieces),))],
+        out_specs=pl.BlockSpec(memory_space=pl.ANY),
+        scratch_shapes=[pltpu.VMEM(shape, pieces[0].dtype), pltpu.SemaphoreType.DMA((2, len(pieces)))],
     )(*pieces)
 
 
@@ -118,9 +145,8 @@
     block = out_ref.shape[1] // 16
     lane = lax.broadcasted_iota(jnp.int32, (block, out_ref.shape[1]), 1)
     line = lax.broadcasted_iota(jnp.int32, (block, out_ref.shape[1]), 0)
-    for i in range(16):
-        step_y, step_x = divmod(i, 4)
-        x_from = step_x if step_y in (0, 3) else (x + HOPS_X[step_x]) & 3
+    for i, (step_y, hop, x_there) in enumerate(BLOCKS):
+        x_from = x_there if hop is None else (x + hop) & 3
         origin = x_from * 4 + ((y - (1 - 2 * core) * step_y) & 3)
         order[i * block : (i + 1) * block] = jnp.where(lane == line + origin * block, 1.0, 0.0).astype(jnp.bfloat16)
 
@@ -179,8 +205,8 @@
     y3 = send(y2, RING_Y)
     width = y0.shape[0]
     aa, dd = share(y0), share(y3)
-    b1, b2 = send(y1, UP_X), send(y1, DOWN_X)
-    c1, c2 = send(y2, UP_X), send(y2, DOWN_X)
+    both = jnp.concatenate([y1, y2], axis=0)
+    m1, m2 = send(both, UP_X), send(both, DOWN_X)
     far = lax.dynamic_index_in_dim(aa, (lax.axis_index("prompt") // 4 + 2) % 4, 0, keepdims=False)
     f1 = send(far, RING_Y)
     f2 = send(f1, RING_Y)
@@ -193,9 +219,9 @@
     u4 = send(u3, UP_Z)
     near = stack(own, u1, w1, u2, w2)
     away = stack(u3, w3, u4)
-    sources = [near, away, send(near, CORE), send(away, CORE)]
-
-    targets = [aa.reshape(4 * width, -1), y1, b1, b2, f1, y2, c1, c2, f2, dd.reshape(4 * width, -1)]
+    sources = [own, u1, w1, u2, w2, u3, w3, u4, send(near, CORE), send(away, CORE)]
+
+    targets = [aa.reshape(4 * width, -1), y1, y2, m1, m2, f1, f2, dd.reshape(4 * width, -1)]
     return product(activity.reshape(-1, 1), sources, targets)[None]
 
 

time: 147 us -> 151 us (1.027)
  starting transfers between devices: 86.9 us -> 81.4 us
  Pallas kernels: 13.9 us -> 19.3 us
  waiting for transfers between devices: 30.1 us -> 35.2 us
    ppermute x19 -> x17, starting transfers between devices: 78 us -> 72.1 us  [send(): return lax.ppermute(value, AXES, pairs)]
    broadcast_in_dim x2 -> x0, local copies, waits for them, and re-layouts: 4.99 us -> none  [share(): copies = jnp.broadcast_to(value[None], (4,) + value.shape)]
    pallas_call x2 -> x4, Pallas kernels: 4.91 us -> 9.07 us  [the longest x2 4.79 us: share(): pl.pallas_call(spread_kernel, out_shape=jax.ShapeDtypeStruct((4,) + value...]
    unnamed x12 -> x27, local copies, waits for them, and re-layouts: 2.69 us -> 6.52 us
    all_to_all x2, waiting for transfers between devices: 0.01 us -> 3.34 us  [share(): lax.all_to_all(copies, 'prompt', 0, 0, axis_index_groups=ROWS_X, tiled=True)]
    concatenate x0 -> x1, local copies, waits for them, and re-layouts: none -> 1.88 us  [edges_of(): both = jnp.concatenate([y1, y2], axis=0)]
    ppermute x19 -> x17, waiting for transfers between devices: 30.1 us -> 31.9 us  [send(): return lax.ppermute(value, AXES, pairs)]
  transfers between devices with their start and end apart: 21 -> 19, of which waited for: 5 -> 6; matrix products, arithmetic and copies ran while one was open for 5% -> 4% of each run, Pallas kernels for 3% -> 6%
where the time goes in v7:
time: 151 us; the launch traced here: 150 us
  starting transfers between devices  81.4 us (54%)
  waiting for transfers between devices  35.2 us (23%)
  Pallas kernels  19.3 us (13%)
  local copies, waits for them, and re-layouts  11 us (7%)
  other arithmetic  2.87 us (2%)
    ppermute x17, starting transfers between devices, send(): return lax.ppermute(value, AXES, pairs)  72.1 us
    ppermute x17, waiting for transfers between devices, send(): return lax.ppermute(value, AXES, pairs)  31.9 us
    pallas_call x1, Pallas kernels, product(): pl.pallas_call(functools.partial(product_kernel, len(sources)), out_shape...  10.3 us
    all_to_all x2, starting transfers between devices, share(): lax.all_to_all(copies, 'prompt', 0, 0, axis_index_groups=ROWS_X, tiled=True)  9.3 us
    unnamed x27, local copies, waits for them, and re-layouts  6.52 us
    pallas_call x2, Pallas kernels, share(): pl.pallas_call(spread_kernel, out_shape=jax.ShapeDtypeStruct((4,) + value...  4.79 us
    pallas_call x2, Pallas kernels, stack(): pl.pallas_call(stack_kernel, out_shape=jax.ShapeDtypeStruct(shape, pieces...  4.28 us
    all_to_all x2, waiting for transfers between devices, share(): lax.all_to_all(copies, 'prompt', 0, 0, axis_index_groups=ROWS_X, tiled=True)  3.34 us
  transfers between devices with their start and end apart: 19, of which 6 were waited for; matrix products, arithmetic and copies ran while one was open for 4% of the time, Pallas kernels for 6%

profile of v7, /device:TPU:1, one launch (start us, length us, event | category | flops | bytes accessed | tf_op | source)
XLA Modules:
  0.0 150.2 jit_solution(17520522401743350326)
XLA Ops:
  0.0 1.4 fusion
  1.4 0.6 iota_compare_fusion
  2.1 0.7 fusion.1
  2.8 0.7 gather_fusion
  3.4 0.1 broadcast_select_fusion
  3.5 8.3 %collective-permute-start = (bf16[16,5376]{1,0:T(8,128)(2,1)S(1)}, bf16[16,5376]{1,0:T(8,128)(2,1)S(1)}, u32[]{:S(2)}, u32[]{:S(2)}) collective-permute-start(bf16[16,5376]{1,0:T(8,128)(2,1)S(1)} %broadcast_select_fusion), channel_id=1, source_target_pairs={{0,16},{1,17},{2,18},{3,19},{4,20},{5,21},{6,22},{7,23},{8,24},{9,... | collective-permute-start | bytes 516104 | tf_op jit(solution)/shard_map/ppermute | solution.py:50
  11.8 6.8 %collective-permute-done = bf16[16,5376]{1,0:T(8,128)(2,1)S(1)} collective-permute-done((bf16[16,5376]{1,0:T(8,128)(2,1)S(1)}, bf16[16,5376]{1,0:T(8,128)(2,1)S(1)}, u32[]{:S(2)}, u32[]{:S(2)}) %collective-permute-start) | collective-permute-done | bytes 172064 | tf_op jit(solution)/shard_map/ppermute | solution.py:50
  18.6 0.0 copy-start.1
  18.6 1.9 %collective-permute-start.1 = (bf16[32,5376]{1,0:T(8,128)(2,1)S(1)}, bf16[32,5376]{1,0:T(8,128)(2,1)S(1)}, u32[]{:S(2)}, u32[]{:S(2)}) collective-permute-start(bf16[32,5376]{1,0:T(8,128)(2,1)S(1)} %pad_maximum_fusion.refs_0_), channel_id=1, source_target_pairs={{0,2},{1,3},{2,4},{3,5},{4,6},{5,7},{6,8},{7,9},{8,10},{9,11},{10,... | collective-permute-start | bytes 1032200 | tf_op jit(solution)/shard_map/ppermute | solution.py:50
  20.6 5.2 %collective-permute-start.10 = (bf16[48,5376]{1,0:T(8,128)(2,1)}, bf16[48,5376]{1,0:T(8,128)(2,1)}, u32[]{:S(2)}, u32[]{:S(2)}) collective-permute-start(bf16[48,5376]{1,0:T(8,128)(2,1)} %value_ref.1), channel_id=1, source_target_pairs={{0,32},{1,97},{2,34},{3,99},{4,36},{5,101},{6,38},{7,103},{8,40},{... | collective-permute-start | bytes 1548296 | tf_op jit(solution)/shard_map/ppermute | solution.py:50
  25.8 8.6 %collective-permute-start.2 = (bf16[32,5376]{1,0:T(8,128)(2,1)S(1)}, bf16[32,5376]{1,0:T(8,128)(2,1)}, u32[]{:S(2)}, u32[]{:S(2)}) collective-permute-start(bf16[32,5376]{1,0:T(8,128)(2,1)S(1)} %pad_maximum_fusion.refs_0_), channel_id=1, source_target_pairs={{0,14},{1,15},{2,0},{3,1},{4,2},{5,3},{6,4},{7,5},{8,6},{9,7},{10,... | collective-permute-start | bytes 1032200 | tf_op jit(solution)/shard_map/ppermute | solution.py:50
  34.4 1.9 %collective-permute-start.3 = (bf16[32,5376]{1,0:T(8,128)(2,1)S(1)}, bf16[32,5376]{1,0:T(8,128)(2,1)}, u32[]{:S(2)}, u32[]{:S(2)}) collective-permute-start(bf16[32,5376]{1,0:T(8,128)(2,1)S(1)} %collective-permute-done.1.refs_1_), channel_id=1, source_target_pairs={{0,2},{1,3},{2,4},{3,5},{4,6},{5,7},{6,8},{7,9},{8,10},{9,11},{10,... | collective-permute-start | bytes 1032200 | tf_op jit(solution)/shard_map/ppermute | solution.py:50
  36.3 2.4 %spread.2 = bf16[4,48,5376]{2,1,0:T(8,128)(2,1)} custom-call(bf16[48,5376]{1,0:T(8,128)(2,1)} %value_ref.1), custom_call_target="tpu_custom_call" | custom-call | tf_op jit(solution)/shard_map/spread/pallas_call | solution.py:65
  38.7 4.5 %all-to-all-start = ((bf16[4,48,5376]{2,1,0:T(8,128)(2,1)}), bf16[4,48,5376]{2,1,0:T(8,128)(2,1)}, u32[]{:S(2)}, u32[]{:S(2)}) async-start(bf16[4,48,5376]{2,1,0:T(8,128)(2,1)} %spread.2), calls=%async_computation | async-start | bytes 4128768 | tf_op jit(solution)/shard_map/all_to_all | solution.py:73
  43.3 5.7 %collective-permute-start.11 = (bf16[48,5376]{1,0:T(8,128)(2,1)}, bf16[48,5376]{1,0:T(8,128)(2,1)}, u32[]{:S(2)}, u32[]{:S(2)}) collective-permute-start(bf16[48,5376]{1,0:T(8,128)(2,1)} %collective-permute-done.10.refs_11_), channel_id=1, source_target_pairs={{0,32},{1,97},{2,34},{3,99},{4,36},{5,101},{6,38},{7,103},{8,40},{... | collective-permute-start | bytes 1548296 | tf_op jit(solution)/shard_map/ppermute | solution.py:50
  48.9 0.0 collective-permute-done.2.refs_2_
  48.9 4.6 %collective-permute-start.4 = (bf16[32,5376]{1,0:T(8,128)(2,1)}, bf16[32,5376]{1,0:T(8,128)(2,1)S(1)}, u32[]{:S(2)}, u32[]{:S(2)}) collective-permute-start(bf16[32,5376]{1,0:T(8,128)(2,1)} %collective-permute-done.2.refs_2_), channel_id=1, source_target_pairs={{0,14},{1,15},{2,0},{3,1},{4,2},{5,3},{6,4},{7,5},{8,6},{9,7},{10,... | collective-permute-start | bytes 1032200 | tf_op jit(solution)/shard_map/ppermute | solution.py:50
  53.5 1.9 %collective-permute-start.5 = (bf16[32,5376]{1,0:T(8,128)(2,1)}, bf16[32,5376]{1,0:T(8,128)(2,1)S(1)}, u32[]{:S(2)}, u32[]{:S(2)}) collective-permute-start(bf16[32,5376]{1,0:T(8,128)(2,1)} %collective-permute-done.3.refs_3_), channel_id=1, source_target_pairs={{0,2},{1,3},{2,4},{3,5},{4,6},{5,7},{6,8},{7,9},{8,10},{9,11},{10,... | collective-permute-start | bytes 1032200 | tf_op jit(solution)/shard_map/ppermute | solution.py:50
  55.5 1.8 %constant_dynamic-update-slice_fusion.1 = bf16[96,5376]{1,0:T(8,128)(2,1)} fusion(bf16[48,5376]{1,0:T(8,128)(2,1)} %collective-permute-done.10.refs_11_), kind=kLoop, calls=%fused_computation.6 | loop fusion | bytes 1032192
  57.3 2.5 %collective-permute-done.4.refs_4_ = bf16[32,5376]{1,0:T(8,128)(2,1)S(1)} collective-permute-done((bf16[32,5376]{1,0:T(8,128)(2,1)}, bf16[32,5376]{1,0:T(8,128)(2,1)S(1)}, u32[]{:S(2)}, u32[]{:S(2)}) %collective-permute-start.4) | collective-permute-done | bytes 344096 | tf_op jit(solution)/shard_map/ppermute | solution.py:50
  59.8 0.7 copy-done.5
  60.5 2.3 %shard_map.55 = bf16[160,5376]{1,0:T(8,128)(2,1)} custom-call(bf16[32,5376]{1,0:T(8,128)(2,1)} %copy-done.1, bf16[32,5376]{1,0:T(8,128)(2,1)} %copy-done.3, bf16[32,5376]{1,0:T(8,128)(2,1)} %collective-permute-done.2.refs_2_, bf16[32,5376]{1,0:T(8,128)(2,1)} %collective-permute-done.3.refs_3_, bf16[32,5376]{1,0:T(8,128)(2,1)} %copy-done.5), custom_call_target="tpu_custom_call" | custom-call | tf_op jit(solution)/shard_map/pallas_call | solution.py:95
  62.8 4.2 %collective-permute-start.8 = (bf16[160,5376]{1,0:T(8,128)(2,1)}, bf16[160,5376]{1,0:T(8,128)(2,1)}, u32[]{:S(2)}, u32[]{:S(2)}) collective-permute-start(bf16[160,5376]{1,0:T(8,128)(2,1)} %shard_map.55), channel_id=1, source_target_pairs={{0,1},{1,0},{2,3},{3,2},{4,5},{5,4},{6,7},{7,6},{8,9},{9,8},{10,11... | collective-permute-start | bytes 5160968 | tf_op jit(solution)/shard_map/ppermute | solution.py:50
  67.1 5.2 %collective-permute-start.6 = (bf16[32,5376]{1,0:T(8,128)(2,1)}, bf16[32,5376]{1,0:T(8,128)(2,1)S(1)}, u32[]{:S(2)}, u32[]{:S(2)}) collective-permute-start(bf16[32,5376]{1,0:T(8,128)(2,1)} %copy-done.5), channel_id=1, source_target_pairs={{0,14},{1,15},{2,0},{3,1},{4,2},{5,3},{6,4},{7,5},{8,6},{9,7},{10,... | collective-permute-start | bytes 1032200 | tf_op jit(solution)/shard_map/ppermute | solution.py:50
  72.3 5.2 %collective-permute-start.16 = (bf16[48,5376]{1,0:T(8,128)(2,1)}, bf16[48,5376]{1,0:T(8,128)(2,1)}, u32[]{:S(2)}, u32[]{:S(2)}) collective-permute-start(bf16[48,5376]{1,0:T(8,128)(2,1)} %collective-permute-done.11.refs_12_), channel_id=1, source_target_pairs={{0,32},{1,97},{2,34},{3,99},{4,36},{5,101},{6,38},{7,103},{8,40},{... | collective-permute-start | bytes 1548296 | tf_op jit(solution)/shard_map/ppermute | solution.py:50
  77.5 1.9 %collective-permute-start.7 = (bf16[32,5376]{1,0:T(8,128)(2,1)S(1)}, bf16[32,5376]{1,0:T(8,128)(2,1)}, u32[]{:S(2)}, u32[]{:S(2)}) collective-permute-start(bf16[32,5376]{1,0:T(8,128)(2,1)S(1)} %collective-permute-done.5.refs_0_.refs_5_), channel_id=1, source_target_pairs={{0,2},{1,3},{2,4},{3,5},{4,6},{5,7},{6,8},{7,9},{8,10},{9,11},{10,... | collective-permute-start | bytes 1032200 | tf_op jit(solution)/shard_map/ppermute | solution.py:50
  79.4 1.9 %constant_dynamic-update-slice_fusion = bf16[96,5376]{1,0:T(8,128)(2,1)} fusion(bf16[96,5376]{1,0:T(8,128)(2,1)} %constant_dynamic-update-slice_fusion.1, bf16[48,5376]{1,0:T(8,128)(2,1)} %collective-permute-done.11.refs_12_), kind=kLoop, calls=%fused_computation.5 | loop fusion | bytes 1032192 | tf_op jit(solution)/shard_map/concatenate | solution.py:208
  81.3 4.4 %collective-permute-start.13 = (bf16[96,5376]{1,0:T(8,128)(2,1)}, bf16[96,5376]{1,0:T(8,128)(2,1)}, u32[]{:S(2)}, u32[]{:S(2)}) collective-permute-start(bf16[96,5376]{1,0:T(8,128)(2,1)} %constant_dynamic-update-slice_fusion), channel_id=1, source_target_pairs={{0,384},{1,385},{2,386},{3,387},{4,388},{5,389},{6,390},{7,391},{8... | collective-permute-start | bytes 3096584 | tf_op jit(solution)/shard_map/ppermute | solution.py:50
  85.7 1.9 %collective-permute-start.12 = (bf16[96,5376]{1,0:T(8,128)(2,1)}, bf16[96,5376]{1,0:T(8,128)(2,1)}, u32[]{:S(2)}, u32[]{:S(2)}) collective-permute-start(bf16[96,5376]{1,0:T(8,128)(2,1)} %constant_dynamic-update-slice_fusion), channel_id=1, source_target_pairs={{0,128},{1,129},{2,130},{3,131},{4,132},{5,133},{6,134},{7,135},{8... | collective-permute-start | bytes 3096584 | tf_op jit(solution)/shard_map/ppermute | solution.py:50
  87.6 2.5 %collective-permute-done.7.refs_2_.refs_7_ = bf16[32,5376]{1,0:T(8,128)(2,1)} collective-permute-done((bf16[32,5376]{1,0:T(8,128)(2,1)S(1)}, bf16[32,5376]{1,0:T(8,128)(2,1)}, u32[]{:S(2)}, u32[]{:S(2)}) %collective-permute-start.7) | collective-permute-done | bytes 344096 | tf_op jit(solution)/shard_map/ppermute | solution.py:50
  90.1 2.0 %shard_map.56 = bf16[96,5376]{1,0:T(8,128)(2,1)} custom-call(bf16[32,5376]{1,0:T(8,128)(2,1)} %copy-done.7, bf16[32,5376]{1,0:T(8,128)(2,1)} %copy-done.9, bf16[32,5376]{1,0:T(8,128)(2,1)} %collective-permute-done.7.refs_2_.refs_7_), custom_call_target="tpu_custom_call" | custom-call | tf_op jit(solution)/shard_map/pallas_call | solution.py:95
  92.1 1.9 %collective-permute-start.9 = (bf16[96,5376]{1,0:T(8,128)(2,1)}, bf16[96,5376]{1,0:T(8,128)(2,1)}, u32[]{:S(2)}, u32[]{:S(2)}) collective-permute-start(bf16[96,5376]{1,0:T(8,128)(2,1)} %shard_map.56), channel_id=1, source_target_pairs={{0,1},{1,0},{2,3},{3,2},{4,5},{5,4},{6,7},{7,6},{8,9},{9,8},{10,11... | collective-permute-start | bytes 3096584 | tf_op jit(solution)/shard_map/ppermute | solution.py:50
  94.0 2.4 %spread.3 = bf16[4,48,5376]{2,1,0:T(8,128)(2,1)} custom-call(bf16[48,5376]{1,0:T(8,128)(2,1)} %collective-permute-done.16.value_ref), custom_call_target="tpu_custom_call" | custom-call | tf_op jit(solution)/shard_map/spread/pallas_call | solution.py:65
  96.5 0.0 copy-start.12
  96.5 0.0 copy-start.2
  96.5 4.8 %all-to-all-start.1 = ((bf16[4,48,5376]{2,1,0:T(8,128)(2,1)}), bf16[4,48,5376]{2,1,0:T(8,128)(2,1)}, u32[]{:S(2)}, u32[]{:S(2)}) async-start(bf16[4,48,5376]{2,1,0:T(8,128)(2,1)} %spread.3), calls=%async_computation.1 | async-start | bytes 4128768 | tf_op jit(solution)/shard_map/all_to_all | solution.py:73
  101.4 1.1 dynamic-slice_bitcast_fusion
  102.4 3.5 %collective-permute-start.14 = (bf16[48,5376]{1,0:T(8,128)(2,1)S(1)}, bf16[48,5376]{1,0:T(8,128)(2,1)}, u32[]{:S(2)}, u32[]{:S(2)}) collective-permute-start(bf16[48,5376]{1,0:T(8,128)(2,1)S(1)} %dynamic-slice_bitcast_fusion), channel_id=1, source_target_pairs={{0,32},{1,97},{2,34},{3,99},{4,36},{5,101},{6,38},{7,103},{8,40},{... | collective-permute-start | bytes 1548296 | tf_op jit(solution)/shard_map/ppermute | solution.py:50
  106.0 10.6 %collective-permute-done.14.refs_15_ = bf16[48,5376]{1,0:T(8,128)(2,1)} collective-permute-done((bf16[48,5376]{1,0:T(8,128)(2,1)S(1)}, bf16[48,5376]{1,0:T(8,128)(2,1)}, u32[]{:S(2)}, u32[]{:S(2)}) %collective-permute-start.14) | collective-permute-done | bytes 516128 | tf_op jit(solution)/shard_map/ppermute | solution.py:50
  116.6 5.7 %collective-permute-start.15 = (bf16[48,5376]{1,0:T(8,128)(2,1)}, bf16[48,5376]{1,0:T(8,128)(2,1)}, u32[]{:S(2)}, u32[]{:S(2)}) collective-permute-start(bf16[48,5376]{1,0:T(8,128)(2,1)} %collective-permute-done.14.refs_15_), channel_id=1, source_target_pairs={{0,32},{1,97},{2,34},{3,99},{4,36},{5,101},{6,38},{7,103},{8,40},{... | collective-permute-start | bytes 1548296 | tf_op jit(solution)/shard_map/ppermute | solution.py:50
  122.3 0.9 copy.6.act_ref
  123.2 9.5 %collective-permute-done.15.refs_16_ = bf16[48,5376]{1,0:T(8,128)(2,1)} collective-permute-done((bf16[48,5376]{1,0:T(8,128)(2,1)}, bf16[48,5376]{1,0:T(8,128)(2,1)}, u32[]{:S(2)}, u32[]{:S(2)}) %collective-permute-start.15) | collective-permute-done | bytes 516128 | tf_op jit(solution)/shard_map/ppermute | solution.py:50
  132.7 3.3 %all-to-all-done.1 = bf16[4,48,5376]{2,1,0:T(8,128)(2,1)} async-done(((bf16[4,48,5376]{2,1,0:T(8,128)(2,1)}), bf16[4,48,5376]{2,1,0:T(8,128)(2,1)}, u32[]{:S(2)}, u32[]{:S(2)}) %all-to-all-start.1) | async-done | bytes 2064416 | tf_op jit(solution)/shard_map/all_to_all | solution.py:73
  136.1 1.0 copy-done.6
  137.0 1.0 copy-done.8
  138.0 1.0 copy-done.10
  139.0 0.9 copy-done.11
  139.9 10.3 %product.1 = bf16[512,768]{1,0:T(8,128)(2,1)} custom-call(f32[512,1]{1,0:T(8,128)S(1)} %copy-done.11, bf16[32,5376]{1,0:T(8,128)(2,1)S(1)} %copy-done.2, bf16[32,5376]{1,0:T(8,128)(2,1)S(1)} %copy-done.4, bf16[32,5376]{1,0:T(8,128)(2,1)} %collective-permute-done.2.refs_2_, bf16[32,5376]{1,0:T(8,128)(2,1)} %collective-permute-done.3.refs_3_, ...), custom_call_target="tpu_custom_call" | custom-call | tf_op jit(solution)/shard_map/product/pallas_call | solution.py:174
  (32 shorter events, 0.1 us)
Async XLA Ops:
  0.0 2.8 %copy-start = (bf16[256,5376]{1,0:T(8,128)(2,1)S(1)}, bf16[256,5376]{1,0:T(8,128)(2,1)}, u32[]{:S(2)}) copy-start(bf16[256,5376]{1,0:T(8,128)(2,1)} %param.5) | copy-start | bytes 8257540
  3.5 15.1 %collective-permute-start = (bf16[16,5376]{1,0:T(8,128)(2,1)S(1)}, bf16[16,5376]{1,0:T(8,128)(2,1)S(1)}, u32[]{:S(2)}, u32[]{:S(2)}) collective-permute-start(bf16[16,5376]{1,0:T(8,128)(2,1)S(1)} %broadcast_select_fusion), channel_id=1, source_target_pairs={{0,16},{1,17},{2,18},{3,19},{4,20},{5,21},{6,22},{7,23},{8,24},{9,... | collective-permute-start | bytes 516104 | tf_op jit(solution)/shard_map/ppermute | solution.py:50
  18.6 20.1 %copy-start.1 = (bf16[32,5376]{1,0:T(8,128)(2,1)}, bf16[32,5376]{1,0:T(8,128)(2,1)S(1)}, u32[]{:S(2)}) copy-start(bf16[32,5376]{1,0:T(8,128)(2,1)S(1)} %pad_maximum_fusion.refs_0_) | copy-start | bytes 1032196
  18.6 15.8 %collective-permute-start.1 = (bf16[32,5376]{1,0:T(8,128)(2,1)S(1)}, bf16[32,5376]{1,0:T(8,128)(2,1)S(1)}, u32[]{:S(2)}, u32[]{:S(2)}) collective-permute-start(bf16[32,5376]{1,0:T(8,128)(2,1)S(1)} %pad_maximum_fusion.refs_0_), channel_id=1, source_target_pairs={{0,2},{1,3},{2,4},{3,5},{4,6},{5,7},{6,8},{7,9},{8,10},{9,11},{10,... | collective-permute-start | bytes 1032200 | tf_op jit(solution)/shard_map/ppermute | solution.py:50
  20.6 22.7 %collective-permute-start.10 = (bf16[48,5376]{1,0:T(8,128)(2,1)}, bf16[48,5376]{1,0:T(8,128)(2,1)}, u32[]{:S(2)}, u32[]{:S(2)}) collective-permute-start(bf16[48,5376]{1,0:T(8,128)(2,1)} %value_ref.1), channel_id=1, source_target_pairs={{0,32},{1,97},{2,34},{3,99},{4,36},{5,101},{6,38},{7,103},{8,40},{... | collective-permute-start | bytes 1548296 | tf_op jit(solution)/shard_map/ppermute | solution.py:50
  25.8 23.1 %collective-permute-start.2 = (bf16[32,5376]{1,0:T(8,128)(2,1)S(1)}, bf16[32,5376]{1,0:T(8,128)(2,1)}, u32[]{:S(2)}, u32[]{:S(2)}) collective-permute-start(bf16[32,5376]{1,0:T(8,128)(2,1)S(1)} %pad_maximum_fusion.refs_0_), channel_id=1, source_target_pairs={{0,14},{1,15},{2,0},{3,1},{4,2},{5,3},{6,4},{7,5},{8,6},{9,7},{10,... | collective-permute-start | bytes 1032200 | tf_op jit(solution)/shard_map/ppermute | solution.py:50
  34.4 4.3 %copy-start.3 = (bf16[32,5376]{1,0:T(8,128)(2,1)}, bf16[32,5376]{1,0:T(8,128)(2,1)S(1)}, u32[]{:S(2)}) copy-start(bf16[32,5376]{1,0:T(8,128)(2,1)S(1)} %collective-permute-done.1.refs_1_) | copy-start | bytes 1032196
  34.4 19.1 %collective-permute-start.3 = (bf16[32,5376]{1,0:T(8,128)(2,1)S(1)}, bf16[32,5376]{1,0:T(8,128)(2,1)}, u32[]{:S(2)}, u32[]{:S(2)}) collective-permute-start(bf16[32,5376]{1,0:T(8,128)(2,1)S(1)} %collective-permute-done.1.refs_1_), channel_id=1, source_target_pairs={{0,2},{1,3},{2,4},{3,5},{4,6},{5,7},{6,8},{7,9},{8,10},{9,11},{10,... | collective-permute-start | bytes 1032200 | tf_op jit(solution)/shard_map/ppermute | solution.py:50
  38.7 57.8 %all-to-all-start = ((bf16[4,48,5376]{2,1,0:T(8,128)(2,1)}), bf16[4,48,5376]{2,1,0:T(8,128)(2,1)}, u32[]{:S(2)}, u32[]{:S(2)}) async-start(bf16[4,48,5376]{2,1,0:T(8,128)(2,1)} %spread.2), calls=%async_computation | async-start | bytes 4128768 | tf_op jit(solution)/shard_map/all_to_all | solution.py:73
  43.3 29.0 %collective-permute-start.11 = (bf16[48,5376]{1,0:T(8,128)(2,1)}, bf16[48,5376]{1,0:T(8,128)(2,1)}, u32[]{:S(2)}, u32[]{:S(2)}) collective-permute-start(bf16[48,5376]{1,0:T(8,128)(2,1)} %collective-permute-done.10.refs_11_), channel_id=1, source_target_pairs={{0,32},{1,97},{2,34},{3,99},{4,36},{5,101},{6,38},{7,103},{8,40},{... | collective-permute-start | bytes 1548296 | tf_op jit(solution)/shard_map/ppermute | solution.py:50
  48.9 10.8 %collective-permute-start.4 = (bf16[32,5376]{1,0:T(8,128)(2,1)}, bf16[32,5376]{1,0:T(8,128)(2,1)S(1)}, u32[]{:S(2)}, u32[]{:S(2)}) collective-permute-start(bf16[32,5376]{1,0:T(8,128)(2,1)} %collective-permute-done.2.refs_2_), channel_id=1, source_target_pairs={{0,14},{1,15},{2,0},{3,1},{4,2},{5,3},{6,4},{7,5},{8,6},{9,7},{10,... | collective-permute-start | bytes 1032200 | tf_op jit(solution)/shard_map/ppermute | solution.py:50
  53.5 23.9 %collective-permute-start.5 = (bf16[32,5376]{1,0:T(8,128)(2,1)}, bf16[32,5376]{1,0:T(8,128)(2,1)S(1)}, u32[]{:S(2)}, u32[]{:S(2)}) collective-permute-start(bf16[32,5376]{1,0:T(8,128)(2,1)} %collective-permute-done.3.refs_3_), channel_id=1, source_target_pairs={{0,2},{1,3},{2,4},{3,5},{4,6},{5,7},{6,8},{7,9},{8,10},{9,11},{10,... | collective-permute-start | bytes 1032200 | tf_op jit(solution)/shard_map/ppermute | solution.py:50
  59.8 0.7 copy-start.5
  62.8 60.4 %collective-permute-start.8 = (bf16[160,5376]{1,0:T(8,128)(2,1)}, bf16[160,5376]{1,0:T(8,128)(2,1)}, u32[]{:S(2)}, u32[]{:S(2)}) collective-permute-start(bf16[160,5376]{1,0:T(8,128)(2,1)} %shard_map.55), channel_id=1, source_target_pairs={{0,1},{1,0},{2,3},{3,2},{4,5},{5,4},{6,7},{7,6},{8,9},{9,8},{10,11... | collective-permute-start | bytes 5160968 | tf_op jit(solution)/shard_map/ppermute | solution.py:50
  67.1 18.6 %collective-permute-start.6 = (bf16[32,5376]{1,0:T(8,128)(2,1)}, bf16[32,5376]{1,0:T(8,128)(2,1)S(1)}, u32[]{:S(2)}, u32[]{:S(2)}) collective-permute-start(bf16[32,5376]{1,0:T(8,128)(2,1)} %copy-done.5), channel_id=1, source_target_pairs={{0,14},{1,15},{2,0},{3,1},{4,2},{5,3},{6,4},{7,5},{8,6},{9,7},{10,... | collective-permute-start | bytes 1032200 | tf_op jit(solution)/shard_map/ppermute | solution.py:50
  72.3 21.7 %collective-permute-start.16 = (bf16[48,5376]{1,0:T(8,128)(2,1)}, bf16[48,5376]{1,0:T(8,128)(2,1)}, u32[]{:S(2)}, u32[]{:S(2)}) collective-permute-start(bf16[48,5376]{1,0:T(8,128)(2,1)} %collective-permute-done.11.refs_12_), channel_id=1, source_target_pairs={{0,32},{1,97},{2,34},{3,99},{4,36},{5,101},{6,38},{7,103},{8,40},{... | collective-permute-start | bytes 1548296 | tf_op jit(solution)/shard_map/ppermute | solution.py:50
  77.5 12.6 %copy-start.7 = (bf16[32,5376]{1,0:T(8,128)(2,1)}, bf16[32,5376]{1,0:T(8,128)(2,1)S(1)}, u32[]{:S(2)}) copy-start(bf16[32,5376]{1,0:T(8,128)(2,1)S(1)} %collective-permute-done.5.refs_0_.refs_5_) | copy-start | bytes 1032196
  77.5 12.6 %collective-permute-start.7 = (bf16[32,5376]{1,0:T(8,128)(2,1)S(1)}, bf16[32,5376]{1,0:T(8,128)(2,1)}, u32[]{:S(2)}, u32[]{:S(2)}) collective-permute-start(bf16[32,5376]{1,0:T(8,128)(2,1)S(1)} %collective-permute-done.5.refs_0_.refs_5_), channel_id=1, source_target_pairs={{0,2},{1,3},{2,4},{3,5},{4,6},{5,7},{6,8},{7,9},{8,10},{9,11},{10,... | collective-permute-start | bytes 1032200 | tf_op jit(solution)/shard_map/ppermute | solution.py:50
  81.3 41.9 %collective-permute-start.13 = (bf16[96,5376]{1,0:T(8,128)(2,1)}, bf16[96,5376]{1,0:T(8,128)(2,1)}, u32[]{:S(2)}, u32[]{:S(2)}) collective-permute-start(bf16[96,5376]{1,0:T(8,128)(2,1)} %constant_dynamic-update-slice_fusion), channel_id=1, source_target_pairs={{0,384},{1,385},{2,386},{3,387},{4,388},{5,389},{6,390},{7,391},{8... | collective-permute-start | bytes 3096584 | tf_op jit(solution)/shard_map/ppermute | solution.py:50
  85.7 4.4 %copy-start.9 = (bf16[32,5376]{1,0:T(8,128)(2,1)}, bf16[32,5376]{1,0:T(8,128)(2,1)S(1)}, u32[]{:S(2)}) copy-start(bf16[32,5376]{1,0:T(8,128)(2,1)S(1)} %collective-permute-done.6.refs_1_.refs_6_) | copy-start | bytes 1032196
  85.7 37.5 %collective-permute-start.12 = (bf16[96,5376]{1,0:T(8,128)(2,1)}, bf16[96,5376]{1,0:T(8,128)(2,1)}, u32[]{:S(2)}, u32[]{:S(2)}) collective-permute-start(bf16[96,5376]{1,0:T(8,128)(2,1)} %constant_dynamic-update-slice_fusion), channel_id=1, source_target_pairs={{0,128},{1,129},{2,130},{3,131},{4,132},{5,133},{6,134},{7,135},{8... | collective-permute-start | bytes 3096584 | tf_op jit(solution)/shard_map/ppermute | solution.py:50
  92.1 31.1 %collective-permute-start.9 = (bf16[96,5376]{1,0:T(8,128)(2,1)}, bf16[96,5376]{1,0:T(8,128)(2,1)}, u32[]{:S(2)}, u32[]{:S(2)}) collective-permute-start(bf16[96,5376]{1,0:T(8,128)(2,1)} %shard_map.56), channel_id=1, source_target_pairs={{0,1},{1,0},{2,3},{3,2},{4,5},{5,4},{6,7},{7,6},{8,9},{9,8},{10,11... | collective-permute-start | bytes 3096584 | tf_op jit(solution)/shard_map/ppermute | solution.py:50
  96.5 25.8 %copy-start.12 = (f32[1,512]{1,0:T(1,128)S(1)}, f32[1,512]{1,0:T(1,128)}, u32[]{:S(2)}) copy-start(f32[1,512]{1,0:T(1,128)} %param.9) | copy-start | bytes 6148
  96.5 39.6 %copy-start.2 = (bf16[32,5376]{1,0:T(8,128)(2,1)S(1)}, bf16[32,5376]{1,0:T(8,128)(2,1)}, u32[]{:S(2)}) copy-start(bf16[32,5376]{1,0:T(8,128)(2,1)} %copy-done.1) | copy-start | bytes 1032196
  96.5 39.6 %copy-start.4 = (bf16[32,5376]{1,0:T(8,128)(2,1)S(1)}, bf16[32,5376]{1,0:T(8,128)(2,1)}, u32[]{:S(2)}) copy-start(bf16[32,5376]{1,0:T(8,128)(2,1)} %copy-done.3) | copy-start | bytes 1032196
  96.5 39.5 %all-to-all-start.1 = ((bf16[4,48,5376]{2,1,0:T(8,128)(2,1)}), bf16[4,48,5376]{2,1,0:T(8,128)(2,1)}, u32[]{:S(2)}, u32[]{:S(2)}) async-start(bf16[4,48,5376]{2,1,0:T(8,128)(2,1)} %spread.3), calls=%async_computation.1 | async-start | bytes 4128768 | tf_op jit(solution)/shard_map/all_to_all | solution.py:73
  102.4 14.2 %collective-permute-start.14 = (bf16[48,5376]{1,0:T(8,128)(2,1)S(1)}, bf16[48,5376]{1,0:T(8,128)(2,1)}, u32[]{:S(2)}, u32[]{:S(2)}) collective-permute-start(bf16[48,5376]{1,0:T(8,128)(2,1)S(1)} %dynamic-slice_bitcast_fusion), channel_id=1, source_target_pairs={{0,32},{1,97},{2,34},{3,99},{4,36},{5,101},{6,38},{7,103},{8,40},{... | collective-permute-start | bytes 1548296 | tf_op jit(solution)/shard_map/ppermute | solution.py:50
  116.6 16.1 %collective-permute-start.15 = (bf16[48,5376]{1,0:T(8,128)(2,1)}, bf16[48,5376]{1,0:T(8,128)(2,1)}, u32[]{:S(2)}, u32[]{:S(2)}) collective-permute-start(bf16[48,5376]{1,0:T(8,128)(2,1)} %collective-permute-done.14.refs_15_), channel_id=1, source_target_pairs={{0,32},{1,97},{2,34},{3,99},{4,36},{5,101},{6,38},{7,103},{8,40},{... | collective-permute-start | bytes 1548296 | tf_op jit(solution)/shard_map/ppermute | solution.py:50
  136.1 1.0 copy-start.6
  137.0 1.0 copy-start.8
  138.0 1.0 copy-start.10
  139.0 0.9 copy-start.11

commit v8 on v6

--- a/solution.py
+++ b/solution.py
@@ -31,12 +31,10 @@
 DOWN_X = routes(lambda x, y, z, c: (x - 1, y, z, c))
 RING_Y = routes(lambda x, y, z, c: (x, y // 4 * 4 + (y + (1 - 2 * c)) % 4, z, c))
 OTHER_Y = routes(lambda x, y, z, c: (x, (y + 4) % 8, z, c))
-UP_Z = routes(lambda x, y, z, c: (x, y, z + 1, c))
-DOWN_Z = routes(lambda x, y, z, c: (x, y, z - 1, c))
 CORE = routes(lambda x, y, z, c: (x, y, z, 1 - c))
 ROWS_X = [[x * 4 + y for x in range(4)] for y in range(4)]
+ROWS_Z = [[(half * 8 + z) * 2 + core for z in range(8)] for half in range(2) for core in range(2)]
 
-HOPS_Z = (0, -1, 1, -2, 2, -3, 3, -4)
 HOPS_X = (0, -1, 1, 2)
 PARTS = 3
 
@@ -50,39 +48,23 @@
     return lax.all_to_all(copies, "prompt", 0, 0, axis_index_groups=ROWS_X, tiled=True)
 
 
-def stack_kernel(*refs):
-    operands, (out_ref, sem) = refs[:-2], refs[-2:]
-    copies, at = [], 0
-    for i, operand in enumerate(operands):
-        size = operand.shape[0]
-        copies.append(pltpu.make_async_copy(operand, out_ref.at[pl.ds(at, size)], sem.at[i]))
-        at += size
-    for copy in copies:
-        copy.start()
-    for copy in copies:
-        copy.wait()
-
-
-def stack(*pieces):
-    n_rows = sum(piece.shape[0] for piece in pieces)
-    return pl.pallas_call(
-        stack_kernel,
-        out_shape=jax.ShapeDtypeStruct((n_rows, pieces[0].shape[1]), pieces[0].dtype),
-        in_specs=[pl.BlockSpec(memory_space=pl.ANY)] * len(pieces),
-        out_specs=pl.BlockSpec(memory_space=pltpu.VMEM),
-        scratch_shapes=[pltpu.SemaphoreType.DMA((len(pieces),))],
-    )(*pieces)
-
-
 def place():
     prompt, owner = lax.axis_index("prompt"), lax.axis_index("feat")
     chip = owner // 2
     return prompt // 4, prompt % 4, chip // 8, chip % 8, owner % 2
 
 
-def product_kernel(n_sources, act_ref, *refs):
+def rows_of(side, place_of, slots):
+    _, _, half, _, core = place_of
+    feats = [((half ^ flip) * 8 + z) * 2 + (core ^ side) for z in range(8) for flip in range(2)]
+    return [pl.multiple_of(feat * slots, slots) for feat in feats]
+
+
+def product_kernel(side, act_ref, *refs):
     operands, (out_ref, rows, cols, acc, order, act, sem) = refs[:-7], refs[-7:]
-    sources, targets = operands[:n_sources], operands[n_sources:]
+    if side:
+        before_ref, operands = operands[0], operands[1:]
+    sources, targets = operands[:1], operands[1:]
     width = rows.shape[1] // PARTS
 
     def copies(part):
@@ -105,14 +87,10 @@
         for copy in copies(part):
             copy.start()
 
-    x, y, half, z, core = place()
+    here = place()
+    x, y, _, _, core = here
     slots = act_ref.shape[0] // 32
-    row_at = []
-    for side in range(2):
-        for hop in HOPS_Z:
-            for flip in range(2):
-                feat = ((half ^ flip) * 8 + ((z + hop) & 7)) * 2 + (core ^ side)
-                row_at.append(pl.multiple_of(feat * slots, slots))
+    row_at = rows_of(side, here, slots)
     for g, at in enumerate(row_at):
         act[g * slots : (g + 1) * slots] = act_ref[pl.ds(at, slots)]
     block = out_ref.shape[1] // 16
@@ -137,18 +115,22 @@
 
     edges = (acc[...] * act[...]).astype(jnp.bfloat16)
     placed = jnp.dot(edges, order[...], preferred_element_type=jnp.float32).astype(jnp.bfloat16)
-    for g, at in enumerate(row_at):
+    if not side:
+        out_ref[...] = placed
+        return
+    for g, (at, before_at) in enumerate(zip(row_at, rows_of(0, here, slots))):
         out_ref[pl.ds(at, slots), :] = placed[g * slots : (g + 1) * slots]
+        out_ref[pl.ds(before_at, slots), :] = before_ref[g * slots : (g + 1) * slots, :]
 
 
-def product(act, sources, targets):
-    depth = targets[0].shape[1]
-    n_rows, n_cols = act.shape[0], sum(t.shape[0] for t in targets)
-    whole, anywhere = pl.BlockSpec(memory_space=pltpu.VMEM), pl.BlockSpec(memory_space=pltpu.HBM)
+def product(act, rows, targets, before=None):
+    (n_rows, depth), n_cols = rows.shape, sum(t.shape[0] for t in targets)
+    whole, anywhere = pl.BlockSpec(memory_space=pltpu.VMEM), pl.BlockSpec(memory_space=pl.ANY)
+    side = 0 if before is None else 1
     return pl.pallas_call(
-        functools.partial(product_kernel, len(sources)),
-        out_shape=jax.ShapeDtypeStruct((n_rows, n_cols), jnp.bfloat16),
-        in_specs=[whole] + [anywhere] * (len(sources) + len(targets)),
+        functools.partial(product_kernel, side),
+        out_shape=jax.ShapeDtypeStruct((n_rows * (1 + side), n_cols), jnp.bfloat16),
+        in_specs=[whole] * (1 + side) + [anywhere] * (1 + len(targets)),
         out_specs=whole,
         scratch_shapes=[
             pltpu.VMEM((n_rows, depth), jnp.bfloat16),
@@ -156,11 +138,10 @@
             pltpu.VMEM((n_rows, n_cols), jnp.float32),
             pltpu.VMEM((n_cols, n_cols), jnp.bfloat16),
             pltpu.VMEM((n_rows, 1), jnp.float32),
-            pltpu.SemaphoreType.DMA((PARTS, len(sources) + len(targets))),
+            pltpu.SemaphoreType.DMA((PARTS, 1 + len(targets))),
         ],
         compiler_params=pltpu.CompilerParams(vmem_limit_bytes=28 << 20),
-        name="product",
-    )(act, *sources, *targets)
+    )(act, *((before,) if side else ()), rows, *targets)
 
 
 def edges_of(decoder, encoder, row_ids, counts, activity):
@@ -187,16 +168,13 @@
 
     other = send(source_rows, OTHER_Y)
     own = jnp.concatenate([source_rows, other], axis=0)
-    u1, w1 = send(own, UP_Z), send(own, DOWN_Z)
-    u2, w2 = send(u1, UP_Z), send(w1, DOWN_Z)
-    u3, w3 = send(u2, UP_Z), send(w2, DOWN_Z)
-    u4 = send(u3, UP_Z)
-    near = stack(own, u1, w1, u2, w2)
-    away = stack(u3, w3, u4)
-    sources = [near, away, send(near, CORE), send(away, CORE)]
+    mine = lax.all_gather(own, "feat", axis=0, tiled=True, axis_index_groups=ROWS_Z)
+    theirs = send(mine, CORE)
 
+    act = activity.reshape(-1, 1)
     targets = [aa.reshape(4 * width, -1), y1, b1, b2, f1, y2, c1, c2, f2, dd.reshape(4 * width, -1)]
-    return product(activity.reshape(-1, 1), sources, targets)[None]
+    part = product(act, mine, targets)
+    return product(act, theirs, targets, part)[None]
 
 
 def solution(mesh):

time: 147 us -> 187 us (1.27)
  waiting for transfers between devices: 30.1 us -> 87.5 us
  starting transfers between devices: 86.9 us -> 61.2 us
  between operations: 0.41 us -> 13.6 us
  Pallas kernels: 13.9 us -> 12 us
    all_gather x0 -> x1, waiting for transfers between devices: none -> 39.3 us  [edges_of(): lax.all_gather(own, 'feat', axis=0, tiled=True, axis_index_groups=ROWS_Z)]
    ppermute x19 -> x11, starting transfers between devices: 78 us -> 52.2 us  [send(): return lax.ppermute(value, AXES, pairs)]
    ppermute x19 -> x11, waiting for transfers between devices: 30.1 us -> 48.2 us  [send(): return lax.ppermute(value, AXES, pairs)]
    pallas_call x3 -> x2, Pallas kernels: 13.9 us -> 12 us  [product(): pl.pallas_call(functools.partial(product_kernel, side), out_shape=jax.Sha...]
  transfers between devices with their start and end apart: 21 -> 14, of which waited for: 5 -> 7; matrix products, arithmetic and copies ran while one was open for 5% -> 3% of each run, Pallas kernels for 3% -> 3%
where the time goes in v8:
time: 187 us
  waiting for transfers between devices  87.5 us (47%)
  starting transfers between devices  61.2 us (33%)
  between operations  13.6 us (7%)
  Pallas kernels  12 us (6%)
  local copies, waits for them, and re-layouts  8.7 us (5%)
  other arithmetic  3.6 us (2%)
    ppermute x11, starting transfers between devices, send(): return lax.ppermute(value, AXES, pairs)  52.2 us
    ppermute x11, waiting for transfers between devices, send(): return lax.ppermute(value, AXES, pairs)  48.2 us
    all_gather x1, waiting for transfers between devices, edges_of(): lax.all_gather(own, 'feat', axis=0, tiled=True, axis_index_groups=ROWS_Z)  39.3 us
    pallas_call x2, Pallas kernels, product(): pl.pallas_call(functools.partial(product_kernel, side), out_shape=jax.Sha...  12 us
    all_to_all x2, starting transfers between devices, share(): lax.all_to_all(copies, 'prompt', 0, 0, axis_index_groups=ROWS_X, tiled=True)  9.03 us
    broadcast_in_dim x2, local copies, waits for them, and re-layouts, share(): copies = jnp.broadcast_to(value[None], (4,) + value.shape)  5.03 us
  transfers between devices with their start and end apart: 14, of which 7 were waited for; matrix products, arithmetic and copies ran while one was open for 3% of the time, Pallas kernels for 3%

profile of v8, /device:TPU:1, one launch (start us, length us, event | category | flops | bytes accessed | tf_op | source)
XLA Modules:
  0.0 186.5 jit_solution(9746020440257178495)
XLA Ops:
  6.5 0.0 copy-start
  6.5 0.0 all-gather.2.cloned.1.call-start
  6.5 1.4 fusion
  8.0 0.6 iota_compare_fusion
  8.6 0.7 fusion.1
  9.3 0.0 copy-done
  9.3 0.7 gather_fusion
  10.0 0.1 broadcast_select_fusion
  10.1 8.3 %collective-permute-start = (bf16[16,5376]{1,0:T(8,128)(2,1)S(1)}, bf16[16,5376]{1,0:T(8,128)(2,1)S(1)}, u32[]{:S(2)}, u32[]{:S(2)}) collective-permute-start(bf16[16,5376]{1,0:T(8,128)(2,1)S(1)} %broadcast_select_fusion), channel_id=1, source_target_pairs={{0,16},{1,17},{2,18},{3,19},{4,20},{5,21},{6,22},{7,23},{8,24},{9,... | collective-permute-start | bytes 516104 | tf_op jit(solution)/shard_map/ppermute | solution.py:43
  18.3 6.8 %collective-permute-done = bf16[16,5376]{1,0:T(8,128)(2,1)S(1)} collective-permute-done((bf16[16,5376]{1,0:T(8,128)(2,1)S(1)}, bf16[16,5376]{1,0:T(8,128)(2,1)S(1)}, u32[]{:S(2)}, u32[]{:S(2)}) %collective-permute-start) | collective-permute-done | bytes 172064 | tf_op jit(solution)/shard_map/ppermute | solution.py:43
  25.1 0.8 pad_maximum_fusion
  25.9 0.0 all-gather.2.cloned.1.call-update
  25.9 3.2 %collective-permute-start.1 = (bf16[48,5376]{1,0:T(8,128)(2,1)}, bf16[48,5376]{1,0:T(8,128)(2,1)S(1)}, u32[]{:S(2)}, u32[]{:S(2)}) collective-permute-start(bf16[48,5376]{1,0:T(8,128)(2,1)} %param.6), channel_id=1, source_target_pairs={{0,32},{1,97},{2,34},{3,99},{4,36},{5,101},{6,38},{7,103},{8,40},{... | collective-permute-start | bytes 1548296 | tf_op jit(solution)/shard_map/ppermute | solution.py:43
  29.1 2.6 %broadcast_in_dim.36 = bf16[4,48,5376]{2,1,0:T(8,128)(2,1)} broadcast(bf16[48,5376]{1,0:T(8,128)(2,1)} %param.6), dimensions={1,2} | broadcast | bytes 2580480 | tf_op jit(solution)/shard_map/broadcast_in_dim | solution.py:47
  31.6 4.4 %all-to-all-start = ((bf16[4,48,5376]{2,1,0:T(8,128)(2,1)}), bf16[4,48,5376]{2,1,0:T(8,128)(2,1)}, u32[]{:S(2)}, u32[]{:S(2)}) async-start(bf16[4,48,5376]{2,1,0:T(8,128)(2,1)} %broadcast_in_dim.36), calls=%async_computation | async-start | bytes 4128768 | tf_op jit(solution)/shard_map/all_to_all | solution.py:48
  36.1 39.3 %all-gather.2.cloned.1.call-done.refs_0_ = bf16[256,5376]{1,0:T(8,128)(2,1)} async-done(((bf16[32,5376]{1,0:T(8,128)(2,1)}), bf16[256,5376]{1,0:T(8,128)(2,1)}) %all-gather.2.cloned.1.call-update) | async-done | bytes 2752528 | tf_op jit(solution)/shard_map/all_gather | solution.py:171
  75.3 5.5 %collective-permute-start.10 = (bf16[256,5376]{1,0:T(8,128)(2,1)}, bf16[256,5376]{1,0:T(8,128)(2,1)}, u32[]{:S(2)}, u32[]{:S(2)}) collective-permute-start(bf16[256,5376]{1,0:T(8,128)(2,1)} %all-gather.2.cloned.1.call-done.refs_0_), channel_id=1, source_target_pairs={{0,1},{1,0},{2,3},{3,2},{4,5},{5,4},{6,7},{7,6},{8,9},{9,8},{10,11... | collective-permute-start | bytes 8257544 | tf_op jit(solution)/shard_map/ppermute | solution.py:43
  80.8 0.0 collective-permute-done.1.refs_2_.refs_3_
  80.9 5.0 %collective-permute-start.5 = (bf16[48,5376]{1,0:T(8,128)(2,1)S(1)}, bf16[48,5376]{1,0:T(8,128)(2,1)}, u32[]{:S(2)}, u32[]{:S(2)}) collective-permute-start(bf16[48,5376]{1,0:T(8,128)(2,1)S(1)} %collective-permute-done.1.refs_2_.refs_3_), channel_id=1, source_target_pairs={{0,32},{1,97},{2,34},{3,99},{4,36},{5,101},{6,38},{7,103},{8,40},{... | collective-permute-start | bytes 1548296 | tf_op jit(solution)/shard_map/ppermute | solution.py:43
  85.8 10.2 %collective-permute-done.5.refs_6_.refs_7_ = bf16[48,5376]{1,0:T(8,128)(2,1)} collective-permute-done((bf16[48,5376]{1,0:T(8,128)(2,1)S(1)}, bf16[48,5376]{1,0:T(8,128)(2,1)}, u32[]{:S(2)}, u32[]{:S(2)}) %collective-permute-start.5) | collective-permute-done | bytes 516128 | tf_op jit(solution)/shard_map/ppermute | solution.py:43
  96.0 5.8 %collective-permute-start.9 = (bf16[48,5376]{1,0:T(8,128)(2,1)}, bf16[48,5376]{1,0:T(8,128)(2,1)}, u32[]{:S(2)}, u32[]{:S(2)}) collective-permute-start(bf16[48,5376]{1,0:T(8,128)(2,1)} %collective-permute-done.5.refs_6_.refs_7_), channel_id=1, source_target_pairs={{0,32},{1,97},{2,34},{3,99},{4,36},{5,101},{6,38},{7,103},{8,40},{... | collective-permute-start | bytes 1548296 | tf_op jit(solution)/shard_map/ppermute | solution.py:43
  101.8 4.3 %collective-permute-start.3 = (bf16[48,5376]{1,0:T(8,128)(2,1)S(1)}, bf16[48,5376]{1,0:T(8,128)(2,1)}, u32[]{:S(2)}, u32[]{:S(2)}) collective-permute-start(bf16[48,5376]{1,0:T(8,128)(2,1)S(1)} %collective-permute-done.1.refs_2_.refs_3_), channel_id=1, source_target_pairs={{0,384},{1,385},{2,386},{3,387},{4,388},{5,389},{6,390},{7,391},{8... | collective-permute-start | bytes 1548296 | tf_op jit(solution)/shard_map/ppermute | solution.py:43
  106.1 6.7 %collective-permute-done.9 = bf16[48,5376]{1,0:T(8,128)(2,1)} collective-permute-done((bf16[48,5376]{1,0:T(8,128)(2,1)}, bf16[48,5376]{1,0:T(8,128)(2,1)}, u32[]{:S(2)}, u32[]{:S(2)}) %collective-permute-start.9) | collective-permute-done | bytes 516128 | tf_op jit(solution)/shard_map/ppermute | solution.py:43
  112.8 0.0 all-to-all-done
  112.8 2.5 %broadcast_in_dim.37 = bf16[4,48,5376]{2,1,0:T(8,128)(2,1)} broadcast(bf16[48,5376]{1,0:T(8,128)(2,1)} %collective-permute-done.9), dimensions={1,2} | broadcast | bytes 2580480 | tf_op jit(solution)/shard_map/broadcast_in_dim | solution.py:47
  115.3 0.0 copy-start.2
  115.3 4.6 %all-to-all-start.1 = ((bf16[4,48,5376]{2,1,0:T(8,128)(2,1)}), bf16[4,48,5376]{2,1,0:T(8,128)(2,1)}, u32[]{:S(2)}, u32[]{:S(2)}) async-start(bf16[4,48,5376]{2,1,0:T(8,128)(2,1)} %broadcast_in_dim.37), calls=%async_computation.1 | async-start | bytes 4128768 | tf_op jit(solution)/shard_map/all_to_all | solution.py:48
  119.9 1.1 dynamic-slice_bitcast_fusion
  121.0 5.6 %collective-permute-start.4 = (bf16[48,5376]{1,0:T(8,128)(2,1)S(1)}, bf16[48,5376]{1,0:T(8,128)(2,1)}, u32[]{:S(2)}, u32[]{:S(2)}) collective-permute-start(bf16[48,5376]{1,0:T(8,128)(2,1)S(1)} %dynamic-slice_bitcast_fusion), channel_id=1, source_target_pairs={{0,32},{1,97},{2,34},{3,99},{4,36},{5,101},{6,38},{7,103},{8,40},{... | collective-permute-start | bytes 1548296 | tf_op jit(solution)/shard_map/ppermute | solution.py:43
  126.6 3.3 %collective-permute-start.2 = (bf16[48,5376]{1,0:T(8,128)(2,1)S(1)}, bf16[48,5376]{1,0:T(8,128)(2,1)}, u32[]{:S(2)}, u32[]{:S(2)}) collective-permute-start(bf16[48,5376]{1,0:T(8,128)(2,1)S(1)} %collective-permute-done.1.refs_2_.refs_3_), channel_id=1, source_target_pairs={{0,128},{1,129},{2,130},{3,131},{4,132},{5,133},{6,134},{7,135},{8... | collective-permute-start | bytes 1548296 | tf_op jit(solution)/shard_map/ppermute | solution.py:43
  129.9 3.2 %collective-permute-start.7 = (bf16[48,5376]{1,0:T(8,128)(2,1)}, bf16[48,5376]{1,0:T(8,128)(2,1)}, u32[]{:S(2)}, u32[]{:S(2)}) collective-permute-start(bf16[48,5376]{1,0:T(8,128)(2,1)} %collective-permute-done.5.refs_6_.refs_7_), channel_id=1, source_target_pairs={{0,384},{1,385},{2,386},{3,387},{4,388},{5,389},{6,390},{7,391},{8... | collective-permute-start | bytes 1548296 | tf_op jit(solution)/shard_map/ppermute | solution.py:43
  133.1 0.0 collective-permute-done.3.refs_4_.refs_5_
  133.1 2.1 %collective-permute-start.6 = (bf16[48,5376]{1,0:T(8,128)(2,1)}, bf16[48,5376]{1,0:T(8,128)(2,1)}, u32[]{:S(2)}, u32[]{:S(2)}) collective-permute-start(bf16[48,5376]{1,0:T(8,128)(2,1)} %collective-permute-done.5.refs_6_.refs_7_), channel_id=1, source_target_pairs={{0,128},{1,129},{2,130},{3,131},{4,132},{5,133},{6,134},{7,135},{8... | collective-permute-start | bytes 1548296 | tf_op jit(solution)/shard_map/ppermute | solution.py:43
  135.2 1.5 collective-permute-done.4.refs_5_.refs_6_
  136.7 6.0 %collective-permute-start.8 = (bf16[48,5376]{1,0:T(8,128)(2,1)}, bf16[48,5376]{1,0:T(8,128)(2,1)}, u32[]{:S(2)}, u32[]{:S(2)}) collective-permute-start(bf16[48,5376]{1,0:T(8,128)(2,1)} %collective-permute-done.4.refs_5_.refs_6_), channel_id=1, source_target_pairs={{0,32},{1,97},{2,34},{3,99},{4,36},{5,101},{6,38},{7,103},{8,40},{... | collective-permute-start | bytes 1548296 | tf_op jit(solution)/shard_map/ppermute | solution.py:43
  142.7 0.0 copy-done.2
  142.7 0.1 copy.7.act_ref
  142.9 12.0 %collective-permute-done.2.refs_3_.refs_4_ = bf16[48,5376]{1,0:T(8,128)(2,1)} collective-permute-done((bf16[48,5376]{1,0:T(8,128)(2,1)S(1)}, bf16[48,5376]{1,0:T(8,128)(2,1)}, u32[]{:S(2)}, u32[]{:S(2)}) %collective-permute-start.2) | collective-permute-done | bytes 516128 | tf_op jit(solution)/shard_map/ppermute | solution.py:43
  154.9 0.0 collective-permute-done.7.refs_8_.refs_9_
  154.9 11.1 %collective-permute-done.6.refs_7_.refs_8_ = bf16[48,5376]{1,0:T(8,128)(2,1)} collective-permute-done((bf16[48,5376]{1,0:T(8,128)(2,1)}, bf16[48,5376]{1,0:T(8,128)(2,1)}, u32[]{:S(2)}, u32[]{:S(2)}) %collective-permute-start.6) | collective-permute-done | bytes 516128 | tf_op jit(solution)/shard_map/ppermute | solution.py:43
  165.9 0.0 collective-permute-done.8.refs_9_.refs_10_
  165.9 0.0 all-to-all-done.1
  165.9 0.0 copy-start.1
  165.9 1.8 copy-done.1
  167.7 5.3 %shard_map.55.refs_0_ = bf16[256,768]{1,0:T(8,128)(2,1)S(1)} custom-call(f32[512,1]{1,0:T(8,128)S(1)} %copy.7.act_ref, bf16[256,5376]{1,0:T(8,128)(2,1)S(1)} %copy-done.1, bf16[192,5376]{1,0:T(8,128)(2,1)} %bitcast.4.refs_1_.refs_2_, bf16[48,5376]{1,0:T(8,128)(2,1)S(1)} %collective-permute-done.1.refs_2_.refs_3_, ...), custom_call_target="tpu_custom_call" | custom-call | tf_op jit(solution)/shard_map/pallas_call | solution.py:130
  173.0 0.0 collective-permute-done.10.refs_1_
  173.0 6.6 %shard_map.56 = bf16[512,768]{1,0:T(8,128)(2,1)} custom-call(f32[512,1]{1,0:T(8,128)S(1)} %copy.7.act_ref, bf16[256,768]{1,0:T(8,128)(2,1)S(1)} %shard_map.55.refs_0_, bf16[256,5376]{1,0:T(8,128)(2,1)} %collective-permute-done.10.refs_1_, bf16[192,5376]{1,0:T(8,128)(2,1)} %bitcast.4.refs_1_.refs_2_, ...), custom_call_target="tpu_custom_call" | custom-call | tf_op jit(solution)/shard_map/pallas_call | solution.py:130
  (1 shorter events, 0.0 us)
Async XLA Ops:
  6.5 2.8 %copy-start = (bf16[256,5376]{1,0:T(8,128)(2,1)S(1)}, bf16[256,5376]{1,0:T(8,128)(2,1)}, u32[]{:S(2)}) copy-start(bf16[256,5376]{1,0:T(8,128)(2,1)} %param.5) | copy-start | bytes 8257540
  6.5 68.8 %all-gather.2.cloned.1.call-start = ((), (), s32[]{:S(2)}) async-start(), calls=%async_computation.2 | async-start | bytes 3096576 | tf_op jit(solution)/shard_map/all_gather | solution.py:171
  10.1 15.1 %collective-permute-start = (bf16[16,5376]{1,0:T(8,128)(2,1)S(1)}, bf16[16,5376]{1,0:T(8,128)(2,1)S(1)}, u32[]{:S(2)}, u32[]{:S(2)}) collective-permute-start(bf16[16,5376]{1,0:T(8,128)(2,1)S(1)} %broadcast_select_fusion), channel_id=1, source_target_pairs={{0,16},{1,17},{2,18},{3,19},{4,20},{5,21},{6,22},{7,23},{8,24},{9,... | collective-permute-start | bytes 516104 | tf_op jit(solution)/shard_map/ppermute | solution.py:43
  25.9 54.9 %collective-permute-start.1 = (bf16[48,5376]{1,0:T(8,128)(2,1)}, bf16[48,5376]{1,0:T(8,128)(2,1)S(1)}, u32[]{:S(2)}, u32[]{:S(2)}) collective-permute-start(bf16[48,5376]{1,0:T(8,128)(2,1)} %param.6), channel_id=1, source_target_pairs={{0,32},{1,97},{2,34},{3,99},{4,36},{5,101},{6,38},{7,103},{8,40},{... | collective-permute-start | bytes 1548296 | tf_op jit(solution)/shard_map/ppermute | solution.py:43
  31.6 81.2 %all-to-all-start = ((bf16[4,48,5376]{2,1,0:T(8,128)(2,1)}), bf16[4,48,5376]{2,1,0:T(8,128)(2,1)}, u32[]{:S(2)}, u32[]{:S(2)}) async-start(bf16[4,48,5376]{2,1,0:T(8,128)(2,1)} %broadcast_in_dim.36), calls=%async_computation | async-start | bytes 4128768 | tf_op jit(solution)/shard_map/all_to_all | solution.py:48
  75.3 97.7 %collective-permute-start.10 = (bf16[256,5376]{1,0:T(8,128)(2,1)}, bf16[256,5376]{1,0:T(8,128)(2,1)}, u32[]{:S(2)}, u32[]{:S(2)}) collective-permute-start(bf16[256,5376]{1,0:T(8,128)(2,1)} %all-gather.2.cloned.1.call-done.refs_0_), channel_id=1, source_target_pairs={{0,1},{1,0},{2,3},{3,2},{4,5},{5,4},{6,7},{7,6},{8,9},{9,8},{10,11... | collective-permute-start | bytes 8257544 | tf_op jit(solution)/shard_map/ppermute | solution.py:43
  80.9 15.1 %collective-permute-start.5 = (bf16[48,5376]{1,0:T(8,128)(2,1)S(1)}, bf16[48,5376]{1,0:T(8,128)(2,1)}, u32[]{:S(2)}, u32[]{:S(2)}) collective-permute-start(bf16[48,5376]{1,0:T(8,128)(2,1)S(1)} %collective-permute-done.1.refs_2_.refs_3_), channel_id=1, source_target_pairs={{0,32},{1,97},{2,34},{3,99},{4,36},{5,101},{6,38},{7,103},{8,40},{... | collective-permute-start | bytes 1548296 | tf_op jit(solution)/shard_map/ppermute | solution.py:43
  96.0 16.8 %collective-permute-start.9 = (bf16[48,5376]{1,0:T(8,128)(2,1)}, bf16[48,5376]{1,0:T(8,128)(2,1)}, u32[]{:S(2)}, u32[]{:S(2)}) collective-permute-start(bf16[48,5376]{1,0:T(8,128)(2,1)} %collective-permute-done.5.refs_6_.refs_7_), channel_id=1, source_target_pairs={{0,32},{1,97},{2,34},{3,99},{4,36},{5,101},{6,38},{7,103},{8,40},{... | collective-permute-start | bytes 1548296 | tf_op jit(solution)/shard_map/ppermute | solution.py:43
  101.8 31.3 %collective-permute-start.3 = (bf16[48,5376]{1,0:T(8,128)(2,1)S(1)}, bf16[48,5376]{1,0:T(8,128)(2,1)}, u32[]{:S(2)}, u32[]{:S(2)}) collective-permute-start(bf16[48,5376]{1,0:T(8,128)(2,1)S(1)} %collective-permute-done.1.refs_2_.refs_3_), channel_id=1, source_target_pairs={{0,384},{1,385},{2,386},{3,387},{4,388},{5,389},{6,390},{7,391},{8... | collective-permute-start | bytes 1548296 | tf_op jit(solution)/shard_map/ppermute | solution.py:43
  115.3 27.4 %copy-start.2 = (f32[1,512]{1,0:T(1,128)S(1)}, f32[1,512]{1,0:T(1,128)}, u32[]{:S(2)}) copy-start(f32[1,512]{1,0:T(1,128)} %param.9) | copy-start | bytes 6148
  115.3 50.6 %all-to-all-start.1 = ((bf16[4,48,5376]{2,1,0:T(8,128)(2,1)}), bf16[4,48,5376]{2,1,0:T(8,128)(2,1)}, u32[]{:S(2)}, u32[]{:S(2)}) async-start(bf16[4,48,5376]{2,1,0:T(8,128)(2,1)} %broadcast_in_dim.37), calls=%async_computation.1 | async-start | bytes 4128768 | tf_op jit(solution)/shard_map/all_to_all | solution.py:48
  121.0 15.7 %collective-permute-start.4 = (bf16[48,5376]{1,0:T(8,128)(2,1)S(1)}, bf16[48,5376]{1,0:T(8,128)(2,1)}, u32[]{:S(2)}, u32[]{:S(2)}) collective-permute-start(bf16[48,5376]{1,0:T(8,128)(2,1)S(1)} %dynamic-slice_bitcast_fusion), channel_id=1, source_target_pairs={{0,32},{1,97},{2,34},{3,99},{4,36},{5,101},{6,38},{7,103},{8,40},{... | collective-permute-start | bytes 1548296 | tf_op jit(solution)/shard_map/ppermute | solution.py:43
  126.6 28.3 %collective-permute-start.2 = (bf16[48,5376]{1,0:T(8,128)(2,1)S(1)}, bf16[48,5376]{1,0:T(8,128)(2,1)}, u32[]{:S(2)}, u32[]{:S(2)}) collective-permute-start(bf16[48,5376]{1,0:T(8,128)(2,1)S(1)} %collective-permute-done.1.refs_2_.refs_3_), channel_id=1, source_target_pairs={{0,128},{1,129},{2,130},{3,131},{4,132},{5,133},{6,134},{7,135},{8... | collective-permute-start | bytes 1548296 | tf_op jit(solution)/shard_map/ppermute | solution.py:43
  129.9 24.9 %collective-permute-start.7 = (bf16[48,5376]{1,0:T(8,128)(2,1)}, bf16[48,5376]{1,0:T(8,128)(2,1)}, u32[]{:S(2)}, u32[]{:S(2)}) collective-permute-start(bf16[48,5376]{1,0:T(8,128)(2,1)} %collective-permute-done.5.refs_6_.refs_7_), channel_id=1, source_target_pairs={{0,384},{1,385},{2,386},{3,387},{4,388},{5,389},{6,390},{7,391},{8... | collective-permute-start | bytes 1548296 | tf_op jit(solution)/shard_map/ppermute | solution.py:43
  133.1 32.8 %collective-permute-start.6 = (bf16[48,5376]{1,0:T(8,128)(2,1)}, bf16[48,5376]{1,0:T(8,128)(2,1)}, u32[]{:S(2)}, u32[]{:S(2)}) collective-permute-start(bf16[48,5376]{1,0:T(8,128)(2,1)} %collective-permute-done.5.refs_6_.refs_7_), channel_id=1, source_target_pairs={{0,128},{1,129},{2,130},{3,131},{4,132},{5,133},{6,134},{7,135},{8... | collective-permute-start | bytes 1548296 | tf_op jit(solution)/shard_map/ppermute | solution.py:43
  136.7 29.2 %collective-permute-start.8 = (bf16[48,5376]{1,0:T(8,128)(2,1)}, bf16[48,5376]{1,0:T(8,128)(2,1)}, u32[]{:S(2)}, u32[]{:S(2)}) collective-permute-start(bf16[48,5376]{1,0:T(8,128)(2,1)} %collective-permute-done.4.refs_5_.refs_6_), channel_id=1, source_target_pairs={{0,32},{1,97},{2,34},{3,99},{4,36},{5,101},{6,38},{7,103},{8,40},{... | collective-permute-start | bytes 1548296 | tf_op jit(solution)/shard_map/ppermute | solution.py:43
  165.9 1.8 copy-start.1
Sparse Core Ops, SparseCore 0:
  26.0 49.2 all-gather.1

commit v9 on v5

--- a/solution.py
+++ b/solution.py
@@ -32,11 +32,9 @@
 FAR_X = routes(lambda x, y, z, c: (x + 2, y, z, c))
 RING_Y = routes(lambda x, y, z, c: (x, y // 4 * 4 + (y + (1 - 2 * c)) % 4, z, c))
 OTHER_Y = routes(lambda x, y, z, c: (x, (y + 4) % 8, z, c))
-UP_Z = routes(lambda x, y, z, c: (x, y, z + 1, c))
-DOWN_Z = routes(lambda x, y, z, c: (x, y, z - 1, c))
 CORE = routes(lambda x, y, z, c: (x, y, z, 1 - c))
+ROWS_Z = [[(half * 8 + z) * 2 + core for z in range(8)] for half in range(2) for core in range(2)]
 
-HOPS_Z = (0, -1, 1, -2, 2, -3, 3, -4)
 HOPS_X = (0, -1, 1, 2)
 PARTS = 3
 
@@ -45,34 +43,10 @@
     return lax.ppermute(value, AXES, pairs)
 
 
-def stack_kernel(*refs):
-    operands, (out_ref, sem) = refs[:-2], refs[-2:]
-    copies, at = [], 0
-    for i, operand in enumerate(operands):
-        size = operand.shape[0]
-        copies.append(pltpu.make_async_copy(operand, out_ref.at[pl.ds(at, size)], sem.at[i]))
-        at += size
-    for copy in copies:
-        copy.start()
-    for copy in copies:
-        copy.wait()
-
-
-def stack(*pieces):
-    n_rows = sum(piece.shape[0] for piece in pieces)
-    return pl.pallas_call(
-        stack_kernel,
-        out_shape=jax.ShapeDtypeStruct((n_rows, pieces[0].shape[1]), pieces[0].dtype),
-        in_specs=[pl.BlockSpec(memory_space=pl.ANY)] * len(pieces),
-        out_specs=pl.BlockSpec(memory_space=pltpu.VMEM),
-        scratch_shapes=[pltpu.SemaphoreType.DMA((len(pieces),))],
-    )(*pieces)
-
-
 def place():
     prompt, owner = lax.axis_index("prompt"), lax.axis_index("feat")
     chip = owner // 2
-    return prompt // 4, prompt % 4, chip // 8, chip % 8, owner % 2
+    return prompt // 4, prompt % 4, chip // 8, owner % 2
 
 
 def product_kernel(n_sources, n_targets, first_block, last, *refs):
@@ -110,13 +84,13 @@
         for copy in copies(part):
             copy.start()
 
-    x, y, half, z, core = place()
+    x, y, half, core = place()
     slots = act_ref.shape[0] // 32
     row_at = []
     for side in range(2):
-        for hop in HOPS_Z:
-            for flip in range(2):
-                feat = ((half ^ flip) * 8 + ((z + hop) & 7)) * 2 + (core ^ side)
+        for flip in range(2):
+            for z in range(8):
+                feat = ((half ^ flip) * 8 + z) * 2 + (core ^ side)
                 row_at.append(pl.multiple_of(feat * slots, slots))
     for g, at in enumerate(row_at):
         act[g * slots : (g + 1) * slots] = act_ref[pl.ds(at, slots)]
@@ -180,9 +154,14 @@
 
     picked_rows = decoder.at[row_ids[0]].get(mode="promise_in_bounds")
     owners = jnp.arange(counts.shape[1], dtype=jnp.int32)
-    live_count = jnp.sum(jnp.where(owners == owner, counts[0], 0))
-    live_slots = jnp.arange(slot_count, dtype=jnp.int32) < live_count
-    source_rows = jnp.where(live_slots[:, None], picked_rows, jnp.zeros((), picked_rows.dtype))
+    slots = jnp.arange(slot_count, dtype=jnp.int32)
+
+    def live(of):
+        return (slots < jnp.sum(jnp.where(owners == of, counts[0], 0)))[:, None]
+
+    zero = jnp.zeros((), picked_rows.dtype)
+    live_here, live_there = live(owner), live(owner ^ 16)
+    source_rows = jnp.where(live_here, picked_rows, zero)
 
     y0 = encoder
     y1 = send(y0, RING_Y)
@@ -195,15 +174,11 @@
     f1 = send(a3, RING_Y)
     f2 = send(f1, RING_Y)
 
-    other = send(source_rows, OTHER_Y)
-    own = jnp.concatenate([source_rows, other], axis=0)
-    u1, w1 = send(own, UP_Z), send(own, DOWN_Z)
-    u2, w2 = send(u1, UP_Z), send(w1, DOWN_Z)
-    u3, w3 = send(u2, UP_Z), send(w2, DOWN_Z)
-    u4 = send(u3, UP_Z)
-    near = stack(own, u1, w1, u2, w2)
-    away = stack(u3, w3, u4)
-    sources = [near, away, send(near, CORE), send(away, CORE)]
+    mine = lax.all_gather(source_rows, "feat", axis=0, tiled=True, axis_index_groups=ROWS_Z)
+    sent = send(picked_rows, OTHER_Y)
+    other = jnp.where(live_there, sent, zero)
+    mine_too = lax.all_gather(other, "feat", axis=0, tiled=True, axis_index_groups=ROWS_Z)
+    sources = [mine, mine_too, send(mine, CORE), send(mine_too, CORE)]
 
     act = activity.reshape(-1, 1)
     part, rows = product(act, 0, sources, [y0, a1, a2, a3, y1, b1, b2, f1, y2, c1, c2, f2])

time: 147 us -> 166 us (1.13)
  the two profiles are of different devices: /device:TPU:62 before, /device:TPU:1 now
where the time goes in v9:
time: 166 us; the launch traced here: 164 us
  starting transfers between devices  81.7 us (49%)
  waiting for transfers between devices  40.3 us (24%)
  between operations  13.7 us (8%)
  Pallas kernels  12.3 us (7%)
  local copies, waits for them, and re-layouts  10.8 us (7%)
  other arithmetic  5.17 us (3%)
    ppermute x18, starting transfers between devices, send(): return lax.ppermute(value, AXES, pairs)  81.6 us
    all_gather x1, waiting for transfers between devices, edges_of(): lax.all_gather(other, 'feat', axis=0, tiled=True, axis_index_groups=ROWS_Z)  25.6 us
    ppermute x18, waiting for transfers between devices, send(): return lax.ppermute(value, AXES, pairs)  14.6 us
    pallas_call x2, Pallas kernels, product(): pl.pallas_call(functools.partial(product_kernel, len(sources), len(target...  12.3 us
    unnamed x26, local copies, waits for them, and re-layouts  10 us
  transfers between devices with their start and end apart: 20, of which 8 were waited for; matrix products, arithmetic and copies ran while one was open for 1% of the time, Pallas kernels for 5%

profile of v9, /device:TPU:1, one launch (start us, length us, event | category | flops | bytes accessed | tf_op | source)
XLA Modules:
  0.0 164.0 jit_solution(10368487740558661465)
XLA Ops:
  6.6 0.8 fusion.2
  7.4 1.5 fusion.1
  8.9 0.6 iota_compare_fusion.1
  9.6 0.7 gather_fusion
  10.2 0.8 broadcast_select_fusion.1
  11.0 0.0 all-gather.5.cloned.1.call-start
  11.1 8.3 %collective-permute-start = (bf16[16,5376]{1,0:T(8,128)(2,1)S(1)}, bf16[16,5376]{1,0:T(8,128)(2,1)S(1)}, u32[]{:S(2)}, u32[]{:S(2)}) collective-permute-start(bf16[16,5376]{1,0:T(8,128)(2,1)S(1)} %gather_fusion), channel_id=1, source_target_pairs={{0,16},{1,17},{2,18},{3,19},{4,20},{5,21},{6,22},{7,23},{8,24},{9,... | collective-permute-start | bytes 516104 | tf_op jit(solution)/shard_map/ppermute | solution.py:43
  19.3 0.7 iota_compare_fusion
  20.0 6.1 %collective-permute-done = bf16[16,5376]{1,0:T(8,128)(2,1)S(1)} collective-permute-done((bf16[16,5376]{1,0:T(8,128)(2,1)S(1)}, bf16[16,5376]{1,0:T(8,128)(2,1)S(1)}, u32[]{:S(2)}, u32[]{:S(2)}) %collective-permute-start) | collective-permute-done | bytes 172064 | tf_op jit(solution)/shard_map/ppermute | solution.py:43
  26.1 0.8 broadcast_select_fusion
  26.9 0.0 all-gather.5.cloned.1.call-update
  26.9 3.2 %collective-permute-start.6 = (bf16[48,5376]{1,0:T(8,128)(2,1)S(1)}, bf16[48,5376]{1,0:T(8,128)(2,1)}, u32[]{:S(2)}, u32[]{:S(2)}) collective-permute-start(bf16[48,5376]{1,0:T(8,128)(2,1)S(1)} %copy-done.3), channel_id=1, source_target_pairs={{0,32},{1,97},{2,34},{3,99},{4,36},{5,101},{6,38},{7,103},{8,40},{... | collective-permute-start | bytes 1548296 | tf_op jit(solution)/shard_map/ppermute | solution.py:43
  30.1 4.7 %collective-permute-start.5 = (bf16[48,5376]{1,0:T(8,128)(2,1)S(1)}, bf16[48,5376]{1,0:T(8,128)(2,1)}, u32[]{:S(2)}, u32[]{:S(2)}) collective-permute-start(bf16[48,5376]{1,0:T(8,128)(2,1)S(1)} %copy-done.3), channel_id=1, source_target_pairs={{0,256},{1,257},{2,258},{3,259},{4,260},{5,261},{6,262},{7,263},{8... | collective-permute-start | bytes 1548296 | tf_op jit(solution)/shard_map/ppermute | solution.py:43
  34.7 2.2 %collective-permute-start.3 = (bf16[48,5376]{1,0:T(8,128)(2,1)S(1)}, bf16[48,5376]{1,0:T(8,128)(2,1)S(1)}, u32[]{:S(2)}, u32[]{:S(2)}) collective-permute-start(bf16[48,5376]{1,0:T(8,128)(2,1)S(1)} %copy-done.3), channel_id=1, source_target_pairs={{0,128},{1,129},{2,130},{3,131},{4,132},{5,133},{6,134},{7,135},{8... | collective-permute-start | bytes 1548296 | tf_op jit(solution)/shard_map/ppermute | solution.py:43
  37.0 0.8 collective-permute-done.6.refs_9_
  37.8 5.7 %collective-permute-start.10 = (bf16[48,5376]{1,0:T(8,128)(2,1)}, bf16[48,5376]{1,0:T(8,128)(2,1)}, u32[]{:S(2)}, u32[]{:S(2)}) collective-permute-start(bf16[48,5376]{1,0:T(8,128)(2,1)} %collective-permute-done.6.refs_9_), channel_id=1, source_target_pairs={{0,32},{1,97},{2,34},{3,99},{4,36},{5,101},{6,38},{7,103},{8,40},{... | collective-permute-start | bytes 1548296 | tf_op jit(solution)/shard_map/ppermute | solution.py:43
  43.5 7.9 %collective-permute-start.4 = (bf16[48,5376]{1,0:T(8,128)(2,1)S(1)}, bf16[48,5376]{1,0:T(8,128)(2,1)S(1)}, u32[]{:S(2)}, u32[]{:S(2)}) collective-permute-start(bf16[48,5376]{1,0:T(8,128)(2,1)S(1)} %copy-done.3), channel_id=1, source_target_pairs={{0,384},{1,385},{2,386},{3,387},{4,388},{5,389},{6,390},{7,391},{8... | collective-permute-start | bytes 1548296 | tf_op jit(solution)/shard_map/ppermute | solution.py:43
  51.5 1.9 %collective-permute-start.7 = (bf16[48,5376]{1,0:T(8,128)(2,1)}, bf16[48,5376]{1,0:T(8,128)(2,1)}, u32[]{:S(2)}, u32[]{:S(2)}) collective-permute-start(bf16[48,5376]{1,0:T(8,128)(2,1)} %collective-permute-done.6.refs_9_), channel_id=1, source_target_pairs={{0,128},{1,129},{2,130},{3,131},{4,132},{5,133},{6,134},{7,135},{8... | collective-permute-start | bytes 1548296 | tf_op jit(solution)/shard_map/ppermute | solution.py:43
  53.4 4.6 %collective-permute-start.8 = (bf16[48,5376]{1,0:T(8,128)(2,1)}, bf16[48,5376]{1,0:T(8,128)(2,1)}, u32[]{:S(2)}, u32[]{:S(2)}) collective-permute-start(bf16[48,5376]{1,0:T(8,128)(2,1)} %collective-permute-done.6.refs_9_), channel_id=1, source_target_pairs={{0,384},{1,385},{2,386},{3,387},{4,388},{5,389},{6,390},{7,391},{8... | collective-permute-start | bytes 1548296 | tf_op jit(solution)/shard_map/ppermute | solution.py:43
  58.0 0.2 collective-permute-done.3.refs_6_
  58.2 0.8 copy-done.4
  59.0 5.4 %collective-permute-start.9 = (bf16[48,5376]{1,0:T(8,128)(2,1)}, bf16[48,5376]{1,0:T(8,128)(2,1)}, u32[]{:S(2)}, u32[]{:S(2)}) collective-permute-start(bf16[48,5376]{1,0:T(8,128)(2,1)} %collective-permute-done.5.refs_8_), channel_id=1, source_target_pairs={{0,32},{1,97},{2,34},{3,99},{4,36},{5,101},{6,38},{7,103},{8,40},{... | collective-permute-start | bytes 1548296 | tf_op jit(solution)/shard_map/ppermute | solution.py:43
  64.4 2.6 %collective-permute-start.11 = (bf16[48,5376]{1,0:T(8,128)(2,1)}, bf16[48,5376]{1,0:T(8,128)(2,1)}, u32[]{:S(2)}, u32[]{:S(2)}) collective-permute-start(bf16[48,5376]{1,0:T(8,128)(2,1)} %collective-permute-done.10.refs_13_), channel_id=1, source_target_pairs={{0,128},{1,129},{2,130},{3,131},{4,132},{5,133},{6,134},{7,135},{8... | collective-permute-start | bytes 1548296 | tf_op jit(solution)/shard_map/ppermute | solution.py:43
  67.1 0.8 copy-done.6
  67.9 3.6 %collective-permute-start.1 = (bf16[128,5376]{1,0:T(8,128)(2,1)}, bf16[128,5376]{1,0:T(8,128)(2,1)}, u32[]{:S(2)}, u32[]{:S(2)}) collective-permute-start(bf16[128,5376]{1,0:T(8,128)(2,1)} %all-gather.3.cloned.1.call-done.refs_1_), channel_id=1, source_target_pairs={{0,1},{1,0},{2,3},{3,2},{4,5},{5,4},{6,7},{7,6},{8,9},{9,8},{10,11... | collective-permute-start | bytes 4128776 | tf_op jit(solution)/shard_map/ppermute | solution.py:43
  71.5 25.6 %all-gather.5.cloned.1.call-done.refs_2_ = bf16[128,5376]{1,0:T(8,128)(2,1)} async-done(((bf16[16,5376]{1,0:T(8,128)(2,1)}), bf16[128,5376]{1,0:T(8,128)(2,1)}) %all-gather.5.cloned.1.call-update) | async-done | bytes 1376272 | tf_op jit(solution)/shard_map/all_gather | solution.py:180
  97.1 7.5 %collective-permute-start.2 = (bf16[128,5376]{1,0:T(8,128)(2,1)}, bf16[128,5376]{1,0:T(8,128)(2,1)}, u32[]{:S(2)}, u32[]{:S(2)}) collective-permute-start(bf16[128,5376]{1,0:T(8,128)(2,1)} %all-gather.5.cloned.1.call-done.refs_2_), channel_id=1, source_target_pairs={{0,1},{1,0},{2,3},{3,2},{4,5},{5,4},{6,7},{7,6},{8,9},{9,8},{10,11... | collective-permute-start | bytes 4128776 | tf_op jit(solution)/shard_map/ppermute | solution.py:43
  104.6 5.0 %collective-permute-start.14 = (bf16[48,5376]{1,0:T(8,128)(2,1)}, bf16[48,5376]{1,0:T(8,128)(2,1)}, u32[]{:S(2)}, u32[]{:S(2)}) collective-permute-start(bf16[48,5376]{1,0:T(8,128)(2,1)} %collective-permute-done.10.refs_13_), channel_id=1, source_target_pairs={{0,32},{1,97},{2,34},{3,99},{4,36},{5,101},{6,38},{7,103},{8,40},{... | collective-permute-start | bytes 1548296 | tf_op jit(solution)/shard_map/ppermute | solution.py:43
  109.6 4.2 %collective-permute-start.12 = (bf16[48,5376]{1,0:T(8,128)(2,1)}, bf16[48,5376]{1,0:T(8,128)(2,1)S(1)}, u32[]{:S(2)}, u32[]{:S(2)}) collective-permute-start(bf16[48,5376]{1,0:T(8,128)(2,1)} %collective-permute-done.10.refs_13_), channel_id=1, source_target_pairs={{0,384},{1,385},{2,386},{3,387},{4,388},{5,389},{6,390},{7,391},{8... | collective-permute-start | bytes 1548296 | tf_op jit(solution)/shard_map/ppermute | solution.py:43
  113.8 2.2 %collective-permute-start.13 = (bf16[48,5376]{1,0:T(8,128)(2,1)}, bf16[48,5376]{1,0:T(8,128)(2,1)S(1)}, u32[]{:S(2)}, u32[]{:S(2)}) collective-permute-start(bf16[48,5376]{1,0:T(8,128)(2,1)} %collective-permute-done.9.refs_12_), channel_id=1, source_target_pairs={{0,32},{1,97},{2,34},{3,99},{4,36},{5,101},{6,38},{7,103},{8,40},{... | collective-permute-start | bytes 1548296 | tf_op jit(solution)/shard_map/ppermute | solution.py:43
  116.0 5.4 %collective-permute-done.14.refs_3_ = bf16[48,5376]{1,0:T(8,128)(2,1)} collective-permute-done((bf16[48,5376]{1,0:T(8,128)(2,1)}, bf16[48,5376]{1,0:T(8,128)(2,1)}, u32[]{:S(2)}, u32[]{:S(2)}) %collective-permute-start.14) | collective-permute-done | bytes 516128 | tf_op jit(solution)/shard_map/ppermute | solution.py:43
  121.4 3.0 %collective-permute-start.15 = (bf16[48,5376]{1,0:T(8,128)(2,1)}, bf16[48,5376]{1,0:T(8,128)(2,1)}, u32[]{:S(2)}, u32[]{:S(2)}) collective-permute-start(bf16[48,5376]{1,0:T(8,128)(2,1)} %collective-permute-done.14.refs_3_), channel_id=1, source_target_pairs={{0,128},{1,129},{2,130},{3,131},{4,132},{5,133},{6,134},{7,135},{8... | collective-permute-start | bytes 1548296 | tf_op jit(solution)/shard_map/ppermute | solution.py:43
  124.4 0.2 collective-permute-done.12.refs_15_
  124.6 0.8 copy-done.8
  125.4 5.2 %collective-permute-start.16 = (bf16[48,5376]{1,0:T(8,128)(2,1)}, bf16[48,5376]{1,0:T(8,128)(2,1)}, u32[]{:S(2)}, u32[]{:S(2)}) collective-permute-start(bf16[48,5376]{1,0:T(8,128)(2,1)} %collective-permute-done.14.refs_3_), channel_id=1, source_target_pairs={{0,384},{1,385},{2,386},{3,387},{4,388},{5,389},{6,390},{7,391},{8... | collective-permute-start | bytes 1548296 | tf_op jit(solution)/shard_map/ppermute | solution.py:43
  130.6 0.5 collective-permute-done.13.refs_16_
  131.1 0.8 copy-done.10
  131.9 4.6 %collective-permute-start.17 = (bf16[48,5376]{1,0:T(8,128)(2,1)}, bf16[48,5376]{1,0:T(8,128)(2,1)}, u32[]{:S(2)}, u32[]{:S(2)}) collective-permute-start(bf16[48,5376]{1,0:T(8,128)(2,1)} %collective-permute-done.14.refs_3_), channel_id=1, source_target_pairs={{0,256},{1,257},{2,258},{3,259},{4,260},{5,261},{6,262},{7,263},{8... | collective-permute-start | bytes 1548296 | tf_op jit(solution)/shard_map/ppermute | solution.py:43
  136.5 0.1 copy.7.refs_0_
  136.6 1.3 copy-done.1
  138.0 1.3 copy-done.2
  139.3 1.0 copy-done.5
  140.4 1.0 copy-done.7
  141.4 1.0 copy-done.9
  142.4 1.0 copy-done.11
  143.5 7.8 %shard_map.55 = (bf16[512,768]{1,0:T(8,128)(2,1)S(1)}, bf16[512,5376]{1,0:T(8,128)(2,1)S(1)}) custom-call(f32[512,1]{1,0:T(8,128)S(1)} %copy.7.refs_0_, bf16[128,5376]{1,0:T(8,128)(2,1)S(1)} %copy-done.1, bf16[128,5376]{1,0:T(8,128)(2,1)S(1)} %copy-done.2, bf16[128,5376]{1,0:T(8,128)(2,1)} %collective-permute-done.1.refs_3_, ...), custom_call_target="tpu_custom_call" | custom-call | tf_op jit(solution)/shard_map/pallas_call | solution.py:135
  151.3 1.4 collective-permute-done.16.refs_5_
  152.6 4.5 %shard_map.56 = bf16[512,768]{1,0:T(8,128)(2,1)} custom-call(f32[512,1]{1,0:T(8,128)S(1)} %copy.7.refs_0_, bf16[512,5376]{1,0:T(8,128)(2,1)S(1)} %get-tuple-element.7.refs_1_, bf16[512,768]{1,0:T(8,128)(2,1)S(1)} %get-tuple-element.8.refs_2_, bf16[48,5376]{1,0:T(8,128)(2,1)} %collective-permute-done.14.refs_3_, ...), custom_call_target="tpu_custom_call" | custom-call | tf_op jit(solution)/shard_map/pallas_call | solution.py:135
  (31 shorter events, 0.1 us)
Async XLA Ops:
  6.5 3.0 %copy-start = (bf16[256,5376]{1,0:T(8,128)(2,1)S(1)}, bf16[256,5376]{1,0:T(8,128)(2,1)}, u32[]{:S(2)}) copy-start(bf16[256,5376]{1,0:T(8,128)(2,1)} %param.5) | copy-start | bytes 8257540
  6.5 20.4 %copy-start.3 = (bf16[48,5376]{1,0:T(8,128)(2,1)S(1)}, bf16[48,5376]{1,0:T(8,128)(2,1)}, u32[]{:S(2)}) copy-start(bf16[48,5376]{1,0:T(8,128)(2,1)} %refs_5_.1) | copy-start | bytes 1548292
  6.5 129.9 %copy-start.12 = (f32[1,512]{1,0:T(1,128)S(1)}, f32[1,512]{1,0:T(1,128)}, u32[]{:S(2)}) copy-start(f32[1,512]{1,0:T(1,128)} %param.9) | copy-start | bytes 6148
  6.5 61.3 %all-gather.3.cloned.1.call-start = ((), (), s32[]{:S(2)}) async-start(), calls=%async_computation | async-start | bytes 1548288 | tf_op jit(solution)/shard_map/all_gather | solution.py:177
  11.0 86.1 %all-gather.5.cloned.1.call-start = ((), (), s32[]{:S(2)}) async-start(), calls=%async_computation.1 | async-start | bytes 1548288 | tf_op jit(solution)/shard_map/all_gather | solution.py:180
  11.1 15.1 %collective-permute-start = (bf16[16,5376]{1,0:T(8,128)(2,1)S(1)}, bf16[16,5376]{1,0:T(8,128)(2,1)S(1)}, u32[]{:S(2)}, u32[]{:S(2)}) collective-permute-start(bf16[16,5376]{1,0:T(8,128)(2,1)S(1)} %gather_fusion), channel_id=1, source_target_pairs={{0,16},{1,17},{2,18},{3,19},{4,20},{5,21},{6,22},{7,23},{8,24},{9,... | collective-permute-start | bytes 516104 | tf_op jit(solution)/shard_map/ppermute | solution.py:43
  26.9 10.9 %collective-permute-start.6 = (bf16[48,5376]{1,0:T(8,128)(2,1)S(1)}, bf16[48,5376]{1,0:T(8,128)(2,1)}, u32[]{:S(2)}, u32[]{:S(2)}) collective-permute-start(bf16[48,5376]{1,0:T(8,128)(2,1)S(1)} %copy-done.3), channel_id=1, source_target_pairs={{0,32},{1,97},{2,34},{3,99},{4,36},{5,101},{6,38},{7,103},{8,40},{... | collective-permute-start | bytes 1548296 | tf_op jit(solution)/shard_map/ppermute | solution.py:43
  30.1 23.3 %collective-permute-start.5 = (bf16[48,5376]{1,0:T(8,128)(2,1)S(1)}, bf16[48,5376]{1,0:T(8,128)(2,1)}, u32[]{:S(2)}, u32[]{:S(2)}) collective-permute-start(bf16[48,5376]{1,0:T(8,128)(2,1)S(1)} %copy-done.3), channel_id=1, source_target_pairs={{0,256},{1,257},{2,258},{3,259},{4,260},{5,261},{6,262},{7,263},{8... | collective-permute-start | bytes 1548296 | tf_op jit(solution)/shard_map/ppermute | solution.py:43
  34.7 23.5 %collective-permute-start.3 = (bf16[48,5376]{1,0:T(8,128)(2,1)S(1)}, bf16[48,5376]{1,0:T(8,128)(2,1)S(1)}, u32[]{:S(2)}, u32[]{:S(2)}) collective-permute-start(bf16[48,5376]{1,0:T(8,128)(2,1)S(1)} %copy-done.3), channel_id=1, source_target_pairs={{0,128},{1,129},{2,130},{3,131},{4,132},{5,133},{6,134},{7,135},{8... | collective-permute-start | bytes 1548296 | tf_op jit(solution)/shard_map/ppermute | solution.py:43
  37.8 26.6 %collective-permute-start.10 = (bf16[48,5376]{1,0:T(8,128)(2,1)}, bf16[48,5376]{1,0:T(8,128)(2,1)}, u32[]{:S(2)}, u32[]{:S(2)}) collective-permute-start(bf16[48,5376]{1,0:T(8,128)(2,1)} %collective-permute-done.6.refs_9_), channel_id=1, source_target_pairs={{0,32},{1,97},{2,34},{3,99},{4,36},{5,101},{6,38},{7,103},{8,40},{... | collective-permute-start | bytes 1548296 | tf_op jit(solution)/shard_map/ppermute | solution.py:43
  43.5 23.6 %collective-permute-start.4 = (bf16[48,5376]{1,0:T(8,128)(2,1)S(1)}, bf16[48,5376]{1,0:T(8,128)(2,1)S(1)}, u32[]{:S(2)}, u32[]{:S(2)}) collective-permute-start(bf16[48,5376]{1,0:T(8,128)(2,1)S(1)} %copy-done.3), channel_id=1, source_target_pairs={{0,384},{1,385},{2,386},{3,387},{4,388},{5,389},{6,390},{7,391},{8... | collective-permute-start | bytes 1548296 | tf_op jit(solution)/shard_map/ppermute | solution.py:43
  51.5 20.0 %collective-permute-start.7 = (bf16[48,5376]{1,0:T(8,128)(2,1)}, bf16[48,5376]{1,0:T(8,128)(2,1)}, u32[]{:S(2)}, u32[]{:S(2)}) collective-permute-start(bf16[48,5376]{1,0:T(8,128)(2,1)} %collective-permute-done.6.refs_9_), channel_id=1, source_target_pairs={{0,128},{1,129},{2,130},{3,131},{4,132},{5,133},{6,134},{7,135},{8... | collective-permute-start | bytes 1548296 | tf_op jit(solution)/shard_map/ppermute | solution.py:43
  53.4 51.2 %collective-permute-start.8 = (bf16[48,5376]{1,0:T(8,128)(2,1)}, bf16[48,5376]{1,0:T(8,128)(2,1)}, u32[]{:S(2)}, u32[]{:S(2)}) collective-permute-start(bf16[48,5376]{1,0:T(8,128)(2,1)} %collective-permute-done.6.refs_9_), channel_id=1, source_target_pairs={{0,384},{1,385},{2,386},{3,387},{4,388},{5,389},{6,390},{7,391},{8... | collective-permute-start | bytes 1548296 | tf_op jit(solution)/shard_map/ppermute | solution.py:43
  58.2 0.8 copy-start.4
  59.0 50.6 %collective-permute-start.9 = (bf16[48,5376]{1,0:T(8,128)(2,1)}, bf16[48,5376]{1,0:T(8,128)(2,1)}, u32[]{:S(2)}, u32[]{:S(2)}) collective-permute-start(bf16[48,5376]{1,0:T(8,128)(2,1)} %collective-permute-done.5.refs_8_), channel_id=1, source_target_pairs={{0,32},{1,97},{2,34},{3,99},{4,36},{5,101},{6,38},{7,103},{8,40},{... | collective-permute-start | bytes 1548296 | tf_op jit(solution)/shard_map/ppermute | solution.py:43
  64.4 49.4 %collective-permute-start.11 = (bf16[48,5376]{1,0:T(8,128)(2,1)}, bf16[48,5376]{1,0:T(8,128)(2,1)}, u32[]{:S(2)}, u32[]{:S(2)}) collective-permute-start(bf16[48,5376]{1,0:T(8,128)(2,1)} %collective-permute-done.10.refs_13_), channel_id=1, source_target_pairs={{0,128},{1,129},{2,130},{3,131},{4,132},{5,133},{6,134},{7,135},{8... | collective-permute-start | bytes 1548296 | tf_op jit(solution)/shard_map/ppermute | solution.py:43
  67.1 0.8 copy-start.6
  67.9 68.7 %collective-permute-start.1 = (bf16[128,5376]{1,0:T(8,128)(2,1)}, bf16[128,5376]{1,0:T(8,128)(2,1)}, u32[]{:S(2)}, u32[]{:S(2)}) collective-permute-start(bf16[128,5376]{1,0:T(8,128)(2,1)} %all-gather.3.cloned.1.call-done.refs_1_), channel_id=1, source_target_pairs={{0,1},{1,0},{2,3},{3,2},{4,5},{5,4},{6,7},{7,6},{8,9},{9,8},{10,11... | collective-permute-start | bytes 4128776 | tf_op jit(solution)/shard_map/ppermute | solution.py:43
  97.1 39.5 %collective-permute-start.2 = (bf16[128,5376]{1,0:T(8,128)(2,1)}, bf16[128,5376]{1,0:T(8,128)(2,1)}, u32[]{:S(2)}, u32[]{:S(2)}) collective-permute-start(bf16[128,5376]{1,0:T(8,128)(2,1)} %all-gather.5.cloned.1.call-done.refs_2_), channel_id=1, source_target_pairs={{0,1},{1,0},{2,3},{3,2},{4,5},{5,4},{6,7},{7,6},{8,9},{9,8},{10,11... | collective-permute-start | bytes 4128776 | tf_op jit(solution)/shard_map/ppermute | solution.py:43
  104.6 16.8 %collective-permute-start.14 = (bf16[48,5376]{1,0:T(8,128)(2,1)}, bf16[48,5376]{1,0:T(8,128)(2,1)}, u32[]{:S(2)}, u32[]{:S(2)}) collective-permute-start(bf16[48,5376]{1,0:T(8,128)(2,1)} %collective-permute-done.10.refs_13_), channel_id=1, source_target_pairs={{0,32},{1,97},{2,34},{3,99},{4,36},{5,101},{6,38},{7,103},{8,40},{... | collective-permute-start | bytes 1548296 | tf_op jit(solution)/shard_map/ppermute | solution.py:43
  109.6 15.0 %collective-permute-start.12 = (bf16[48,5376]{1,0:T(8,128)(2,1)}, bf16[48,5376]{1,0:T(8,128)(2,1)S(1)}, u32[]{:S(2)}, u32[]{:S(2)}) collective-permute-start(bf16[48,5376]{1,0:T(8,128)(2,1)} %collective-permute-done.10.refs_13_), channel_id=1, source_target_pairs={{0,384},{1,385},{2,386},{3,387},{4,388},{5,389},{6,390},{7,391},{8... | collective-permute-start | bytes 1548296 | tf_op jit(solution)/shard_map/ppermute | solution.py:43
  113.8 17.2 %collective-permute-start.13 = (bf16[48,5376]{1,0:T(8,128)(2,1)}, bf16[48,5376]{1,0:T(8,128)(2,1)S(1)}, u32[]{:S(2)}, u32[]{:S(2)}) collective-permute-start(bf16[48,5376]{1,0:T(8,128)(2,1)} %collective-permute-done.9.refs_12_), channel_id=1, source_target_pairs={{0,32},{1,97},{2,34},{3,99},{4,36},{5,101},{6,38},{7,103},{8,40},{... | collective-permute-start | bytes 1548296 | tf_op jit(solution)/shard_map/ppermute | solution.py:43
  121.4 29.8 %collective-permute-start.15 = (bf16[48,5376]{1,0:T(8,128)(2,1)}, bf16[48,5376]{1,0:T(8,128)(2,1)}, u32[]{:S(2)}, u32[]{:S(2)}) collective-permute-start(bf16[48,5376]{1,0:T(8,128)(2,1)} %collective-permute-done.14.refs_3_), channel_id=1, source_target_pairs={{0,128},{1,129},{2,130},{3,131},{4,132},{5,133},{6,134},{7,135},{8... | collective-permute-start | bytes 1548296 | tf_op jit(solution)/shard_map/ppermute | solution.py:43
  124.6 0.8 copy-start.8
  125.4 27.3 %collective-permute-start.16 = (bf16[48,5376]{1,0:T(8,128)(2,1)}, bf16[48,5376]{1,0:T(8,128)(2,1)}, u32[]{:S(2)}, u32[]{:S(2)}) collective-permute-start(bf16[48,5376]{1,0:T(8,128)(2,1)} %collective-permute-done.14.refs_3_), channel_id=1, source_target_pairs={{0,384},{1,385},{2,386},{3,387},{4,388},{5,389},{6,390},{7,391},{8... | collective-permute-start | bytes 1548296 | tf_op jit(solution)/shard_map/ppermute | solution.py:43
  131.0 0.8 copy-start.10
  131.9 20.8 %collective-permute-start.17 = (bf16[48,5376]{1,0:T(8,128)(2,1)}, bf16[48,5376]{1,0:T(8,128)(2,1)}, u32[]{:S(2)}, u32[]{:S(2)}) collective-permute-start(bf16[48,5376]{1,0:T(8,128)(2,1)} %collective-permute-done.14.refs_3_), channel_id=1, source_target_pairs={{0,256},{1,257},{2,258},{3,259},{4,260},{5,261},{6,262},{7,263},{8... | collective-permute-start | bytes 1548296 | tf_op jit(solution)/shard_map/ppermute | solution.py:43
  136.6 1.3 copy-start.1
  138.0 1.3 copy-start.2
  139.3 1.0 copy-start.5
  140.4 1.0 copy-start.7
  141.4 1.0 copy-start.9
  142.4 1.0 copy-start.11
Sparse Core Ops, SparseCore 0:
  11.1 43.5 all-gather.2
  56.8 40.2 all-gather.4

commit v10 on v7

--- a/solution.py
+++ b/solution.py
@@ -40,36 +40,18 @@
 ALL_X = tuple((None, x) for x in range(4))
 BLOCKS = (
     *((0, *at) for at in ALL_X),
-    *((step, hop, None) for hop in (0, -1, 1, 2) for step in (1, 2)),
+    *((step, hop, None) for step in (1, 2) for hop in (0, -1, 1, 2)),
     *((3, *at) for at in ALL_X),
 )
-PARTS = 7
+PARTS = 3
 
 
 def send(value, pairs):
     return lax.ppermute(value, AXES, pairs)
 
 
-def spread_kernel(value_ref, out_ref, held, sem):
-    copy = pltpu.make_async_copy(value_ref, held, sem.at[4])
-    copy.start()
-    copy.wait()
-    copies = [pltpu.make_async_copy(held, out_ref.at[i], sem.at[i]) for i in range(4)]
-    for copy in copies:
-        copy.start()
-    for copy in copies:
-        copy.wait()
-
-
 def share(value):
-    copies = pl.pallas_call(
-        spread_kernel,
-        out_shape=jax.ShapeDtypeStruct((4,) + value.shape, value.dtype),
-        in_specs=[pl.BlockSpec(memory_space=pl.ANY)],
-        out_specs=pl.BlockSpec(memory_space=pl.ANY),
-        scratch_shapes=[pltpu.VMEM(value.shape, value.dtype), pltpu.SemaphoreType.DMA((5,))],
-        name="spread",
-    )(value)
+    copies = jnp.broadcast_to(value[None], (4,) + value.shape)
     return lax.all_to_all(copies, "prompt", 0, 0, axis_index_groups=ROWS_X, tiled=True)
 
 
@@ -108,7 +90,7 @@
 
 
 def product_kernel(n_sources, act_ref, *refs):
-    operands, (out_ref, rows, cols, acc, order, act, sem) = refs[:-7], refs[-7:]
+    operands, (out_ref, rows, cols, acc, order, natural, act, sem) = refs[:-8], refs[-8:]
     sources, targets = operands[:n_sources], operands[n_sources:]
     width = rows.shape[1] // PARTS
 
@@ -133,15 +115,16 @@
             copy.start()
 
     x, y, half, z, core = place()
-    slots = act_ref.shape[0] // 32
+    slots = act_ref.shape[1] // 32
     row_at = []
     for side in range(2):
         for hop in HOPS_Z:
             for flip in range(2):
                 feat = ((half ^ flip) * 8 + ((z + hop) & 7)) * 2 + (core ^ side)
                 row_at.append(pl.multiple_of(feat * slots, slots))
+    natural[...] = jnp.broadcast_to(act_ref[...], (128, act_ref.shape[1])).T
     for g, at in enumerate(row_at):
-        act[g * slots : (g + 1) * slots] = act_ref[pl.ds(at, slots)]
+        act[g * slots : (g + 1) * slots] = natural[pl.ds(at, slots), :1]
     block = out_ref.shape[1] // 16
     lane = lax.broadcasted_iota(jnp.int32, (block, out_ref.shape[1]), 1)
     line = lax.broadcasted_iota(jnp.int32, (block, out_ref.shape[1]), 0)
@@ -169,7 +152,7 @@
 
 def product(act, sources, targets):
     depth = targets[0].shape[1]
-    n_rows, n_cols = act.shape[0], sum(t.shape[0] for t in targets)
+    n_rows, n_cols = act.shape[1], sum(t.shape[0] for t in targets)
     whole, anywhere = pl.BlockSpec(memory_space=pltpu.VMEM), pl.BlockSpec(memory_space=pltpu.HBM)
     return pl.pallas_call(
         functools.partial(product_kernel, len(sources)),
@@ -181,6 +164,7 @@
             pltpu.VMEM((n_cols, depth), jnp.bfloat16),
             pltpu.VMEM((n_rows, n_cols), jnp.float32),
             pltpu.VMEM((n_cols, n_cols), jnp.bfloat16),
+            pltpu.VMEM((n_rows, 128), jnp.float32),
             pltpu.VMEM((n_rows, 1), jnp.float32),
             pltpu.SemaphoreType.DMA((PARTS, len(sources) + len(targets))),
         ],
@@ -205,8 +189,8 @@
     y3 = send(y2, RING_Y)
     width = y0.shape[0]
     aa, dd = share(y0), share(y3)
-    both = jnp.concatenate([y1, y2], axis=0)
-    m1, m2 = send(both, UP_X), send(both, DOWN_X)
+    b1, b2 = send(y1, UP_X), send(y1, DOWN_X)
+    c1, c2 = send(y2, UP_X), send(y2, DOWN_X)
     far = lax.dynamic_index_in_dim(aa, (lax.axis_index("prompt") // 4 + 2) % 4, 0, keepdims=False)
     f1 = send(far, RING_Y)
     f2 = send(f1, RING_Y)
@@ -221,8 +205,8 @@
     away = stack(u3, w3, u4)
     sources = [own, u1, w1, u2, w2, u3, w3, u4, send(near, CORE), send(away, CORE)]
 
-    targets = [aa.reshape(4 * width, -1), y1, y2, m1, m2, f1, f2, dd.reshape(4 * width, -1)]
-    return product(activity.reshape(-1, 1), sources, targets)[None]
+    targets = [aa.reshape(4 * width, -1), y1, b1, b2, f1, y2, c1, c2, f2, dd.reshape(4 * width, -1)]
+    return product(activity, sources, targets)[None]
 
 
 def solution(mesh):

time: 151 us -> 152 us (level)
  starting transfers between devices: 81.4 us -> 87.1 us
  Pallas kernels: 19.3 us -> 13.7 us
  local copies, waits for them, and re-layouts: 11 us -> 15.3 us
  waiting for transfers between devices: 35.2 us -> 31.2 us
    ppermute x17 -> x19, starting transfers between devices: 72.1 us -> 78.2 us  [send(): return lax.ppermute(value, AXES, pairs)]
    broadcast_in_dim x0 -> x2, local copies, waits for them, and re-layouts: none -> 4.98 us  [share(): copies = jnp.broadcast_to(value[None], (4,) + value.shape)]
    pallas_call x2 -> x0, Pallas kernels: 4.79 us -> none  [share(): pl.pallas_call(spread_kernel, out_shape=jax.ShapeDtypeStruct((4,) + value...]
    all_to_all x2, waiting for transfers between devices: 3.34 us -> 0.01 us  [share(): lax.all_to_all(copies, 'prompt', 0, 0, axis_index_groups=ROWS_X, tiled=True)]
    concatenate x1 -> x0, local copies, waits for them, and re-layouts: 1.88 us -> none  [edges_of(): both = jnp.concatenate([y1, y2], axis=0)]
    unnamed x27 -> x28, local copies, waits for them, and re-layouts: 6.52 us -> 7.77 us
    ppermute x17 -> x19, waiting for transfers between devices: 31.9 us -> 31.2 us  [send(): return lax.ppermute(value, AXES, pairs)]
  transfers between devices with their start and end apart: 19 -> 21, of which waited for: 6 -> 5; matrix products, arithmetic and copies ran while one was open for 4% -> 5% of each run, Pallas kernels for 6% -> 3%
where the time goes in v10:
time: 152 us; the launch traced here: 151 us
  starting transfers between devices  87.1 us (57%)
  waiting for transfers between devices  31.2 us (21%)
  local copies, waits for them, and re-layouts  15.3 us (10%)
  Pallas kernels  13.7 us (9%)
  other arithmetic  2.87 us (2%)
    ppermute x19, starting transfers between devices, send(): return lax.ppermute(value, AXES, pairs)  78.2 us
    ppermute x19, waiting for transfers between devices, send(): return lax.ppermute(value, AXES, pairs)  31.2 us
    pallas_call x1, Pallas kernels, product(): pl.pallas_call(functools.partial(product_kernel, len(sources)), out_shape...  9.35 us
    all_to_all x2, starting transfers between devices, share(): lax.all_to_all(copies, 'prompt', 0, 0, axis_index_groups=ROWS_X, tiled=True)  8.9 us
    unnamed x28, local copies, waits for them, and re-layouts  7.77 us
    broadcast_in_dim x2, local copies, waits for them, and re-layouts, share(): copies = jnp.broadcast_to(value[None], (4,) + value.shape)  4.98 us
    pallas_call x2, Pallas kernels, stack(): pl.pallas_call(stack_kernel, out_shape=jax.ShapeDtypeStruct(shape, pieces...  4.32 us
  transfers between devices with their start and end apart: 21, of which 5 were waited for; matrix products, arithmetic and copies ran while one was open for 5% of the time, Pallas kernels for 3%

profile of v10, /device:TPU:1, one launch (start us, length us, event | category | flops | bytes accessed | tf_op | source)
XLA Modules:
  0.0 150.6 jit_solution(16426061125748632643)
XLA Ops:
  0.0 1.4 fusion
  1.4 0.6 iota_compare_fusion
  2.1 0.7 fusion.1
  2.8 0.7 gather_fusion
  3.4 0.1 broadcast_select_fusion
  3.5 8.3 %collective-permute-start = (bf16[16,5376]{1,0:T(8,128)(2,1)S(1)}, bf16[16,5376]{1,0:T(8,128)(2,1)S(1)}, u32[]{:S(2)}, u32[]{:S(2)}) collective-permute-start(bf16[16,5376]{1,0:T(8,128)(2,1)S(1)} %broadcast_select_fusion), channel_id=1, source_target_pairs={{0,16},{1,17},{2,18},{3,19},{4,20},{5,21},{6,22},{7,23},{8,24},{9,... | collective-permute-start | bytes 516104 | tf_op jit(solution)/shard_map/ppermute | solution.py:50
  11.8 2.5 %collective-permute-start.10 = (bf16[48,5376]{1,0:T(8,128)(2,1)}, bf16[48,5376]{1,0:T(8,128)(2,1)}, u32[]{:S(2)}, u32[]{:S(2)}) collective-permute-start(bf16[48,5376]{1,0:T(8,128)(2,1)} %param.6), channel_id=1, source_target_pairs={{0,32},{1,97},{2,34},{3,99},{4,36},{5,101},{6,38},{7,103},{8,40},{... | collective-permute-start | bytes 1548296 | tf_op jit(solution)/shard_map/ppermute | solution.py:50
  14.3 2.5 %broadcast_in_dim.36 = bf16[4,48,5376]{2,1,0:T(8,128)(2,1)} broadcast(bf16[48,5376]{1,0:T(8,128)(2,1)} %param.6), dimensions={1,2} | broadcast | bytes 2580480 | tf_op jit(solution)/shard_map/broadcast_in_dim | solution.py:54
  16.8 4.4 %all-to-all-start = ((bf16[4,48,5376]{2,1,0:T(8,128)(2,1)}), bf16[4,48,5376]{2,1,0:T(8,128)(2,1)}, u32[]{:S(2)}, u32[]{:S(2)}) async-start(bf16[4,48,5376]{2,1,0:T(8,128)(2,1)} %broadcast_in_dim.36), calls=%async_computation | async-start | bytes 4128768 | tf_op jit(solution)/shard_map/all_to_all | solution.py:55
  21.3 0.0 collective-permute-done
  21.3 4.0 %collective-permute-start.1 = (bf16[32,5376]{1,0:T(8,128)(2,1)S(1)}, bf16[32,5376]{1,0:T(8,128)(2,1)S(1)}, u32[]{:S(2)}, u32[]{:S(2)}) collective-permute-start(bf16[32,5376]{1,0:T(8,128)(2,1)S(1)} %pad_maximum_fusion.refs_0_), channel_id=1, source_target_pairs={{0,2},{1,3},{2,4},{3,5},{4,6},{5,7},{6,8},{7,9},{8,10},{9,11},{10,... | collective-permute-start | bytes 1032200 | tf_op jit(solution)/shard_map/ppermute | solution.py:50
  25.3 6.1 %collective-permute-done.10.refs_11_ = bf16[48,5376]{1,0:T(8,128)(2,1)} collective-permute-done((bf16[48,5376]{1,0:T(8,128)(2,1)}, bf16[48,5376]{1,0:T(8,128)(2,1)}, u32[]{:S(2)}, u32[]{:S(2)}) %collective-permute-start.10) | collective-permute-done | bytes 516128 | tf_op jit(solution)/shard_map/ppermute | solution.py:50
  31.4 4.0 %collective-permute-start.14 = (bf16[48,5376]{1,0:T(8,128)(2,1)}, bf16[48,5376]{1,0:T(8,128)(2,1)}, u32[]{:S(2)}, u32[]{:S(2)}) collective-permute-start(bf16[48,5376]{1,0:T(8,128)(2,1)} %collective-permute-done.10.refs_11_), channel_id=1, source_target_pairs={{0,32},{1,97},{2,34},{3,99},{4,36},{5,101},{6,38},{7,103},{8,40},{... | collective-permute-start | bytes 1548296 | tf_op jit(solution)/shard_map/ppermute | solution.py:50
  35.5 10.7 %collective-permute-start.2 = (bf16[32,5376]{1,0:T(8,128)(2,1)S(1)}, bf16[32,5376]{1,0:T(8,128)(2,1)}, u32[]{:S(2)}, u32[]{:S(2)}) collective-permute-start(bf16[32,5376]{1,0:T(8,128)(2,1)S(1)} %pad_maximum_fusion.refs_0_), channel_id=1, source_target_pairs={{0,14},{1,15},{2,0},{3,1},{4,2},{5,3},{6,4},{7,5},{8,6},{9,7},{10,... | collective-permute-start | bytes 1032200 | tf_op jit(solution)/shard_map/ppermute | solution.py:50
  46.1 0.0 collective-permute-done.1.refs_1_
  46.1 1.9 %collective-permute-start.3 = (bf16[32,5376]{1,0:T(8,128)(2,1)S(1)}, bf16[32,5376]{1,0:T(8,128)(2,1)}, u32[]{:S(2)}, u32[]{:S(2)}) collective-permute-start(bf16[32,5376]{1,0:T(8,128)(2,1)S(1)} %collective-permute-done.1.refs_1_), channel_id=1, source_target_pairs={{0,2},{1,3},{2,4},{3,5},{4,6},{5,7},{6,8},{7,9},{8,10},{9,11},{10,... | collective-permute-start | bytes 1032200 | tf_op jit(solution)/shard_map/ppermute | solution.py:50
  48.1 4.4 %collective-permute-start.18 = (bf16[48,5376]{1,0:T(8,128)(2,1)}, bf16[48,5376]{1,0:T(8,128)(2,1)}, u32[]{:S(2)}, u32[]{:S(2)}) collective-permute-start(bf16[48,5376]{1,0:T(8,128)(2,1)} %collective-permute-done.14.refs_15_), channel_id=1, source_target_pairs={{0,32},{1,97},{2,34},{3,99},{4,36},{5,101},{6,38},{7,103},{8,40},{... | collective-permute-start | bytes 1548296 | tf_op jit(solution)/shard_map/ppermute | solution.py:50
  52.5 0.8 collective-permute-done.2.refs_2_
  53.3 9.9 %collective-permute-start.4 = (bf16[32,5376]{1,0:T(8,128)(2,1)}, bf16[32,5376]{1,0:T(8,128)(2,1)}, u32[]{:S(2)}, u32[]{:S(2)}) collective-permute-start(bf16[32,5376]{1,0:T(8,128)(2,1)} %collective-permute-done.2.refs_2_), channel_id=1, source_target_pairs={{0,14},{1,15},{2,0},{3,1},{4,2},{5,3},{6,4},{7,5},{8,6},{9,7},{10,... | collective-permute-start | bytes 1032200 | tf_op jit(solution)/shard_map/ppermute | solution.py:50
  63.2 1.9 %collective-permute-start.5 = (bf16[32,5376]{1,0:T(8,128)(2,1)}, bf16[32,5376]{1,0:T(8,128)(2,1)}, u32[]{:S(2)}, u32[]{:S(2)}) collective-permute-start(bf16[32,5376]{1,0:T(8,128)(2,1)} %collective-permute-done.3.refs_3_), channel_id=1, source_target_pairs={{0,2},{1,3},{2,4},{3,5},{4,6},{5,7},{6,8},{7,9},{8,10},{9,11},{10,... | collective-permute-start | bytes 1032200 | tf_op jit(solution)/shard_map/ppermute | solution.py:50
  65.2 6.2 %collective-permute-done.4.refs_4_ = bf16[32,5376]{1,0:T(8,128)(2,1)} collective-permute-done((bf16[32,5376]{1,0:T(8,128)(2,1)}, bf16[32,5376]{1,0:T(8,128)(2,1)}, u32[]{:S(2)}, u32[]{:S(2)}) %collective-permute-start.4) | collective-permute-done | bytes 344096 | tf_op jit(solution)/shard_map/ppermute | solution.py:50
  71.4 2.3 %shard_map.55 = bf16[160,5376]{1,0:T(8,128)(2,1)} custom-call(bf16[32,5376]{1,0:T(8,128)(2,1)} %copy-done.1, bf16[32,5376]{1,0:T(8,128)(2,1)} %copy-done.3, bf16[32,5376]{1,0:T(8,128)(2,1)} %collective-permute-done.2.refs_2_, bf16[32,5376]{1,0:T(8,128)(2,1)} %collective-permute-done.3.refs_3_, bf16[32,5376]{1,0:T(8,128)(2,1)} %collective-permute-done.4.refs_4_), custom_call_target="tpu_custom_call" | custom-call | tf_op jit(solution)/shard_map/pallas_call | solution.py:77
  73.7 2.3 %collective-permute-start.8 = (bf16[160,5376]{1,0:T(8,128)(2,1)}, bf16[160,5376]{1,0:T(8,128)(2,1)}, u32[]{:S(2)}, u32[]{:S(2)}) collective-permute-start(bf16[160,5376]{1,0:T(8,128)(2,1)} %shard_map.55), channel_id=1, source_target_pairs={{0,1},{1,0},{2,3},{3,2},{4,5},{5,4},{6,7},{7,6},{8,9},{9,8},{10,11... | collective-permute-start | bytes 5160968 | tf_op jit(solution)/shard_map/ppermute | solution.py:50
  76.1 3.1 %collective-permute-start.11 = (bf16[48,5376]{1,0:T(8,128)(2,1)}, bf16[48,5376]{1,0:T(8,128)(2,1)}, u32[]{:S(2)}, u32[]{:S(2)}) collective-permute-start(bf16[48,5376]{1,0:T(8,128)(2,1)} %collective-permute-done.10.refs_11_), channel_id=1, source_target_pairs={{0,128},{1,129},{2,130},{3,131},{4,132},{5,133},{6,134},{7,135},{8... | collective-permute-start | bytes 1548296 | tf_op jit(solution)/shard_map/ppermute | solution.py:50
  79.2 3.4 %collective-permute-start.12 = (bf16[48,5376]{1,0:T(8,128)(2,1)}, bf16[48,5376]{1,0:T(8,128)(2,1)}, u32[]{:S(2)}, u32[]{:S(2)}) collective-permute-start(bf16[48,5376]{1,0:T(8,128)(2,1)} %collective-permute-done.10.refs_11_), channel_id=1, source_target_pairs={{0,384},{1,385},{2,386},{3,387},{4,388},{5,389},{6,390},{7,391},{8... | collective-permute-start | bytes 1548296 | tf_op jit(solution)/shard_map/ppermute | solution.py:50
  82.6 5.3 %collective-permute-start.6 = (bf16[32,5376]{1,0:T(8,128)(2,1)}, bf16[32,5376]{1,0:T(8,128)(2,1)}, u32[]{:S(2)}, u32[]{:S(2)}) collective-permute-start(bf16[32,5376]{1,0:T(8,128)(2,1)} %collective-permute-done.4.refs_4_), channel_id=1, source_target_pairs={{0,14},{1,15},{2,0},{3,1},{4,2},{5,3},{6,4},{7,5},{8,6},{9,7},{10,... | collective-permute-start | bytes 1032200 | tf_op jit(solution)/shard_map/ppermute | solution.py:50
  87.9 1.9 %collective-permute-start.7 = (bf16[32,5376]{1,0:T(8,128)(2,1)}, bf16[32,5376]{1,0:T(8,128)(2,1)}, u32[]{:S(2)}, u32[]{:S(2)}) collective-permute-start(bf16[32,5376]{1,0:T(8,128)(2,1)} %collective-permute-done.5.refs_0_.refs_5_), channel_id=1, source_target_pairs={{0,2},{1,3},{2,4},{3,5},{4,6},{5,7},{6,8},{7,9},{8,10},{9,11},{10,... | collective-permute-start | bytes 1032200 | tf_op jit(solution)/shard_map/ppermute | solution.py:50
  89.9 2.5 %broadcast_in_dim.37 = bf16[4,48,5376]{2,1,0:T(8,128)(2,1)} broadcast(bf16[48,5376]{1,0:T(8,128)(2,1)} %collective-permute-done.18), dimensions={1,2} | broadcast | bytes 2580480 | tf_op jit(solution)/shard_map/broadcast_in_dim | solution.py:54
  92.4 4.5 %all-to-all-start.1 = ((bf16[4,48,5376]{2,1,0:T(8,128)(2,1)}), bf16[4,48,5376]{2,1,0:T(8,128)(2,1)}, u32[]{:S(2)}, u32[]{:S(2)}) async-start(bf16[4,48,5376]{2,1,0:T(8,128)(2,1)} %broadcast_in_dim.37), calls=%async_computation.1 | async-start | bytes 4128768 | tf_op jit(solution)/shard_map/all_to_all | solution.py:55
  96.9 0.0 copy-start.13
  96.9 1.9 %dynamic-slice_bitcast_fusion = bf16[48,5376]{1,0:T(8,128)(2,1)} fusion(bf16[4,48,5376]{2,1,0:T(8,128)(2,1)} %all-to-all-done, s32[]{:T(128)S(6)} %select_n.38), kind=kLoop, calls=%fused_computation.1 | loop fusion | bytes 1032196 | tf_op jit(solution)/shard_map/jit(dynamic_index_in_dim)/squeeze | solution.py:194
  98.8 1.9 %collective-permute-start.13 = (bf16[48,5376]{1,0:T(8,128)(2,1)}, bf16[48,5376]{1,0:T(8,128)(2,1)}, u32[]{:S(2)}, u32[]{:S(2)}) collective-permute-start(bf16[48,5376]{1,0:T(8,128)(2,1)} %dynamic-slice_bitcast_fusion), channel_id=1, source_target_pairs={{0,32},{1,97},{2,34},{3,99},{4,36},{5,101},{6,38},{7,103},{8,40},{... | collective-permute-start | bytes 1548296 | tf_op jit(solution)/shard_map/ppermute | solution.py:50
  100.7 2.0 %shard_map.56 = bf16[96,5376]{1,0:T(8,128)(2,1)} custom-call(bf16[32,5376]{1,0:T(8,128)(2,1)} %collective-permute-done.5.refs_0_.refs_5_, bf16[32,5376]{1,0:T(8,128)(2,1)} %collective-permute-done.6.refs_1_.refs_6_, bf16[32,5376]{1,0:T(8,128)(2,1)} %collective-permute-done.7.refs_2_.refs_7_), custom_call_target="tpu_custom_call" | custom-call | tf_op jit(solution)/shard_map/pallas_call | solution.py:77
  102.8 3.0 %collective-permute-start.9 = (bf16[96,5376]{1,0:T(8,128)(2,1)}, bf16[96,5376]{1,0:T(8,128)(2,1)S(1)}, u32[]{:S(2)}, u32[]{:S(2)}) collective-permute-start(bf16[96,5376]{1,0:T(8,128)(2,1)} %shard_map.56), channel_id=1, source_target_pairs={{0,1},{1,0},{2,3},{3,2},{4,5},{5,4},{6,7},{7,6},{8,9},{9,8},{10,11... | collective-permute-start | bytes 3096584 | tf_op jit(solution)/shard_map/ppermute | solution.py:50
  105.8 3.4 %collective-permute-start.15 = (bf16[48,5376]{1,0:T(8,128)(2,1)}, bf16[48,5376]{1,0:T(8,128)(2,1)S(1)}, u32[]{:S(2)}, u32[]{:S(2)}) collective-permute-start(bf16[48,5376]{1,0:T(8,128)(2,1)} %collective-permute-done.14.refs_15_), channel_id=1, source_target_pairs={{0,128},{1,129},{2,130},{3,131},{4,132},{5,133},{6,134},{7,135},{8... | collective-permute-start | bytes 1548296 | tf_op jit(solution)/shard_map/ppermute | solution.py:50
  109.2 3.1 %collective-permute-start.16 = (bf16[48,5376]{1,0:T(8,128)(2,1)}, bf16[48,5376]{1,0:T(8,128)(2,1)S(1)}, u32[]{:S(2)}, u32[]{:S(2)}) collective-permute-start(bf16[48,5376]{1,0:T(8,128)(2,1)} %collective-permute-done.14.refs_15_), channel_id=1, source_target_pairs={{0,384},{1,385},{2,386},{3,387},{4,388},{5,389},{6,390},{7,391},{8... | collective-permute-start | bytes 1548296 | tf_op jit(solution)/shard_map/ppermute | solution.py:50
  112.4 2.4 %collective-permute-done.13.refs_14_ = bf16[48,5376]{1,0:T(8,128)(2,1)} collective-permute-done((bf16[48,5376]{1,0:T(8,128)(2,1)}, bf16[48,5376]{1,0:T(8,128)(2,1)}, u32[]{:S(2)}, u32[]{:S(2)}) %collective-permute-start.13) | collective-permute-done | bytes 516128 | tf_op jit(solution)/shard_map/ppermute | solution.py:50
  114.8 3.0 %collective-permute-start.17 = (bf16[48,5376]{1,0:T(8,128)(2,1)}, bf16[48,5376]{1,0:T(8,128)(2,1)S(1)}, u32[]{:S(2)}, u32[]{:S(2)}) collective-permute-start(bf16[48,5376]{1,0:T(8,128)(2,1)} %collective-permute-done.13.refs_14_), channel_id=1, source_target_pairs={{0,32},{1,97},{2,34},{3,99},{4,36},{5,101},{6,38},{7,103},{8,40},{... | collective-permute-start | bytes 1548296 | tf_op jit(solution)/shard_map/ppermute | solution.py:50
  117.8 15.7 %collective-permute-done.15.refs_16_ = bf16[48,5376]{1,0:T(8,128)(2,1)S(1)} collective-permute-done((bf16[48,5376]{1,0:T(8,128)(2,1)}, bf16[48,5376]{1,0:T(8,128)(2,1)S(1)}, u32[]{:S(2)}, u32[]{:S(2)}) %collective-permute-start.15) | collective-permute-done | bytes 516128 | tf_op jit(solution)/shard_map/ppermute | solution.py:50
  133.5 0.8 copy-done.7
  134.3 0.8 copy-done.9
  135.1 0.8 copy-done.11
  135.9 1.0 copy-done.5
  137.0 1.2 copy-done.6
  138.2 1.0 copy-done.8
  139.2 1.0 copy-done.10
  140.2 1.0 copy-done.12
  141.3 9.3 %product.1 = bf16[512,768]{1,0:T(8,128)(2,1)} custom-call(f32[1,512]{1,0:T(1,128)S(1)} %copy-done.13, bf16[32,5376]{1,0:T(8,128)(2,1)S(1)} %copy-done.2, bf16[32,5376]{1,0:T(8,128)(2,1)S(1)} %copy-done.4, bf16[32,5376]{1,0:T(8,128)(2,1)} %collective-permute-done.2.refs_2_, bf16[32,5376]{1,0:T(8,128)(2,1)} %collective-permute-done.3.refs_3_, ...), custom_call_target="tpu_custom_call" | custom-call | tf_op jit(solution)/shard_map/product/pallas_call | solution.py:157
  (35 shorter events, 0.1 us)
Async XLA Ops:
  0.0 2.8 %copy-start = (bf16[256,5376]{1,0:T(8,128)(2,1)S(1)}, bf16[256,5376]{1,0:T(8,128)(2,1)}, u32[]{:S(2)}) copy-start(bf16[256,5376]{1,0:T(8,128)(2,1)} %param.5) | copy-start | bytes 8257540
  3.5 17.7 %collective-permute-start = (bf16[16,5376]{1,0:T(8,128)(2,1)S(1)}, bf16[16,5376]{1,0:T(8,128)(2,1)S(1)}, u32[]{:S(2)}, u32[]{:S(2)}) collective-permute-start(bf16[16,5376]{1,0:T(8,128)(2,1)S(1)} %broadcast_select_fusion), channel_id=1, source_target_pairs={{0,16},{1,17},{2,18},{3,19},{4,20},{5,21},{6,22},{7,23},{8,24},{9,... | collective-permute-start | bytes 516104 | tf_op jit(solution)/shard_map/ppermute | solution.py:50
  11.8 19.6 %collective-permute-start.10 = (bf16[48,5376]{1,0:T(8,128)(2,1)}, bf16[48,5376]{1,0:T(8,128)(2,1)}, u32[]{:S(2)}, u32[]{:S(2)}) collective-permute-start(bf16[48,5376]{1,0:T(8,128)(2,1)} %param.6), channel_id=1, source_target_pairs={{0,32},{1,97},{2,34},{3,99},{4,36},{5,101},{6,38},{7,103},{8,40},{... | collective-permute-start | bytes 1548296 | tf_op jit(solution)/shard_map/ppermute | solution.py:50
  16.8 73.0 %all-to-all-start = ((bf16[4,48,5376]{2,1,0:T(8,128)(2,1)}), bf16[4,48,5376]{2,1,0:T(8,128)(2,1)}, u32[]{:S(2)}, u32[]{:S(2)}) async-start(bf16[4,48,5376]{2,1,0:T(8,128)(2,1)} %broadcast_in_dim.36), calls=%async_computation | async-start | bytes 4128768 | tf_op jit(solution)/shard_map/all_to_all | solution.py:55
  21.3 50.1 %copy-start.1 = (bf16[32,5376]{1,0:T(8,128)(2,1)}, bf16[32,5376]{1,0:T(8,128)(2,1)S(1)}, u32[]{:S(2)}) copy-start(bf16[32,5376]{1,0:T(8,128)(2,1)S(1)} %pad_maximum_fusion.refs_0_) | copy-start | bytes 1032196
  21.3 24.8 %collective-permute-start.1 = (bf16[32,5376]{1,0:T(8,128)(2,1)S(1)}, bf16[32,5376]{1,0:T(8,128)(2,1)S(1)}, u32[]{:S(2)}, u32[]{:S(2)}) collective-permute-start(bf16[32,5376]{1,0:T(8,128)(2,1)S(1)} %pad_maximum_fusion.refs_0_), channel_id=1, source_target_pairs={{0,2},{1,3},{2,4},{3,5},{4,6},{5,7},{6,8},{7,9},{8,10},{9,11},{10,... | collective-permute-start | bytes 1032200 | tf_op jit(solution)/shard_map/ppermute | solution.py:50
  31.4 16.7 %collective-permute-start.14 = (bf16[48,5376]{1,0:T(8,128)(2,1)}, bf16[48,5376]{1,0:T(8,128)(2,1)}, u32[]{:S(2)}, u32[]{:S(2)}) collective-permute-start(bf16[48,5376]{1,0:T(8,128)(2,1)} %collective-permute-done.10.refs_11_), channel_id=1, source_target_pairs={{0,32},{1,97},{2,34},{3,99},{4,36},{5,101},{6,38},{7,103},{8,40},{... | collective-permute-start | bytes 1548296 | tf_op jit(solution)/shard_map/ppermute | solution.py:50
  35.5 17.9 %collective-permute-start.2 = (bf16[32,5376]{1,0:T(8,128)(2,1)S(1)}, bf16[32,5376]{1,0:T(8,128)(2,1)}, u32[]{:S(2)}, u32[]{:S(2)}) collective-permute-start(bf16[32,5376]{1,0:T(8,128)(2,1)S(1)} %pad_maximum_fusion.refs_0_), channel_id=1, source_target_pairs={{0,14},{1,15},{2,0},{3,1},{4,2},{5,3},{6,4},{7,5},{8,6},{9,7},{10,... | collective-permute-start | bytes 1032200 | tf_op jit(solution)/shard_map/ppermute | solution.py:50
  46.1 25.3 %copy-start.3 = (bf16[32,5376]{1,0:T(8,128)(2,1)}, bf16[32,5376]{1,0:T(8,128)(2,1)S(1)}, u32[]{:S(2)}) copy-start(bf16[32,5376]{1,0:T(8,128)(2,1)S(1)} %collective-permute-done.1.refs_1_) | copy-start | bytes 1032196
  46.1 17.1 %collective-permute-start.3 = (bf16[32,5376]{1,0:T(8,128)(2,1)S(1)}, bf16[32,5376]{1,0:T(8,128)(2,1)}, u32[]{:S(2)}, u32[]{:S(2)}) collective-permute-start(bf16[32,5376]{1,0:T(8,128)(2,1)S(1)} %collective-permute-done.1.refs_1_), channel_id=1, source_target_pairs={{0,2},{1,3},{2,4},{3,5},{4,6},{5,7},{6,8},{7,9},{8,10},{9,11},{10,... | collective-permute-start | bytes 1032200 | tf_op jit(solution)/shard_map/ppermute | solution.py:50
  48.1 39.8 %collective-permute-start.18 = (bf16[48,5376]{1,0:T(8,128)(2,1)}, bf16[48,5376]{1,0:T(8,128)(2,1)}, u32[]{:S(2)}, u32[]{:S(2)}) collective-permute-start(bf16[48,5376]{1,0:T(8,128)(2,1)} %collective-permute-done.14.refs_15_), channel_id=1, source_target_pairs={{0,32},{1,97},{2,34},{3,99},{4,36},{5,101},{6,38},{7,103},{8,40},{... | collective-permute-start | bytes 1548296 | tf_op jit(solution)/shard_map/ppermute | solution.py:50
  53.3 18.1 %collective-permute-start.4 = (bf16[32,5376]{1,0:T(8,128)(2,1)}, bf16[32,5376]{1,0:T(8,128)(2,1)}, u32[]{:S(2)}, u32[]{:S(2)}) collective-permute-start(bf16[32,5376]{1,0:T(8,128)(2,1)} %collective-permute-done.2.refs_2_), channel_id=1, source_target_pairs={{0,14},{1,15},{2,0},{3,1},{4,2},{5,3},{6,4},{7,5},{8,6},{9,7},{10,... | collective-permute-start | bytes 1032200 | tf_op jit(solution)/shard_map/ppermute | solution.py:50
  63.2 19.3 %collective-permute-start.5 = (bf16[32,5376]{1,0:T(8,128)(2,1)}, bf16[32,5376]{1,0:T(8,128)(2,1)}, u32[]{:S(2)}, u32[]{:S(2)}) collective-permute-start(bf16[32,5376]{1,0:T(8,128)(2,1)} %collective-permute-done.3.refs_3_), channel_id=1, source_target_pairs={{0,2},{1,3},{2,4},{3,5},{4,6},{5,7},{6,8},{7,9},{8,10},{9,11},{10,... | collective-permute-start | bytes 1032200 | tf_op jit(solution)/shard_map/ppermute | solution.py:50
  73.7 62.1 %collective-permute-start.8 = (bf16[160,5376]{1,0:T(8,128)(2,1)}, bf16[160,5376]{1,0:T(8,128)(2,1)}, u32[]{:S(2)}, u32[]{:S(2)}) collective-permute-start(bf16[160,5376]{1,0:T(8,128)(2,1)} %shard_map.55), channel_id=1, source_target_pairs={{0,1},{1,0},{2,3},{3,2},{4,5},{5,4},{6,7},{7,6},{8,9},{9,8},{10,11... | collective-permute-start | bytes 5160968 | tf_op jit(solution)/shard_map/ppermute | solution.py:50
  76.1 29.7 %collective-permute-start.11 = (bf16[48,5376]{1,0:T(8,128)(2,1)}, bf16[48,5376]{1,0:T(8,128)(2,1)}, u32[]{:S(2)}, u32[]{:S(2)}) collective-permute-start(bf16[48,5376]{1,0:T(8,128)(2,1)} %collective-permute-done.10.refs_11_), channel_id=1, source_target_pairs={{0,128},{1,129},{2,130},{3,131},{4,132},{5,133},{6,134},{7,135},{8... | collective-permute-start | bytes 1548296 | tf_op jit(solution)/shard_map/ppermute | solution.py:50
  79.2 30.0 %collective-permute-start.12 = (bf16[48,5376]{1,0:T(8,128)(2,1)}, bf16[48,5376]{1,0:T(8,128)(2,1)}, u32[]{:S(2)}, u32[]{:S(2)}) collective-permute-start(bf16[48,5376]{1,0:T(8,128)(2,1)} %collective-permute-done.10.refs_11_), channel_id=1, source_target_pairs={{0,384},{1,385},{2,386},{3,387},{4,388},{5,389},{6,390},{7,391},{8... | collective-permute-start | bytes 1548296 | tf_op jit(solution)/shard_map/ppermute | solution.py:50
  82.6 16.2 %collective-permute-start.6 = (bf16[32,5376]{1,0:T(8,128)(2,1)}, bf16[32,5376]{1,0:T(8,128)(2,1)}, u32[]{:S(2)}, u32[]{:S(2)}) collective-permute-start(bf16[32,5376]{1,0:T(8,128)(2,1)} %collective-permute-done.4.refs_4_), channel_id=1, source_target_pairs={{0,14},{1,15},{2,0},{3,1},{4,2},{5,3},{6,4},{7,5},{8,6},{9,7},{10,... | collective-permute-start | bytes 1032200 | tf_op jit(solution)/shard_map/ppermute | solution.py:50
  87.9 12.8 %collective-permute-start.7 = (bf16[32,5376]{1,0:T(8,128)(2,1)}, bf16[32,5376]{1,0:T(8,128)(2,1)}, u32[]{:S(2)}, u32[]{:S(2)}) collective-permute-start(bf16[32,5376]{1,0:T(8,128)(2,1)} %collective-permute-done.5.refs_0_.refs_5_), channel_id=1, source_target_pairs={{0,2},{1,3},{2,4},{3,5},{4,6},{5,7},{6,8},{7,9},{8,10},{9,11},{10,... | collective-permute-start | bytes 1032200 | tf_op jit(solution)/shard_map/ppermute | solution.py:50
  92.4 44.5 %all-to-all-start.1 = ((bf16[4,48,5376]{2,1,0:T(8,128)(2,1)}), bf16[4,48,5376]{2,1,0:T(8,128)(2,1)}, u32[]{:S(2)}, u32[]{:S(2)}) async-start(bf16[4,48,5376]{2,1,0:T(8,128)(2,1)} %broadcast_in_dim.37), calls=%async_computation.1 | async-start | bytes 4128768 | tf_op jit(solution)/shard_map/all_to_all | solution.py:55
  96.8 40.1 %copy-start.2 = (bf16[32,5376]{1,0:T(8,128)(2,1)S(1)}, bf16[32,5376]{1,0:T(8,128)(2,1)}, u32[]{:S(2)}) copy-start(bf16[32,5376]{1,0:T(8,128)(2,1)} %copy-done.1) | copy-start | bytes 1032196
  96.9 40.1 %copy-start.4 = (bf16[32,5376]{1,0:T(8,128)(2,1)S(1)}, bf16[32,5376]{1,0:T(8,128)(2,1)}, u32[]{:S(2)}) copy-start(bf16[32,5376]{1,0:T(8,128)(2,1)} %copy-done.3) | copy-start | bytes 1032196
  96.9 40.1 %copy-start.13 = (f32[1,512]{1,0:T(1,128)S(1)}, f32[1,512]{1,0:T(1,128)}, u32[]{:S(2)}) copy-start(f32[1,512]{1,0:T(1,128)} %act_ref.1) | copy-start | bytes 6148
  98.8 16.0 %collective-permute-start.13 = (bf16[48,5376]{1,0:T(8,128)(2,1)}, bf16[48,5376]{1,0:T(8,128)(2,1)}, u32[]{:S(2)}, u32[]{:S(2)}) collective-permute-start(bf16[48,5376]{1,0:T(8,128)(2,1)} %dynamic-slice_bitcast_fusion), channel_id=1, source_target_pairs={{0,32},{1,97},{2,34},{3,99},{4,36},{5,101},{6,38},{7,103},{8,40},{... | collective-permute-start | bytes 1548296 | tf_op jit(solution)/shard_map/ppermute | solution.py:50
  102.8 33.1 %collective-permute-start.9 = (bf16[96,5376]{1,0:T(8,128)(2,1)}, bf16[96,5376]{1,0:T(8,128)(2,1)S(1)}, u32[]{:S(2)}, u32[]{:S(2)}) collective-permute-start(bf16[96,5376]{1,0:T(8,128)(2,1)} %shard_map.56), channel_id=1, source_target_pairs={{0,1},{1,0},{2,3},{3,2},{4,5},{5,4},{6,7},{7,6},{8,9},{9,8},{10,11... | collective-permute-start | bytes 3096584 | tf_op jit(solution)/shard_map/ppermute | solution.py:50
  105.8 27.7 %collective-permute-start.15 = (bf16[48,5376]{1,0:T(8,128)(2,1)}, bf16[48,5376]{1,0:T(8,128)(2,1)S(1)}, u32[]{:S(2)}, u32[]{:S(2)}) collective-permute-start(bf16[48,5376]{1,0:T(8,128)(2,1)} %collective-permute-done.14.refs_15_), channel_id=1, source_target_pairs={{0,128},{1,129},{2,130},{3,131},{4,132},{5,133},{6,134},{7,135},{8... | collective-permute-start | bytes 1548296 | tf_op jit(solution)/shard_map/ppermute | solution.py:50
  109.2 25.1 %collective-permute-start.16 = (bf16[48,5376]{1,0:T(8,128)(2,1)}, bf16[48,5376]{1,0:T(8,128)(2,1)S(1)}, u32[]{:S(2)}, u32[]{:S(2)}) collective-permute-start(bf16[48,5376]{1,0:T(8,128)(2,1)} %collective-permute-done.14.refs_15_), channel_id=1, source_target_pairs={{0,384},{1,385},{2,386},{3,387},{4,388},{5,389},{6,390},{7,391},{8... | collective-permute-start | bytes 1548296 | tf_op jit(solution)/shard_map/ppermute | solution.py:50
  114.8 20.3 %collective-permute-start.17 = (bf16[48,5376]{1,0:T(8,128)(2,1)}, bf16[48,5376]{1,0:T(8,128)(2,1)S(1)}, u32[]{:S(2)}, u32[]{:S(2)}) collective-permute-start(bf16[48,5376]{1,0:T(8,128)(2,1)} %collective-permute-done.13.refs_14_), channel_id=1, source_target_pairs={{0,32},{1,97},{2,34},{3,99},{4,36},{5,101},{6,38},{7,103},{8,40},{... | collective-permute-start | bytes 1548296 | tf_op jit(solution)/shard_map/ppermute | solution.py:50
  133.5 0.8 copy-start.7
  134.3 0.8 copy-start.9
  135.1 0.8 copy-start.11
  135.9 1.0 copy-start.5
  136.9 1.2 copy-start.6
  138.2 1.0 copy-start.8
  139.2 1.0 copy-start.10
  140.2 1.0 copy-start.12
